TPU v7x, 32 devices: a whole 2x2x4 slice. The times are simulated.
32 devices in a mesh: batch: 8 (over y, x, core), wide: 4 (over z).
Axes of the slice: x: 2, y: 2, z: 4, core: 2. Of those that a mesh axis runs over, the one named last changes fastest.
Arguments:
- inputs: bfloat16 [2, 8, 2048, 1024], P(None, 'batch', 'wide'), may hold values from -6 to 6
- skips: bfloat16 [2, 8, 2048, 1024], P(None, 'batch', 'wide'), may hold values from -6 to 6
- cotangent: bfloat16 [2, 8, 2048, 1024], P(None, 'batch', 'wide'), may hold values from -6 to 6
- segment_ids: int32 [2, 8, 2048], P(None, 'batch'), may hold values from 0 to 3, never falling along the last dimension, each value on 1 to 1024 neighbouring positions
- time_steps: int32 [2, 8, 4], P(None, 'batch'), may hold values from 0 to 999
- w_skip: bfloat16 [2048, 1024], P(('batch', 'wide')), may hold values from -0.125 to 0.125
- w_qkv: bfloat16 [1024, 3072], P(('batch', 'wide')), may hold values from -0.1875 to 0.1875
- w_out: bfloat16 [1024, 1024], P(('batch', 'wide')), may hold values from -1.5 to 1.5
- w_up: bfloat16 [1024, 4096], P(('batch', 'wide')), may hold values from -0.1875 to 0.1875
- w_down: bfloat16 [4096, 1024], P(('batch', 'wide')), may hold values from -0.09375 to 0.09375
- w_mod: bfloat16 [256, 4096], P(None, ('batch', 'wide')), may hold values from -0.25 to 0.25
Outputs:
- block_out: bfloat16 [2, 8, 2048, 1024], P(None, 'batch', 'wide')
- grad_inputs: bfloat16 [2, 8, 2048, 1024], P(None, 'batch', 'wide')
- grad_skips: bfloat16 [2, 8, 2048, 1024], P(None, 'batch', 'wide')
- grad_w_skip: float32 [2048, 1024], P(('batch', 'wide'))
- grad_w_qkv: float32 [1024, 3072], P(('batch', 'wide'))
- grad_w_out: float32 [1024, 1024], P(('batch', 'wide'))
- grad_w_up: float32 [1024, 4096], P(('batch', 'wide'))
- grad_w_down: float32 [4096, 1024], P(('batch', 'wide'))
- grad_w_mod: float32 [256, 4096], P(None, ('batch', 'wide'))
Inputs may be any that keep to these rules, and one draw needn't show every extreme that they name: `segment_ids`: segment ids never fall along a row; each of the 4 ids holds 1 to 1024 frames of its row, and some row of every draw has an utterance of exactly 1024 frames.
All inputs are finite; a program needn't handle non-finite values.
Results may differ from a plain program's by a relative error of at most 0.017.
Values may be sent and summed in bfloat16 or wider, within the bound.
No kernel may reach another device: no remote copies, remote signals or barrier semaphores. Data moves between devices by JAX's collectives and lax.ppermute only.
A program may use at most 320 MiB of HBM per device.

v0:
```python
import functools
import math

import jax
import jax.numpy as jnp
from jax import lax
from jax.sharding import PartitionSpec as P

HEAD_DIM = 64


def modulate(residual, shift_part, scale_part):
    centred = residual - jnp.mean(residual, axis=-1, keepdims=True)
    variance = jnp.mean(centred * centred, axis=-1, keepdims=True)
    return centred * lax.rsqrt(variance + 1e-06) * (1.0 + scale_part) + shift_part


def tanh_gelu(values):
    return jax.nn.gelu(values, approximate=True)


def sinus(step_ids, freq_width):
    half_dim = freq_width // 2
    frequency = jnp.exp(-math.log(10000.0) * jnp.arange(half_dim, dtype=jnp.float32) / half_dim)
    angles = step_ids.astype(jnp.float32)[..., None] * frequency
    return jnp.concatenate([jnp.sin(angles), jnp.cos(angles)], axis=-1)


def positions(segment_row, labels_count):
    labels = jnp.arange(labels_count, dtype=jnp.int32)
    member = (segment_row[:, None] == labels[None, :]).astype(jnp.int32)
    counts = jnp.sum(member, axis=0)
    starts = jnp.cumsum(counts) - counts
    offsets = jnp.sum(member * starts[None, :], axis=1)
    return jnp.arange(segment_row.shape[0], dtype=jnp.int32) - offsets


def rotate(features, where_at, direction):
    half_dim = features.shape[-1] // 2
    frequency = jnp.exp(-math.log(10000.0) * jnp.arange(half_dim, dtype=jnp.float32) / half_dim)
    angles = where_at.astype(jnp.float32)[..., None] * frequency
    cosine = jnp.cos(angles)[..., None, :]
    sine_part = direction * jnp.sin(angles)[..., None, :]
    first_half = features[..., :half_dim]
    second_half = features[..., half_dim:]
    return jnp.concatenate(
        [
            first_half * cosine - second_half * sine_part,
            second_half * cosine + first_half * sine_part,
        ],
        axis=-1,
    )


def masked_scores(query_part, keys_all, segment_part, segment_rows, score_scale):
    scores = (
        jnp.einsum("rqhd,rkhd->rhqk", query_part, keys_all, preferred_element_type=jnp.float32)
        * score_scale
    )
    allowed = (segment_part[:, :, None] == segment_rows[:, None, :])[:, None]
    return jnp.where(allowed, scores, -1e30)


def attend_forward(queries, keys_all, values_all, segment_rows):
    row_count, length, head_count, head_dim = queries.shape
    block_len = min(512, length)
    count_blocks = length // block_len
    score_scale = 1.0 / math.sqrt(head_dim)

    def one_block(block_index):
        block_start = block_index * block_len
        query_part = lax.dynamic_slice_in_dim(queries, block_start, block_len, 1)
        segment_part = lax.dynamic_slice_in_dim(segment_rows, block_start, block_len, 1)
        scores = masked_scores(query_part, keys_all, segment_part, segment_rows, score_scale)
        highest = jnp.max(scores, axis=-1, keepdims=True)
        powers = jnp.exp(scores - highest)
        totals = jnp.sum(powers, axis=-1, keepdims=True)
        probability = (powers / totals).astype(jnp.bfloat16)
        mixed_part = jnp.einsum(
            "rhqk,rkhd->rqhd", probability, values_all, preferred_element_type=jnp.float32
        )
        return (mixed_part.astype(jnp.bfloat16), (highest + jnp.log(totals))[..., 0])

    mixed_heads, logsum = lax.map(one_block, jnp.arange(count_blocks, dtype=jnp.int32))
    mixed_heads = jnp.moveaxis(mixed_heads, 0, 1).reshape(row_count, length, head_count * head_dim)
    logsum = jnp.moveaxis(logsum, 0, 2).reshape(row_count, head_count, length)
    return (mixed_heads, logsum)


def attend_backward(queries, keys_all, values_all, segment_rows, logsum, grad_heads):
    row_count, length, head_count, head_dim = queries.shape
    block_len = min(512, length)
    count_blocks = length // block_len
    score_scale = 1.0 / math.sqrt(head_dim)

    def one_block(running, block_index):
        grad_keys, grad_values = running
        block_start = block_index * block_len
        query_part = lax.dynamic_slice_in_dim(queries, block_start, block_len, 1)
        segment_part = lax.dynamic_slice_in_dim(segment_rows, block_start, block_len, 1)
        grad_part = lax.dynamic_slice_in_dim(grad_heads, block_start, block_len, 1)
        logsum_part = lax.dynamic_slice_in_dim(logsum, block_start, block_len, 2)
        scores = masked_scores(query_part, keys_all, segment_part, segment_rows, score_scale)
        probability = jnp.exp(scores - logsum_part[..., None])
        grad_values = grad_values + jnp.einsum(
            "rhqk,rqhd->rkhd",
            probability.astype(jnp.bfloat16),
            grad_part,
            preferred_element_type=jnp.float32,
        )
        grad_prob = jnp.einsum(
            "rqhd,rkhd->rhqk", grad_part, values_all, preferred_element_type=jnp.float32
        )
        inner_sum = jnp.sum(probability * grad_prob, axis=-1, keepdims=True)
        grad_scores = (probability * (grad_prob - inner_sum)).astype(jnp.bfloat16)
        grad_query = (
            jnp.einsum("rhqk,rkhd->rqhd", grad_scores, keys_all, preferred_element_type=jnp.float32)
            * score_scale
        )
        grad_keys = (
            grad_keys
            + jnp.einsum(
                "rhqk,rqhd->rkhd", grad_scores, query_part, preferred_element_type=jnp.float32
            )
            * score_scale
        )
        return ((grad_keys, grad_values), grad_query)

    zero_grads = jnp.zeros(keys_all.shape, jnp.float32)
    (grad_keys, grad_values), grad_queries = lax.scan(
        one_block, (zero_grads, zero_grads), jnp.arange(count_blocks, dtype=jnp.int32)
    )
    grad_queries = jnp.moveaxis(grad_queries, 0, 1).reshape(queries.shape)
    return (grad_queries, grad_keys, grad_values)


def run_batch(gathered, inputs, skips, cotangent, segment_rows, step_ids):
    w_skip, w_qkv, w_out, w_up, w_down, w_mod = gathered
    row_count, local_len, model_dim = inputs.shape
    wide_count = lax.axis_size("wide")
    frame_start = lax.axis_index("wide") * local_len
    labels_count = step_ids.shape[-1]
    segment_local = lax.dynamic_slice_in_dim(segment_rows, frame_start, local_len, 1)
    member = (segment_local[..., None] == jnp.arange(labels_count, dtype=jnp.int32)).astype(
        jnp.float32
    )
    stacked = jnp.concatenate([inputs, skips], axis=-1)
    resid_in = jnp.einsum("rfc,cd->rfd", stacked, w_skip, preferred_element_type=jnp.float32)
    embedded = sinus(step_ids, w_mod.shape[0]).astype(jnp.bfloat16)
    modulation = jnp.einsum("rsf,fd->rsd", embedded, w_mod, preferred_element_type=jnp.float32)
    per_frame = jnp.einsum("rfs,rsd->rfd", member, modulation, precision=lax.Precision.HIGHEST)
    shift_one, scale_one, shift_two, scale_two = jnp.split(per_frame, 4, axis=-1)
    normed_one, pull_one = jax.vjp(modulate, resid_in, shift_one, scale_one)
    normed_one = normed_one.astype(jnp.bfloat16)
    projected = jnp.einsum("rfd,de->rfe", normed_one, w_qkv, preferred_element_type=jnp.float32)
    projected = projected.astype(jnp.bfloat16).reshape(row_count, local_len, 3, model_dim)
    by_heads = lax.all_to_all(projected, "wide", split_axis=3, concat_axis=1, tiled=True)
    head_width = model_dim // wide_count
    head_count = head_width // HEAD_DIM
    full_len = by_heads.shape[1]
    shaped = by_heads.reshape(row_count, full_len, 3, head_count, HEAD_DIM)
    where_at = jax.vmap(functools.partial(positions, labels_count=labels_count))(segment_rows)
    queries = rotate(shaped[:, :, 0].astype(jnp.float32), where_at, 1.0).astype(jnp.bfloat16)
    keys_all = rotate(shaped[:, :, 1].astype(jnp.float32), where_at, 1.0).astype(jnp.bfloat16)
    values_all = shaped[:, :, 2]
    mixed_heads, logsum = attend_forward(queries, keys_all, values_all, segment_rows)
    by_frames = lax.all_to_all(mixed_heads, "wide", split_axis=1, concat_axis=2, tiled=True)
    attended = jnp.einsum("rfc,cd->rfd", by_frames, w_out, preferred_element_type=jnp.float32)
    resid_mid = resid_in + attended
    normed_two, pull_two = jax.vjp(modulate, resid_mid, shift_two, scale_two)
    normed_two = normed_two.astype(jnp.bfloat16)
    hidden_pre = jnp.einsum("rfc,ch->rfh", normed_two, w_up, preferred_element_type=jnp.float32)
    activated, pull_gelu = jax.vjp(tanh_gelu, hidden_pre)
    activated = activated.astype(jnp.bfloat16)
    result = resid_mid + jnp.einsum(
        "rfh,hd->rfd", activated, w_down, preferred_element_type=jnp.float32
    )
    grad_down = jnp.einsum("rfh,rfd->hd", activated, cotangent, preferred_element_type=jnp.float32)
    grad_act = jnp.einsum("rfd,hd->rfh", cotangent, w_down, preferred_element_type=jnp.float32)
    grad_pre = pull_gelu(grad_act)[0].astype(jnp.bfloat16)
    grad_up = jnp.einsum("rfc,rfh->ch", normed_two, grad_pre, preferred_element_type=jnp.float32)
    grad_normed_two = jnp.einsum("rfh,ch->rfc", grad_pre, w_up, preferred_element_type=jnp.float32)
    grad_mid_norm, grad_shift_two, grad_scale_two = pull_two(grad_normed_two)
    grad_mid = cotangent.astype(jnp.float32) + grad_mid_norm
    grad_mid_low = grad_mid.astype(jnp.bfloat16)
    grad_out = jnp.einsum(
        "rfc,rfd->cd", by_frames, grad_mid_low, preferred_element_type=jnp.float32
    )
    grad_frames = jnp.einsum("rfd,cd->rfc", grad_mid_low, w_out, preferred_element_type=jnp.float32)
    grad_frames = grad_frames.astype(jnp.bfloat16)
    grad_heads = lax.all_to_all(grad_frames, "wide", split_axis=2, concat_axis=1, tiled=True)
    grad_heads = grad_heads.reshape(row_count, full_len, head_count, HEAD_DIM)
    grad_queries, grad_keys, grad_values = attend_backward(
        queries, keys_all, values_all, segment_rows, logsum, grad_heads
    )
    grad_queries = rotate(grad_queries, where_at, -1.0)
    grad_keys = rotate(grad_keys, where_at, -1.0)
    grad_proj = jnp.stack([grad_queries, grad_keys, grad_values], axis=2).astype(jnp.bfloat16)
    grad_proj = grad_proj.reshape(row_count, full_len, 3, head_width)
    grad_proj = lax.all_to_all(grad_proj, "wide", split_axis=1, concat_axis=3, tiled=True)
    grad_proj = grad_proj.reshape(row_count, local_len, 3 * model_dim)
    grad_qkv = jnp.einsum("rfd,rfe->de", normed_one, grad_proj, preferred_element_type=jnp.float32)
    grad_normed_one = jnp.einsum(
        "rfe,de->rfd", grad_proj, w_qkv, preferred_element_type=jnp.float32
    )
    grad_in_norm, grad_shift_one, grad_scale_one = pull_one(grad_normed_one)
    grad_in = (grad_mid + grad_in_norm).astype(jnp.bfloat16)
    grad_skip_w = jnp.einsum("rfc,rfd->cd", stacked, grad_in, preferred_element_type=jnp.float32)
    grad_stacked = jnp.einsum("rfd,cd->rfc", grad_in, w_skip, preferred_element_type=jnp.float32)
    grad_stacked = grad_stacked.astype(jnp.bfloat16)
    grad_per_frame = jnp.concatenate(
        [grad_shift_one, grad_scale_one, grad_shift_two, grad_scale_two], axis=-1
    )
    grad_modulation = jnp.einsum(
        "rfs,rfd->rsd", member, grad_per_frame, precision=lax.Precision.HIGHEST
    )
    grad_mod = jnp.einsum(
        "rsf,rsd->fd",
        embedded.astype(jnp.float32),
        grad_modulation,
        precision=lax.Precision.HIGHEST,
    )
    grad_terms = (grad_skip_w, grad_qkv, grad_out, grad_up, grad_down, grad_mod)
    return (
        result.astype(jnp.bfloat16),
        grad_stacked[..., :model_dim],
        grad_stacked[..., model_dim:],
        grad_terms,
    )


def body(
    inputs, skips, cotangent, segment_ids, time_steps, w_skip, w_qkv, w_out, w_up, w_down, w_mod
):
    outputs = []
    grad_input_list = []
    grad_skip_list = []
    totals = None
    for batch_index in range(inputs.shape[0]):
        gathered = (
            lax.all_gather(w_skip, ("batch", "wide"), axis=0, tiled=True),
            lax.all_gather(w_qkv, ("batch", "wide"), axis=0, tiled=True),
            lax.all_gather(w_out, ("batch", "wide"), axis=0, tiled=True),
            lax.all_gather(w_up, ("batch", "wide"), axis=0, tiled=True),
            lax.all_gather(w_down, ("batch", "wide"), axis=0, tiled=True),
            lax.all_gather(w_mod, ("batch", "wide"), axis=1, tiled=True),
        )
        result, grad_input, grad_skip, grad_terms = run_batch(
            gathered,
            inputs[batch_index],
            skips[batch_index],
            cotangent[batch_index],
            segment_ids[batch_index],
            time_steps[batch_index],
        )
        outputs.append(result)
        grad_input_list.append(grad_input)
        grad_skip_list.append(grad_skip)
        grad_terms = (
            lax.psum_scatter(grad_terms[0], ("batch", "wide"), scatter_dimension=0, tiled=True),
            lax.psum_scatter(grad_terms[1], ("batch", "wide"), scatter_dimension=0, tiled=True),
            lax.psum_scatter(grad_terms[2], ("batch", "wide"), scatter_dimension=0, tiled=True),
            lax.psum_scatter(grad_terms[3], ("batch", "wide"), scatter_dimension=0, tiled=True),
            lax.psum_scatter(grad_terms[4], ("batch", "wide"), scatter_dimension=0, tiled=True),
            lax.psum_scatter(grad_terms[5], ("batch", "wide"), scatter_dimension=1, tiled=True),
        )
        if totals is None:
            totals = tuple(grad_terms)
        else:
            totals = tuple((earlier + latest for earlier, latest in zip(totals, grad_terms)))
    return (
        jnp.stack(outputs),
        jnp.stack(grad_input_list),
        jnp.stack(grad_skip_list),
        totals[0],
        totals[1],
        totals[2],
        totals[3],
        totals[4],
        totals[5],
    )


def solution(mesh):
    placed = (
        P(None, "batch", "wide", None),
        P(None, "batch", "wide", None),
        P(None, "batch", "wide", None),
        P(None, "batch", None),
        P(None, "batch", None),
        P(("batch", "wide"), None),
        P(("batch", "wide"), None),
        P(("batch", "wide"), None),
        P(("batch", "wide"), None),
        P(("batch", "wide"), None),
        P(None, ("batch", "wide")),
    )
    return jax.shard_map(
        body,
        mesh=mesh,
        in_specs=placed,
        out_specs=(
            P(None, "batch", "wide", None),
            P(None, "batch", "wide", None),
            P(None, "batch", "wide", None),
            P(("batch", "wide"), None),
            P(("batch", "wide"), None),
            P(("batch", "wide"), None),
            P(("batch", "wide"), None),
            P(("batch", "wide"), None),
            P(None, ("batch", "wide")),
        ),
        check_vma=False,
    )
```

profile of v0, /device:TPU:0, one launch (start us, length us, event | category | flops | bytes accessed | tf_op | source)
XLA Modules:
  0.0 2747.1 jit_solution(576185961764375189)
XLA Ops:
  17.0 49.9 %all-gather.9.cloned.1.call-done = bf16[256,4096]{1,0:T(8,128)(2,1)} async-done(((bf16[256,128]{1,0:T(8,128)(2,1)}), bf16[256,4096]{1,0:T(8,128)(2,1)}) %all-gather.9.cloned.1.call-update) | async-done | bytes 2097168 | tf_op jit(solution)/shard_map/all_gather | solution.py:246
  74.6 56.3 %all-gather.7.cloned.1.call-done = bf16[2048,1024]{1,0:T(8,128)(2,1)} async-done(((bf16[64,1024]{1,0:T(8,128)(2,1)}), bf16[2048,1024]{1,0:T(8,128)(2,1)}) %all-gather.7.cloned.1.call-update) | async-done | bytes 4194320 | tf_op jit(solution)/shard_map/all_gather | solution.py:241
  137.6 64.4 %all-gather.11.cloned.1.call-done = bf16[1024,3072]{1,0:T(8,128)(2,1)} async-done(((bf16[32,3072]{1,0:T(8,128)(2,1)}), bf16[1024,3072]{1,0:T(8,128)(2,1)}) %all-gather.11.cloned.1.call-update) | async-done | bytes 6291472 | tf_op jit(solution)/shard_map/all_gather | solution.py:242
  248.9 79.6 %all-to-all-done.2 = bf16[1,512,3,1024]{1,2,0,3:T(4,128)(2,1)} async-done(((bf16[1,512,3,1024]{1,2,0,3:T(4,128)(2,1)}), bf16[1,512,3,1024]{1,2,0,3:T(4,128)(2,1)}, u32[]{:S(2)}, u32[]{:S(2)}) %all-to-all-start.2) | async-done | bytes 3145760 | tf_op jit(solution)/shard_map/all_to_all | solution.py:157
  347.5 61.8 %while.55 = (s32[]{:T(128)}, bf16[4,1,512,4,64]{2,4,3,1,0:T(8,128)(2,1)}, f32[4,1,4,512]{3,2,1,0:T(4,128)S(1)}, s32[4]{0:T(128)S(1)}, s32[1,2048]{1,0:T(1,128)S(...) while((s32[]{:T(128)}, ...), condition=%wide.region_19.20_spmd, body=%wide.region_16.19_spmd.sunk | while | flops 1125251072 | bytes 57227472 | solution.py:84
  435.8 24.7 all-to-all-done
  478.6 67.9 %while.54 = (s32[]{:T(128)}, bf16[4,1,512,4,64]{2,4,3,1,0:T(8,128)(2,1)S(1)}, f32[4,1,4,512]{3,2,1,0:T(4,128)S(1)}, s32[4]{0:T(128)S(1)}, s32[1,2048]{1,0:T(1,12...) while((s32[]{:T(128)}, ...), condition=%wide.region_8.9_spmd, body=%wide.region_5.8_spmd.sunk | while | flops 1125251072 | bytes 57227472 | solution.py:84
  582.1 18.7 all-to-all-done.1
  633.3 13.0 fusion.98
  668.6 15.2 fusion.105
  760.4 248.6 %while.56 = (s32[]{:T(128)}, f32[1,2048,4,64]{1,3,2,0:T(8,128)}, f32[1,2048,4,64]{1,3,2,0:T(8,128)}, f32[4,1,512,4,64]{2,0,4,3,1:T(4,128)}, s32[4]{0:T(128)S(1)}...) while((s32[]{:T(128)}, f32[1,2048,4,64]{1,3,2,0:T(8,128)}, ...), condition=%wide.region_26.27_spmd.clone, body=%wide.region_24.26_spmd.clone.sunk | while | flops 2751068160 | bytes 258841104 | solution.py:130
  769.2 12.8 multiply_reduce_fusion.8
  830.8 12.8 multiply_reduce_fusion.8
  893.0 12.8 multiply_reduce_fusion.8
  955.1 12.8 multiply_reduce_fusion.8
  1036.2 248.8 %while.57 = (s32[]{:T(128)}, f32[1,2048,4,64]{1,3,2,0:T(8,128)}, f32[1,2048,4,64]{1,3,2,0:T(8,128)}, f32[4,1,512,4,64]{2,0,4,3,1:T(4,128)}, s32[4]{0:T(128)S(1)}...) while((s32[]{:T(128)}, f32[1,2048,4,64]{1,3,2,0:T(8,128)}, ...), condition=%wide.region_33.34_spmd.clone, body=%wide.region_31.33_spmd.clone.sunk | while | flops 2751068160 | bytes 258578896 | solution.py:130
  1323.3 124.2 %all-to-all-done.7 = bf16[1,2048,3,256]{3,2,0,1:T(4,128)(2,1)} async-done(((bf16[1,2048,3,256]{3,2,0,1:T(4,128)(2,1)}), bf16[1,2048,3,256]{3,2,0,1:T(4,128)(2,1)}, u32[]{:S(2)}, u32[]{:S(2)}) %all-to-all-start.7) | async-done | bytes 3145760 | tf_op jit(solution)/shard_map/all_to_all | solution.py:200
  1543.8 15.0 fusion.160
  1558.8 14.8 convolution_add_fusion.1
  1608.3 53.1 %reduce-scatter.17.cloned.1.call-done = f32[256,128]{1,0:T(8,128)} async-done(((f32[256,4096]{1,0:T(8,128)}), f32[256,128]{1,0:T(8,128)}) %reduce-scatter.17.cloned.1.call-update) | async-done | bytes 131088 | tf_op jit(solution)/shard_map/reduce_scatter | solution.py:265
  1661.4 187.6 %reduce-scatter.7.cloned.1.call-done = f32[64,1024]{1,0:T(8,128)} async-done(((f32[2048,1024]{1,0:T(8,128)}), f32[64,1024]{1,0:T(8,128)}) %reduce-scatter.7.cloned.1.call-update) | async-done | bytes 262160 | tf_op jit(solution)/shard_map/reduce_scatter | solution.py:260
  1849.0 159.6 %reduce-scatter.9.cloned.1.call-done = f32[32,3072]{1,0:T(8,128)} async-done(((f32[1024,3072]{1,0:T(8,128)}), f32[32,3072]{1,0:T(8,128)}) %reduce-scatter.9.cloned.1.call-update) | async-done | bytes 393232 | tf_op jit(solution)/shard_map/reduce_scatter | solution.py:261
  2008.5 366.3 %reduce-scatter.13.cloned.1.call-done = f32[32,4096]{1,0:T(8,128)} async-done(((f32[1024,4096]{1,0:T(8,128)}), f32[32,4096]{1,0:T(8,128)}) %reduce-scatter.13.cloned.1.call-update) | async-done | bytes 524304 | tf_op jit(solution)/shard_map/reduce_scatter | solution.py:263
  2374.8 365.0 %reduce-scatter.15.cloned.1.call-done = f32[128,1024]{1,0:T(8,128)} async-done(((f32[4096,1024]{1,0:T(8,128)}), f32[128,1024]{1,0:T(8,128)}) %reduce-scatter.15.cloned.1.call-update) | async-done | bytes 524304 | tf_op jit(solution)/shard_map/reduce_scatter | solution.py:264
  (763 shorter events, 1059.1 us)
Async XLA Ops:
  7.2 59.7 %all-gather.9.cloned.1.call-start = ((), (), s32[]{:S(2)}) async-start(), calls=%async_computation.15 | async-start | bytes 2162688 | tf_op jit(solution)/shard_map/all_gather | solution.py:246
  7.9 123.0 %all-gather.7.cloned.1.call-start = ((), (), s32[]{:S(2)}) async-start(), calls=%async_computation.14 | async-start | bytes 4325376 | tf_op jit(solution)/shard_map/all_gather | solution.py:241
  8.7 193.3 %all-gather.11.cloned.1.call-start = ((), (), s32[]{:S(2)}) async-start(), calls=%async_computation.16 | async-start | bytes 6488064 | tf_op jit(solution)/shard_map/all_gather | solution.py:242
  9.4 600.6 %all-gather.13.cloned.1.call-start = ((), (), s32[]{:S(2)}) async-start(), calls=%async_computation.17 | async-start | bytes 2162688 | tf_op jit(solution)/shard_map/all_gather | solution.py:243
  10.0 611.7 %all-gather.15.cloned.1.call-start = ((), (), s32[]{:S(2)}) async-start(), calls=%async_computation.18 | async-start | bytes 8650752 | tf_op jit(solution)/shard_map/all_gather | solution.py:244
  11.9 211.9 %copy-start.71 = (s32[1,1,2048]{2,1,0:T(1,128)}, s32[1,1,2048]{2,1,0:T(1,128)S(1)}, u32[]{:S(2)}) copy-start(s32[1,1,2048]{2,1,0:T(1,128)S(1)} %get-tuple-element.863) | copy-start | bytes 24580
  11.9 215.4 %copy-start.93 = (s32[1,1,512]{2,1,0:T(1,128)}, s32[1,1,512]{2,1,0:T(1,128)S(1)}, u32[]{:S(2)}) copy-start(s32[1,1,512]{2,1,0:T(1,128)S(1)} %get-tuple-element.503) | copy-start | bytes 6148
  12.7 214.2 %copy-start.123 = (bf16[4,128]{1,0:T(4,128)(2,1)}, bf16[4,128]{1,0:T(4,128)(2,1)S(1)}, u32[]{:S(2)}) copy-start(bf16[4,128]{1,0:T(4,128)(2,1)S(1)} %get-tuple-element.473) | copy-start | bytes 3076
  12.7 214.2 %copy-start.125 = (bf16[4,128]{1,0:T(4,128)(2,1)}, bf16[4,128]{1,0:T(4,128)(2,1)S(1)}, u32[]{:S(2)}) copy-start(bf16[4,128]{1,0:T(4,128)(2,1)S(1)} %get-tuple-element.474) | copy-start | bytes 3076
  217.5 111.0 %all-to-all-start.2 = ((bf16[1,512,3,1024]{1,2,0,3:T(4,128)(2,1)}), bf16[1,512,3,1024]{1,2,0,3:T(4,128)(2,1)}, u32[]{:S(2)}, u32[]{:S(2)}) async-start(bf16[1,512,3,1024]{1,2,0,3:T(4,128)(2,1)} %copy.152), calls=%async_computation.2 | async-start | bytes 8388608 | tf_op jit(solution)/shard_map/all_to_all | solution.py:157
  222.5 410.8 %all-gather.17.cloned.1.call-start = ((), (), s32[]{:S(2)}) async-start(), calls=%async_computation.19 | async-start | bytes 8650752 | tf_op jit(solution)/shard_map/all_gather | solution.py:245
  328.5 132.0 %all-to-all-start = ((bf16[1,512,3,1024]{1,2,0,3:T(4,128)(2,1)}), bf16[1,512,3,1024]{1,2,0,3:T(4,128)(2,1)}, u32[]{:S(2)}, u32[]{:S(2)}) async-start(bf16[1,512,3,1024]{1,2,0,3:T(4,128)(2,1)} %copy.145), calls=%async_computation | async-start | bytes 8388608 | tf_op jit(solution)/shard_map/all_to_all | solution.py:157
  460.5 110.0 %all-to-all-start.3 = ((bf16[4,2,65536]{2,1,0:T(2,128)(2,1)}), bf16[4,2,65536]{2,1,0:T(2,128)(2,1)}, u32[]{:S(2)}, u32[]{:S(2)}) async-start(bf16[4,2,65536]{2,1,0:T(2,128)(2,1)} %reshape.1998), calls=%async_computation.3 | async-start | bytes 2097152 | tf_op jit(solution)/shard_map/all_to_all | solution.py:167
  570.5 30.3 %all-to-all-start.1 = ((bf16[4,2,65536]{2,1,0:T(2,128)(2,1)}), bf16[4,2,65536]{2,1,0:T(2,128)(2,1)}, u32[]{:S(2)}, u32[]{:S(2)}) async-start(bf16[4,2,65536]{2,1,0:T(2,128)(2,1)} %reshape.2000), calls=%async_computation.1 | async-start | bytes 2097152 | tf_op jit(solution)/shard_map/all_to_all | solution.py:167
  719.4 29.7 %all-to-all-start.4 = ((bf16[4,2,65536]{2,1,0:T(2,128)(2,1)}), bf16[4,2,65536]{2,1,0:T(2,128)(2,1)}, u32[]{:S(2)}, u32[]{:S(2)}) async-start(bf16[4,2,65536]{2,1,0:T(2,128)(2,1)} %reshape.2004), calls=%async_computation.4 | async-start | bytes 2097152 | tf_op jit(solution)/shard_map/all_to_all | solution.py:191
  749.1 275.0 %all-to-all-start.6 = ((bf16[4,2,65536]{2,1,0:T(2,128)(2,1)}), bf16[4,2,65536]{2,1,0:T(2,128)(2,1)}, u32[]{:S(2)}, u32[]{:S(2)}) async-start(bf16[4,2,65536]{2,1,0:T(2,128)(2,1)} %reshape.2002), calls=%async_computation.6 | async-start | bytes 2097152 | tf_op jit(solution)/shard_map/all_to_all | solution.py:191
  1024.1 276.0 %all-to-all-start.5 = ((bf16[1,2048,3,256]{3,2,0,1:T(4,128)(2,1)}), bf16[1,2048,3,256]{3,2,0,1:T(4,128)(2,1)}, u32[]{:S(2)}, u32[]{:S(2)}) async-start(bf16[1,2048,3,256]{3,2,0,1:T(4,128)(2,1)} %copy.161), calls=%async_computation.5 | async-start | bytes 8388608 | tf_op jit(solution)/shard_map/all_to_all | solution.py:200
  1300.1 147.4 %all-to-all-start.7 = ((bf16[1,2048,3,256]{3,2,0,1:T(4,128)(2,1)}), bf16[1,2048,3,256]{3,2,0,1:T(4,128)(2,1)}, u32[]{:S(2)}, u32[]{:S(2)}) async-start(bf16[1,2048,3,256]{3,2,0,1:T(4,128)(2,1)} %copy.167), calls=%async_computation.7 | async-start | bytes 8388608 | tf_op jit(solution)/shard_map/all_to_all | solution.py:200
  1305.4 302.9 %reduce-scatter.11.cloned.1.call-start = ((), (), s32[]{:S(2)}) async-start(), calls=%async_computation.22 | async-start | bytes 4325376 | tf_op jit(solution)/shard_map/reduce_scatter | solution.py:262
  1311.4 350.0 %reduce-scatter.17.cloned.1.call-start = ((), (), s32[]{:S(2)}) async-start(), calls=%async_computation.25 | async-start | bytes 4325376 | tf_op jit(solution)/shard_map/reduce_scatter | solution.py:265
  1488.3 360.7 %reduce-scatter.7.cloned.1.call-start = ((), (), s32[]{:S(2)}) async-start(), calls=%async_computation.20 | async-start | bytes 8650752 | tf_op jit(solution)/shard_map/reduce_scatter | solution.py:260
  1506.2 502.3 %reduce-scatter.9.cloned.1.call-start = ((), (), s32[]{:S(2)}) async-start(), calls=%async_computation.21 | async-start | bytes 12976128 | tf_op jit(solution)/shard_map/reduce_scatter | solution.py:261
  1518.6 856.2 %reduce-scatter.13.cloned.1.call-start = ((), (), s32[]{:S(2)}) async-start(), calls=%async_computation.23 | async-start | bytes 17301504 | tf_op jit(solution)/shard_map/reduce_scatter | solution.py:263
  1542.2 1197.6 %reduce-scatter.15.cloned.1.call-start = ((), (), s32[]{:S(2)}) async-start(), calls=%async_computation.24 | async-start | bytes 17301504 | tf_op jit(solution)/shard_map/reduce_scatter | solution.py:264
  (192 other events, 2055.0 us)
Sparse Core Ops, SparseCore 0:
  10.9 55.9 all-gather.8
  69.8 60.9 all-gather.6
  133.8 68.0 all-gather.10
  204.7 75.5 all-gather.12
  283.0 157.9 all-gather.14
  443.8 95.2 all-gather.16
  1311.5 198.1 reduce-scatter.10
  1512.5 148.8 reduce-scatter.16
  1664.3 184.6 reduce-scatter.6
  1855.4 153.0 reduce-scatter.8
  2011.5 363.2 reduce-scatter.12
  2377.6 362.1 reduce-scatter.14
where the time goes:
time: 2760 us; the launch traced here: 2750 us
  waiting for transfers between devices  1560 us (57%)
  matrix products  591 us (21%)
  local copies, waits for them, and re-layouts  287 us (10%)
  other arithmetic  243 us (9%)
  starting transfers between devices  39.4 us (1%)
    reduce_scatter x1, waiting for transfers between devices, body(): lax.psum_scatter(grad_terms[3], ('batch', 'wide'), scatter_dimension=0, t...  366 us
    reduce_scatter x1, waiting for transfers between devices, body(): lax.psum_scatter(grad_terms[4], ('batch', 'wide'), scatter_dimension=0, t...  365 us
    reduce_scatter x1, waiting for transfers between devices, body(): lax.psum_scatter(grad_terms[0], ('batch', 'wide'), scatter_dimension=0, t...  188 us
    reduce_scatter x1, waiting for transfers between devices, body(): lax.psum_scatter(grad_terms[1], ('batch', 'wide'), scatter_dimension=0, t...  160 us
    all_to_all x2, waiting for transfers between devices, run_batch(): lax.all_to_all(grad_proj, 'wide', split_axis=1, concat_axis=3, tiled=True)  124 us
    all_to_all x2, waiting for transfers between devices, run_batch(): lax.all_to_all(projected, 'wide', split_axis=3, concat_axis=1, tiled=True)  104 us
    dot_general x8, matrix products, one_block(): jnp.einsum('rqhd,rkhd->rhqk', grad_part, values_all, preferred_element_ty...  103 us
    dynamic_update_slice x16, local copies, waits for them, and re-layouts, attend_backward(): lax.scan(one_block, (zero_grads, zero_grads), jnp.arange(count_blocks, dt...  92.9 us
  transfers between devices with their start and end apart: 20, of which 13 were waited for; matrix products, arithmetic and copies ran while one was open for 37% of the time, Pallas kernels for 0%

commit v1 on v0

v1 whole, which is shorter than its diff:
```python
import functools
import math

import jax
import jax.numpy as jnp
from jax import lax
from jax.experimental import pallas as pl
from jax.experimental.pallas import tpu as pltpu
from jax.sharding import Mesh
from jax.sharding import PartitionSpec as P

HEAD_DIM = 64
PAIR = 2 * HEAD_DIM
BLOCK = 256
VMEM_BYTES = 60 * 1024 * 1024
ROW_AXES = ("core", "lo")
LINE_AXES = ("core", "hi", "lo")
ALL_AXES = ("plane", "core", "hi", "lo")
f32 = jnp.float32
bf16 = jnp.bfloat16


def dot_nn(left, right):
    return lax.dot_general(left, right, (((1,), (0,)), ((), ())), preferred_element_type=f32)


def dot_nt(left, right):
    return lax.dot_general(left, right, (((1,), (1,)), ((), ())), preferred_element_type=f32)


def dot_tn(left, right):
    return lax.dot_general(left, right, (((0,), (0,)), ((), ())), preferred_element_type=f32)


def params(*semantics):
    return pltpu.CompilerParams(dimension_semantics=semantics, vmem_limit_bytes=VMEM_BYTES)


def cost(flops, moved, special=0):
    return pl.CostEstimate(flops=int(flops), bytes_accessed=int(moved), transcendentals=int(special))


def choose(segment_column, table_ref):
    count = table_ref.shape[0]
    picked = table_ref[count - 1 : count, :]
    for label in range(count - 2, -1, -1):
        picked = jnp.where(segment_column == label, table_ref[label : label + 1, :], picked)
    return picked


def normalise(values):
    centred = values - jnp.mean(values, axis=-1, keepdims=True)
    variance = jnp.mean(centred * centred, axis=-1, keepdims=True)
    inverse = lax.rsqrt(variance + 1e-06)
    return centred * inverse, inverse


def skip_norm_kernel(x_ref, s_ref, top_ref, bottom_ref, seg_ref, shift_ref, scale_ref, resid_ref, normed_ref):
    resid = dot_nn(x_ref[...], top_ref[...]) + dot_nn(s_ref[...], bottom_ref[...])
    resid_ref[...] = resid
    unit, _ = normalise(resid)
    label = seg_ref[...]
    normed = unit * (1.0 + choose(label, scale_ref)) + choose(label, shift_ref)
    normed_ref[...] = normed.astype(bf16)


def out_norm_kernel(mixed_ref, w_ref, resid_in_ref, seg_ref, shift_ref, scale_ref, resid_ref, normed_ref):
    resid = resid_in_ref[...] + dot_nn(mixed_ref[...], w_ref[...])
    resid_ref[...] = resid
    unit, _ = normalise(resid)
    label = seg_ref[...]
    normed = unit * (1.0 + choose(label, scale_ref)) + choose(label, shift_ref)
    normed_ref[...] = normed.astype(bf16)


def segment_sums(row_labels, values, total_ref):
    members = lax.broadcasted_iota(jnp.int32, (total_ref.shape[0], row_labels.shape[1]), 0) == row_labels
    members = members.astype(f32).astype(bf16)
    high = values.astype(bf16)
    low = (values - high.astype(f32)).astype(bf16)
    total_ref[...] += dot_nn(members, high) + dot_nn(members, low)


def norm_pull(grad, resid, scale):
    unit, inverse = normalise(resid)
    inner = grad * (1.0 + scale)
    pulled = inverse * (
        inner
        - jnp.mean(inner, axis=-1, keepdims=True)
        - unit * jnp.mean(inner * unit, axis=-1, keepdims=True)
    )
    return pulled, grad * unit


def norm_two_back_kernel(
    g_ref, resid_ref, cot_ref, seg_ref, segr_ref, scale_ref, w_ref, mid_ref, low_ref, mix_ref, dshift_ref, dscale_ref
):
    @pl.when(pl.program_id(0) == 0)
    def _():
        dshift_ref[...] = jnp.zeros_like(dshift_ref)
        dscale_ref[...] = jnp.zeros_like(dscale_ref)

    grad = g_ref[...]
    pulled, by_scale = norm_pull(grad, resid_ref[...], choose(seg_ref[...], scale_ref))
    grad_mid = cot_ref[...].astype(f32) + pulled
    low = grad_mid.astype(bf16)
    mid_ref[...] = grad_mid
    low_ref[...] = low
    mix_ref[...] = dot_nt(low, w_ref[...]).astype(bf16)
    segment_sums(segr_ref[...], grad, dshift_ref)
    segment_sums(segr_ref[...], by_scale, dscale_ref)


def norm_one_back_kernel(
    own_ref, other_ref, resid_ref, mid_ref, seg_ref, segr_ref, scale_ref, grad_ref, dshift_ref, dscale_ref
):
    @pl.when(pl.program_id(0) == 0)
    def _():
        dshift_ref[...] = jnp.zeros_like(dshift_ref)
        dscale_ref[...] = jnp.zeros_like(dscale_ref)

    grad = own_ref[...] + other_ref[...].astype(f32)
    pulled, by_scale = norm_pull(grad, resid_ref[...], choose(seg_ref[...], scale_ref))
    grad_ref[...] = (mid_ref[...] + pulled).astype(bf16)
    segment_sums(segr_ref[...], grad, dshift_ref)
    segment_sums(segr_ref[...], by_scale, dscale_ref)


def rowwise(kernel, frames, blocked, whole, outs, sums=0, flops=0):
    tile = min(BLOCK, frames)
    in_specs, args, moved = [], [], 0
    for kind, value in blocked:
        if kind == "row":
            in_specs.append(pl.BlockSpec((1, tile), lambda i: (0, i)))
        elif kind == "whole":
            in_specs.append(pl.BlockSpec(value.shape, lambda i: (0, 0)))
        else:
            in_specs.append(pl.BlockSpec((tile, value.shape[1]), lambda i: (i, 0)))
        args.append(value)
        moved += value.size * value.dtype.itemsize
    out_specs, shapes = [], []
    for width, kind in outs:
        out_specs.append(pl.BlockSpec((tile, width), lambda i: (i, 0)))
        shapes.append(jax.ShapeDtypeStruct((frames, width), kind))
        moved += frames * width * jnp.dtype(kind).itemsize
    for _ in range(sums):
        out_specs.append(pl.BlockSpec((8, outs[0][0]), lambda i: (0, 0)))
        shapes.append(jax.ShapeDtypeStruct((8, outs[0][0]), f32))
    return pl.pallas_call(
        kernel,
        grid=(frames // tile,),
        in_specs=in_specs,
        out_specs=out_specs,
        out_shape=shapes,
        compiler_params=params("arbitrary"),
        cost_estimate=cost(flops, moved),
    )(*args)


def swap_halves(values, lanes):
    half = HEAD_DIM // 2
    ahead = pltpu.roll(values, PAIR - half, 1)
    behind = pltpu.roll(values, half, 1)
    return jnp.where(lanes % HEAD_DIM < half, ahead, behind)


def attend_forward_kernel(
    range_ref, q_ref, k_ref, v_ref, cos_ref, sin_ref, segc_ref, segr_ref,
    out_ref, qrot_ref, krot_ref, lse_ref, scores, seg_wide,
):
    length = q_ref.shape[0]
    blocks = length // BLOCK
    lanes = lax.broadcasted_iota(jnp.int32, (BLOCK, PAIR), 1)
    first = lanes < HEAD_DIM

    def turn(i, carry):
        rows = pl.ds(pl.multiple_of(i * BLOCK, BLOCK), BLOCK)
        cosine, sine = cos_ref[rows, :], sin_ref[rows, :]
        for source, target, factor in ((q_ref, qrot_ref, HEAD_DIM**-0.5), (k_ref, krot_ref, None)):
            values = source[rows, :].astype(f32)
            turned = (values * cosine + swap_halves(values, lanes) * sine).astype(bf16)
            if factor is not None:
                turned = turned * jnp.asarray(factor, bf16)
            target[rows, :] = turned
        seg_wide[rows, :] = jnp.broadcast_to(segc_ref[rows, :], (BLOCK, PAIR))
        return carry

    lax.fori_loop(0, blocks, turn, 0)

    def one_query(i, carry):
        rows = pl.ds(pl.multiple_of(i * BLOCK, BLOCK), BLOCK)
        low, high = range_ref[0, i], range_ref[1, i]
        query = qrot_ref[rows, :]
        zero = jnp.zeros_like(query)
        both = jnp.concatenate([jnp.where(first, query, zero), jnp.where(first, zero, query)], axis=0)
        label = seg_wide[rows, :]
        label = jnp.concatenate([label] * (BLOCK // PAIR), axis=1)

        def score(j, highest):
            keys = krot_ref[pl.ds(pl.multiple_of(j * BLOCK, BLOCK), BLOCK), :]
            found = dot_nt(both, keys)
            allowed = label == segr_ref[:, pl.ds(pl.multiple_of(j * BLOCK, BLOCK), BLOCK)]
            allowed = jnp.concatenate([allowed, allowed], axis=0)
            found = jnp.where(allowed, found, -1e30)
            scores[j] = found
            for part in range(BLOCK // PAIR):
                highest = jnp.maximum(highest, found[:, part * PAIR : (part + 1) * PAIR])
            return highest

        highest = lax.fori_loop(low, high, score, jnp.full((2 * BLOCK, PAIR), -1e30, f32))
        highest = jnp.max(highest, axis=1, keepdims=True)

        def gather(j, running):
            totals, mixed = running
            powers = jnp.exp(scores[j] - highest)
            for part in range(BLOCK // PAIR):
                totals = totals + powers[:, part * PAIR : (part + 1) * PAIR]
            values = v_ref[pl.ds(pl.multiple_of(j * BLOCK, BLOCK), BLOCK), :]
            return totals, mixed + dot_nn(powers.astype(bf16), values)

        blank = jnp.zeros((2 * BLOCK, PAIR), f32)
        totals, mixed = lax.fori_loop(low, high, gather, (blank, blank))
        totals = jnp.sum(totals, axis=1, keepdims=True)
        mixed = mixed * (1.0 / totals)
        logsum = jnp.broadcast_to(highest + jnp.log(totals), (2 * BLOCK, PAIR))
        out_ref[rows, :] = jnp.where(first, mixed[:BLOCK], mixed[BLOCK:]).astype(bf16)
        turned = jnp.where(first, logsum[:BLOCK], logsum[BLOCK:]).T
        lse_ref[0, 0:1, rows] = turned[0:1]
        lse_ref[0, 1:2, rows] = turned[HEAD_DIM : HEAD_DIM + 1]
        return carry

    lax.fori_loop(0, blocks, one_query, 0)


def attend_forward(ranges, projected, cosine, sine, seg_column, seg_row):
    length, width = projected.shape
    width //= 3
    pairs = width // PAIR
    panel = lambda shift: pl.BlockSpec((length, PAIR), lambda p, r: (0, shift * pairs + p))
    whole = lambda shape: pl.BlockSpec(shape, lambda p, r: (0,) * len(shape))
    return pl.pallas_call(
        attend_forward_kernel,
        grid_spec=pltpu.PrefetchScalarGridSpec(
            num_scalar_prefetch=1,
            grid=(pairs,),
            in_specs=[panel(0), panel(1), panel(2), whole(cosine.shape), whole(sine.shape),
                      whole(seg_column.shape), whole(seg_row.shape)],
            out_specs=[panel(0), panel(0), panel(0), pl.BlockSpec((1, 2, length), lambda p, r: (p, 0, 0))],
            scratch_shapes=[
                pltpu.VMEM((length // BLOCK, 2 * BLOCK, BLOCK), f32),
                pltpu.VMEM((length, PAIR), jnp.int32),
            ],
        ),
        out_shape=[jax.ShapeDtypeStruct((length, width), bf16)] * 3
        + [jax.ShapeDtypeStruct((pairs, 2, length), f32)],
        compiler_params=params("arbitrary"),
        cost_estimate=cost(4 * length * length * width, 14 * length * width, length * length * 2 * pairs),
    )(ranges, projected, projected, projected, cosine, sine, seg_column, seg_row)


def attend_backward_kernel(
    range_ref, q_ref, k_ref, v_ref, out_ref, do_ref, lse_ref, cos_ref, sin_ref, segc_ref, segr_ref,
    grad_ref, dq, dk_low, dv_low, delta, seg_wide,
):
    length = q_ref.shape[0]
    blocks = length // BLOCK
    step = pl.program_id(1)

    def span(i):
        return pl.ds(pl.multiple_of(i * BLOCK, BLOCK), BLOCK)

    @pl.when(step == 0)
    def _():
        lanes = lax.broadcasted_iota(jnp.int32, (BLOCK, PAIR), 1)
        first = lanes < HEAD_DIM
        picker = (
            lax.broadcasted_iota(jnp.int32, (8, PAIR), 0)
            == lax.broadcasted_iota(jnp.int32, (8, PAIR), 1) // HEAD_DIM
        ).astype(f32)

        def prepare(i, carry):
            rows = span(i)
            product = do_ref[rows, :].astype(f32) * out_ref[rows, :].astype(f32)
            delta[:, rows] = lax.dot_general(
                picker, product, (((1,), (1,)), ((), ())),
                precision=lax.Precision.HIGHEST, preferred_element_type=f32,
            )
            dq[rows, :] = jnp.zeros((BLOCK, PAIR), f32)
            seg_wide[rows, :] = jnp.broadcast_to(segc_ref[rows, :], (BLOCK, PAIR))
            return carry

        lax.fori_loop(0, blocks, prepare, 0)

        def unturn(values, rows):
            return values * cos_ref[rows, :] - swap_halves(values, lanes) * sin_ref[rows, :]

        def one_key(j, carry):
            rows = span(j)
            keys, values = k_ref[rows, :], v_ref[rows, :]
            zero = jnp.zeros_like(keys)
            keys = jnp.concatenate([jnp.where(first, keys, zero), jnp.where(first, zero, keys)], axis=0)
            values = jnp.concatenate([jnp.where(first, values, zero), jnp.where(first, zero, values)], axis=0)
            label = seg_wide[rows, :]
            label = jnp.concatenate([label] * (BLOCK // PAIR), axis=1)

            def one_query(i, running):
                grad_k, grad_v = running
                there = span(i)
                query, grad_out = q_ref[there, :], do_ref[there, :]
                allowed = label == segr_ref[:, there]
                scores = dot_nt(keys, query)
                grad_prob = dot_nt(values, grad_out)
                parts, lows = [], []
                for head in range(2):
                    half = slice(head * BLOCK, (head + 1) * BLOCK)
                    found = scores[half] - lse_ref[0, head : head + 1, there]
                    part = jnp.exp(jnp.where(allowed, found, -1e30))
                    parts.append(part.astype(bf16))
                    lows.append((part * (grad_prob[half] - delta[head : head + 1, there])).astype(bf16))
                probability = jnp.concatenate(parts, axis=0)
                grad_scores = jnp.concatenate(lows, axis=0)
                dq[there, :] += dot_tn(grad_scores, keys)
                return grad_k + dot_nn(grad_scores, query), grad_v + dot_nn(probability, grad_out)

            blank = jnp.zeros((2 * BLOCK, PAIR), f32)
            grad_k, grad_v = lax.fori_loop(range_ref[0, j], range_ref[1, j], one_query, (blank, blank))
            grad_k = jnp.where(first, grad_k[:BLOCK], grad_k[BLOCK:])
            grad_v = jnp.where(first, grad_v[:BLOCK], grad_v[BLOCK:])
            dk_low[rows, :] = unturn(grad_k, rows).astype(bf16)
            dv_low[rows, :] = grad_v.astype(bf16)
            return carry

        lax.fori_loop(0, blocks, one_key, 0)

        def finish(i, carry):
            rows = span(i)
            grad_ref[rows, :] = unturn(dq[rows, :] * HEAD_DIM**-0.5, rows).astype(bf16)
            return carry

        lax.fori_loop(0, blocks, finish, 0)

    @pl.when(step == 1)
    def _():
        grad_ref[...] = dk_low[...]

    @pl.when(step == 2)
    def _():
        grad_ref[...] = dv_low[...]


def attend_backward(ranges, queries, keys, projected, mixed, grad_mixed, logsum, cosine, sine, seg_column, seg_row):
    length, width = queries.shape
    pairs = width // PAIR
    panel = lambda shift: pl.BlockSpec((length, PAIR), lambda p, t, r: (0, shift * pairs + p))
    whole = lambda shape: pl.BlockSpec(shape, lambda p, t, r: (0,) * len(shape))
    return pl.pallas_call(
        attend_backward_kernel,
        grid_spec=pltpu.PrefetchScalarGridSpec(
            num_scalar_prefetch=1,
            grid=(pairs, 3),
            in_specs=[panel(0), panel(0), panel(2), panel(0), panel(0),
                      pl.BlockSpec((1, 2, length), lambda p, t, r: (p, 0, 0)),
                      whole(cosine.shape), whole(sine.shape), whole(seg_column.shape), whole(seg_row.shape)],
            out_specs=pl.BlockSpec((length, PAIR), lambda p, t, r: (0, t * pairs + p)),
            scratch_shapes=[
                pltpu.VMEM((length, PAIR), f32),
                pltpu.VMEM((length, PAIR), bf16),
                pltpu.VMEM((length, PAIR), bf16),
                pltpu.VMEM((8, length), f32),
                pltpu.VMEM((length, PAIR), jnp.int32),
            ],
        ),
        out_shape=jax.ShapeDtypeStruct((length, 3 * width), bf16),
        compiler_params=params("arbitrary", "arbitrary"),
        cost_estimate=cost(10 * length * length * width, 16 * length * width, length * length * 2 * pairs),
    )(ranges, queries, keys, projected, mixed, grad_mixed, logsum, cosine, sine, seg_column, seg_row)


def gelu_and_slope(x):
    root = math.sqrt(2.0 / math.pi)
    square = x * x
    bend = jnp.tanh(x * (root + root * 0.044715 * square))
    half = 0.5 * x
    half_up = 0.5 + 0.5 * bend
    slope = half_up + half * (1.0 - bend * bend) * (root + 3.0 * root * 0.044715 * square)
    return half + half * bend, slope


def feed_kernel(
    n_ref, cot_ref, resid_ref, up_ref, down_ref, out_ref, back_ref, gup_ref, gdown_ref,
    total, n_turned, cot_turned, act, pre,
):
    step, last = pl.program_id(0), pl.num_programs(0) - 1
    frames, width = n_ref.shape
    tile = min(BLOCK, frames)
    planes = gup_ref.shape[1]
    part = width // planes

    def rows_of(i):
        return pl.ds(pl.multiple_of(i * tile, tile), tile)

    @pl.when(step == 0)
    def _():
        def turn(i, carry):
            rows = rows_of(i)
            n_turned[:, rows] = n_ref[rows, :].T
            cot_turned[:, rows] = cot_ref[rows, :].T
            total[rows, :] = resid_ref[rows, :]
            back_ref[rows, :] = jnp.zeros((tile, width), f32)
            return carry

        lax.fori_loop(0, frames // tile, turn, 0)

    def chunk(i, carry):
        rows = rows_of(i)
        hidden = dot_nn(n_ref[rows, :], up_ref[...])
        grad_act = dot_nt(cot_ref[rows, :], down_ref[...])
        activated, slope = gelu_and_slope(hidden)
        activated = activated.astype(bf16)
        grad_pre = (grad_act * slope).astype(bf16)
        act[rows, :] = activated
        pre[rows, :] = grad_pre
        total[rows, :] += dot_nn(activated, down_ref[...])
        back_ref[rows, :] += dot_nt(grad_pre, up_ref[...])
        return carry

    lax.fori_loop(0, frames // tile, chunk, 0)

    def weights(i, carry):
        rows = pl.ds(pl.multiple_of(i * part, part), part)
        grad_up = dot_nn(n_turned[rows, :], pre[...]).astype(bf16)
        gup_ref[0, i] = grad_up[: part // 2]
        gup_ref[1, i] = grad_up[part // 2 :]
        gdown_ref[0, 0, rows, :] = dot_nn(cot_turned[rows, :], act[...]).astype(bf16)
        return carry

    lax.fori_loop(0, planes, weights, 0)

    @pl.when(step == last)
    def _():
        out_ref[...] = total[...].astype(bf16)


def feed_forward_and_back(normed, cot, resid, w_up, w_down, planes):
    frames, width = normed.shape
    hidden = w_up.shape[1]
    piece = hidden // (2 * planes)
    once = dict(pipeline_mode=pl.Buffered(1))
    return pl.pallas_call(
        feed_kernel,
        grid=(hidden // piece,),
        in_specs=[
            pl.BlockSpec((frames, width), lambda j: (0, 0), **once),
            pl.BlockSpec((frames, width), lambda j: (0, 0), **once),
            pl.BlockSpec((frames, width), lambda j: (0, 0), **once),
            pl.BlockSpec((width, piece), lambda j: (0, j)),
            pl.BlockSpec((piece, width), lambda j: (j, 0)),
        ],
        out_specs=[
            pl.BlockSpec((frames, width), lambda j: (0, 0)),
            pl.BlockSpec((frames, width), lambda j: (0, 0)),
            pl.BlockSpec((2, planes, width // (2 * planes), piece), lambda j: (0, 0, 0, j)),
            pl.BlockSpec((1, 1, width, piece), lambda j: (j % 2, j // 2, 0, 0)),
        ],
        out_shape=[
            jax.ShapeDtypeStruct((frames, width), bf16),
            jax.ShapeDtypeStruct((frames, width), f32),
            jax.ShapeDtypeStruct((2, planes, width // (2 * planes), hidden), bf16),
            jax.ShapeDtypeStruct((2, planes, width, piece), bf16),
        ],
        scratch_shapes=[
            pltpu.VMEM((frames, width), f32),
            pltpu.VMEM((width, frames), bf16),
            pltpu.VMEM((width, frames), bf16),
            pltpu.VMEM((frames, piece), bf16),
            pltpu.VMEM((frames, piece), bf16),
        ],
        compiler_params=params("arbitrary"),
        cost_estimate=cost(12 * frames * width * hidden, 8 * width * hidden + 16 * frames * width, frames * hidden),
    )(normed, cot, resid, w_up, w_down)


def body(inputs, skips, cotangent, segment_ids, time_steps, w_skip, w_qkv, w_out, w_up, w_down, w_mod):
    micro, _, piece, width = inputs.shape
    length = segment_ids.shape[-1]
    labels = time_steps.shape[-1]
    planes, lows, highs = lax.axis_size("plane"), lax.axis_size("lo"), lax.axis_size("hi")
    line = highs * lows
    group = 2 * lows
    devices = planes * 2 * line
    core, high, low = lax.axis_index("core"), lax.axis_index("hi"), lax.axis_index("lo")
    place = high * lows + low
    member = core * lows + low
    frames = 2 * piece
    heads_wide = width // group
    first_core = core == 0
    swap = [(0, 1), (1, 0)]

    def route(parity):
        pairs = []
        for c in range(2):
            for z in range(line):
                row = c * micro + ((z % 2) ^ parity)
                to_core, to_low = divmod(z // 2, lows)
                pairs.append((c * line + z, (to_core * highs + row) * lows + to_low))
        return pairs

    there = (route(0), route(1))
    back = tuple([(b, a) for a, b in pairs] for pairs in there)
    odd_place = place % 2
    even_row = high % 2 == 0

    def to_rows(value):
        value = value[:, 0]
        near = lax.ppermute(lax.dynamic_index_in_dim(value, odd_place, 0, False), LINE_AXES, there[0])
        far = lax.ppermute(lax.dynamic_index_in_dim(value, 1 - odd_place, 0, False), LINE_AXES, there[1])
        return jnp.concatenate([jnp.where(even_row, near, far), jnp.where(even_row, far, near)], axis=0)

    def from_rows(value):
        value = value.reshape(2, piece, width)
        near = lax.ppermute(lax.dynamic_index_in_dim(value, high % 2, 0, False), LINE_AXES, back[0])
        far = lax.ppermute(lax.dynamic_index_in_dim(value, 1 - high % 2, 0, False), LINE_AXES, back[1])
        even = odd_place == 0
        return jnp.stack([jnp.where(even, near, far), jnp.where(even, far, near)])[:, None]

    def frames_to_row(value):
        if group > 2:
            return lax.all_gather(value, ROW_AXES, axis=0, tiled=True)
        other = lax.ppermute(value, "core", swap)
        return jnp.concatenate([jnp.where(first_core, value, other), jnp.where(first_core, other, value)], axis=0)

    def heads_to_frames(value):
        if group > 2:
            return lax.all_to_all(value, ROW_AXES, split_axis=0, concat_axis=1, tiled=True)
        other = lax.ppermute(lax.dynamic_slice_in_dim(value, (1 - core) * frames, frames, 0), "core", swap)
        own = lax.dynamic_slice_in_dim(value, core * frames, frames, 0)
        return jnp.concatenate([jnp.where(first_core, own, other), jnp.where(first_core, other, own)], axis=1)

    def frames_to_heads(value):
        if group > 2:
            return lax.all_to_all(value, ROW_AXES, split_axis=1, concat_axis=0, tiled=True)
        other = lax.ppermute(lax.dynamic_slice_in_dim(value, (1 - core) * heads_wide, heads_wide, 1), "core", swap)
        own = lax.dynamic_slice_in_dim(value, core * heads_wide, heads_wide, 1)
        return jnp.concatenate([jnp.where(first_core, own, other), jnp.where(first_core, other, own)], axis=0)

    up_rows, down_rows, out_rows = w_up.shape[0], w_down.shape[0], w_out.shape[0]
    skip_rows = w_skip.shape[0]
    early = jnp.concatenate([w_skip] + [w_qkv[:, i * width : (i + 1) * width] for i in range(3)], axis=0)
    early = lax.all_gather(early, ALL_AXES, axis=0, tiled=True).reshape(devices, -1, width)
    skip_full = early[:, :skip_rows].reshape(-1, width)
    qkv_parts = []
    for i in range(3):
        begin = skip_rows + i * out_rows
        whole = early[:, begin : begin + out_rows].reshape(width, width)
        qkv_parts.append(lax.dynamic_slice_in_dim(whole, member * heads_wide, heads_wide, 1))
    qkv_own = jnp.concatenate(qkv_parts, axis=1)
    columns = w_up.shape[1] // width
    late = jnp.concatenate([w_down, w_out] + [w_up[:, i * width : (i + 1) * width] for i in range(columns)], axis=0)
    late, early = lax.optimization_barrier((late, early))
    late = lax.all_gather(late, ALL_AXES, axis=0, tiled=True).reshape(devices, -1, width)
    down_full = late[:, :down_rows].reshape(-1, width)
    out_full = late[:, down_rows : down_rows + out_rows].reshape(width, width)
    up_full = jnp.concatenate(
        [
            late[:, down_rows + out_rows + i * up_rows : down_rows + out_rows + (i + 1) * up_rows].reshape(width, width)
            for i in range(columns)
        ],
        axis=1,
    )

    labels_own = segment_ids[:, 0]
    labels_other = lax.ppermute(labels_own, "core", swap)
    labels_pick = jnp.where(core == high // micro, labels_own, labels_other)
    seg = lax.dynamic_index_in_dim(labels_pick, high % micro, 0, False)
    names = jnp.arange(labels, dtype=jnp.int32)
    starts = jnp.sum((seg[:, None] < names[None, :]).astype(jnp.int32), axis=0)
    ends = jnp.sum((seg[:, None] <= names[None, :]).astype(jnp.int32), axis=0)
    offset = jnp.sum(jnp.where(seg[:, None] == names[None, :], starts[None, :], 0), axis=1)
    where_at = jnp.arange(length, dtype=jnp.int32) - offset
    by_block = seg.reshape(-1, BLOCK)
    begin = jnp.sum(jnp.where(by_block[:, :1] == names[None, :], starts[None, :], 0), axis=1)
    finish = jnp.sum(jnp.where(by_block[:, -1:] == names[None, :], ends[None, :], 0), axis=1)
    ranges = jnp.stack([begin // BLOCK, (finish + BLOCK - 1) // BLOCK]).astype(jnp.int32)
    half = HEAD_DIM // 2
    rates = jnp.exp(-math.log(10000.0) * jnp.arange(half, dtype=f32) / half)
    angles = where_at.astype(f32)[:, None] * rates
    cosine = jnp.tile(jnp.cos(angles), (1, 4))
    sine = jnp.sin(angles)
    sine = jnp.concatenate([-sine, sine, -sine, sine], axis=1)
    seg_column, seg_row = seg[:, None], seg[None, :]
    mine = lax.dynamic_slice_in_dim(seg, member * frames, frames, 0)
    mine_column, mine_row = mine[:, None], mine[None, :]

    steps = lax.all_gather(time_steps[:, 0], ("plane", "core"), axis=0, tiled=True).reshape(-1)
    quarter = w_mod.shape[0] // 2
    pace = jnp.exp(-math.log(10000.0) * jnp.arange(quarter, dtype=f32) / quarter)
    turns = steps.astype(f32)[:, None] * pace
    embedded = jnp.concatenate([jnp.sin(turns), jnp.cos(turns)], axis=1).astype(bf16)
    block_mod = jnp.dot(embedded, w_mod, preferred_element_type=f32)
    own_columns = block_mod.shape[1]
    block_mod = block_mod.reshape(planes, 1, highs, 1, labels, own_columns)
    block_mod = jnp.broadcast_to(block_mod, (planes, 2, highs, lows, labels, own_columns))
    block_mod = lax.all_to_all(
        block_mod.reshape(devices, labels, own_columns), ALL_AXES, split_axis=0, concat_axis=0, tiled=True
    )
    modulation = jnp.moveaxis(block_mod, 0, 1).reshape(labels, 4, width)
    shift_one, scale_one, shift_two, scale_two = (modulation[:, i] for i in range(4))

    x, s = to_rows(inputs), to_rows(skips)
    cot_in, x = lax.optimization_barrier((cotangent, x))
    cot = to_rows(cot_in)
    resid_in, normed_one = rowwise(
        skip_norm_kernel,
        frames,
        [("", x), ("", s), ("whole", skip_full[:width]), ("whole", skip_full[width:]), ("", mine_column),
         ("whole", shift_one), ("whole", scale_one)],
        None,
        [(width, f32), (width, bf16)],
        flops=4 * frames * width * width,
    )
    normed_row = frames_to_row(normed_one)
    projected = jnp.dot(normed_row, qkv_own, preferred_element_type=f32).astype(bf16)
    mixed_heads, queries, keys, logsum = attend_forward(ranges, projected, cosine, sine, seg_column, seg_row)
    mixed = heads_to_frames(mixed_heads)
    resid_mid, normed_two = rowwise(
        out_norm_kernel,
        frames,
        [("", mixed), ("whole", out_full), ("", resid_in), ("", mine_column), ("whole", shift_two), ("whole", scale_two)],
        None,
        [(width, f32), (width, bf16)],
        flops=2 * frames * width * width,
    )
    result, grad_normed_two, grad_up, grad_down = feed_forward_and_back(
        normed_two, cot, resid_mid, up_full, down_full, planes
    )

    def over_cores(kept):
        other = lax.ppermute(lax.dynamic_index_in_dim(kept, 1 - core, 0, False), "core", swap)
        own = lax.dynamic_index_in_dim(kept, core, 0, False)
        return (own.astype(f32) + other.astype(f32)).astype(bf16)

    def scatter(value):
        return lax.psum_scatter(value, ("plane", "hi", "lo"), scatter_dimension=0, tiled=True)

    def scatter_rows(value):
        split = jnp.moveaxis(value.reshape(planes, 2, -1, value.shape[1]), 1, 0)
        return scatter(over_cores(split).reshape(-1, value.shape[1]))

    grad_up = scatter(over_cores(grad_up).reshape(-1, grad_up.shape[-1])).astype(f32)
    grad_down = over_cores(grad_down)
    grad_down = grad_down.reshape(planes, width, line, -1)
    grad_down = jnp.moveaxis(grad_down, 2, 1).reshape(planes * line * width, -1)
    grad_down = scatter(grad_down).T.astype(f32)

    grad_mid, grad_mid_low, grad_frames, grad_shift_two, grad_scale_two = rowwise(
        norm_two_back_kernel,
        frames,
        [("", grad_normed_two), ("", resid_mid), ("", cot), ("", mine_column), ("row", mine_row),
         ("whole", scale_two), ("whole", out_full)],
        None,
        [(width, f32), (width, bf16), (width, bf16)],
        sums=2,
        flops=2 * frames * width * width,
    )
    grad_heads = frames_to_heads(grad_frames)
    grad_out = lax.dot_general(mixed, grad_mid_low, (((0,), (0,)), ((), ())), preferred_element_type=f32)
    grad_out = scatter_rows(grad_out.astype(bf16)).astype(f32)
    grad_proj = attend_backward(
        ranges, queries, keys, projected, mixed_heads, grad_heads, logsum, cosine, sine, seg_column, seg_row
    )
    if group > 2:
        partial = dot_nt(grad_proj, qkv_own).astype(bf16)
        grad_one = lax.psum_scatter(partial, ROW_AXES, scatter_dimension=0, tiled=True).astype(f32)
        grad_one_other = jnp.zeros((frames, width), bf16)
    else:
        away = lax.dynamic_slice_in_dim(grad_proj, (1 - core) * frames, frames, 0)
        home = lax.dynamic_slice_in_dim(grad_proj, core * frames, frames, 0)
        grad_one_other = lax.ppermute(dot_nt(away, qkv_own).astype(bf16), "core", swap)
        grad_one = dot_nt(home, qkv_own)
    grad_in, grad_shift_one, grad_scale_one = rowwise(
        norm_one_back_kernel,
        frames,
        [("", grad_one), ("", grad_one_other), ("", resid_in), ("", grad_mid), ("", mine_column), ("row", mine_row),
         ("whole", scale_one)],
        None,
        [(width, bf16)],
        sums=2,
    )
    grad_in_home = from_rows(grad_in)
    grad_qkv = lax.dot_general(normed_row, grad_proj, (((0,), (0,)), ((), ())), preferred_element_type=f32)
    grad_qkv = grad_qkv.astype(bf16)
    if group > 2:
        grad_qkv = grad_qkv.reshape(planes, 2, highs, lows, -1, 3, 1, heads_wide)
        grad_qkv = jnp.moveaxis(grad_qkv, (1, 3), (0, 1)).reshape(group, -1, 3, 1, heads_wide)
        grad_qkv = lax.all_to_all(grad_qkv, ROW_AXES, split_axis=0, concat_axis=3, tiled=True)
        grad_qkv = grad_qkv.reshape(-1, 3 * width)
        grad_qkv = lax.psum_scatter(grad_qkv, ("plane", "hi"), scatter_dimension=0, tiled=True)
    else:
        split = grad_qkv.reshape(planes, 2, -1, 3 * heads_wide)
        other = lax.ppermute(lax.dynamic_index_in_dim(split, 1 - core, 1, False), "core", swap)
        own = lax.dynamic_index_in_dim(split, core, 1, False)
        own, other = (v.reshape(-1, 3 * heads_wide) for v in (own, other))
        left, right = jnp.where(first_core, own, other), jnp.where(first_core, other, own)
        grad_qkv = jnp.concatenate(
            [v[:, i * heads_wide : (i + 1) * heads_wide] for i in range(3) for v in (left, right)], axis=1
        )
        grad_qkv = scatter(grad_qkv)
    grad_qkv = grad_qkv.astype(f32)

    grad_skip_w = jnp.concatenate(
        [
            lax.dot_general(v, grad_in, (((0,), (0,)), ((), ())), preferred_element_type=f32).astype(bf16)
            for v in (x, s)
        ],
        axis=0,
    )
    grad_skip_w = scatter_rows(grad_skip_w).astype(f32)

    grad_inputs = jnp.einsum("mrfd,cd->mrfc", grad_in_home, skip_full[:width], preferred_element_type=f32).astype(bf16)
    grad_skips = jnp.einsum("mrfd,cd->mrfc", grad_in_home, skip_full[width:], preferred_element_type=f32).astype(bf16)

    grad_mod = jnp.stack([v[:labels] for v in (grad_shift_one, grad_scale_one, grad_shift_two, grad_scale_two)], axis=1)
    grad_mod = jnp.moveaxis(grad_mod.reshape(labels, devices, own_columns), 1, 0)
    grad_mod = lax.all_to_all(grad_mod, ALL_AXES, split_axis=0, concat_axis=0, tiled=True)
    grad_mod = jnp.sum(grad_mod.reshape(planes, 2, highs, lows, labels, own_columns), axis=(1, 3))
    grad_mod = lax.dot_general(
        embedded.astype(f32),
        grad_mod.reshape(-1, own_columns),
        (((0,), (0,)), ((), ())),
        precision=lax.Precision.HIGHEST,
        preferred_element_type=f32,
    )
    return (
        from_rows(result),
        grad_inputs,
        grad_skips,
        grad_skip_w,
        grad_qkv,
        grad_out,
        grad_up,
        grad_down,
        grad_mod,
    )


def solution(mesh):
    batch, wide = mesh.devices.shape

    def run(inputs, *rest):
        rows = 2 * inputs.shape[0]
        assert inputs.shape[0] == 2 and inputs.shape[1] == batch and wide % rows == 0
        fine = Mesh(mesh.devices.reshape(batch // 2, 2, rows, wide // rows), ALL_AXES)
        by_batch, by_wide = ("plane", "core"), ("hi", "lo")
        frames = P(None, by_batch, by_wide, None)
        rowed = P(None, by_batch, None)
        weight, columns = P(ALL_AXES, None), P(None, ALL_AXES)
        mapped = jax.shard_map(
            body,
            mesh=fine,
            in_specs=(frames, frames, frames, rowed, rowed) + (weight,) * 5 + (columns,),
            out_specs=(frames, frames, frames) + (weight,) * 5 + (columns,),
            check_vma=False,
        )
        return mapped(inputs, *rest)

    return run
```

time: 2760 us -> 1310 us (0.47)
  waiting for transfers between devices: 1560 us -> 544 us
  matrix products: 591 us -> 50.6 us
  Pallas kernels: 0 us -> 307 us
  starting transfers between devices: 39.4 us -> 235 us
  local copies, waits for them, and re-layouts: 287 us -> 93.1 us
  other arithmetic: 243 us -> 56.9 us
    reduce_scatter x6 -> x5, waiting for transfers between devices: 1130 us -> 320 us  [scatter(): lax.psum_scatter(value, ('plane', 'hi', 'lo'), scatter_dimension=0, tiled...]
    dot_general x94 -> x11, matrix products: 591 us -> 50.6 us  [the longest x2 13.3 us: dot_nt(): lax.dot_general(left, right, (((1,), (1,)), ((), ())), preferred_element_...]
    pallas_call x0 -> x7, Pallas kernels: none -> 307 us  [the longest x1 109 us: attend_backward(): pl.pallas_call(attend_backward_kernel, grid_spec=pltpu.PrefetchScalarGrid...]
    all_to_all x8 -> x2, waiting for transfers between devices: 252 us -> 33.1 us  [the longest x1 33.1 us: body(): lax.all_to_all(grad_mod, ALL_AXES, split_axis=0, concat_axis=0, tiled=True)]
    ppermute x0 -> x20, starting transfers between devices: none -> 166 us  [the longest x1 79.7 us: frames_to_row(): other = lax.ppermute(value, 'core', swap)]
    ppermute x0 -> x20, waiting for transfers between devices: none -> 105 us  [the longest x3 63 us: to_rows(): lax.ppermute(lax.dynamic_index_in_dim(value, 1 - odd_place, 0, False), LI...]
    dynamic_update_slice x16 -> x0, local copies, waits for them, and re-layouts: 92.9 us -> none  [attend_backward(): lax.scan(one_block, (zero_grads, zero_grads), jnp.arange(count_blocks, dt...]
    all_gather x6 -> x2, waiting for transfers between devices: 171 us -> 85.7 us  [the longest x1 85.7 us: body(): lax.all_gather(early, ALL_AXES, axis=0, tiled=True)]
  transfers between devices with their start and end apart: 20 -> 29, of which waited for: 13 -> 15; matrix products, arithmetic and copies ran while one was open for 37% -> 11% of each run, Pallas kernels for 0% -> 8%
where the time goes in v1:
time: 1310 us
  waiting for transfers between devices  544 us (42%)
  Pallas kernels  307 us (23%)
  starting transfers between devices  235 us (18%)
  local copies, waits for them, and re-layouts  93.1 us (7%)
  other arithmetic  56.9 us (4%)
  matrix products  50.6 us (4%)
  between operations  15.4 us (1%)
    reduce_scatter x5, waiting for transfers between devices, scatter(): lax.psum_scatter(value, ('plane', 'hi', 'lo'), scatter_dimension=0, tiled...  320 us
    pallas_call x1, Pallas kernels, attend_backward(): pl.pallas_call(attend_backward_kernel, grid_spec=pltpu.PrefetchScalarGrid...  109 us
    all_gather x1, waiting for transfers between devices, body(): lax.all_gather(early, ALL_AXES, axis=0, tiled=True)  85.7 us
    ppermute x1, starting transfers between devices, frames_to_row(): other = lax.ppermute(value, 'core', swap)  79.7 us
    pallas_call x1, Pallas kernels, attend_forward(): pl.pallas_call(attend_forward_kernel, grid_spec=pltpu.PrefetchScalarGridS...  79.4 us
    pallas_call x1, Pallas kernels, feed_forward_and_back(): pl.pallas_call(feed_kernel, grid=(hidden // piece,), in_specs=[pl.BlockSp...  78.3 us
    all_to_all x1, starting transfers between devices, body(): lax.all_to_all(grad_mod, ALL_AXES, split_axis=0, concat_axis=0, tiled=True)  65 us
    ppermute x3, waiting for transfers between devices, to_rows(): lax.ppermute(lax.dynamic_index_in_dim(value, 1 - odd_place, 0, False), LI...  63 us
  transfers between devices with their start and end apart: 29, of which 15 were waited for; matrix products, arithmetic and copies ran while one was open for 11% of the time, Pallas kernels for 8%

profile of v1, /device:TPU:0, one launch (start us, length us, event | category | flops | bytes accessed | tf_op | source)
XLA Modules:
  0.0 1310.9 jit_solution(11358775219348671453)
XLA Ops:
  15.3 85.7 %all-gather.4.cloned.1.call-done = bf16[5120,1024]{1,0:T(8,128)(2,1)} async-done(((bf16[160,1024]{1,0:T(8,128)(2,1)}), bf16[5120,1024]{1,0:T(8,128)(2,1)}) %all-gather.4.cloned.1.call-update) | async-done | bytes 10485776 | tf_op jit(solution)/shard_map/all_gather | solution.py:549
  116.6 9.5 collective-permute-start.1
  134.5 47.6 %collective-permute-done.2 = bf16[512,1024]{1,0:T(8,128)(2,1)} collective-permute-done((bf16[512,1024]{1,0:T(8,128)(2,1)}, bf16[512,1024]{1,0:T(8,128)(2,1)}, u32[]{:S(2)}, u32[]{:S(2)}) %collective-permute-start.2) | collective-permute-done | bytes 1048608 | tf_op jit(solution)/shard_map/ppermute | solution.py:516
  185.3 15.4 %collective-permute-done.4 = bf16[512,1024]{1,0:T(8,128)(2,1)S(1)} collective-permute-done((bf16[512,1024]{1,0:T(8,128)(2,1)S(1)}, bf16[512,1024]{1,0:T(8,128)(2,1)S(1)}, u32[]{:S(2)}, u32[]{:S(2)}) %collective-permute-start.4) | collective-permute-done | bytes 1048608 | tf_op jit(solution)/shard_map/ppermute | solution.py:516
  208.6 11.0 shard_map.178
  219.6 79.7 %collective-permute-start.5 = (bf16[1024,1024]{1,0:T(8,128)(2,1)}, bf16[1024,1024]{1,0:T(8,128)(2,1)}, u32[]{:S(2)}, u32[]{:S(2)}) collective-permute-start(bf16[1024,1024]{1,0:T(8,128)(2,1)} %get-tuple-element.33), channel_id=1, source_target_pairs={{0,4},{4,0},{1,5},{5,1},{2,6},{6,2},{3,7},{7,3},{8,12},{12,8},{9,1... | collective-permute-start | bytes 6291464 | tf_op jit(solution)/shard_map/ppermute | solution.py:529
  312.5 15.0 %collective-permute-start.8 = (bf16[512,1024]{1,0:T(8,128)(2,1)S(1)}, bf16[512,1024]{1,0:T(8,128)(2,1)S(1)}, u32[]{:S(2)}, u32[]{:S(2)}) collective-permute-start(bf16[512,1024]{1,0:T(8,128)(2,1)S(1)} %get-tuple-element.155), channel_id=1, source_target_pairs={{0,1},{1,0},{2,5},{3,4},{4,3},{5,2},{6,7},{7,6},{8,9},{9,8},{10,13... | collective-permute-start | bytes 3145736 | tf_op jit(solution)/shard_map/ppermute | solution.py:516
  338.6 10.3 convolution_convert_fusion.q_ref.k_ref.v_ref
  348.9 79.4 %shard_map.179 = (bf16[2048,512]{1,0:T(8,128)(2,1)}, bf16[2048,512]{1,0:T(8,128)(2,1)}, bf16[2048,512]{1,0:T(8,128)(2,1)}, f32[4,2,2048]{2,1,0:T(2,128)}) custom-call(s32[2,8]{1,0:T(2,128)} %pad_add_fusion.range_ref, bf16[2048,1536]{1,0:T(8,128)(2,1)} %convolution_convert_fusion.q_ref.k_ref.v_ref, ...), custom_call_target="tpu_custom_call" | custom-call | flops 8589934592 | bytes 14680064 | tf_op jit(solution)/shard_map/pallas_call | solution.py:241
  457.7 8.9 shard_map.180
  466.6 78.3 %shard_map.181 = (bf16[1024,1024]{1,0:T(8,128)(2,1)}, f32[1024,1024]{1,0:T(8,128)}, bf16[2,4,128,4096]{3,2,1,0:T(8,128)(2,1)}, bf16[2,4,1024,512]{3,2,1,0:T(8,128)(2,1)}) custom-call(bf16[1024,1024]{1,0:T(8,128)(2,1)} %get-tuple-element.37.n_ref, bf16[1024,1024]{1,0:T(8,128)(2,1)} %pad_maximum_fusion.9.cot_ref, f32[1024,1024]{1,0:T(8,128)} %get-tuple-element.39.resid_ref, ...), custom_call_target="tpu_custom_call" | custom-call | flops 51539607552 | bytes 50331648 | tf_op jit(solution)/shard_map/pallas_call | solution.py:449
  544.9 10.8 shard_map.182
  563.9 109.3 %shard_map.183 = bf16[2048,1536]{1,0:T(8,128)(2,1)} custom-call(s32[2,8]{1,0:T(2,128)} %pad_add_fusion.range_ref, bf16[2048,512]{1,0:T(8,128)(2,1)} %get-tuple-element.41.q_ref, bf16[2048,512]{1,0:T(8,128)(2,1)} %get-tuple-element.42.k_ref, bf16[2048,1536]{1,0:T(8,128)(2,1)} %convolution_convert_fusion.q_ref.k_ref.v_ref, ...), custom_call_target="tpu_custom_call" | custom-call | flops 21474836480 | bytes 16777216 | tf_op jit(solution)/shard_map/pallas_call | solution.py:356
  673.3 9.6 convolution_convert_fusion.1
  711.0 9.7 shard_map.184
  752.2 10.0 copy.112
  788.0 48.6 %collective-permute-start.10 = (bf16[512,1024]{1,0:T(8,128)(2,1)S(1)}, bf16[512,1024]{1,0:T(8,128)(2,1)S(1)}, u32[]{:S(2)}, u32[]{:S(2)}) collective-permute-start(bf16[512,1024]{1,0:T(8,128)(2,1)S(1)} %get-tuple-element.151), channel_id=1, source_target_pairs={{1,0},{0,1},{5,2},{4,3},{3,4},{2,5},{7,6},{6,7},{9,8},{8,9},{13,10... | collective-permute-start | bytes 3145736 | tf_op jit(solution)/shard_map/ppermute | solution.py:522
  840.2 24.4 %collective-permute-done.10 = bf16[512,1024]{1,0:T(8,128)(2,1)S(1)} collective-permute-done((bf16[512,1024]{1,0:T(8,128)(2,1)S(1)}, bf16[512,1024]{1,0:T(8,128)(2,1)S(1)}, u32[]{:S(2)}, u32[]{:S(2)}) %collective-permute-start.10) | collective-permute-done | bytes 1048608 | tf_op jit(solution)/shard_map/ppermute | solution.py:522
  865.7 65.0 %all-to-all-start.1 = ((f32[32,4,128]{2,1,0:T(4,128)}), f32[32,4,128]{2,1,0:T(4,128)S(1)}, u32[]{:S(2)}, u32[]{:S(2)}) async-start(f32[32,4,128]{2,1,0:T(4,128)} %copy.114), calls=%async_computation.6 | async-start | bytes 131072 | tf_op jit(solution)/shard_map/all_to_all | solution.py:724
  933.8 33.1 %all-to-all-done.1 = f32[32,4,128]{2,1,0:T(4,128)S(1)} async-done(((f32[32,4,128]{2,1,0:T(4,128)}), f32[32,4,128]{2,1,0:T(4,128)S(1)}, u32[]{:S(2)}, u32[]{:S(2)}) %all-to-all-start.1) | async-done | bytes 65568 | tf_op jit(solution)/shard_map/all_to_all | solution.py:724
  976.7 47.0 %reduce-scatter.8.cloned.1.call-done = bf16[32,3072]{1,0:T(8,128)(2,1)} async-done(((bf16[512,3072]{1,0:T(8,128)(2,1)}), bf16[32,3072]{1,0:T(8,128)(2,1)}) %reduce-scatter.8.cloned.1.call-update) | async-done | bytes 196624 | tf_op jit(solution)/shard_map/reduce_scatter | solution.py:643
  1025.4 84.2 %reduce-scatter.6.cloned.1.call-done = bf16[64,1024]{1,0:T(8,128)(2,1)} async-done(((bf16[1024,1024]{1,0:T(8,128)(2,1)}), bf16[64,1024]{1,0:T(8,128)(2,1)}) %reduce-scatter.6.cloned.1.call-update) | async-done | bytes 131088 | tf_op jit(solution)/shard_map/reduce_scatter | solution.py:643
  1111.2 93.6 %reduce-scatter.14.cloned.1.call-done = bf16[1024,128]{0,1:T(8,128)(2,1)} async-done(((bf16[16384,128]{0,1:T(8,128)(2,1)}), bf16[1024,128]{0,1:T(8,128)(2,1)}) %reduce-scatter.14.cloned.1.call-update) | async-done | bytes 262160 | tf_op jit(solution)/shard_map/reduce_scatter | solution.py:643
  1206.6 95.3 %reduce-scatter.12.cloned.1.call-done = bf16[32,4096]{1,0:T(8,128)(2,1)} async-done(((bf16[512,4096]{1,0:T(8,128)(2,1)}), bf16[32,4096]{1,0:T(8,128)(2,1)}) %reduce-scatter.12.cloned.1.call-update) | async-done | bytes 262160 | tf_op jit(solution)/shard_map/reduce_scatter | solution.py:643
  (250 shorter events, 214.0 us)
Async XLA Ops:
  7.2 93.8 %all-gather.4.cloned.1.call-start = ((), (), s32[]{:S(2)}) async-start(), calls=%async_computation.7 | async-start | bytes 10813440 | tf_op jit(solution)/shard_map/all_gather | solution.py:549
  10.0 430.1 %all-gather.6.cloned.1.call-start = ((), (), s32[]{:S(2)}) async-start(), calls=%async_computation.8 | async-start | bytes 19464192 | tf_op jit(solution)/shard_map/all_gather | solution.py:560
  101.1 30.1 %collective-permute-start = (s32[2,2048]{1,0:T(2,128)S(1)}, s32[2,2048]{1,0:T(2,128)S(1)}, u32[]{:S(2)}, u32[]{:S(2)}) collective-permute-start(s32[2,2048]{1,0:T(2,128)S(1)} %bitcast.197), channel_id=1, source_target_pairs={{0,4},{4,0},{1,5},{5,1},{2,6},{6,2},{3,7},{7,3},{8,12},{12,8},{9,1... | collective-permute-start | bytes 49160 | tf_op jit(solution)/shard_map/ppermute | solution.py:572
  112.0 21.9 %all-to-all-start = ((f32[32,4,128]{2,1,0:T(4,128)}), f32[32,4,128]{2,1,0:T(4,128)S(1)}, u32[]{:S(2)}, u32[]{:S(2)}) async-start(f32[32,4,128]{2,1,0:T(4,128)} %bitcast.12), calls=%async_computation | async-start | bytes 131072 | tf_op jit(solution)/shard_map/all_to_all | solution.py:603
  115.0 817.1 %reduce-scatter.10.cloned.1.call-start = ((), (), s32[]{:S(2)}) async-start(), calls=%async_computation.11 | async-start | bytes 1114112 | tf_op jit(solution)/shard_map/reduce_scatter | solution.py:643
  116.6 17.8 %collective-permute-start.1 = (bf16[512,1024]{1,0:T(8,128)(2,1)}, bf16[512,1024]{1,0:T(8,128)(2,1)}, u32[]{:S(2)}, u32[]{:S(2)}) collective-permute-start(bf16[512,1024]{1,0:T(8,128)(2,1)} %get-tuple-element.162), channel_id=1, source_target_pairs={{0,0},{1,1},{2,4},{3,5},{4,2},{5,3},{6,6},{7,7},{8,8},{9,9},{10,12... | collective-permute-start | bytes 3145736 | tf_op jit(solution)/shard_map/ppermute | solution.py:515
  126.1 56.0 %collective-permute-start.2 = (bf16[512,1024]{1,0:T(8,128)(2,1)}, bf16[512,1024]{1,0:T(8,128)(2,1)}, u32[]{:S(2)}, u32[]{:S(2)}) collective-permute-start(bf16[512,1024]{1,0:T(8,128)(2,1)} %get-tuple-element.163), channel_id=1, source_target_pairs={{0,1},{1,0},{2,5},{3,4},{4,3},{5,2},{6,7},{7,6},{8,9},{9,8},{10,13... | collective-permute-start | bytes 3145736 | tf_op jit(solution)/shard_map/ppermute | solution.py:516
  129.0 56.2 %collective-permute-start.3 = (bf16[512,1024]{1,0:T(8,128)(2,1)}, bf16[512,1024]{1,0:T(8,128)(2,1)S(1)}, u32[]{:S(2)}, u32[]{:S(2)}) collective-permute-start(bf16[512,1024]{1,0:T(8,128)(2,1)} %get-tuple-element.158), channel_id=1, source_target_pairs={{0,0},{1,1},{2,4},{3,5},{4,2},{5,3},{6,6},{7,7},{8,8},{9,9},{10,12... | collective-permute-start | bytes 3145736 | tf_op jit(solution)/shard_map/ppermute | solution.py:515
  130.9 69.7 %collective-permute-start.4 = (bf16[512,1024]{1,0:T(8,128)(2,1)S(1)}, bf16[512,1024]{1,0:T(8,128)(2,1)S(1)}, u32[]{:S(2)}, u32[]{:S(2)}) collective-permute-start(bf16[512,1024]{1,0:T(8,128)(2,1)S(1)} %get-tuple-element.159), channel_id=1, source_target_pairs={{0,1},{1,0},{2,5},{3,4},{4,3},{5,2},{6,7},{7,6},{8,9},{9,8},{10,13... | collective-permute-start | bytes 3145736 | tf_op jit(solution)/shard_map/ppermute | solution.py:516
  219.6 112.5 %collective-permute-start.5 = (bf16[1024,1024]{1,0:T(8,128)(2,1)}, bf16[1024,1024]{1,0:T(8,128)(2,1)}, u32[]{:S(2)}, u32[]{:S(2)}) collective-permute-start(bf16[1024,1024]{1,0:T(8,128)(2,1)} %get-tuple-element.33), channel_id=1, source_target_pairs={{0,4},{4,0},{1,5},{5,1},{2,6},{6,2},{3,7},{7,3},{8,12},{12,8},{9,1... | collective-permute-start | bytes 6291464 | tf_op jit(solution)/shard_map/ppermute | solution.py:529
  310.2 123.1 %collective-permute-start.7 = (bf16[512,1024]{1,0:T(8,128)(2,1)}, bf16[512,1024]{1,0:T(8,128)(2,1)S(1)}, u32[]{:S(2)}, u32[]{:S(2)}) collective-permute-start(bf16[512,1024]{1,0:T(8,128)(2,1)} %get-tuple-element.154), channel_id=1, source_target_pairs={{0,0},{1,1},{2,4},{3,5},{4,2},{5,3},{6,6},{7,7},{8,8},{9,9},{10,12... | collective-permute-start | bytes 3145736 | tf_op jit(solution)/shard_map/ppermute | solution.py:515
  312.5 120.8 %collective-permute-start.8 = (bf16[512,1024]{1,0:T(8,128)(2,1)S(1)}, bf16[512,1024]{1,0:T(8,128)(2,1)S(1)}, u32[]{:S(2)}, u32[]{:S(2)}) collective-permute-start(bf16[512,1024]{1,0:T(8,128)(2,1)S(1)} %get-tuple-element.155), channel_id=1, source_target_pairs={{0,1},{1,0},{2,5},{3,4},{4,3},{5,2},{6,7},{7,6},{8,9},{9,8},{10,13... | collective-permute-start | bytes 3145736 | tf_op jit(solution)/shard_map/ppermute | solution.py:516
  684.4 7.8 collective-permute-start.16
  692.1 331.6 %reduce-scatter.8.cloned.1.call-start = ((), (), s32[]{:S(2)}) async-start(), calls=%async_computation.10 | async-start | bytes 3342336 | tf_op jit(solution)/shard_map/reduce_scatter | solution.py:643
  695.9 413.7 %reduce-scatter.6.cloned.1.call-start = ((), (), s32[]{:S(2)}) async-start(), calls=%async_computation.9 | async-start | bytes 2228224 | tf_op jit(solution)/shard_map/reduce_scatter | solution.py:643
  730.7 7.8 collective-permute-start.19
  734.5 470.3 %reduce-scatter.14.cloned.1.call-start = ((), (), s32[]{:S(2)}) async-start(), calls=%async_computation.13 | async-start | bytes 4456448 | tf_op jit(solution)/shard_map/reduce_scatter | solution.py:643
  770.1 531.8 %reduce-scatter.12.cloned.1.call-start = ((), (), s32[]{:S(2)}) async-start(), calls=%async_computation.12 | async-start | bytes 4456448 | tf_op jit(solution)/shard_map/reduce_scatter | solution.py:643
  772.6 7.2 collective-permute-start.18
  787.3 52.9 %collective-permute-start.9 = (bf16[512,1024]{1,0:T(8,128)(2,1)S(1)}, bf16[512,1024]{1,0:T(8,128)(2,1)S(1)}, u32[]{:S(2)}, u32[]{:S(2)}) collective-permute-start(bf16[512,1024]{1,0:T(8,128)(2,1)S(1)} %get-tuple-element.150), channel_id=1, source_target_pairs={{0,0},{1,1},{4,2},{5,3},{2,4},{3,5},{6,6},{7,7},{8,8},{9,9},{12,10... | collective-permute-start | bytes 3145736 | tf_op jit(solution)/shard_map/ppermute | solution.py:521
  788.0 76.6 %collective-permute-start.10 = (bf16[512,1024]{1,0:T(8,128)(2,1)S(1)}, bf16[512,1024]{1,0:T(8,128)(2,1)S(1)}, u32[]{:S(2)}, u32[]{:S(2)}) collective-permute-start(bf16[512,1024]{1,0:T(8,128)(2,1)S(1)} %get-tuple-element.151), channel_id=1, source_target_pairs={{1,0},{0,1},{5,2},{4,3},{3,4},{2,5},{7,6},{6,7},{9,8},{8,9},{13,10... | collective-permute-start | bytes 3145736 | tf_op jit(solution)/shard_map/ppermute | solution.py:522
  838.2 129.7 %collective-permute-start.13 = (bf16[512,1024]{1,0:T(8,128)(2,1)}, bf16[512,1024]{1,0:T(8,128)(2,1)S(1)}, u32[]{:S(2)}, u32[]{:S(2)}) collective-permute-start(bf16[512,1024]{1,0:T(8,128)(2,1)} %get-tuple-element.146), channel_id=1, source_target_pairs={{0,0},{1,1},{4,2},{5,3},{2,4},{3,5},{6,6},{7,7},{8,8},{9,9},{12,10... | collective-permute-start | bytes 3145736 | tf_op jit(solution)/shard_map/ppermute | solution.py:521
  840.2 127.7 %collective-permute-start.14 = (bf16[512,1024]{1,0:T(8,128)(2,1)}, bf16[512,1024]{1,0:T(8,128)(2,1)}, u32[]{:S(2)}, u32[]{:S(2)}) collective-permute-start(bf16[512,1024]{1,0:T(8,128)(2,1)} %get-tuple-element.147), channel_id=1, source_target_pairs={{1,0},{0,1},{5,2},{4,3},{3,4},{2,5},{7,6},{6,7},{9,8},{8,9},{13,10... | collective-permute-start | bytes 3145736 | tf_op jit(solution)/shard_map/ppermute | solution.py:522
  865.7 101.3 %all-to-all-start.1 = ((f32[32,4,128]{2,1,0:T(4,128)}), f32[32,4,128]{2,1,0:T(4,128)S(1)}, u32[]{:S(2)}, u32[]{:S(2)}) async-start(f32[32,4,128]{2,1,0:T(4,128)} %copy.114), calls=%async_computation.6 | async-start | bytes 131072 | tf_op jit(solution)/shard_map/all_to_all | solution.py:724
  (50 other events, 1679.1 us)
Sparse Core Ops, SparseCore 0:
  11.5 89.4 all-gather.3
  103.8 184.3 all-gather.5
  692.2 150.6 reduce-scatter.9
  848.6 175.0 reduce-scatter.7
  1025.9 83.6 reduce-scatter.5
  1111.9 92.8 reduce-scatter.13
  1207.2 94.6 reduce-scatter.11

commit v2 on v1

--- a/solution.py
+++ b/solution.py
@@ -10,7 +10,7 @@
 from jax.sharding import PartitionSpec as P
 
 HEAD_DIM = 64
-PAIR = 2 * HEAD_DIM
+TILE = 128
 BLOCK = 256
 VMEM_BYTES = 60 * 1024 * 1024
 ROW_AXES = ("core", "lo")
@@ -159,74 +159,75 @@
 
 def swap_halves(values, lanes):
     half = HEAD_DIM // 2
-    ahead = pltpu.roll(values, PAIR - half, 1)
+    ahead = pltpu.roll(values, values.shape[1] - half, 1)
     behind = pltpu.roll(values, half, 1)
     return jnp.where(lanes % HEAD_DIM < half, ahead, behind)
 
 
+def widen(table, width):
+    return jnp.concatenate([table] * (width // table.shape[1]), axis=1)
+
+
+def span(i):
+    return pl.ds(pl.multiple_of(i * BLOCK, BLOCK), BLOCK)
+
+
+def own_lanes(parts, lanes):
+    picked = parts[0]
+    for h in range(1, len(parts)):
+        picked = jnp.where(lanes // HEAD_DIM == h, parts[h], picked)
+    return picked
+
+
+def by_count(count, most, run):
+    for each in range(1, most + 1):
+        pl.when(count == each)(functools.partial(run, each))
+
+
 def attend_forward_kernel(
     range_ref, q_ref, k_ref, v_ref, cos_ref, sin_ref, segc_ref, segr_ref,
-    out_ref, qrot_ref, krot_ref, lse_ref, scores, seg_wide,
+    out_ref, qrot_ref, krot_ref, lse_ref, seg_wide,
 ):
-    length = q_ref.shape[0]
+    length, width = q_ref.shape
+    heads = width // HEAD_DIM
     blocks = length // BLOCK
-    lanes = lax.broadcasted_iota(jnp.int32, (BLOCK, PAIR), 1)
-    first = lanes < HEAD_DIM
+    lanes = lax.broadcasted_iota(jnp.int32, (BLOCK, width), 1)
 
     def turn(i, carry):
-        rows = pl.ds(pl.multiple_of(i * BLOCK, BLOCK), BLOCK)
-        cosine, sine = cos_ref[rows, :], sin_ref[rows, :]
+        rows = span(i)
+        cosine, sine = widen(cos_ref[rows, :], width), widen(sin_ref[rows, :], width)
         for source, target, factor in ((q_ref, qrot_ref, HEAD_DIM**-0.5), (k_ref, krot_ref, None)):
             values = source[rows, :].astype(f32)
             turned = (values * cosine + swap_halves(values, lanes) * sine).astype(bf16)
             if factor is not None:
                 turned = turned * jnp.asarray(factor, bf16)
             target[rows, :] = turned
-        seg_wide[rows, :] = jnp.broadcast_to(segc_ref[rows, :], (BLOCK, PAIR))
+        seg_wide[rows, :] = jnp.broadcast_to(segc_ref[rows, :], (BLOCK, TILE))
         return carry
 
     lax.fori_loop(0, blocks, turn, 0)
 
     def one_query(i, carry):
-        rows = pl.ds(pl.multiple_of(i * BLOCK, BLOCK), BLOCK)
-        low, high = range_ref[0, i], range_ref[1, i]
-        query = qrot_ref[rows, :]
-        zero = jnp.zeros_like(query)
-        both = jnp.concatenate([jnp.where(first, query, zero), jnp.where(first, zero, query)], axis=0)
-        label = seg_wide[rows, :]
-        label = jnp.concatenate([label] * (BLOCK // PAIR), axis=1)
-
-        def score(j, highest):
-            keys = krot_ref[pl.ds(pl.multiple_of(j * BLOCK, BLOCK), BLOCK), :]
-            found = dot_nt(both, keys)
-            allowed = label == segr_ref[:, pl.ds(pl.multiple_of(j * BLOCK, BLOCK), BLOCK)]
-            allowed = jnp.concatenate([allowed, allowed], axis=0)
-            found = jnp.where(allowed, found, -1e30)
-            scores[j] = found
-            for part in range(BLOCK // PAIR):
-                highest = jnp.maximum(highest, found[:, part * PAIR : (part + 1) * PAIR])
-            return highest
-
-        highest = lax.fori_loop(low, high, score, jnp.full((2 * BLOCK, PAIR), -1e30, f32))
-        highest = jnp.max(highest, axis=1, keepdims=True)
-
-        def gather(j, running):
-            totals, mixed = running
-            powers = jnp.exp(scores[j] - highest)
-            for part in range(BLOCK // PAIR):
-                totals = totals + powers[:, part * PAIR : (part + 1) * PAIR]
-            values = v_ref[pl.ds(pl.multiple_of(j * BLOCK, BLOCK), BLOCK), :]
-            return totals, mixed + dot_nn(powers.astype(bf16), values)
-
-        blank = jnp.zeros((2 * BLOCK, PAIR), f32)
-        totals, mixed = lax.fori_loop(low, high, gather, (blank, blank))
-        totals = jnp.sum(totals, axis=1, keepdims=True)
-        mixed = mixed * (1.0 / totals)
-        logsum = jnp.broadcast_to(highest + jnp.log(totals), (2 * BLOCK, PAIR))
-        out_ref[rows, :] = jnp.where(first, mixed[:BLOCK], mixed[BLOCK:]).astype(bf16)
-        turned = jnp.where(first, logsum[:BLOCK], logsum[BLOCK:]).T
-        lse_ref[0, 0:1, rows] = turned[0:1]
-        lse_ref[0, 1:2, rows] = turned[HEAD_DIM : HEAD_DIM + 1]
+        rows = span(i)
+
+        def work(count):
+            keys = pl.ds(pl.multiple_of(range_ref[0, i] * BLOCK, BLOCK), count * BLOCK)
+            allowed = widen(seg_wide[rows, :], count * BLOCK) == segr_ref[:, keys]
+            query = qrot_ref[rows, :]
+            zero = jnp.zeros_like(query)
+            mixed = []
+            for h in range(heads):
+                scores = dot_nt(jnp.where(lanes // HEAD_DIM == h, query, zero), krot_ref[keys, :])
+                scores = jnp.where(allowed, scores, -1e30)
+                highest = jnp.max(scores, axis=1, keepdims=True)
+                powers = jnp.exp(scores - highest)
+                totals = jnp.sum(powers, axis=1, keepdims=True)
+                mixed.append(dot_nn(powers.astype(bf16), v_ref[keys, :]) * (1.0 / totals))
+                logsum = jnp.broadcast_to(highest + jnp.log(totals), (BLOCK, TILE))
+                lse_ref[0, h : h + 1, rows] = logsum.T[0:1]
+            out_ref[rows, :] = own_lanes(mixed, lanes).astype(bf16)
+
+        by_count(range_ref[1, i] - range_ref[0, i], blocks, work)
         return carry
 
     lax.fori_loop(0, blocks, one_query, 0)
@@ -235,26 +236,23 @@
 def attend_forward(ranges, projected, cosine, sine, seg_column, seg_row):
     length, width = projected.shape
     width //= 3
-    pairs = width // PAIR
-    panel = lambda shift: pl.BlockSpec((length, PAIR), lambda p, r: (0, shift * pairs + p))
+    panels, heads = width // TILE, TILE // HEAD_DIM
+    panel = lambda shift: pl.BlockSpec((length, TILE), lambda p, r: (0, shift * panels + p))
     whole = lambda shape: pl.BlockSpec(shape, lambda p, r: (0,) * len(shape))
     return pl.pallas_call(
         attend_forward_kernel,
         grid_spec=pltpu.PrefetchScalarGridSpec(
             num_scalar_prefetch=1,
-            grid=(pairs,),
+            grid=(panels,),
             in_specs=[panel(0), panel(1), panel(2), whole(cosine.shape), whole(sine.shape),
                       whole(seg_column.shape), whole(seg_row.shape)],
-            out_specs=[panel(0), panel(0), panel(0), pl.BlockSpec((1, 2, length), lambda p, r: (p, 0, 0))],
-            scratch_shapes=[
-                pltpu.VMEM((length // BLOCK, 2 * BLOCK, BLOCK), f32),
-                pltpu.VMEM((length, PAIR), jnp.int32),
-            ],
+            out_specs=[panel(0), panel(0), panel(0), pl.BlockSpec((1, heads, length), lambda p, r: (p, 0, 0))],
+            scratch_shapes=[pltpu.VMEM((length, TILE), jnp.int32)],
         ),
         out_shape=[jax.ShapeDtypeStruct((length, width), bf16)] * 3
-        + [jax.ShapeDtypeStruct((pairs, 2, length), f32)],
+        + [jax.ShapeDtypeStruct((panels, heads, length), f32)],
         compiler_params=params("arbitrary"),
-        cost_estimate=cost(4 * length * length * width, 14 * length * width, length * length * 2 * pairs),
+        cost_estimate=cost(8 * length * length * width, 14 * length * width, length * length * width // HEAD_DIM),
     )(ranges, projected, projected, projected, cosine, sine, seg_column, seg_row)
 
 
@@ -262,20 +260,17 @@
     range_ref, q_ref, k_ref, v_ref, out_ref, do_ref, lse_ref, cos_ref, sin_ref, segc_ref, segr_ref,
     grad_ref, dq, dk_low, dv_low, delta, seg_wide,
 ):
-    length = q_ref.shape[0]
+    length, width = q_ref.shape
+    heads = width // HEAD_DIM
     blocks = length // BLOCK
     step = pl.program_id(1)
 
-    def span(i):
-        return pl.ds(pl.multiple_of(i * BLOCK, BLOCK), BLOCK)
-
     @pl.when(step == 0)
     def _():
-        lanes = lax.broadcasted_iota(jnp.int32, (BLOCK, PAIR), 1)
-        first = lanes < HEAD_DIM
+        lanes = lax.broadcasted_iota(jnp.int32, (BLOCK, width), 1)
         picker = (
-            lax.broadcasted_iota(jnp.int32, (8, PAIR), 0)
-            == lax.broadcasted_iota(jnp.int32, (8, PAIR), 1) // HEAD_DIM
+            lax.broadcasted_iota(jnp.int32, (8, width), 0)
+            == lax.broadcasted_iota(jnp.int32, (8, width), 1) // HEAD_DIM
         ).astype(f32)
 
         def prepare(i, carry):
@@ -285,49 +280,39 @@
                 picker, product, (((1,), (1,)), ((), ())),
                 precision=lax.Precision.HIGHEST, preferred_element_type=f32,
             )
-            dq[rows, :] = jnp.zeros((BLOCK, PAIR), f32)
-            seg_wide[rows, :] = jnp.broadcast_to(segc_ref[rows, :], (BLOCK, PAIR))
+            dq[rows, :] = jnp.zeros((BLOCK, width), f32)
+            seg_wide[rows, :] = jnp.broadcast_to(segc_ref[rows, :], (BLOCK, TILE))
             return carry
 
         lax.fori_loop(0, blocks, prepare, 0)
 
         def unturn(values, rows):
-            return values * cos_ref[rows, :] - swap_halves(values, lanes) * sin_ref[rows, :]
+            return values * widen(cos_ref[rows, :], width) - swap_halves(values, lanes) * widen(sin_ref[rows, :], width)
 
         def one_key(j, carry):
             rows = span(j)
-            keys, values = k_ref[rows, :], v_ref[rows, :]
-            zero = jnp.zeros_like(keys)
-            keys = jnp.concatenate([jnp.where(first, keys, zero), jnp.where(first, zero, keys)], axis=0)
-            values = jnp.concatenate([jnp.where(first, values, zero), jnp.where(first, zero, values)], axis=0)
-            label = seg_wide[rows, :]
-            label = jnp.concatenate([label] * (BLOCK // PAIR), axis=1)
-
-            def one_query(i, running):
-                grad_k, grad_v = running
-                there = span(i)
-                query, grad_out = q_ref[there, :], do_ref[there, :]
-                allowed = label == segr_ref[:, there]
-                scores = dot_nt(keys, query)
-                grad_prob = dot_nt(values, grad_out)
-                parts, lows = [], []
-                for head in range(2):
-                    half = slice(head * BLOCK, (head + 1) * BLOCK)
-                    found = scores[half] - lse_ref[0, head : head + 1, there]
-                    part = jnp.exp(jnp.where(allowed, found, -1e30))
-                    parts.append(part.astype(bf16))
-                    lows.append((part * (grad_prob[half] - delta[head : head + 1, there])).astype(bf16))
-                probability = jnp.concatenate(parts, axis=0)
-                grad_scores = jnp.concatenate(lows, axis=0)
-                dq[there, :] += dot_tn(grad_scores, keys)
-                return grad_k + dot_nn(grad_scores, query), grad_v + dot_nn(probability, grad_out)
-
-            blank = jnp.zeros((2 * BLOCK, PAIR), f32)
-            grad_k, grad_v = lax.fori_loop(range_ref[0, j], range_ref[1, j], one_query, (blank, blank))
-            grad_k = jnp.where(first, grad_k[:BLOCK], grad_k[BLOCK:])
-            grad_v = jnp.where(first, grad_v[:BLOCK], grad_v[BLOCK:])
-            dk_low[rows, :] = unturn(grad_k, rows).astype(bf16)
-            dv_low[rows, :] = grad_v.astype(bf16)
+
+            def work(count):
+                there = pl.ds(pl.multiple_of(range_ref[0, j] * BLOCK, BLOCK), count * BLOCK)
+                allowed = widen(seg_wide[rows, :], count * BLOCK) == segr_ref[:, there]
+                zero = jnp.zeros((BLOCK, width), bf16)
+                grad_k, grad_v, grad_q = [], [], None
+                for h in range(heads):
+                    key = jnp.where(lanes // HEAD_DIM == h, k_ref[rows, :], zero)
+                    value = jnp.where(lanes // HEAD_DIM == h, v_ref[rows, :], zero)
+                    scores = dot_nt(key, q_ref[there, :]) - lse_ref[0, h : h + 1, there]
+                    probability = jnp.exp(jnp.where(allowed, scores, -1e30))
+                    grad_prob = dot_nt(value, do_ref[there, :])
+                    grad_scores = (probability * (grad_prob - delta[h : h + 1, there])).astype(bf16)
+                    grad_v.append(dot_nn(probability.astype(bf16), do_ref[there, :]))
+                    grad_k.append(dot_nn(grad_scores, q_ref[there, :]))
+                    part = dot_tn(grad_scores, key)
+                    grad_q = part if grad_q is None else grad_q + part
+                dq[there, :] += grad_q
+                dk_low[rows, :] = unturn(own_lanes(grad_k, lanes), rows).astype(bf16)
+                dv_low[rows, :] = own_lanes(grad_v, lanes).astype(bf16)
+
+            by_count(range_ref[1, j] - range_ref[0, j], blocks, work)
             return carry
 
         lax.fori_loop(0, blocks, one_key, 0)
@@ -350,29 +335,29 @@
 
 def attend_backward(ranges, queries, keys, projected, mixed, grad_mixed, logsum, cosine, sine, seg_column, seg_row):
     length, width = queries.shape
-    pairs = width // PAIR
-    panel = lambda shift: pl.BlockSpec((length, PAIR), lambda p, t, r: (0, shift * pairs + p))
+    panels, heads = width // TILE, TILE // HEAD_DIM
+    panel = lambda shift: pl.BlockSpec((length, TILE), lambda p, t, r: (0, shift * panels + p))
     whole = lambda shape: pl.BlockSpec(shape, lambda p, t, r: (0,) * len(shape))
     return pl.pallas_call(
         attend_backward_kernel,
         grid_spec=pltpu.PrefetchScalarGridSpec(
             num_scalar_prefetch=1,
-            grid=(pairs, 3),
+            grid=(panels, 3),
             in_specs=[panel(0), panel(0), panel(2), panel(0), panel(0),
-                      pl.BlockSpec((1, 2, length), lambda p, t, r: (p, 0, 0)),
+                      pl.BlockSpec((1, heads, length), lambda p, t, r: (p, 0, 0)),
                       whole(cosine.shape), whole(sine.shape), whole(seg_column.shape), whole(seg_row.shape)],
-            out_specs=pl.BlockSpec((length, PAIR), lambda p, t, r: (0, t * pairs + p)),
+            out_specs=pl.BlockSpec((length, TILE), lambda p, t, r: (0, t * panels + p)),
             scratch_shapes=[
-                pltpu.VMEM((length, PAIR), f32),
-                pltpu.VMEM((length, PAIR), bf16),
-                pltpu.VMEM((length, PAIR), bf16),
+                pltpu.VMEM((length, TILE), f32),
+                pltpu.VMEM((length, TILE), bf16),
+                pltpu.VMEM((length, TILE), bf16),
                 pltpu.VMEM((8, length), f32),
-                pltpu.VMEM((length, PAIR), jnp.int32),
+                pltpu.VMEM((length, TILE), jnp.int32),
             ],
         ),
         out_shape=jax.ShapeDtypeStruct((length, 3 * width), bf16),
         compiler_params=params("arbitrary", "arbitrary"),
-        cost_estimate=cost(10 * length * length * width, 16 * length * width, length * length * 2 * pairs),
+        cost_estimate=cost(20 * length * length * width, 16 * length * width, length * length * width // HEAD_DIM),
     )(ranges, queries, keys, projected, mixed, grad_mixed, logsum, cosine, sine, seg_column, seg_row)
 
 
@@ -388,7 +373,7 @@
 
 def feed_kernel(
     n_ref, cot_ref, resid_ref, up_ref, down_ref, out_ref, back_ref, gup_ref, gdown_ref,
-    total, n_turned, cot_turned, act, pre,
+    total, n_turned, act_turned, pre,
 ):
     step, last = pl.program_id(0), pl.num_programs(0) - 1
     frames, width = n_ref.shape
@@ -404,7 +389,6 @@
         def turn(i, carry):
             rows = rows_of(i)
             n_turned[:, rows] = n_ref[rows, :].T
-            cot_turned[:, rows] = cot_ref[rows, :].T
             total[rows, :] = resid_ref[rows, :]
             back_ref[rows, :] = jnp.zeros((tile, width), f32)
             return carry
@@ -418,7 +402,7 @@
         activated, slope = gelu_and_slope(hidden)
         activated = activated.astype(bf16)
         grad_pre = (grad_act * slope).astype(bf16)
-        act[rows, :] = activated
+        act_turned[:, rows] = activated.T
         pre[rows, :] = grad_pre
         total[rows, :] += dot_nn(activated, down_ref[...])
         back_ref[rows, :] += dot_nt(grad_pre, up_ref[...])
@@ -431,10 +415,16 @@
         grad_up = dot_nn(n_turned[rows, :], pre[...]).astype(bf16)
         gup_ref[0, i] = grad_up[: part // 2]
         gup_ref[1, i] = grad_up[part // 2 :]
-        gdown_ref[0, 0, rows, :] = dot_nn(cot_turned[rows, :], act[...]).astype(bf16)
         return carry
 
     lax.fori_loop(0, planes, weights, 0)
+
+    def down_weights(i, carry):
+        rows = span(i)
+        gdown_ref[0, 0, rows, :] = dot_nn(act_turned[rows, :], cot_ref[...]).astype(bf16)
+        return carry
+
+    lax.fori_loop(0, act_turned.shape[0] // BLOCK, down_weights, 0)
 
     @pl.when(step == last)
     def _():
@@ -460,19 +450,18 @@
             pl.BlockSpec((frames, width), lambda j: (0, 0)),
             pl.BlockSpec((frames, width), lambda j: (0, 0)),
             pl.BlockSpec((2, planes, width // (2 * planes), piece), lambda j: (0, 0, 0, j)),
-            pl.BlockSpec((1, 1, width, piece), lambda j: (j % 2, j // 2, 0, 0)),
+            pl.BlockSpec((1, 1, piece, width), lambda j: (j % 2, j // 2, 0, 0)),
         ],
         out_shape=[
             jax.ShapeDtypeStruct((frames, width), bf16),
             jax.ShapeDtypeStruct((frames, width), f32),
             jax.ShapeDtypeStruct((2, planes, width // (2 * planes), hidden), bf16),
-            jax.ShapeDtypeStruct((2, planes, width, piece), bf16),
+            jax.ShapeDtypeStruct((2, planes, piece, width), bf16),
         ],
         scratch_shapes=[
             pltpu.VMEM((frames, width), f32),
             pltpu.VMEM((width, frames), bf16),
-            pltpu.VMEM((width, frames), bf16),
-            pltpu.VMEM((frames, piece), bf16),
+            pltpu.VMEM((piece, frames), bf16),
             pltpu.VMEM((frames, piece), bf16),
         ],
         compiler_params=params("arbitrary"),
@@ -547,26 +536,7 @@
     skip_rows = w_skip.shape[0]
     early = jnp.concatenate([w_skip] + [w_qkv[:, i * width : (i + 1) * width] for i in range(3)], axis=0)
     early = lax.all_gather(early, ALL_AXES, axis=0, tiled=True).reshape(devices, -1, width)
-    skip_full = early[:, :skip_rows].reshape(-1, width)
-    qkv_parts = []
-    for i in range(3):
-        begin = skip_rows + i * out_rows
-        whole = early[:, begin : begin + out_rows].reshape(width, width)
-        qkv_parts.append(lax.dynamic_slice_in_dim(whole, member * heads_wide, heads_wide, 1))
-    qkv_own = jnp.concatenate(qkv_parts, axis=1)
-    columns = w_up.shape[1] // width
-    late = jnp.concatenate([w_down, w_out] + [w_up[:, i * width : (i + 1) * width] for i in range(columns)], axis=0)
-    late, early = lax.optimization_barrier((late, early))
-    late = lax.all_gather(late, ALL_AXES, axis=0, tiled=True).reshape(devices, -1, width)
-    down_full = late[:, :down_rows].reshape(-1, width)
-    out_full = late[:, down_rows : down_rows + out_rows].reshape(width, width)
-    up_full = jnp.concatenate(
-        [
-            late[:, down_rows + out_rows + i * up_rows : down_rows + out_rows + (i + 1) * up_rows].reshape(width, width)
-            for i in range(columns)
-        ],
-        axis=1,
-    )
+    x, s = to_rows(inputs), to_rows(skips)
 
     labels_own = segment_ids[:, 0]
     labels_other = lax.ppermute(labels_own, "core", swap)
@@ -589,7 +559,6 @@
     sine = jnp.concatenate([-sine, sine, -sine, sine], axis=1)
     seg_column, seg_row = seg[:, None], seg[None, :]
     mine = lax.dynamic_slice_in_dim(seg, member * frames, frames, 0)
-    mine_column, mine_row = mine[:, None], mine[None, :]
 
     steps = lax.all_gather(time_steps[:, 0], ("plane", "core"), axis=0, tiled=True).reshape(-1)
     quarter = w_mod.shape[0] // 2
@@ -604,11 +573,33 @@
         block_mod.reshape(devices, labels, own_columns), ALL_AXES, split_axis=0, concat_axis=0, tiled=True
     )
     modulation = jnp.moveaxis(block_mod, 0, 1).reshape(labels, 4, width)
+
+    columns = w_up.shape[1] // width
+    late = jnp.concatenate([w_down, w_out] + [w_up[:, i * width : (i + 1) * width] for i in range(columns)], axis=0)
+    late, cotangent, x, s, modulation, cosine, sine, ranges, mine = lax.optimization_barrier(
+        (late, cotangent, x, s, modulation, cosine, sine, ranges, mine)
+    )
+    late = lax.all_gather(late, ALL_AXES, axis=0, tiled=True).reshape(devices, -1, width)
+    cot = to_rows(cotangent)
+    down_full = late[:, :down_rows].reshape(-1, width)
+    out_full = late[:, down_rows : down_rows + out_rows].reshape(width, width)
+    up_full = jnp.concatenate(
+        [
+            late[:, down_rows + out_rows + i * up_rows : down_rows + out_rows + (i + 1) * up_rows].reshape(width, width)
+            for i in range(columns)
+        ],
+        axis=1,
+    )
+    skip_full = early[:, :skip_rows].reshape(-1, width)
+    qkv_parts = []
+    for i in range(3):
+        begin = skip_rows + i * out_rows
+        whole = early[:, begin : begin + out_rows].reshape(width, width)
+        qkv_parts.append(lax.dynamic_slice_in_dim(whole, member * heads_wide, heads_wide, 1))
+    qkv_own = jnp.concatenate(qkv_parts, axis=1)
+    mine_column, mine_row = mine[:, None], mine[None, :]
     shift_one, scale_one, shift_two, scale_two = (modulation[:, i] for i in range(4))
 
-    x, s = to_rows(inputs), to_rows(skips)
-    cot_in, x = lax.optimization_barrier((cotangent, x))
-    cot = to_rows(cot_in)
     resid_in, normed_one = rowwise(
         skip_norm_kernel,
         frames,
@@ -634,23 +625,32 @@
         normed_two, cot, resid_mid, up_full, down_full, planes
     )
 
-    def over_cores(kept):
-        other = lax.ppermute(lax.dynamic_index_in_dim(kept, 1 - core, 0, False), "core", swap)
-        own = lax.dynamic_index_in_dim(kept, core, 0, False)
+    def over_cores(kept, axis):
+        other = lax.ppermute(lax.dynamic_index_in_dim(kept, 1 - core, axis, False), "core", swap)
+        own = lax.dynamic_index_in_dim(kept, core, axis, False)
         return (own.astype(f32) + other.astype(f32)).astype(bf16)
 
-    def scatter(value):
-        return lax.psum_scatter(value, ("plane", "hi", "lo"), scatter_dimension=0, tiled=True)
-
-    def scatter_rows(value):
-        split = jnp.moveaxis(value.reshape(planes, 2, -1, value.shape[1]), 1, 0)
-        return scatter(over_cores(split).reshape(-1, value.shape[1]))
-
-    grad_up = scatter(over_cores(grad_up).reshape(-1, grad_up.shape[-1])).astype(f32)
-    grad_down = over_cores(grad_down)
-    grad_down = grad_down.reshape(planes, width, line, -1)
-    grad_down = jnp.moveaxis(grad_down, 2, 1).reshape(planes * line * width, -1)
-    grad_down = scatter(grad_down).T.astype(f32)
+    plane = lax.axis_index("plane")
+
+    def exchange(value, axes, here, count):
+        total = lax.dynamic_index_in_dim(value, here, 0, False).astype(f32)
+        for flip in range(1, count):
+            sent = lax.dynamic_index_in_dim(value, here ^ flip, 0, False)
+            total += lax.ppermute(sent, axes, [(i, i ^ flip) for i in range(count)]).astype(f32)
+        return total
+
+    def exchange_planes(value):
+        return exchange(value, "plane", plane, planes).astype(bf16)
+
+    def exchange_line(value):
+        return exchange(value.reshape(line, -1, value.shape[1]), ("hi", "lo"), place, line)
+
+    def over_planes(value):
+        value = value.reshape(-1, value.shape[-1])
+        return lax.psum_scatter(value, "plane", scatter_dimension=0, tiled=True)
+
+    grad_up, grad_down = over_cores(grad_up, 0), over_cores(grad_down, 0)
+    block_out = from_rows(result)
 
     grad_mid, grad_mid_low, grad_frames, grad_shift_two, grad_scale_two = rowwise(
         norm_two_back_kernel,
@@ -662,12 +662,20 @@
         sums=2,
         flops=2 * frames * width * width,
     )
+    grad_frames, grad_up = lax.optimization_barrier((grad_frames, grad_up))
+    grad_up = over_planes(grad_up)
     grad_heads = frames_to_heads(grad_frames)
     grad_out = lax.dot_general(mixed, grad_mid_low, (((0,), (0,)), ((), ())), preferred_element_type=f32)
-    grad_out = scatter_rows(grad_out.astype(bf16)).astype(f32)
+    grad_out = over_cores(grad_out.astype(bf16).reshape(planes, 2, -1, width), 1)
+    grad_down = jnp.concatenate(
+        [v.reshape(planes, line, -1, width) for v in (grad_down, grad_out)], axis=2
+    )
+    grad_heads, grad_down, block_out = lax.optimization_barrier((grad_heads, grad_down, block_out))
+    grad_down = over_planes(grad_down)
     grad_proj = attend_backward(
         ranges, queries, keys, projected, mixed_heads, grad_heads, logsum, cosine, sine, seg_column, seg_row
     )
+    grad_proj, grad_up, grad_down = lax.optimization_barrier((grad_proj, grad_up, grad_down))
     if group > 2:
         partial = dot_nt(grad_proj, qkv_own).astype(bf16)
         grad_one = lax.psum_scatter(partial, ROW_AXES, scatter_dimension=0, tiled=True).astype(f32)
@@ -677,6 +685,10 @@
         home = lax.dynamic_slice_in_dim(grad_proj, core * frames, frames, 0)
         grad_one_other = lax.ppermute(dot_nt(away, qkv_own).astype(bf16), "core", swap)
         grad_one = dot_nt(home, qkv_own)
+    over_line = lambda value: lax.psum_scatter(value, ("hi", "lo"), scatter_dimension=0, tiled=True).astype(f32)
+    grad_up = over_line(grad_up)
+    grad_down = over_line(grad_down)
+    grad_down, grad_out = grad_down[:down_rows], grad_down[down_rows:]
     grad_in, grad_shift_one, grad_scale_one = rowwise(
         norm_one_back_kernel,
         frames,
@@ -687,6 +699,7 @@
         sums=2,
     )
     grad_in_home = from_rows(grad_in)
+    grad_proj, grad_in = lax.optimization_barrier((grad_proj, grad_in))
     grad_qkv = lax.dot_general(normed_row, grad_proj, (((0,), (0,)), ((), ())), preferred_element_type=f32)
     grad_qkv = grad_qkv.astype(bf16)
     if group > 2:
@@ -694,7 +707,7 @@
         grad_qkv = jnp.moveaxis(grad_qkv, (1, 3), (0, 1)).reshape(group, -1, 3, 1, heads_wide)
         grad_qkv = lax.all_to_all(grad_qkv, ROW_AXES, split_axis=0, concat_axis=3, tiled=True)
         grad_qkv = grad_qkv.reshape(-1, 3 * width)
-        grad_qkv = lax.psum_scatter(grad_qkv, ("plane", "hi"), scatter_dimension=0, tiled=True)
+        grad_qkv = lax.psum_scatter(grad_qkv, ("plane", "hi"), scatter_dimension=0, tiled=True).astype(f32)
     else:
         split = grad_qkv.reshape(planes, 2, -1, 3 * heads_wide)
         other = lax.ppermute(lax.dynamic_index_in_dim(split, 1 - core, 1, False), "core", swap)
@@ -704,8 +717,7 @@
         grad_qkv = jnp.concatenate(
             [v[:, i * heads_wide : (i + 1) * heads_wide] for i in range(3) for v in (left, right)], axis=1
         )
-        grad_qkv = scatter(grad_qkv)
-    grad_qkv = grad_qkv.astype(f32)
+        grad_qkv = exchange_planes(grad_qkv.reshape(planes, -1, 3 * width))
 
     grad_skip_w = jnp.concatenate(
         [
@@ -714,14 +726,20 @@
         ],
         axis=0,
     )
-    grad_skip_w = scatter_rows(grad_skip_w).astype(f32)
-
+    grad_skip_w = exchange_planes(over_cores(grad_skip_w.reshape(planes, 2, -1, width), 1))
+    grad_in_home, grad_qkv = lax.optimization_barrier((grad_in_home, grad_qkv))
+    if group == 2:
+        grad_qkv = exchange_line(grad_qkv)
+    grad_skip_w = exchange_line(grad_skip_w)
     grad_inputs = jnp.einsum("mrfd,cd->mrfc", grad_in_home, skip_full[:width], preferred_element_type=f32).astype(bf16)
     grad_skips = jnp.einsum("mrfd,cd->mrfc", grad_in_home, skip_full[width:], preferred_element_type=f32).astype(bf16)
 
     grad_mod = jnp.stack([v[:labels] for v in (grad_shift_one, grad_scale_one, grad_shift_two, grad_scale_two)], axis=1)
     grad_mod = jnp.moveaxis(grad_mod.reshape(labels, devices, own_columns), 1, 0)
     grad_mod = lax.all_to_all(grad_mod, ALL_AXES, split_axis=0, concat_axis=0, tiled=True)
+    grad_inputs, grad_mod, grad_up, grad_down, grad_out = lax.optimization_barrier(
+        (grad_inputs, grad_mod, grad_up, grad_down, grad_out)
+    )
     grad_mod = jnp.sum(grad_mod.reshape(planes, 2, highs, lows, labels, own_columns), axis=(1, 3))
     grad_mod = lax.dot_general(
         embedded.astype(f32),
@@ -731,7 +749,7 @@
         preferred_element_type=f32,
     )
     return (
-        from_rows(result),
+        block_out,
         grad_inputs,
         grad_skips,
         grad_skip_w,

time: 1310 us -> 790 us (0.60)
  waiting for transfers between devices: 544 us -> 210 us
  starting transfers between devices: 235 us -> 109 us
  Pallas kernels: 307 us -> 245 us
    reduce_scatter x5 -> x4, waiting for transfers between devices: 320 us -> 20.4 us  [the longest x2 20.4 us: body(): lax.psum_scatter(value, ('hi', 'lo'), scatter_dimension=0, tiled=True)]
    all_gather x1, waiting for transfers between devices: 85.7 us -> 0.01 us  [body(): lax.all_gather(early, ALL_AXES, axis=0, tiled=True)]
    ppermute x1, starting transfers between devices: 79.7 us -> 0.12 us  [frames_to_row(): other = lax.ppermute(value, 'core', swap)]
    all_to_all x1, waiting for transfers between devices: 0.01 us -> 55.6 us  [body(): lax.all_to_all(block_mod.reshape(devices, labels, own_columns), ALL_AXES,...]
    all_to_all x1, starting transfers between devices: 65 us -> 20.9 us  [body(): lax.all_to_all(grad_mod, ALL_AXES, split_axis=0, concat_axis=0, tiled=True)]
    ppermute x2, starting transfers between devices: 48.6 us -> 11.5 us  [from_rows(): lax.ppermute(lax.dynamic_index_in_dim(value, 1 - high % 2, 0, False), LIN...]
    pallas_call x1, Pallas kernels: 109 us -> 75.1 us  [attend_backward(): pl.pallas_call(attend_backward_kernel, grid_spec=pltpu.PrefetchScalarGrid...]
    all_to_all x1, waiting for transfers between devices: 33.1 us -> 0.01 us  [body(): lax.all_to_all(grad_mod, ALL_AXES, split_axis=0, concat_axis=0, tiled=True)]
  transfers between devices with their start and end apart: 29 -> 40, of which waited for: 15 -> 11; matrix products, arithmetic and copies ran while one was open for 11% -> 18% of each run, Pallas kernels for 8% -> 20%
where the time goes in v2:
time: 790 us; the launch traced here: 784 us
  Pallas kernels  245 us (31%)
  waiting for transfers between devices  210 us (27%)
  starting transfers between devices  109 us (14%)
  local copies, waits for them, and re-layouts  82 us (10%)
  other arithmetic  59.8 us (8%)
  matrix products  53.3 us (7%)
  between operations  15.3 us (2%)
  blocking collectives  9.35 us (1%)
    pallas_call x1, Pallas kernels, feed_forward_and_back(): pl.pallas_call(feed_kernel, grid=(hidden // piece,), in_specs=[pl.BlockSp...  79.9 us
    pallas_call x1, Pallas kernels, attend_backward(): pl.pallas_call(attend_backward_kernel, grid_spec=pltpu.PrefetchScalarGrid...  75.1 us
    all_to_all x1, waiting for transfers between devices, body(): lax.all_to_all(block_mod.reshape(devices, labels, own_columns), ALL_AXES,...  55.6 us
    pallas_call x1, Pallas kernels, attend_forward(): pl.pallas_call(attend_forward_kernel, grid_spec=pltpu.PrefetchScalarGridS...  49.6 us
    pallas_call x4, Pallas kernels, rowwise(): pl.pallas_call(kernel, grid=(frames // tile,), in_specs=in_specs, out_spe...  40.3 us
    ppermute x3, waiting for transfers between devices, to_rows(): lax.ppermute(lax.dynamic_index_in_dim(value, 1 - odd_place, 0, False), LI...  37.4 us
    all_gather x1, waiting for transfers between devices, body(): lax.all_gather(late, ALL_AXES, axis=0, tiled=True)  32.7 us
    ppermute x3, starting transfers between devices, to_rows(): lax.ppermute(lax.dynamic_index_in_dim(value, odd_place, 0, False), LINE_A...  32.5 us
  transfers between devices with their start and end apart: 40, of which 11 were waited for; matrix products, arithmetic and copies ran while one was open for 18% of the time, Pallas kernels for 20%

profile of v2, /device:TPU:0, one launch (start us, length us, event | category | flops | bytes accessed | tf_op | source)
XLA Modules:
  0.0 784.2 jit_solution(1836120661914654081)
XLA Ops:
  13.1 9.6 %collective-permute-start.2 = (bf16[512,1024]{1,0:T(8,128)(2,1)}, bf16[512,1024]{1,0:T(8,128)(2,1)}, u32[]{:S(2)}, u32[]{:S(2)}) collective-permute-start(bf16[512,1024]{1,0:T(8,128)(2,1)} %get-tuple-element.210), channel_id=1, source_target_pairs={{0,0},{1,1},{2,4},{3,5},{4,2},{5,3},{6,6},{7,7},{8,8},{9,9},{10,12... | collective-permute-start | bytes 3145736 | tf_op jit(solution)/shard_map/ppermute | solution.py:504
  27.2 9.5 %collective-permute-start = (bf16[512,1024]{1,0:T(8,128)(2,1)}, bf16[512,1024]{1,0:T(8,128)(2,1)}, u32[]{:S(2)}, u32[]{:S(2)}) collective-permute-start(bf16[512,1024]{1,0:T(8,128)(2,1)} %get-tuple-element.214), channel_id=1, source_target_pairs={{0,0},{1,1},{2,4},{3,5},{4,2},{5,3},{6,6},{7,7},{8,8},{9,9},{10,12... | collective-permute-start | bytes 3145736 | tf_op jit(solution)/shard_map/ppermute | solution.py:504
  36.8 9.3 %all-gather = s32[16,1,4]{2,1,0:T(1,128)S(1)} all-gather(s32[2,1,4]{2,1,0:T(1,128)S(1)} %copy-done.45), channel_id=2, replica_groups=mesh['plane'=4,'core'=2,'hi'=4,'lo'=1] {'plane','core'}, dimensions={0}, use_global_device_ids=true | all-gather | bytes 288 | tf_op jit(solution)/shard_map/all_gather | solution.py:563
  64.3 15.4 %collective-permute-done.3 = bf16[512,1024]{1,0:T(8,128)(2,1)} collective-permute-done((bf16[512,1024]{1,0:T(8,128)(2,1)}, bf16[512,1024]{1,0:T(8,128)(2,1)}, u32[]{:S(2)}, u32[]{:S(2)}) %collective-permute-start.3) | collective-permute-done | bytes 1048608 | tf_op jit(solution)/shard_map/ppermute | solution.py:505
  81.4 22.0 %collective-permute-done.1 = bf16[512,1024]{1,0:T(8,128)(2,1)} collective-permute-done((bf16[512,1024]{1,0:T(8,128)(2,1)}, bf16[512,1024]{1,0:T(8,128)(2,1)}, u32[]{:S(2)}, u32[]{:S(2)}) %collective-permute-start.1) | collective-permute-done | bytes 1048608 | tf_op jit(solution)/shard_map/ppermute | solution.py:505
  107.5 55.6 %all-to-all-done = f32[32,4,128]{2,1,0:T(4,128)S(1)} async-done(((f32[32,4,128]{2,1,0:T(4,128)}), f32[32,4,128]{2,1,0:T(4,128)S(1)}, u32[]{:S(2)}, u32[]{:S(2)}) %all-to-all-start) | async-done | bytes 65568 | tf_op jit(solution)/shard_map/all_to_all | solution.py:572
  169.8 11.1 %shard_map.178 = (f32[1024,1024]{1,0:T(8,128)}, bf16[1024,1024]{1,0:T(8,128)(2,1)}) custom-call(bf16[1024,1024]{1,0:T(8,128)(2,1)} %get-tuple-element.56.x_ref, bf16[1024,1024]{1,0:T(8,128)(2,1)} %get-tuple-element.57.s_ref, bf16[1024,1024]{1,0:T(8,128)(2,1)} %bitcast.236, bf16[1024,1024]{1,0:T(8,128)(2,1)} %bitcast.234, s32[1024,1]{1,0:T(8,128)} %copy.98.seg_ref, ...), custom_call_target="tpu_custom_call" | custom-call | flops 4294967296 | bytes 14716928 | tf_op jit(solution)/shard_map/pallas_call | solution.py:149
  184.0 13.5 %collective-permute-start.7 = (bf16[512,1024]{1,0:T(8,128)(2,1)}, bf16[512,1024]{1,0:T(8,128)(2,1)S(1)}, u32[]{:S(2)}, u32[]{:S(2)}) collective-permute-start(bf16[512,1024]{1,0:T(8,128)(2,1)} %get-tuple-element.206), channel_id=1, source_target_pairs={{0,0},{1,1},{2,4},{3,5},{4,2},{5,3},{6,6},{7,7},{8,8},{9,9},{10,12... | collective-permute-start | bytes 3145736 | tf_op jit(solution)/shard_map/ppermute | solution.py:504
  212.7 10.3 %convolution_convert_fusion.q_ref.k_ref.v_ref = bf16[2048,1536]{1,0:T(8,128)(2,1)} fusion(bf16[1024,1024]{1,0:T(8,128)(2,1)S(1)} %get-tuple-element.181, bf16[1024,1024]{1,0:T(8,128)(2,1)S(1)} %get-tuple-element.180, bf16[1024,512]{1,0:T(8,128)(2,1)S(1)} %get-tuple-element.238, bf16[1024,512]{1,0:T(8,128)(2,1)S(1)} %get-tuple-element.239, ...), kind=kOutput, calls=%fused_computation.5 | convolution fusion | flops 6463422464 | bytes 13631488 | tf_op jit(solution)/shard_map/dot_general | solution.py:613
  223.0 49.6 %shard_map.179 = (bf16[2048,512]{1,0:T(8,128)(2,1)}, bf16[2048,512]{1,0:T(8,128)(2,1)}, bf16[2048,512]{1,0:T(8,128)(2,1)}, f32[4,2,2048]{2,1,0:T(2,128)}) custom-call(s32[2,8]{1,0:T(2,128)} %pad_add_fusion.range_ref, bf16[2048,1536]{1,0:T(8,128)(2,1)} %convolution_convert_fusion.q_ref.k_ref.v_ref, ...), custom_call_target="tpu_custom_call" | custom-call | flops 17179869184 | bytes 14680064 | tf_op jit(solution)/shard_map/pallas_call | solution.py:242
  283.3 32.7 %all-gather.6.cloned.1.call-done = bf16[9216,1024]{1,0:T(8,128)(2,1)} async-done(((bf16[288,1024]{1,0:T(8,128)(2,1)}), bf16[9216,1024]{1,0:T(8,128)(2,1)}) %all-gather.6.cloned.1.call-update) | async-done | bytes 18874384 | tf_op jit(solution)/shard_map/all_gather | solution.py:582
  322.4 8.3 %slice.169 = bf16[32,128,1024]{2,1,0:T(8,128)(2,1)} slice(bf16[32,288,1024]{2,1,0:T(8,128)(2,1)} %bitcast.207), slice={[0:32], [0:128], [0:1024]} | slice | bytes 16777216 | tf_op jit(solution)/shard_map/slice | solution.py:584
  336.2 8.9 %shard_map.180 = (f32[1024,1024]{1,0:T(8,128)}, bf16[1024,1024]{1,0:T(8,128)(2,1)}) custom-call(bf16[1024,1024]{1,0:T(8,128)(2,1)} %pad_maximum_fusion.9.mixed_ref, bf16[1024,1024]{1,0:T(8,128)(2,1)} %bitcast.204, f32[1024,1024]{1,0:T(8,128)} %get-tuple-element.65.resid_in_ref.resid_ref, s32[1024,1]{1,0:T(8,128)} %copy.98.seg_ref, ...), custom_call_target="tpu_custom_call" | custom-call | flops 2147483648 | bytes 14716928 | tf_op jit(solution)/shard_map/pallas_call | solution.py:149
  345.1 79.9 %shard_map.181 = (bf16[1024,1024]{1,0:T(8,128)(2,1)}, f32[1024,1024]{1,0:T(8,128)}, bf16[2,4,128,4096]{3,2,1,0:T(8,128)(2,1)}, bf16[2,4,512,1024]{3,2,1,0:T(8,128)(2,1)}) custom-call(bf16[1024,1024]{1,0:T(8,128)(2,1)} %get-tuple-element.66.n_ref, bf16[1024,1024]{1,0:T(8,128)(2,1)} %pad_maximum_fusion.10.cot_ref, f32[1024,1024]{1,0:T(8,128)} %get-tuple-element.68.resid_ref, ...), custom_call_target="tpu_custom_call" | custom-call | flops 51539607552 | bytes 50331648 | tf_op jit(solution)/shard_map/pallas_call | solution.py:439
  429.9 10.6 %shard_map.182 = (f32[1024,1024]{1,0:T(8,128)}, bf16[1024,1024]{1,0:T(8,128)(2,1)}, bf16[1024,1024]{1,0:T(8,128)(2,1)}, f32[8,1024]{1,0:T(8,128)}, f32[8,1024]{1,0:T(8,128)}) custom-call(f32[1024,1024]{1,0:T(8,128)} %get-tuple-element.69.g_ref, f32[1024,1024]{1,0:T(8,128)} %get-tuple-element.68.resid_ref, bf16[1024,1024]{1,0:T(8,128)(2,1)} %pad_maximum_fusion.10.cot_ref, ...), custom_call_target="tpu_custom_call" | custom-call | flops 2147483648 | bytes 20996096 | tf_op jit(solution)/shard_map/pallas_call | solution.py:149
  462.3 31.7 %collective-permute-done.14 = bf16[512,1024]{1,0:T(8,128)(2,1)} collective-permute-done((bf16[512,1024]{1,0:T(8,128)(2,1)}, bf16[512,1024]{1,0:T(8,128)(2,1)}, u32[]{:S(2)}, u32[]{:S(2)}) %collective-permute-start.14) | collective-permute-done | bytes 1048608 | tf_op jit(solution)/shard_map/ppermute | solution.py:511
  509.9 75.1 %shard_map.183 = bf16[2048,1536]{1,0:T(8,128)(2,1)} custom-call(s32[2,8]{1,0:T(2,128)} %pad_add_fusion.range_ref, bf16[2048,512]{1,0:T(8,128)(2,1)} %get-tuple-element.77.q_ref, bf16[2048,512]{1,0:T(8,128)(2,1)} %get-tuple-element.78.k_ref, bf16[2048,1536]{1,0:T(8,128)(2,1)} %convolution_convert_fusion.q_ref.k_ref.v_ref, ...), custom_call_target="tpu_custom_call" | custom-call | flops 42949672960 | bytes 16777216 | tf_op jit(solution)/shard_map/pallas_call | solution.py:341
  601.1 9.7 %shard_map.184 = (bf16[1024,1024]{1,0:T(8,128)(2,1)}, f32[8,1024]{1,0:T(8,128)}, f32[8,1024]{1,0:T(8,128)}) custom-call(f32[1024,1024]{1,0:T(8,128)} %fusion.5.own_ref, bf16[1024,1024]{1,0:T(8,128)(2,1)} %copy-done.10, f32[1024,1024]{1,0:T(8,128)} %get-tuple-element.65.resid_in_ref.resid_ref, f32[1024,1024]{1,0:T(8,128)} %get-tuple-element.84.mid_ref, ...), custom_call_target="tpu_custom_call" | custom-call | bytes 16801792 | tf_op jit(solution)/shard_map/pallas_call | solution.py:149
  610.8 10.4 %convolution_convert_fusion.1 = bf16[1024,1536]{1,0:T(8,128)(2,1)S(1)} fusion(bf16[2048,1536]{1,0:T(8,128)(2,1)} %shard_map.183, bf16[1024,1024]{1,0:T(8,128)(2,1)} %copy-done.22, bf16[1024,1024]{1,0:T(8,128)(2,1)} %copy-done.21), kind=kOutput, calls=%fused_computation.13 | convolution fusion | flops 6452412416 | bytes 13631488 | tf_op jit(solution)/shard_map/dot_general | solution.py:703
  624.9 9.5 %collective-permute-start.16 = (bf16[512,1024]{1,0:T(8,128)(2,1)}, bf16[512,1024]{1,0:T(8,128)(2,1)}, u32[]{:S(2)}, u32[]{:S(2)}) collective-permute-start(bf16[512,1024]{1,0:T(8,128)(2,1)} %get-tuple-element.198), channel_id=1, source_target_pairs={{0,0},{1,1},{4,2},{5,3},{2,4},{3,5},{6,6},{7,7},{8,8},{9,9},{12,10... | collective-permute-start | bytes 3145736 | tf_op jit(solution)/shard_map/ppermute | solution.py:510
  634.4 11.5 %collective-permute-start.17 = (bf16[512,1024]{1,0:T(8,128)(2,1)}, bf16[512,1024]{1,0:T(8,128)(2,1)}, u32[]{:S(2)}, u32[]{:S(2)}) collective-permute-start(bf16[512,1024]{1,0:T(8,128)(2,1)} %get-tuple-element.199), channel_id=1, source_target_pairs={{1,0},{0,1},{5,2},{4,3},{3,4},{2,5},{7,6},{6,7},{9,8},{8,9},{13,10... | collective-permute-start | bytes 3145736 | tf_op jit(solution)/shard_map/ppermute | solution.py:511
  655.6 20.9 %all-to-all-start.1 = ((f32[32,4,128]{2,1,0:T(4,128)}), f32[32,4,128]{2,1,0:T(4,128)S(1)}, u32[]{:S(2)}, u32[]{:S(2)}) async-start(f32[32,4,128]{2,1,0:T(4,128)} %copy.107), calls=%async_computation.3 | async-start | bytes 131072 | tf_op jit(solution)/shard_map/all_to_all | solution.py:739
  678.3 20.4 %reduce-scatter.11.cloned.1.call-done = bf16[160,1024]{1,0:T(8,128)(2,1)} async-done(((bf16[640,1024]{1,0:T(8,128)(2,1)}), bf16[160,1024]{1,0:T(8,128)(2,1)}) %reduce-scatter.11.cloned.1.call-update) | async-done | bytes 327696 | tf_op jit(solution)/shard_map/reduce_scatter | solution.py:688
  725.9 19.8 %collective-permute-done.20 = bf16[128,3072]{1,0:T(8,128)(2,1)S(1)} collective-permute-done((bf16[128,3072]{1,0:T(8,128)(2,1)S(1)}, bf16[128,3072]{1,0:T(8,128)(2,1)S(1)}, u32[]{:S(2)}, u32[]{:S(2)}) %collective-permute-start.20) | collective-permute-done | bytes 786464 | tf_op jit(solution)/shard_map/ppermute | solution.py:639
  (277 shorter events, 213.9 us)
Async XLA Ops:
  7.2 157.7 %all-gather.4.cloned.1.call-start = ((), (), s32[]{:S(2)}) async-start(), calls=%async_computation.6 | async-start | bytes 10813440 | tf_op jit(solution)/shard_map/all_gather | solution.py:538
  13.1 51.2 %collective-permute-start.2 = (bf16[512,1024]{1,0:T(8,128)(2,1)}, bf16[512,1024]{1,0:T(8,128)(2,1)}, u32[]{:S(2)}, u32[]{:S(2)}) collective-permute-start(bf16[512,1024]{1,0:T(8,128)(2,1)} %get-tuple-element.210), channel_id=1, source_target_pairs={{0,0},{1,1},{2,4},{3,5},{4,2},{5,3},{6,6},{7,7},{8,8},{9,9},{10,12... | collective-permute-start | bytes 3145736 | tf_op jit(solution)/shard_map/ppermute | solution.py:504
  22.7 57.0 %collective-permute-start.3 = (bf16[512,1024]{1,0:T(8,128)(2,1)}, bf16[512,1024]{1,0:T(8,128)(2,1)}, u32[]{:S(2)}, u32[]{:S(2)}) collective-permute-start(bf16[512,1024]{1,0:T(8,128)(2,1)} %get-tuple-element.211), channel_id=1, source_target_pairs={{0,1},{1,0},{2,5},{3,4},{4,3},{5,2},{6,7},{7,6},{8,9},{9,8},{10,13... | collective-permute-start | bytes 3145736 | tf_op jit(solution)/shard_map/ppermute | solution.py:505
  27.2 54.2 %collective-permute-start = (bf16[512,1024]{1,0:T(8,128)(2,1)}, bf16[512,1024]{1,0:T(8,128)(2,1)}, u32[]{:S(2)}, u32[]{:S(2)}) collective-permute-start(bf16[512,1024]{1,0:T(8,128)(2,1)} %get-tuple-element.214), channel_id=1, source_target_pairs={{0,0},{1,1},{2,4},{3,5},{4,2},{5,3},{6,6},{7,7},{8,8},{9,9},{10,12... | collective-permute-start | bytes 3145736 | tf_op jit(solution)/shard_map/ppermute | solution.py:504
  36.7 66.7 %collective-permute-start.1 = (bf16[512,1024]{1,0:T(8,128)(2,1)}, bf16[512,1024]{1,0:T(8,128)(2,1)}, u32[]{:S(2)}, u32[]{:S(2)}) collective-permute-start(bf16[512,1024]{1,0:T(8,128)(2,1)} %get-tuple-element.215), channel_id=1, source_target_pairs={{0,1},{1,0},{2,5},{3,4},{4,3},{5,2},{6,7},{7,6},{8,9},{9,8},{10,13... | collective-permute-start | bytes 3145736 | tf_op jit(solution)/shard_map/ppermute | solution.py:505
  47.8 115.2 %all-to-all-start = ((f32[32,4,128]{2,1,0:T(4,128)}), f32[32,4,128]{2,1,0:T(4,128)S(1)}, u32[]{:S(2)}, u32[]{:S(2)}) async-start(f32[32,4,128]{2,1,0:T(4,128)} %bitcast.5), calls=%async_computation | async-start | bytes 131072 | tf_op jit(solution)/shard_map/all_to_all | solution.py:572
  52.0 264.0 %all-gather.6.cloned.1.call-start = ((), (), s32[]{:S(2)}) async-start(), calls=%async_computation.7 | async-start | bytes 19464192 | tf_op jit(solution)/shard_map/all_gather | solution.py:582
  163.2 421.8 %reduce-scatter.5.cloned.1.call-start = ((), (), s32[]{:S(2)}) async-start(), calls=%async_computation.8 | async-start | bytes 5242880 | tf_op jit(solution)/shard_map/reduce_scatter | solution.py:650
  184.0 93.4 %collective-permute-start.7 = (bf16[512,1024]{1,0:T(8,128)(2,1)}, bf16[512,1024]{1,0:T(8,128)(2,1)S(1)}, u32[]{:S(2)}, u32[]{:S(2)}) collective-permute-start(bf16[512,1024]{1,0:T(8,128)(2,1)} %get-tuple-element.206), channel_id=1, source_target_pairs={{0,0},{1,1},{2,4},{3,5},{4,2},{5,3},{6,6},{7,7},{8,8},{9,9},{10,12... | collective-permute-start | bytes 3145736 | tf_op jit(solution)/shard_map/ppermute | solution.py:504
  197.4 80.0 %collective-permute-start.8 = (bf16[512,1024]{1,0:T(8,128)(2,1)}, bf16[512,1024]{1,0:T(8,128)(2,1)S(1)}, u32[]{:S(2)}, u32[]{:S(2)}) collective-permute-start(bf16[512,1024]{1,0:T(8,128)(2,1)} %get-tuple-element.207), channel_id=1, source_target_pairs={{0,1},{1,0},{2,5},{3,4},{4,3},{5,2},{6,7},{7,6},{8,9},{9,8},{10,13... | collective-permute-start | bytes 3145736 | tf_op jit(solution)/shard_map/ppermute | solution.py:505
  447.9 137.1 %reduce-scatter.7.cloned.1.call-start = ((), (), s32[]{:S(2)}) async-start(), calls=%async_computation.9 | async-start | bytes 6553600 | tf_op jit(solution)/shard_map/reduce_scatter | solution.py:650
  452.7 46.6 %collective-permute-start.11 = (bf16[4,512,1024]{2,1,0:T(8,128)(2,1)}, bf16[4,512,1024]{2,1,0:T(8,128)(2,1)}, u32[]{:S(2)}, u32[]{:S(2)}) collective-permute-start(bf16[4,512,1024]{2,1,0:T(8,128)(2,1)} %dynamic-slice_bitcast_fusion), channel_id=1, source_target_pairs={{0,4},{4,0},{1,5},{5,1},{2,6},{6,2},{3,7},{7,3},{8,12},{12,8},{9,1... | collective-permute-start | bytes 12582920 | tf_op jit(solution)/shard_map/ppermute | solution.py:629
  509.9 166.6 %reduce-scatter.9.cloned.1.call-start = ((), (), s32[]{:S(2)}) async-start(), calls=%async_computation.10 | async-start | bytes 1310720 | tf_op jit(solution)/shard_map/reduce_scatter | solution.py:688
  585.1 113.5 %reduce-scatter.11.cloned.1.call-start = ((), (), s32[]{:S(2)}) async-start(), calls=%async_computation.11 | async-start | bytes 1638400 | tf_op jit(solution)/shard_map/reduce_scatter | solution.py:688
  622.7 79.2 %collective-permute-start.18 = (bf16[4,128,1536]{2,1,0:T(8,128)(2,1)}, bf16[4,128,1536]{2,1,0:T(8,128)(2,1)S(1)}, u32[]{:S(2)}, u32[]{:S(2)}) collective-permute-start(bf16[4,128,1536]{2,1,0:T(8,128)(2,1)} %get-tuple-element.188), channel_id=1, source_target_pairs={{0,4},{4,0},{1,5},{5,1},{2,6},{6,2},{3,7},{7,3},{8,12},{12,8},{9,1... | collective-permute-start | bytes 4718600 | tf_op jit(solution)/shard_map/ppermute | solution.py:713
  624.9 81.0 %collective-permute-start.16 = (bf16[512,1024]{1,0:T(8,128)(2,1)}, bf16[512,1024]{1,0:T(8,128)(2,1)}, u32[]{:S(2)}, u32[]{:S(2)}) collective-permute-start(bf16[512,1024]{1,0:T(8,128)(2,1)} %get-tuple-element.198), channel_id=1, source_target_pairs={{0,0},{1,1},{4,2},{5,3},{2,4},{3,5},{6,6},{7,7},{8,8},{9,9},{12,10... | collective-permute-start | bytes 3145736 | tf_op jit(solution)/shard_map/ppermute | solution.py:510
  634.4 72.1 %collective-permute-start.17 = (bf16[512,1024]{1,0:T(8,128)(2,1)}, bf16[512,1024]{1,0:T(8,128)(2,1)}, u32[]{:S(2)}, u32[]{:S(2)}) collective-permute-start(bf16[512,1024]{1,0:T(8,128)(2,1)} %get-tuple-element.199), channel_id=1, source_target_pairs={{1,0},{0,1},{5,2},{4,3},{3,4},{2,5},{7,6},{6,7},{9,8},{8,9},{13,10... | collective-permute-start | bytes 3145736 | tf_op jit(solution)/shard_map/ppermute | solution.py:511
  654.8 53.6 %collective-permute-start.22 = (bf16[4,256,1024]{2,1,0:T(8,128)(2,1)}, bf16[4,256,1024]{2,1,0:T(8,128)(2,1)}, u32[]{:S(2)}, u32[]{:S(2)}) collective-permute-start(bf16[4,256,1024]{2,1,0:T(8,128)(2,1)} %dynamic-slice_bitcast_fusion.2), channel_id=1, source_target_pairs={{0,4},{4,0},{1,5},{5,1},{2,6},{6,2},{3,7},{7,3},{8,12},{12,8},{9,1... | collective-permute-start | bytes 6291464 | tf_op jit(solution)/shard_map/ppermute | solution.py:629
  655.6 95.2 %all-to-all-start.1 = ((f32[32,4,128]{2,1,0:T(4,128)}), f32[32,4,128]{2,1,0:T(4,128)S(1)}, u32[]{:S(2)}, u32[]{:S(2)}) async-start(f32[32,4,128]{2,1,0:T(4,128)} %copy.107), calls=%async_computation.3 | async-start | bytes 131072 | tf_op jit(solution)/shard_map/all_to_all | solution.py:739
  703.0 42.7 %collective-permute-start.20 = (bf16[128,3072]{1,0:T(8,128)(2,1)S(1)}, bf16[128,3072]{1,0:T(8,128)(2,1)S(1)}, u32[]{:S(2)}, u32[]{:S(2)}) collective-permute-start(bf16[128,3072]{1,0:T(8,128)(2,1)S(1)} %get-tuple-element.184), channel_id=1, source_target_pairs={{0,16},{8,24},{16,0},{24,8},{1,17},{9,25},{17,1},{25,9},{2,18},{10... | collective-permute-start | bytes 2359304 | tf_op jit(solution)/shard_map/ppermute | solution.py:639
  705.9 39.8 %collective-permute-start.21 = (bf16[128,3072]{1,0:T(8,128)(2,1)S(1)}, bf16[128,3072]{1,0:T(8,128)(2,1)S(1)}, u32[]{:S(2)}, u32[]{:S(2)}) collective-permute-start(bf16[128,3072]{1,0:T(8,128)(2,1)S(1)} %get-tuple-element.183), channel_id=1, source_target_pairs={{0,24},{8,16},{16,8},{24,0},{1,25},{9,17},{17,9},{25,1},{2,26},{10... | collective-permute-start | bytes 2359304 | tf_op jit(solution)/shard_map/ppermute | solution.py:639
  714.8 42.9 %collective-permute-start.23 = (bf16[256,1024]{1,0:T(8,128)(2,1)}, bf16[256,1024]{1,0:T(8,128)(2,1)}, u32[]{:S(2)}, u32[]{:S(2)}) collective-permute-start(bf16[256,1024]{1,0:T(8,128)(2,1)} %get-tuple-element.193), channel_id=1, source_target_pairs={{0,8},{8,0},{16,24},{24,16},{1,9},{9,1},{17,25},{25,17},{2,10},{10... | collective-permute-start | bytes 1572872 | tf_op jit(solution)/shard_map/ppermute | solution.py:639
  715.7 46.3 %collective-permute-start.24 = (bf16[256,1024]{1,0:T(8,128)(2,1)}, bf16[256,1024]{1,0:T(8,128)(2,1)}, u32[]{:S(2)}, u32[]{:S(2)}) collective-permute-start(bf16[256,1024]{1,0:T(8,128)(2,1)} %get-tuple-element.195), channel_id=1, source_target_pairs={{0,16},{8,24},{16,0},{24,8},{1,17},{9,25},{17,1},{25,9},{2,18},{10... | collective-permute-start | bytes 1572872 | tf_op jit(solution)/shard_map/ppermute | solution.py:639
  723.3 38.8 %collective-permute-start.25 = (bf16[256,1024]{1,0:T(8,128)(2,1)S(1)}, bf16[256,1024]{1,0:T(8,128)(2,1)}, u32[]{:S(2)}, u32[]{:S(2)}) collective-permute-start(bf16[256,1024]{1,0:T(8,128)(2,1)S(1)} %get-tuple-element.194), channel_id=1, source_target_pairs={{0,24},{8,16},{16,8},{24,0},{1,25},{9,17},{17,9},{25,1},{2,26},{10... | collective-permute-start | bytes 1572872 | tf_op jit(solution)/shard_map/ppermute | solution.py:639
  (63 other events, 1208.5 us)
Sparse Core Ops, SparseCore 0:
  11.4 134.6 all-gather.3
  163.3 152.6 all-gather.5
  448.1 50.9 reduce-scatter.4
  510.0 69.8 reduce-scatter.6
  585.2 53.0 reduce-scatter.8
  640.4 58.1 reduce-scatter.10

commit v3 on v2

--- a/solution.py
+++ b/solution.py
@@ -12,6 +12,9 @@
 HEAD_DIM = 64
 TILE = 128
 BLOCK = 256
+ROW_TILE = 256
+FEED_TILE = 256
+FEED_PART = 256
 VMEM_BYTES = 60 * 1024 * 1024
 ROW_AXES = ("core", "lo")
 LINE_AXES = ("core", "hi", "lo")
@@ -40,6 +43,10 @@
     return pl.CostEstimate(flops=int(flops), bytes_accessed=int(moved), transcendentals=int(special))
 
 
+def flat(ref):
+    return ref[...].reshape(-1, ref.shape[-1])
+
+
 def choose(segment_column, table_ref):
     count = table_ref.shape[0]
     picked = table_ref[count - 1 : count, :]
@@ -56,7 +63,7 @@
 
 
 def skip_norm_kernel(x_ref, s_ref, top_ref, bottom_ref, seg_ref, shift_ref, scale_ref, resid_ref, normed_ref):
-    resid = dot_nn(x_ref[...], top_ref[...]) + dot_nn(s_ref[...], bottom_ref[...])
+    resid = dot_nn(x_ref[...], flat(top_ref)) + dot_nn(s_ref[...], flat(bottom_ref))
     resid_ref[...] = resid
     unit, _ = normalise(resid)
     label = seg_ref[...]
@@ -65,7 +72,7 @@
 
 
 def out_norm_kernel(mixed_ref, w_ref, resid_in_ref, seg_ref, shift_ref, scale_ref, resid_ref, normed_ref):
-    resid = resid_in_ref[...] + dot_nn(mixed_ref[...], w_ref[...])
+    resid = resid_in_ref[...] + dot_nn(mixed_ref[...], flat(w_ref))
     resid_ref[...] = resid
     unit, _ = normalise(resid)
     label = seg_ref[...]
@@ -106,7 +113,7 @@
     low = grad_mid.astype(bf16)
     mid_ref[...] = grad_mid
     low_ref[...] = low
-    mix_ref[...] = dot_nt(low, w_ref[...]).astype(bf16)
+    mix_ref[...] = dot_nt(low, flat(w_ref)).astype(bf16)
     segment_sums(segr_ref[...], grad, dshift_ref)
     segment_sums(segr_ref[...], by_scale, dscale_ref)
 
@@ -126,12 +133,44 @@
     segment_sums(segr_ref[...], by_scale, dscale_ref)
 
 
-def rowwise(kernel, frames, blocked, whole, outs, sums=0, flops=0):
-    tile = min(BLOCK, frames)
+def unmerge_kernel(g_ref, top_ref, bottom_ref, inputs_ref, skips_ref):
+    inputs_ref[...] = dot_nt(g_ref[...], flat(top_ref)).astype(bf16)
+    skips_ref[...] = dot_nt(g_ref[...], flat(bottom_ref)).astype(bf16)
+
+
+def project_kernel(place_ref, x_ref, w_ref, out_ref):
+    out_ref[...] = dot_nn(x_ref[...], flat(w_ref)).astype(bf16)
+
+
+def project(value, gathered, begin, rows, heads_wide, member):
+    length, width = value.shape
+    tile = min(ROW_TILE, length)
+    return pl.pallas_call(
+        project_kernel,
+        grid_spec=pltpu.PrefetchScalarGridSpec(
+            num_scalar_prefetch=1,
+            grid=(3, length // tile),
+            in_specs=[
+                pl.BlockSpec((tile, width), lambda t, i, r: (i, 0)),
+                pl.BlockSpec((width // rows, rows, heads_wide), lambda t, i, r: (0, begin // rows + t, r[0])),
+            ],
+            out_specs=pl.BlockSpec((tile, heads_wide), lambda t, i, r: (i, t)),
+        ),
+        out_shape=jax.ShapeDtypeStruct((length, 3 * heads_wide), bf16),
+        compiler_params=params("arbitrary", "arbitrary"),
+        cost_estimate=cost(6 * length * width * heads_wide, 8 * length * width),
+    )(member.reshape(1), value, gathered)
+
+
+def rowwise(kernel, frames, blocked, outs, sums=0, flops=0, light=False):
+    tile = min(ROW_TILE, frames)
     in_specs, args, moved = [], [], 0
     for kind, value in blocked:
         if kind == "row":
             in_specs.append(pl.BlockSpec((1, tile), lambda i: (0, i)))
+        elif kind == "weight":
+            value, block, index = value
+            in_specs.append(pl.BlockSpec(block, functools.partial(lambda index, i: index, index)))
         elif kind == "whole":
             in_specs.append(pl.BlockSpec(value.shape, lambda i: (0, 0)))
         else:
@@ -153,7 +192,7 @@
         out_specs=out_specs,
         out_shape=shapes,
         compiler_params=params("arbitrary"),
-        cost_estimate=cost(flops, moved),
+        cost_estimate=cost(1, 1) if light else cost(flops, moved),
     )(*args)
 
 
@@ -377,7 +416,7 @@
 ):
     step, last = pl.program_id(0), pl.num_programs(0) - 1
     frames, width = n_ref.shape
-    tile = min(BLOCK, frames)
+    tile = min(FEED_TILE, frames)
     planes = gup_ref.shape[1]
     part = width // planes
 
@@ -397,44 +436,37 @@
 
     def chunk(i, carry):
         rows = rows_of(i)
-        hidden = dot_nn(n_ref[rows, :], up_ref[...])
-        grad_act = dot_nt(cot_ref[rows, :], down_ref[...])
+        up, down = flat(up_ref), flat(down_ref)
+        hidden = dot_nn(n_ref[rows, :], up)
+        grad_act = dot_nt(cot_ref[rows, :], down)
         activated, slope = gelu_and_slope(hidden)
         activated = activated.astype(bf16)
         grad_pre = (grad_act * slope).astype(bf16)
         act_turned[:, rows] = activated.T
         pre[rows, :] = grad_pre
-        total[rows, :] += dot_nn(activated, down_ref[...])
-        back_ref[rows, :] += dot_nt(grad_pre, up_ref[...])
+        total[rows, :] += dot_nn(activated, down)
+        back_ref[rows, :] += dot_nt(grad_pre, up)
         return carry
 
     lax.fori_loop(0, frames // tile, chunk, 0)
 
-    def weights(i, carry):
-        rows = pl.ds(pl.multiple_of(i * part, part), part)
-        grad_up = dot_nn(n_turned[rows, :], pre[...]).astype(bf16)
-        gup_ref[0, i] = grad_up[: part // 2]
-        gup_ref[1, i] = grad_up[part // 2 :]
-        return carry
-
-    lax.fori_loop(0, planes, weights, 0)
-
-    def down_weights(i, carry):
-        rows = span(i)
+    for begin in range(0, width, FEED_PART):
+        grad_up = dot_nn(n_turned[begin : begin + FEED_PART, :], pre[...]).astype(bf16)
+        for first in range(begin, begin + FEED_PART, part // 2):
+            which, half = first // part, first % part // (part // 2)
+            gup_ref[half, which] = grad_up[first - begin : first - begin + part // 2]
+    piece = act_turned.shape[0]
+    for begin in range(0, piece, FEED_PART):
+        rows = slice(begin, begin + FEED_PART)
         gdown_ref[0, 0, rows, :] = dot_nn(act_turned[rows, :], cot_ref[...]).astype(bf16)
-        return carry
-
-    lax.fori_loop(0, act_turned.shape[0] // BLOCK, down_weights, 0)
 
     @pl.when(step == last)
     def _():
         out_ref[...] = total[...].astype(bf16)
 
 
-def feed_forward_and_back(normed, cot, resid, w_up, w_down, planes):
+def feed_forward_and_back(normed, cot, resid, hidden, piece, w_up, w_down, planes):
     frames, width = normed.shape
-    hidden = w_up.shape[1]
-    piece = hidden // (2 * planes)
     once = dict(pipeline_mode=pl.Buffered(1))
     return pl.pallas_call(
         feed_kernel,
@@ -443,8 +475,8 @@
             pl.BlockSpec((frames, width), lambda j: (0, 0), **once),
             pl.BlockSpec((frames, width), lambda j: (0, 0), **once),
             pl.BlockSpec((frames, width), lambda j: (0, 0), **once),
-            pl.BlockSpec((width, piece), lambda j: (0, j)),
-            pl.BlockSpec((piece, width), lambda j: (j, 0)),
+            pl.BlockSpec(*w_up[1:]),
+            pl.BlockSpec(*w_down[1:]),
         ],
         out_specs=[
             pl.BlockSpec((frames, width), lambda j: (0, 0)),
@@ -466,7 +498,7 @@
         ],
         compiler_params=params("arbitrary"),
         cost_estimate=cost(12 * frames * width * hidden, 8 * width * hidden + 16 * frames * width, frames * hidden),
-    )(normed, cot, resid, w_up, w_down)
+    )(normed, cot, resid, w_up[0], w_down[0])
 
 
 def body(inputs, skips, cotangent, segment_ids, time_steps, w_skip, w_qkv, w_out, w_up, w_down, w_mod):
@@ -534,9 +566,8 @@
 
     up_rows, down_rows, out_rows = w_up.shape[0], w_down.shape[0], w_out.shape[0]
     skip_rows = w_skip.shape[0]
-    early = jnp.concatenate([w_skip] + [w_qkv[:, i * width : (i + 1) * width] for i in range(3)], axis=0)
+    early = jnp.concatenate([w_skip] + [w_qkv[:, i * width : (i + 1) * width] for i in range(3)] + [w_out], axis=0)
     early = lax.all_gather(early, ALL_AXES, axis=0, tiled=True).reshape(devices, -1, width)
-    x, s = to_rows(inputs), to_rows(skips)
 
     labels_own = segment_ids[:, 0]
     labels_other = lax.ppermute(labels_own, "core", swap)
@@ -574,55 +605,76 @@
     )
     modulation = jnp.moveaxis(block_mod, 0, 1).reshape(labels, 4, width)
 
+    inputs, skips, modulation, seg = lax.optimization_barrier((inputs, skips, modulation, seg))
+    x, s = to_rows(inputs), to_rows(skips)
     columns = w_up.shape[1] // width
-    late = jnp.concatenate([w_down, w_out] + [w_up[:, i * width : (i + 1) * width] for i in range(columns)], axis=0)
+    late = jnp.concatenate([w_down] + [w_up[:, i * width : (i + 1) * width] for i in range(columns)], axis=0)
     late, cotangent, x, s, modulation, cosine, sine, ranges, mine = lax.optimization_barrier(
         (late, cotangent, x, s, modulation, cosine, sine, ranges, mine)
     )
     late = lax.all_gather(late, ALL_AXES, axis=0, tiled=True).reshape(devices, -1, width)
     cot = to_rows(cotangent)
-    down_full = late[:, :down_rows].reshape(-1, width)
-    out_full = late[:, down_rows : down_rows + out_rows].reshape(width, width)
-    up_full = jnp.concatenate(
-        [
-            late[:, down_rows + out_rows + i * up_rows : down_rows + out_rows + (i + 1) * up_rows].reshape(width, width)
-            for i in range(columns)
-        ],
-        axis=1,
-    )
-    skip_full = early[:, :skip_rows].reshape(-1, width)
-    qkv_parts = []
-    for i in range(3):
-        begin = skip_rows + i * out_rows
-        whole = early[:, begin : begin + out_rows].reshape(width, width)
-        qkv_parts.append(lax.dynamic_slice_in_dim(whole, member * heads_wide, heads_wide, 1))
-    qkv_own = jnp.concatenate(qkv_parts, axis=1)
+    in_place = out_rows % 16 == 0
+    hidden = w_up.shape[1]
+    chunk = hidden // (2 * planes)
+
+    def weight(gathered, begin, rows, first, count):
+        block = (count // rows, rows, width)
+        if in_place:
+            return gathered, block, (first // count, begin // rows, 0)
+        taken = gathered[first // rows : (first + count) // rows, begin : begin + rows]
+        return taken.reshape(1, count, width), (1, count, width), (0, 0, 0)
+
+    skip_top, skip_bottom = (weight(early, 0, skip_rows, i * width, width) for i in range(2))
+    out_weight = weight(early, skip_rows + 3 * out_rows, out_rows, 0, width)
+    if in_place:
+        per = width // chunk
+        up_weight = (late, (devices, up_rows, chunk), lambda j: (0, down_rows // up_rows + j // per, j % per))
+        down_weight = (late, (chunk // down_rows, down_rows, width), lambda j: (j, 0, 0))
+    else:
+        pieces = [late[:, down_rows + i * up_rows : down_rows + (i + 1) * up_rows] for i in range(columns)]
+        up_full = jnp.concatenate([v.reshape(width, width) for v in pieces], axis=1)
+        up_weight = (up_full[None], (1, width, chunk), lambda j: (0, 0, j))
+        down_weight = (late[:, :down_rows].reshape(1, -1, width), (1, chunk, width), lambda j: (0, j, 0))
+
+    def own_qkv(gathered):
+        parts = []
+        for i in range(3):
+            begin = skip_rows + i * out_rows
+            whole = gathered[:, begin : begin + out_rows].reshape(width, width)
+            parts.append(lax.dynamic_slice_in_dim(whole, member * heads_wide, heads_wide, 1))
+        return jnp.concatenate(parts, axis=1)
+
     mine_column, mine_row = mine[:, None], mine[None, :]
     shift_one, scale_one, shift_two, scale_two = (modulation[:, i] for i in range(4))
 
     resid_in, normed_one = rowwise(
         skip_norm_kernel,
         frames,
-        [("", x), ("", s), ("whole", skip_full[:width]), ("whole", skip_full[width:]), ("", mine_column),
+        [("", x), ("", s), ("weight", skip_top), ("weight", skip_bottom), ("", mine_column),
          ("whole", shift_one), ("whole", scale_one)],
-        None,
         [(width, f32), (width, bf16)],
         flops=4 * frames * width * width,
     )
     normed_row = frames_to_row(normed_one)
-    projected = jnp.dot(normed_row, qkv_own, preferred_element_type=f32).astype(bf16)
+    if in_place:
+        projected = project(normed_row, early, skip_rows, out_rows, heads_wide, member)
+    else:
+        projected = jnp.dot(normed_row, own_qkv(early), preferred_element_type=f32).astype(bf16)
     mixed_heads, queries, keys, logsum = attend_forward(ranges, projected, cosine, sine, seg_column, seg_row)
     mixed = heads_to_frames(mixed_heads)
     resid_mid, normed_two = rowwise(
         out_norm_kernel,
         frames,
-        [("", mixed), ("whole", out_full), ("", resid_in), ("", mine_column), ("whole", shift_two), ("whole", scale_two)],
-        None,
+        [("", mixed), ("weight", out_weight), ("", resid_in), ("", mine_column), ("whole", shift_two), ("whole", scale_two)],
         [(width, f32), (width, bf16)],
         flops=2 * frames * width * width,
     )
+    early, normed_two = lax.optimization_barrier((early, normed_two))
+    qkv_own = own_qkv(early)
+    normed_two, qkv_own = lax.optimization_barrier((normed_two, qkv_own))
     result, grad_normed_two, grad_up, grad_down = feed_forward_and_back(
-        normed_two, cot, resid_mid, up_full, down_full, planes
+        normed_two, cot, resid_mid, hidden, chunk, up_weight, down_weight, planes
     )
 
     def over_cores(kept, axis):
@@ -645,37 +697,38 @@
     def exchange_line(value):
         return exchange(value.reshape(line, -1, value.shape[1]), ("hi", "lo"), place, line)
 
-    def over_planes(value):
+    def scatter(value):
         value = value.reshape(-1, value.shape[-1])
-        return lax.psum_scatter(value, "plane", scatter_dimension=0, tiled=True)
+        return lax.psum_scatter(value, ("plane", "hi", "lo"), scatter_dimension=0, tiled=True)
 
     grad_up, grad_down = over_cores(grad_up, 0), over_cores(grad_down, 0)
-    block_out = from_rows(result)
 
     grad_mid, grad_mid_low, grad_frames, grad_shift_two, grad_scale_two = rowwise(
         norm_two_back_kernel,
         frames,
         [("", grad_normed_two), ("", resid_mid), ("", cot), ("", mine_column), ("row", mine_row),
-         ("whole", scale_two), ("whole", out_full)],
-        None,
+         ("whole", scale_two), ("weight", out_weight)],
         [(width, f32), (width, bf16), (width, bf16)],
         sums=2,
-        flops=2 * frames * width * width,
+        light=True,
     )
     grad_frames, grad_up = lax.optimization_barrier((grad_frames, grad_up))
-    grad_up = over_planes(grad_up)
+    grad_up = scatter(grad_up)
     grad_heads = frames_to_heads(grad_frames)
     grad_out = lax.dot_general(mixed, grad_mid_low, (((0,), (0,)), ((), ())), preferred_element_type=f32)
     grad_out = over_cores(grad_out.astype(bf16).reshape(planes, 2, -1, width), 1)
     grad_down = jnp.concatenate(
         [v.reshape(planes, line, -1, width) for v in (grad_down, grad_out)], axis=2
     )
-    grad_heads, grad_down, block_out = lax.optimization_barrier((grad_heads, grad_down, block_out))
-    grad_down = over_planes(grad_down)
+    grad_heads, grad_down, result = lax.optimization_barrier((grad_heads, grad_down, result))
+    block_out = from_rows(result)
+    grad_down = exchange_planes(grad_down.reshape(planes, -1, width))
     grad_proj = attend_backward(
         ranges, queries, keys, projected, mixed_heads, grad_heads, logsum, cosine, sine, seg_column, seg_row
     )
-    grad_proj, grad_up, grad_down = lax.optimization_barrier((grad_proj, grad_up, grad_down))
+    grad_proj, grad_up, grad_down, block_out = lax.optimization_barrier((grad_proj, grad_up, grad_down, block_out))
+    grad_down = grad_down.reshape(line, -1, width)
+    grad_down = lax.all_to_all(grad_down, ("hi", "lo"), split_axis=0, concat_axis=0, tiled=True)
     if group > 2:
         partial = dot_nt(grad_proj, qkv_own).astype(bf16)
         grad_one = lax.psum_scatter(partial, ROW_AXES, scatter_dimension=0, tiled=True).astype(f32)
@@ -685,16 +738,11 @@
         home = lax.dynamic_slice_in_dim(grad_proj, core * frames, frames, 0)
         grad_one_other = lax.ppermute(dot_nt(away, qkv_own).astype(bf16), "core", swap)
         grad_one = dot_nt(home, qkv_own)
-    over_line = lambda value: lax.psum_scatter(value, ("hi", "lo"), scatter_dimension=0, tiled=True).astype(f32)
-    grad_up = over_line(grad_up)
-    grad_down = over_line(grad_down)
-    grad_down, grad_out = grad_down[:down_rows], grad_down[down_rows:]
     grad_in, grad_shift_one, grad_scale_one = rowwise(
         norm_one_back_kernel,
         frames,
         [("", grad_one), ("", grad_one_other), ("", resid_in), ("", grad_mid), ("", mine_column), ("row", mine_row),
          ("whole", scale_one)],
-        None,
         [(width, bf16)],
         sums=2,
     )
@@ -731,15 +779,24 @@
     if group == 2:
         grad_qkv = exchange_line(grad_qkv)
     grad_skip_w = exchange_line(grad_skip_w)
-    grad_inputs = jnp.einsum("mrfd,cd->mrfc", grad_in_home, skip_full[:width], preferred_element_type=f32).astype(bf16)
-    grad_skips = jnp.einsum("mrfd,cd->mrfc", grad_in_home, skip_full[width:], preferred_element_type=f32).astype(bf16)
-
+    grad_inputs, grad_skips = rowwise(
+        unmerge_kernel,
+        frames,
+        [("", grad_in_home.reshape(frames, width)), ("weight", skip_top), ("weight", skip_bottom)],
+        [(width, bf16), (width, bf16)],
+        flops=4 * frames * width * width,
+    )
+    grad_inputs, grad_skips = (v.reshape(grad_in_home.shape) for v in (grad_inputs, grad_skips))
+
+    grad_shift_one, grad_qkv = lax.optimization_barrier((grad_shift_one, grad_qkv))
     grad_mod = jnp.stack([v[:labels] for v in (grad_shift_one, grad_scale_one, grad_shift_two, grad_scale_two)], axis=1)
     grad_mod = jnp.moveaxis(grad_mod.reshape(labels, devices, own_columns), 1, 0)
     grad_mod = lax.all_to_all(grad_mod, ALL_AXES, split_axis=0, concat_axis=0, tiled=True)
-    grad_inputs, grad_mod, grad_up, grad_down, grad_out = lax.optimization_barrier(
-        (grad_inputs, grad_mod, grad_up, grad_down, grad_out)
-    )
+    grad_inputs, grad_mod, grad_up, grad_down, grad_skip_w = lax.optimization_barrier(
+        (grad_inputs, grad_mod, grad_up, grad_down, grad_skip_w)
+    )
+    grad_up, grad_down = grad_up.astype(f32), jnp.sum(grad_down.astype(f32), axis=0)
+    grad_down, grad_out = grad_down[:down_rows], grad_down[down_rows:]
     grad_mod = jnp.sum(grad_mod.reshape(planes, 2, highs, lows, labels, own_columns), axis=(1, 3))
     grad_mod = lax.dot_general(
         embedded.astype(f32),

time: 790 us -> 742 us (0.939)
  waiting for transfers between devices: 210 us -> 167 us
  local copies, waits for them, and re-layouts: 82 us -> 53.5 us
  Pallas kernels: 245 us -> 269 us
  matrix products: 53.3 us -> 34.7 us
  starting transfers between devices: 109 us -> 127 us
    all_to_all x1, waiting for transfers between devices: 55.6 us -> 0.01 us  [body(): lax.all_to_all(block_mod.reshape(devices, labels, own_columns), ALL_AXES,...]
    ppermute x3, waiting for transfers between devices: 37.4 us -> 92 us  [to_rows(): lax.ppermute(lax.dynamic_index_in_dim(value, 1 - odd_place, 0, False), LI...]
    ppermute x1, starting transfers between devices: 0.12 us -> 33.4 us  [frames_to_row(): other = lax.ppermute(value, 'core', swap)]
    ppermute x12 -> x15, starting transfers between devices: 17.9 us -> 43 us  [exchange(): lax.ppermute(sent, axes, [(i, i ^ flip) for i in range(count)]).astype(f32)]
    pallas_call x0 -> x1, Pallas kernels: none -> 22.4 us  [project(): pl.pallas_call(project_kernel, grid_spec=pltpu.PrefetchScalarGridSpec(num...]
    ppermute x3, starting transfers between devices: 32.5 us -> 11 us  [to_rows(): lax.ppermute(lax.dynamic_index_in_dim(value, odd_place, 0, False), LINE_A...]
    slice x5 -> x1, local copies, waits for them, and re-layouts: 24.9 us -> 4.65 us  [own_qkv(): whole = gathered[:, begin:begin + out_rows].reshape(width, width)]
    dot_general x3 -> x0, matrix products: 19.9 us -> none  [the longest x1 10.3 us: body(): jnp.dot(normed_row, qkv_own, preferred_element_type=f32).astype(bf16)]
  transfers between devices with their start and end apart: 40 -> 41, of which waited for: 11 -> 13; matrix products, arithmetic and copies ran while one was open for 18% -> 16% of each run, Pallas kernels for 20% -> 27%
where the time goes in v3:
time: 742 us; the launch traced here: 732 us
  Pallas kernels  269 us (36%)
  waiting for transfers between devices  167 us (23%)
  starting transfers between devices  127 us (17%)
  other arithmetic  54.9 us (7%)
  local copies, waits for them, and re-layouts  53.5 us (7%)
  matrix products  34.7 us (5%)
  between operations  14.8 us (2%)
  blocking collectives  10.5 us (1%)
    ppermute x3, waiting for transfers between devices, to_rows(): lax.ppermute(lax.dynamic_index_in_dim(value, 1 - odd_place, 0, False), LI...  92 us
    pallas_call x1, Pallas kernels, attend_backward(): pl.pallas_call(attend_backward_kernel, grid_spec=pltpu.PrefetchScalarGrid...  75.1 us
    pallas_call x1, Pallas kernels, feed_forward_and_back(): pl.pallas_call(feed_kernel, grid=(hidden // piece,), in_specs=[pl.BlockSp...  73.1 us
    pallas_call x1, Pallas kernels, attend_forward(): pl.pallas_call(attend_forward_kernel, grid_spec=pltpu.PrefetchScalarGridS...  49.5 us
    pallas_call x5, Pallas kernels, rowwise(): pl.pallas_call(kernel, grid=(frames // tile,), in_specs=in_specs, out_spe...  48.5 us
    ppermute x15, starting transfers between devices, exchange(): lax.ppermute(sent, axes, [(i, i ^ flip) for i in range(count)]).astype(f32)  43 us
    ppermute x1, starting transfers between devices, frames_to_row(): other = lax.ppermute(value, 'core', swap)  33.4 us
    pallas_call x1, Pallas kernels, project(): pl.pallas_call(project_kernel, grid_spec=pltpu.PrefetchScalarGridSpec(num...  22.4 us
  transfers between devices with their start and end apart: 41, of which 13 were waited for; matrix products, arithmetic and copies ran while one was open for 16% of the time, Pallas kernels for 27%

profile of v3, /device:TPU:0, one launch (start us, length us, event | category | flops | bytes accessed | tf_op | source)
XLA Modules:
  0.0 731.7 jit_solution(2867958674076700180)
XLA Ops:
  12.4 10.5 %all-gather = s32[16,1,4]{2,1,0:T(1,128)S(1)} all-gather(s32[2,1,4]{2,1,0:T(1,128)} %param.15), channel_id=2, replica_groups=mesh['plane'=4,'core'=2,'hi'=4,'lo'=1] {'plane','core'}, dimensions={0}, use_global_device_ids=true | all-gather | bytes 288 | tf_op jit(solution)/shard_map/all_gather | solution.py:594
  48.8 36.9 %collective-permute-done.3 = bf16[512,1024]{1,0:T(8,128)(2,1)S(1)} collective-permute-done((bf16[512,1024]{1,0:T(8,128)(2,1)S(1)}, bf16[512,1024]{1,0:T(8,128)(2,1)S(1)}, u32[]{:S(2)}, u32[]{:S(2)}) %collective-permute-start.3) | collective-permute-done | bytes 1048608 | tf_op jit(solution)/shard_map/ppermute | solution.py:537
  85.9 55.1 %collective-permute-done.1 = bf16[512,1024]{1,0:T(8,128)(2,1)S(1)} collective-permute-done((bf16[512,1024]{1,0:T(8,128)(2,1)S(1)}, bf16[512,1024]{1,0:T(8,128)(2,1)S(1)}, u32[]{:S(2)}, u32[]{:S(2)}) %collective-permute-start.1) | collective-permute-done | bytes 1048608 | tf_op jit(solution)/shard_map/ppermute | solution.py:537
  147.4 11.0 %shard_map.178 = (f32[1024,1024]{1,0:T(8,128)}, bf16[1024,1024]{1,0:T(8,128)(2,1)}) custom-call(bf16[1024,1024]{1,0:T(8,128)(2,1)} %get-tuple-element.71.x_ref, bf16[1024,1024]{1,0:T(8,128)(2,1)} %get-tuple-element.72.s_ref, bf16[32,192,1024]{2,1,0:T(8,128)(2,1)} %bitcast.192, bf16[32,192,1024]{2,1,0:T(8,128)(2,1)} %bitcast.193, s32[1024,1]{1,0:T(8,128)} %copy.98.seg_ref, ...), custom_call_target="tpu_custom_call" | custom-call | flops 4294967296 | bytes 35688448 | tf_op jit(solution)/shard_map/pallas_call | solution.py:188
  158.4 33.4 %collective-permute-start.5 = (bf16[1024,1024]{1,0:T(8,128)(2,1)}, bf16[1024,1024]{1,0:T(8,128)(2,1)}, u32[]{:S(2)}, u32[]{:S(2)}) collective-permute-start(bf16[1024,1024]{1,0:T(8,128)(2,1)} %get-tuple-element.75), channel_id=1, source_target_pairs={{0,4},{4,0},{1,5},{5,1},{2,6},{6,2},{3,7},{7,3},{8,12},{12,8},{9,1... | collective-permute-start | bytes 6291464 | tf_op jit(solution)/shard_map/ppermute | solution.py:550
  194.7 9.6 %collective-permute-start.7 = (bf16[512,1024]{1,0:T(8,128)(2,1)}, bf16[512,1024]{1,0:T(8,128)(2,1)}, u32[]{:S(2)}, u32[]{:S(2)}) collective-permute-start(bf16[512,1024]{1,0:T(8,128)(2,1)} %get-tuple-element.226), channel_id=1, source_target_pairs={{0,0},{1,1},{2,4},{3,5},{4,2},{5,3},{6,6},{7,7},{8,8},{9,9},{10,12... | collective-permute-start | bytes 3145736 | tf_op jit(solution)/shard_map/ppermute | solution.py:536
  204.3 11.8 %collective-permute-start.8 = (bf16[512,1024]{1,0:T(8,128)(2,1)}, bf16[512,1024]{1,0:T(8,128)(2,1)}, u32[]{:S(2)}, u32[]{:S(2)}) collective-permute-start(bf16[512,1024]{1,0:T(8,128)(2,1)} %get-tuple-element.227), channel_id=1, source_target_pairs={{0,1},{1,0},{2,5},{3,4},{4,3},{5,2},{6,7},{7,6},{8,9},{9,8},{10,13... | collective-permute-start | bytes 3145736 | tf_op jit(solution)/shard_map/ppermute | solution.py:537
  222.7 22.4 %shard_map.179.q_ref.k_ref.v_ref = bf16[2048,1536]{1,0:T(8,128)(2,1)} custom-call(s32[1]{0:T(128)} %bitcast.13.place_ref, bf16[2048,1024]{1,0:T(8,128)(2,1)} %pad_maximum_fusion.1.x_ref, bf16[32,192,1024]{2,1,0:T(8,128)(2,1)} %bitcast.194), custom_call_target="tpu_custom_call" | custom-call | flops 6442450944 | bytes 16777216 | tf_op jit(solution)/shard_map/pallas_call | solution.py:148
  245.1 49.5 %shard_map.180 = (bf16[2048,512]{1,0:T(8,128)(2,1)}, bf16[2048,512]{1,0:T(8,128)(2,1)}, bf16[2048,512]{1,0:T(8,128)(2,1)}, f32[4,2,2048]{2,1,0:T(2,128)}) custom-call(s32[2,8]{1,0:T(2,128)} %pad_add_fusion.range_ref, bf16[2048,1536]{1,0:T(8,128)(2,1)} %shard_map.179.q_ref.k_ref.v_ref, bf16[2048,1536]{1,0:T(8,128)(2,1)} %shard_map.179.q_ref.k_ref.v_ref, ...), custom_call_target="tpu_custom_call" | custom-call | flops 17179869184 | bytes 14680064 | tf_op jit(solution)/shard_map/pallas_call | solution.py:281
  302.3 8.7 %shard_map.181 = (f32[1024,1024]{1,0:T(8,128)}, bf16[1024,1024]{1,0:T(8,128)(2,1)}) custom-call(bf16[1024,1024]{1,0:T(8,128)(2,1)} %pad_maximum_fusion.6.mixed_ref, bf16[32,192,1024]{2,1,0:T(8,128)(2,1)} %bitcast.195, f32[1024,1024]{1,0:T(8,128)} %get-tuple-element.81.resid_in_ref.resid_ref, s32[1024,1]{1,0:T(8,128)} %copy.98.seg_ref, ...), custom_call_target="tpu_custom_call" | custom-call | flops 2147483648 | bytes 25202688 | tf_op jit(solution)/shard_map/pallas_call | solution.py:188
  317.8 14.1 %all-gather.6.cloned.1.call-done = bf16[8192,1024]{1,0:T(8,128)(2,1)} async-done(((bf16[256,1024]{1,0:T(8,128)(2,1)}), bf16[8192,1024]{1,0:T(8,128)(2,1)}) %all-gather.6.cloned.1.call-update) | async-done | bytes 16777232 | tf_op jit(solution)/shard_map/all_gather | solution.py:615
  332.0 73.1 %shard_map.182 = (bf16[1024,1024]{1,0:T(8,128)(2,1)}, f32[1024,1024]{1,0:T(8,128)}, bf16[2,4,128,4096]{3,2,1,0:T(8,128)(2,1)}, bf16[2,4,512,1024]{3,2,1,0:T(8,128)(2,1)}) custom-call(bf16[1024,1024]{1,0:T(8,128)(2,1)} %get-tuple-element.85.n_ref, bf16[1024,1024]{1,0:T(8,128)(2,1)} %pad_maximum_fusion.7.cot_ref, f32[1024,1024]{1,0:T(8,128)} %get-tuple-element.87.resid_ref, ...), custom_call_target="tpu_custom_call" | custom-call | flops 51539607552 | bytes 50331648 | tf_op jit(solution)/shard_map/pallas_call | solution.py:471
  414.0 10.5 %shard_map.183 = (f32[1024,1024]{1,0:T(8,128)}, bf16[1024,1024]{1,0:T(8,128)(2,1)}, bf16[1024,1024]{1,0:T(8,128)(2,1)}, f32[8,1024]{1,0:T(8,128)}, f32[8,1024]{1,0:T(8,128)}) custom-call(f32[1024,1024]{1,0:T(8,128)} %get-tuple-element.89.g_ref, f32[1024,1024]{1,0:T(8,128)} %get-tuple-element.87.resid_ref, bf16[1024,1024]{1,0:T(8,128)(2,1)} %pad_maximum_fusion.7.cot_ref, ...), custom_call_target="tpu_custom_call" | custom-call | flops 1 | bytes 1 | tf_op jit(solution)/shard_map/pallas_call | solution.py:188
  424.5 7.2 fusion.1
  462.0 75.1 %shard_map.184 = bf16[2048,1536]{1,0:T(8,128)(2,1)} custom-call(s32[2,8]{1,0:T(2,128)} %pad_add_fusion.range_ref, bf16[2048,512]{1,0:T(8,128)(2,1)} %get-tuple-element.78.q_ref, bf16[2048,512]{1,0:T(8,128)(2,1)} %get-tuple-element.79.k_ref, bf16[2048,1536]{1,0:T(8,128)(2,1)} %shard_map.179.q_ref.k_ref.v_ref, bf16[2048,512]{1,0:T(8,128)(2,1)} %get-tuple-element.80.out_ref, ...), custom_call_target="tpu_custom_call" | custom-call | flops 42949672960 | bytes 16777216 | tf_op jit(solution)/shard_map/pallas_call | solution.py:380
  544.9 20.0 %reduce-scatter.2.cloned.1.call-done = bf16[32,4096]{1,0:T(8,128)(2,1)} async-done(((bf16[512,4096]{1,0:T(8,128)(2,1)}), bf16[32,4096]{1,0:T(8,128)(2,1)}) %reduce-scatter.2.cloned.1.call-update) | async-done | bytes 262160 | tf_op jit(solution)/shard_map/reduce_scatter | solution.py:702
  571.5 11.7 %all-to-all-start.2 = ((bf16[4,160,1024]{2,1,0:T(8,128)(2,1)}), bf16[4,160,1024]{2,1,0:T(8,128)(2,1)S(1)}, u32[]{:S(2)}, u32[]{:S(2)}) async-start(bf16[4,160,1024]{2,1,0:T(8,128)(2,1)} %bitcast.77), calls=%async_computation.3 | async-start | bytes 2621440 | tf_op jit(solution)/shard_map/all_to_all | solution.py:731
  583.1 8.3 %fusion.5.own_ref = f32[1024,1024]{1,0:T(8,128)} fusion(bf16[1024,1536]{1,0:T(8,128)(2,1)} %pad_maximum_fusion.3, bf16[2048,1536]{1,0:T(8,128)(2,1)} %shard_map.184, s32[]{:T(128)S(6)} %select_n.268), kind=kOutput, calls=%fused_computation.15 | convolution fusion | flops 3221225472 | bytes 10485764 | tf_op jit(solution)/shard_map/dot_general | solution.py:31
  591.5 9.8 %shard_map.185 = (bf16[1024,1024]{1,0:T(8,128)(2,1)}, f32[8,1024]{1,0:T(8,128)}, f32[8,1024]{1,0:T(8,128)}) custom-call(f32[1024,1024]{1,0:T(8,128)} %fusion.5.own_ref, bf16[1024,1024]{1,0:T(8,128)(2,1)} %collective-permute-done.18.other_ref, f32[1024,1024]{1,0:T(8,128)} %get-tuple-element.81.resid_in_ref.resid_ref, ...), custom_call_target="tpu_custom_call" | custom-call | bytes 16801792 | tf_op jit(solution)/shard_map/pallas_call | solution.py:188
  601.3 9.8 %convolution_convert_fusion = bf16[1024,1536]{1,0:T(8,128)(2,1)S(1)} fusion(bf16[2048,1536]{1,0:T(8,128)(2,1)} %shard_map.184, bf16[1024,1024]{1,0:T(8,128)(2,1)} %copy-done.8, bf16[1024,1024]{1,0:T(8,128)(2,1)S(1)} %copy-done.7), kind=kOutput, calls=%fused_computation.11 | convolution fusion | flops 6452412416 | bytes 13631488 | tf_op jit(solution)/shard_map/dot_general | solution.py:751
  626.6 19.1 %collective-permute-done.20 = bf16[512,1024]{1,0:T(8,128)(2,1)S(1)} collective-permute-done((bf16[512,1024]{1,0:T(8,128)(2,1)S(1)}, bf16[512,1024]{1,0:T(8,128)(2,1)S(1)}, u32[]{:S(2)}, u32[]{:S(2)}) %collective-permute-start.20) | collective-permute-done | bytes 1048608 | tf_op jit(solution)/shard_map/ppermute | solution.py:543
  655.6 26.1 %collective-permute-start.26 = (bf16[32,3072]{1,0:T(8,128)(2,1)}, bf16[32,3072]{1,0:T(8,128)(2,1)}, u32[]{:S(2)}, u32[]{:S(2)}) collective-permute-start(bf16[32,3072]{1,0:T(8,128)(2,1)} %get-tuple-element.238), channel_id=1, source_target_pairs={{0,2},{1,3},{2,0},{3,1},{4,6},{5,7},{6,4},{7,5},{8,10},{9,11},{10,... | collective-permute-start | bytes 589832 | tf_op jit(solution)/shard_map/ppermute | solution.py:691
  683.1 8.4 %shard_map.186 = (bf16[1024,1024]{1,0:T(8,128)(2,1)}, bf16[1024,1024]{1,0:T(8,128)(2,1)}) custom-call(bf16[1024,1024]{1,0:T(8,128)(2,1)} %bitcast.206, bf16[32,192,1024]{2,1,0:T(8,128)(2,1)} %bitcast.198, bf16[32,192,1024]{2,1,0:T(8,128)(2,1)} %bitcast.199), custom_call_target="tpu_custom_call" | custom-call | flops 4294967296 | bytes 31457280 | tf_op jit(solution)/shard_map/pallas_call | solution.py:188
  697.3 7.0 collective-permute-done.31
  (251 shorter events, 167.7 us)
Async XLA Ops:
  7.2 140.2 %all-gather.4.cloned.1.call-start = ((), (), s32[]{:S(2)}) async-start(), calls=%async_computation.4 | async-start | bytes 12976128 | tf_op jit(solution)/shard_map/all_gather | solution.py:570
  29.4 302.6 %all-gather.6.cloned.1.call-start = ((), (), s32[]{:S(2)}) async-start(), calls=%async_computation.5 | async-start | bytes 17301504 | tf_op jit(solution)/shard_map/all_gather | solution.py:615
  43.1 42.6 %collective-permute-start.3 = (bf16[512,1024]{1,0:T(8,128)(2,1)S(1)}, bf16[512,1024]{1,0:T(8,128)(2,1)S(1)}, u32[]{:S(2)}, u32[]{:S(2)}) collective-permute-start(bf16[512,1024]{1,0:T(8,128)(2,1)S(1)} %get-tuple-element.231), channel_id=1, source_target_pairs={{0,1},{1,0},{2,5},{3,4},{4,3},{5,2},{6,7},{7,6},{8,9},{9,8},{10,13... | collective-permute-start | bytes 3145736 | tf_op jit(solution)/shard_map/ppermute | solution.py:537
  45.1 40.7 %collective-permute-start = (bf16[512,1024]{1,0:T(8,128)(2,1)S(1)}, bf16[512,1024]{1,0:T(8,128)(2,1)S(1)}, u32[]{:S(2)}, u32[]{:S(2)}) collective-permute-start(bf16[512,1024]{1,0:T(8,128)(2,1)S(1)} %get-tuple-element.234), channel_id=1, source_target_pairs={{0,0},{1,1},{2,4},{3,5},{4,2},{5,3},{6,6},{7,7},{8,8},{9,9},{10,12... | collective-permute-start | bytes 3145736 | tf_op jit(solution)/shard_map/ppermute | solution.py:536
  45.9 95.1 %collective-permute-start.1 = (bf16[512,1024]{1,0:T(8,128)(2,1)S(1)}, bf16[512,1024]{1,0:T(8,128)(2,1)S(1)}, u32[]{:S(2)}, u32[]{:S(2)}) collective-permute-start(bf16[512,1024]{1,0:T(8,128)(2,1)S(1)} %get-tuple-element.235), channel_id=1, source_target_pairs={{0,1},{1,0},{2,5},{3,4},{4,3},{5,2},{6,7},{7,6},{8,9},{9,8},{10,13... | collective-permute-start | bytes 3145736 | tf_op jit(solution)/shard_map/ppermute | solution.py:537
  143.7 421.1 %reduce-scatter.2.cloned.1.call-start = ((), (), s32[]{:S(2)}) async-start(), calls=%async_computation.6 | async-start | bytes 4456448 | tf_op jit(solution)/shard_map/reduce_scatter | solution.py:702
  158.4 58.9 %collective-permute-start.5 = (bf16[1024,1024]{1,0:T(8,128)(2,1)}, bf16[1024,1024]{1,0:T(8,128)(2,1)}, u32[]{:S(2)}, u32[]{:S(2)}) collective-permute-start(bf16[1024,1024]{1,0:T(8,128)(2,1)} %get-tuple-element.75), channel_id=1, source_target_pairs={{0,4},{4,0},{1,5},{5,1},{2,6},{6,2},{3,7},{7,3},{8,12},{12,8},{9,1... | collective-permute-start | bytes 6291464 | tf_op jit(solution)/shard_map/ppermute | solution.py:550
  194.7 101.3 %collective-permute-start.7 = (bf16[512,1024]{1,0:T(8,128)(2,1)}, bf16[512,1024]{1,0:T(8,128)(2,1)}, u32[]{:S(2)}, u32[]{:S(2)}) collective-permute-start(bf16[512,1024]{1,0:T(8,128)(2,1)} %get-tuple-element.226), channel_id=1, source_target_pairs={{0,0},{1,1},{2,4},{3,5},{4,2},{5,3},{6,6},{7,7},{8,8},{9,9},{10,12... | collective-permute-start | bytes 3145736 | tf_op jit(solution)/shard_map/ppermute | solution.py:536
  204.3 91.7 %collective-permute-start.8 = (bf16[512,1024]{1,0:T(8,128)(2,1)}, bf16[512,1024]{1,0:T(8,128)(2,1)}, u32[]{:S(2)}, u32[]{:S(2)}) collective-permute-start(bf16[512,1024]{1,0:T(8,128)(2,1)} %get-tuple-element.227), channel_id=1, source_target_pairs={{0,1},{1,0},{2,5},{3,4},{4,3},{5,2},{6,7},{7,6},{8,9},{9,8},{10,13... | collective-permute-start | bytes 3145736 | tf_op jit(solution)/shard_map/ppermute | solution.py:537
  413.7 29.4 %collective-permute-start.11 = (bf16[4,512,1024]{2,1,0:T(8,128)(2,1)}, bf16[4,512,1024]{2,1,0:T(8,128)(2,1)}, u32[]{:S(2)}, u32[]{:S(2)}) collective-permute-start(bf16[4,512,1024]{2,1,0:T(8,128)(2,1)} %dynamic-slice_bitcast_fusion), channel_id=1, source_target_pairs={{0,4},{4,0},{1,5},{5,1},{2,6},{6,2},{3,7},{7,3},{8,12},{12,8},{9,1... | collective-permute-start | bytes 12582920 | tf_op jit(solution)/shard_map/ppermute | solution.py:681
  454.3 82.8 %collective-permute-start.16 = (bf16[512,1024]{1,0:T(8,128)(2,1)}, bf16[512,1024]{1,0:T(8,128)(2,1)S(1)}, u32[]{:S(2)}, u32[]{:S(2)}) collective-permute-start(bf16[512,1024]{1,0:T(8,128)(2,1)} %get-tuple-element.222), channel_id=1, source_target_pairs={{0,0},{1,1},{4,2},{5,3},{2,4},{3,5},{6,6},{7,7},{8,8},{9,9},{12,10... | collective-permute-start | bytes 3145736 | tf_op jit(solution)/shard_map/ppermute | solution.py:542
  456.2 80.9 %collective-permute-start.17 = (bf16[512,1024]{1,0:T(8,128)(2,1)S(1)}, bf16[512,1024]{1,0:T(8,128)(2,1)S(1)}, u32[]{:S(2)}, u32[]{:S(2)}) collective-permute-start(bf16[512,1024]{1,0:T(8,128)(2,1)S(1)} %get-tuple-element.223), channel_id=1, source_target_pairs={{1,0},{0,1},{5,2},{4,3},{3,4},{2,5},{7,6},{6,7},{9,8},{8,9},{13,10... | collective-permute-start | bytes 3145736 | tf_op jit(solution)/shard_map/ppermute | solution.py:543
  458.5 80.3 %collective-permute-start.13 = (bf16[640,1024]{1,0:T(8,128)(2,1)}, bf16[640,1024]{1,0:T(8,128)(2,1)}, u32[]{:S(2)}, u32[]{:S(2)}) collective-permute-start(bf16[640,1024]{1,0:T(8,128)(2,1)} %get-tuple-element.197), channel_id=1, source_target_pairs={{0,8},{8,0},{16,24},{24,16},{1,9},{9,1},{17,25},{25,17},{2,10},{10... | collective-permute-start | bytes 3932168 | tf_op jit(solution)/shard_map/ppermute | solution.py:691
  459.7 79.0 %collective-permute-start.14 = (bf16[640,1024]{1,0:T(8,128)(2,1)}, bf16[640,1024]{1,0:T(8,128)(2,1)}, u32[]{:S(2)}, u32[]{:S(2)}) collective-permute-start(bf16[640,1024]{1,0:T(8,128)(2,1)} %get-tuple-element.199), channel_id=1, source_target_pairs={{0,16},{8,24},{16,0},{24,8},{1,17},{9,25},{17,1},{25,9},{2,18},{10... | collective-permute-start | bytes 3932168 | tf_op jit(solution)/shard_map/ppermute | solution.py:691
  460.5 79.7 %collective-permute-start.15 = (bf16[640,1024]{1,0:T(8,128)(2,1)}, bf16[640,1024]{1,0:T(8,128)(2,1)}, u32[]{:S(2)}, u32[]{:S(2)}) collective-permute-start(bf16[640,1024]{1,0:T(8,128)(2,1)} %get-tuple-element.198), channel_id=1, source_target_pairs={{0,24},{8,16},{16,8},{24,0},{1,25},{9,17},{17,9},{25,1},{2,26},{10... | collective-permute-start | bytes 3932168 | tf_op jit(solution)/shard_map/ppermute | solution.py:691
  571.5 139.7 %all-to-all-start.2 = ((bf16[4,160,1024]{2,1,0:T(8,128)(2,1)}), bf16[4,160,1024]{2,1,0:T(8,128)(2,1)S(1)}, u32[]{:S(2)}, u32[]{:S(2)}) async-start(bf16[4,160,1024]{2,1,0:T(8,128)(2,1)} %bitcast.77), calls=%async_computation.3 | async-start | bytes 2621440 | tf_op jit(solution)/shard_map/all_to_all | solution.py:731
  618.9 28.5 %collective-permute-start.28 = (bf16[4,256,1024]{2,1,0:T(8,128)(2,1)S(1)}, bf16[4,256,1024]{2,1,0:T(8,128)(2,1)S(1)}, u32[]{:S(2)}, u32[]{:S(2)}) collective-permute-start(bf16[4,256,1024]{2,1,0:T(8,128)(2,1)S(1)} %dynamic-slice_bitcast_fusion.2), channel_id=1, source_target_pairs={{0,4},{4,0},{1,5},{5,1},{2,6},{6,2},{3,7},{7,3},{8,12},{12,8},{9,1... | collective-permute-start | bytes 6291464 | tf_op jit(solution)/shard_map/ppermute | solution.py:681
  623.1 29.3 %collective-permute-start.22 = (bf16[128,3072]{1,0:T(8,128)(2,1)S(1)}, bf16[128,3072]{1,0:T(8,128)(2,1)S(1)}, u32[]{:S(2)}, u32[]{:S(2)}) collective-permute-start(bf16[128,3072]{1,0:T(8,128)(2,1)S(1)} %get-tuple-element.202), channel_id=1, source_target_pairs={{0,8},{8,0},{16,24},{24,16},{1,9},{9,1},{17,25},{25,17},{2,10},{10... | collective-permute-start | bytes 2359304 | tf_op jit(solution)/shard_map/ppermute | solution.py:691
  624.6 27.8 %collective-permute-start.23 = (bf16[128,3072]{1,0:T(8,128)(2,1)S(1)}, bf16[128,3072]{1,0:T(8,128)(2,1)S(1)}, u32[]{:S(2)}, u32[]{:S(2)}) collective-permute-start(bf16[128,3072]{1,0:T(8,128)(2,1)S(1)} %get-tuple-element.204), channel_id=1, source_target_pairs={{0,16},{8,24},{16,0},{24,8},{1,17},{9,25},{17,1},{25,9},{2,18},{10... | collective-permute-start | bytes 2359304 | tf_op jit(solution)/shard_map/ppermute | solution.py:691
  626.1 26.9 %collective-permute-start.24 = (bf16[128,3072]{1,0:T(8,128)(2,1)S(1)}, bf16[128,3072]{1,0:T(8,128)(2,1)S(1)}, u32[]{:S(2)}, u32[]{:S(2)}) collective-permute-start(bf16[128,3072]{1,0:T(8,128)(2,1)S(1)} %get-tuple-element.203), channel_id=1, source_target_pairs={{0,24},{8,16},{16,8},{24,0},{1,25},{9,17},{17,9},{25,1},{2,26},{10... | collective-permute-start | bytes 2359304 | tf_op jit(solution)/shard_map/ppermute | solution.py:691
  649.5 47.8 %collective-permute-start.29 = (bf16[256,1024]{1,0:T(8,128)(2,1)}, bf16[256,1024]{1,0:T(8,128)(2,1)}, u32[]{:S(2)}, u32[]{:S(2)}) collective-permute-start(bf16[256,1024]{1,0:T(8,128)(2,1)} %get-tuple-element.213), channel_id=1, source_target_pairs={{0,8},{8,0},{16,24},{24,16},{1,9},{9,1},{17,25},{25,17},{2,10},{10... | collective-permute-start | bytes 1572872 | tf_op jit(solution)/shard_map/ppermute | solution.py:691
  650.9 46.4 %collective-permute-start.30 = (bf16[256,1024]{1,0:T(8,128)(2,1)}, bf16[256,1024]{1,0:T(8,128)(2,1)}, u32[]{:S(2)}, u32[]{:S(2)}) collective-permute-start(bf16[256,1024]{1,0:T(8,128)(2,1)} %get-tuple-element.215), channel_id=1, source_target_pairs={{0,16},{8,24},{16,0},{24,8},{1,17},{9,25},{17,1},{25,9},{2,18},{10... | collective-permute-start | bytes 1572872 | tf_op jit(solution)/shard_map/ppermute | solution.py:691
  655.2 36.4 %collective-permute-start.25 = (bf16[32,3072]{1,0:T(8,128)(2,1)}, bf16[32,3072]{1,0:T(8,128)(2,1)}, u32[]{:S(2)}, u32[]{:S(2)}) collective-permute-start(bf16[32,3072]{1,0:T(8,128)(2,1)} %get-tuple-element.236), channel_id=1, source_target_pairs={{0,1},{1,0},{2,3},{3,2},{4,5},{5,4},{6,7},{7,6},{8,9},{9,8},{10,11... | collective-permute-start | bytes 589832 | tf_op jit(solution)/shard_map/ppermute | solution.py:691
  655.6 39.7 %collective-permute-start.26 = (bf16[32,3072]{1,0:T(8,128)(2,1)}, bf16[32,3072]{1,0:T(8,128)(2,1)}, u32[]{:S(2)}, u32[]{:S(2)}) collective-permute-start(bf16[32,3072]{1,0:T(8,128)(2,1)} %get-tuple-element.238), channel_id=1, source_target_pairs={{0,2},{1,3},{2,0},{3,1},{4,6},{5,7},{6,4},{7,5},{8,10},{9,11},{10,... | collective-permute-start | bytes 589832 | tf_op jit(solution)/shard_map/ppermute | solution.py:691
  (50 other events, 764.1 us)
Sparse Core Ops, SparseCore 0:
  12.5 134.8 all-gather.3
  151.0 180.9 all-gather.5
  431.9 132.9 reduce-scatter.1

commit v4 on v3

--- a/solution.py
+++ b/solution.py
@@ -13,8 +13,8 @@
 TILE = 128
 BLOCK = 256
 ROW_TILE = 256
-FEED_TILE = 256
-FEED_PART = 256
+FEED_TILE = 1024
+FEED_PART = 512
 VMEM_BYTES = 60 * 1024 * 1024
 ROW_AXES = ("core", "lo")
 LINE_AXES = ("core", "hi", "lo")
@@ -144,7 +144,7 @@
 
 def project(value, gathered, begin, rows, heads_wide, member):
     length, width = value.shape
-    tile = min(ROW_TILE, length)
+    tile = min(8 * ROW_TILE, length)
     return pl.pallas_call(
         project_kernel,
         grid_spec=pltpu.PrefetchScalarGridSpec(
@@ -564,10 +564,24 @@
         own = lax.dynamic_slice_in_dim(value, core * heads_wide, heads_wide, 1)
         return jnp.concatenate([jnp.where(first_core, own, other), jnp.where(first_core, other, own)], axis=0)
 
+    def share_on_line(value):
+        pieces = [value]
+        for flip in range(1, line):
+            pieces.append(lax.ppermute(value, ("hi", "lo"), [(i, i ^ flip) for i in range(line)]))
+        pieces = jnp.stack(pieces)
+        return jnp.stack([lax.dynamic_index_in_dim(pieces, place ^ i, 0, False) for i in range(line)])
+
+    def gather_planes(value):
+        return lax.all_gather(value, ("plane", "core"), axis=0, tiled=True).reshape(devices, -1, width)
+
     up_rows, down_rows, out_rows = w_up.shape[0], w_down.shape[0], w_out.shape[0]
     skip_rows = w_skip.shape[0]
     early = jnp.concatenate([w_skip] + [w_qkv[:, i * width : (i + 1) * width] for i in range(3)] + [w_out], axis=0)
-    early = lax.all_gather(early, ALL_AXES, axis=0, tiled=True).reshape(devices, -1, width)
+    early_line = share_on_line(early)
+    early = gather_planes(early_line)
+    columns = w_up.shape[1] // width
+    late = jnp.concatenate([w_down] + [w_up[:, i * width : (i + 1) * width] for i in range(columns)], axis=0)
+    late_line = share_on_line(late)
 
     labels_own = segment_ids[:, 0]
     labels_other = lax.ppermute(labels_own, "core", swap)
@@ -600,19 +614,17 @@
     own_columns = block_mod.shape[1]
     block_mod = block_mod.reshape(planes, 1, highs, 1, labels, own_columns)
     block_mod = jnp.broadcast_to(block_mod, (planes, 2, highs, lows, labels, own_columns))
+    late_line, inputs, skips, block_mod, cosine, sine, ranges, mine = lax.optimization_barrier(
+        (late_line, inputs, skips, block_mod, cosine, sine, ranges, mine)
+    )
+    late = gather_planes(late_line)
+    x, s = to_rows(inputs), to_rows(skips)
     block_mod = lax.all_to_all(
         block_mod.reshape(devices, labels, own_columns), ALL_AXES, split_axis=0, concat_axis=0, tiled=True
     )
     modulation = jnp.moveaxis(block_mod, 0, 1).reshape(labels, 4, width)
 
-    inputs, skips, modulation, seg = lax.optimization_barrier((inputs, skips, modulation, seg))
-    x, s = to_rows(inputs), to_rows(skips)
-    columns = w_up.shape[1] // width
-    late = jnp.concatenate([w_down] + [w_up[:, i * width : (i + 1) * width] for i in range(columns)], axis=0)
-    late, cotangent, x, s, modulation, cosine, sine, ranges, mine = lax.optimization_barrier(
-        (late, cotangent, x, s, modulation, cosine, sine, ranges, mine)
-    )
-    late = lax.all_gather(late, ALL_AXES, axis=0, tiled=True).reshape(devices, -1, width)
+    x, s, cotangent, modulation = lax.optimization_barrier((x, s, cotangent, modulation))
     cot = to_rows(cotangent)
     in_place = out_rows % 16 == 0
     hidden = w_up.shape[1]
@@ -627,6 +639,30 @@
 
     skip_top, skip_bottom = (weight(early, 0, skip_rows, i * width, width) for i in range(2))
     out_weight = weight(early, skip_rows + 3 * out_rows, out_rows, 0, width)
+    def own_qkv(gathered):
+        parts = []
+        for i in range(3):
+            begin = skip_rows + i * out_rows
+            whole = gathered[:, begin : begin + out_rows].reshape(width, width)
+            parts.append(lax.dynamic_slice_in_dim(whole, member * heads_wide, heads_wide, 1))
+        return jnp.concatenate(parts, axis=1)
+
+    mine_column, mine_row = mine[:, None], mine[None, :]
+    shift_one, scale_one, shift_two, scale_two = (modulation[:, i] for i in range(4))
+
+    resid_in, normed_one = rowwise(
+        skip_norm_kernel,
+        frames,
+        [("", x), ("", s), ("weight", skip_top), ("weight", skip_bottom), ("", mine_column),
+         ("whole", shift_one), ("whole", scale_one)],
+        [(width, f32), (width, bf16)],
+        flops=4 * frames * width * width,
+    )
+    normed_row = frames_to_row(normed_one)
+    if in_place:
+        projected = project(normed_row, early, skip_rows, out_rows, heads_wide, member)
+    else:
+        projected = jnp.dot(normed_row, own_qkv(early), preferred_element_type=f32).astype(bf16)
     if in_place:
         per = width // chunk
         up_weight = (late, (devices, up_rows, chunk), lambda j: (0, down_rows // up_rows + j // per, j % per))
@@ -636,31 +672,6 @@
         up_full = jnp.concatenate([v.reshape(width, width) for v in pieces], axis=1)
         up_weight = (up_full[None], (1, width, chunk), lambda j: (0, 0, j))
         down_weight = (late[:, :down_rows].reshape(1, -1, width), (1, chunk, width), lambda j: (0, j, 0))
-
-    def own_qkv(gathered):
-        parts = []
-        for i in range(3):
-            begin = skip_rows + i * out_rows
-            whole = gathered[:, begin : begin + out_rows].reshape(width, width)
-            parts.append(lax.dynamic_slice_in_dim(whole, member * heads_wide, heads_wide, 1))
-        return jnp.concatenate(parts, axis=1)
-
-    mine_column, mine_row = mine[:, None], mine[None, :]
-    shift_one, scale_one, shift_two, scale_two = (modulation[:, i] for i in range(4))
-
-    resid_in, normed_one = rowwise(
-        skip_norm_kernel,
-        frames,
-        [("", x), ("", s), ("weight", skip_top), ("weight", skip_bottom), ("", mine_column),
-         ("whole", shift_one), ("whole", scale_one)],
-        [(width, f32), (width, bf16)],
-        flops=4 * frames * width * width,
-    )
-    normed_row = frames_to_row(normed_one)
-    if in_place:
-        projected = project(normed_row, early, skip_rows, out_rows, heads_wide, member)
-    else:
-        projected = jnp.dot(normed_row, own_qkv(early), preferred_element_type=f32).astype(bf16)
     mixed_heads, queries, keys, logsum = attend_forward(ranges, projected, cosine, sine, seg_column, seg_row)
     mixed = heads_to_frames(mixed_heads)
     resid_mid, normed_two = rowwise(

time: 742 us -> 727 us (0.980)
  waiting for transfers between devices: 167 us -> 154 us
    ppermute x3, waiting for transfers between devices: 92 us -> 24 us  [to_rows(): lax.ppermute(lax.dynamic_index_in_dim(value, 1 - odd_place, 0, False), LI...]
    ppermute x0 -> x6, waiting for transfers between devices: none -> 44.7 us  [share_on_line(): lax.ppermute(value, ('hi', 'lo'), [(i, i ^ flip) for i in range(line)])]
    all_to_all x1, waiting for transfers between devices: 0.01 us -> 36.9 us  [body(): lax.all_to_all(block_mod.reshape(devices, labels, own_columns), ALL_AXES,...]
    ppermute x1, starting transfers between devices: 33.4 us -> 0.02 us  [frames_to_row(): other = lax.ppermute(value, 'core', swap)]
    all_gather x2, waiting for transfers between devices: 16.1 us -> 0.01 us  [gather_planes(): lax.all_gather(value, ('plane', 'core'), axis=0, tiled=True)]
    ppermute x0 -> x6, starting transfers between devices: none -> 15.7 us  [share_on_line(): lax.ppermute(value, ('hi', 'lo'), [(i, i ^ flip) for i in range(line)])]
    pallas_call x1, Pallas kernels: 75.1 us -> 87.2 us  [attend_backward(): pl.pallas_call(attend_backward_kernel, grid_spec=pltpu.PrefetchScalarGrid...]
    pallas_call x1, Pallas kernels: 22.4 us -> 11 us  [project(): pl.pallas_call(project_kernel, grid_spec=pltpu.PrefetchScalarGridSpec(num...]
  transfers between devices with their start and end apart: 41 -> 47, of which waited for: 13 -> 15; matrix products, arithmetic and copies ran while one was open for 16% -> 17% of each run, Pallas kernels for 27% -> 28%
where the time goes in v4:
time: 727 us; the launch traced here: 718 us
  Pallas kernels  269 us (37%)
  waiting for transfers between devices  154 us (21%)
  starting transfers between devices  122 us (17%)
  other arithmetic  62.2 us (9%)
  local copies, waits for them, and re-layouts  52.2 us (7%)
  matrix products  34.5 us (5%)
  between operations  14.8 us (2%)
  blocking collectives  8.92 us (1%)
    pallas_call x1, Pallas kernels, attend_backward(): pl.pallas_call(attend_backward_kernel, grid_spec=pltpu.PrefetchScalarGrid...  87.2 us
    pallas_call x1, Pallas kernels, feed_forward_and_back(): pl.pallas_call(feed_kernel, grid=(hidden // piece,), in_specs=[pl.BlockSp...  66.5 us
    pallas_call x1, Pallas kernels, attend_forward(): pl.pallas_call(attend_forward_kernel, grid_spec=pltpu.PrefetchScalarGridS...  55.9 us
    pallas_call x5, Pallas kernels, rowwise(): pl.pallas_call(kernel, grid=(frames // tile,), in_specs=in_specs, out_spe...  48.5 us
    ppermute x6, waiting for transfers between devices, share_on_line(): lax.ppermute(value, ('hi', 'lo'), [(i, i ^ flip) for i in range(line)])  44.7 us
    ppermute x15, starting transfers between devices, exchange(): lax.ppermute(sent, axes, [(i, i ^ flip) for i in range(count)]).astype(f32)  43.9 us
    all_to_all x1, waiting for transfers between devices, body(): lax.all_to_all(block_mod.reshape(devices, labels, own_columns), ALL_AXES,...  36.9 us
    ppermute x3, waiting for transfers between devices, to_rows(): lax.ppermute(lax.dynamic_index_in_dim(value, 1 - odd_place, 0, False), LI...  24 us
  transfers between devices with their start and end apart: 47, of which 15 were waited for; matrix products, arithmetic and copies ran while one was open for 17% of the time, Pallas kernels for 28%

profile of v4, /device:TPU:0, one launch (start us, length us, event | category | flops | bytes accessed | tf_op | source)
XLA Modules:
  0.0 717.8 jit_solution(9176531588823977440)
XLA Ops:
  17.2 14.2 %collective-permute-done.8 = bf16[192,1024]{1,0:T(8,128)(2,1)S(1)} collective-permute-done((bf16[192,1024]{1,0:T(8,128)(2,1)S(1)}, bf16[192,1024]{1,0:T(8,128)(2,1)S(1)}, u32[]{:S(2)}, u32[]{:S(2)}) %collective-permute-start.8) | collective-permute-done | bytes 393248 | tf_op jit(solution)/shard_map/ppermute | solution.py:570
  31.3 13.0 %collective-permute-done.9 = bf16[192,1024]{1,0:T(8,128)(2,1)S(1)} collective-permute-done((bf16[192,1024]{1,0:T(8,128)(2,1)S(1)}, bf16[192,1024]{1,0:T(8,128)(2,1)S(1)}, u32[]{:S(2)}, u32[]{:S(2)}) %collective-permute-start.9) | collective-permute-done | bytes 393248 | tf_op jit(solution)/shard_map/ppermute | solution.py:570
  59.6 8.9 %all-gather = s32[16,1,4]{2,1,0:T(1,128)S(1)} all-gather(s32[2,1,4]{2,1,0:T(1,128)S(1)} %copy-done.34), channel_id=2, replica_groups=mesh['plane'=4,'core'=2,'hi'=4,'lo'=1] {'plane','core'}, dimensions={0}, use_global_device_ids=true | all-gather | bytes 288 | tf_op jit(solution)/shard_map/all_gather | solution.py:608
  78.0 17.5 %collective-permute-done.1 = bf16[256,1024]{1,0:T(8,128)(2,1)} collective-permute-done((bf16[256,1024]{1,0:T(8,128)(2,1)}, bf16[256,1024]{1,0:T(8,128)(2,1)}, u32[]{:S(2)}, u32[]{:S(2)}) %collective-permute-start.1) | collective-permute-done | bytes 524320 | tf_op jit(solution)/shard_map/ppermute | solution.py:570
  102.2 9.4 %collective-permute-start.6 = (bf16[512,1024]{1,0:T(8,128)(2,1)}, bf16[512,1024]{1,0:T(8,128)(2,1)}, u32[]{:S(2)}, u32[]{:S(2)}) collective-permute-start(bf16[512,1024]{1,0:T(8,128)(2,1)} %get-tuple-element.230), channel_id=1, source_target_pairs={{0,0},{1,1},{2,4},{3,5},{4,2},{5,3},{6,6},{7,7},{8,8},{9,9},{10,12... | collective-permute-start | bytes 3145736 | tf_op jit(solution)/shard_map/ppermute | solution.py:536
  111.6 9.2 %collective-permute-start.7 = (bf16[512,1024]{1,0:T(8,128)(2,1)}, bf16[512,1024]{1,0:T(8,128)(2,1)}, u32[]{:S(2)}, u32[]{:S(2)}) collective-permute-start(bf16[512,1024]{1,0:T(8,128)(2,1)} %get-tuple-element.231), channel_id=1, source_target_pairs={{0,1},{1,0},{2,5},{3,4},{4,3},{5,2},{6,7},{7,6},{8,9},{9,8},{10,13... | collective-permute-start | bytes 3145736 | tf_op jit(solution)/shard_map/ppermute | solution.py:537
  128.2 11.2 %reduce-scatter.2.cloned.1.call-start = ((), (), s32[]{:S(2)}) async-start(), calls=%async_computation.6 | async-start | bytes 4456448 | tf_op jit(solution)/shard_map/reduce_scatter | solution.py:713
  140.5 15.8 %collective-permute-done.7 = bf16[512,1024]{1,0:T(8,128)(2,1)} collective-permute-done((bf16[512,1024]{1,0:T(8,128)(2,1)}, bf16[512,1024]{1,0:T(8,128)(2,1)}, u32[]{:S(2)}, u32[]{:S(2)}) %collective-permute-start.7) | collective-permute-done | bytes 1048608 | tf_op jit(solution)/shard_map/ppermute | solution.py:537
  170.8 36.9 %all-to-all-done = f32[32,4,128]{2,1,0:T(4,128)S(1)} async-done(((f32[32,4,128]{2,1,0:T(4,128)}), f32[32,4,128]{2,1,0:T(4,128)S(1)}, u32[]{:S(2)}, u32[]{:S(2)}) %all-to-all-start) | async-done | bytes 65568 | tf_op jit(solution)/shard_map/all_to_all | solution.py:622
  208.4 11.0 %shard_map.178 = (f32[1024,1024]{1,0:T(8,128)}, bf16[1024,1024]{1,0:T(8,128)(2,1)}) custom-call(bf16[1024,1024]{1,0:T(8,128)(2,1)} %pad_maximum_fusion.6.x_ref, bf16[1024,1024]{1,0:T(8,128)(2,1)} %pad_maximum_fusion.7.s_ref, bf16[32,192,1024]{2,1,0:T(8,128)(2,1)} %all-gather.4.cloned.1.call-done.top_ref.bottom_ref.w_ref, ...), custom_call_target="tpu_custom_call" | custom-call | flops 4294967296 | bytes 35688448 | tf_op jit(solution)/shard_map/pallas_call | solution.py:188
  232.3 11.0 %shard_map.179.q_ref.k_ref.v_ref = bf16[2048,1536]{1,0:T(8,128)(2,1)} custom-call(s32[1]{0:T(128)} %bitcast.10.place_ref, bf16[2048,1024]{1,0:T(8,128)(2,1)} %pad_maximum_fusion.1.x_ref, bf16[32,192,1024]{2,1,0:T(8,128)(2,1)} %all-gather.4.cloned.1.call-done.top_ref.bottom_ref.w_ref), custom_call_target="tpu_custom_call" | custom-call | flops 6442450944 | bytes 16777216 | tf_op jit(solution)/shard_map/pallas_call | solution.py:148
  243.3 55.9 %shard_map.180 = (bf16[2048,512]{1,0:T(8,128)(2,1)}, bf16[2048,512]{1,0:T(8,128)(2,1)}, bf16[2048,512]{1,0:T(8,128)(2,1)}, f32[4,2,2048]{2,1,0:T(2,128)}) custom-call(s32[2,8]{1,0:T(2,128)} %pad_add_fusion.range_ref, bf16[2048,1536]{1,0:T(8,128)(2,1)} %shard_map.179.q_ref.k_ref.v_ref, bf16[2048,1536]{1,0:T(8,128)(2,1)} %shard_map.179.q_ref.k_ref.v_ref, ...), custom_call_target="tpu_custom_call" | custom-call | flops 17179869184 | bytes 14680064 | tf_op jit(solution)/shard_map/pallas_call | solution.py:281
  308.2 8.6 %shard_map.181 = (f32[1024,1024]{1,0:T(8,128)}, bf16[1024,1024]{1,0:T(8,128)(2,1)}) custom-call(bf16[1024,1024]{1,0:T(8,128)(2,1)} %pad_maximum_fusion.8.mixed_ref, bf16[32,192,1024]{2,1,0:T(8,128)(2,1)} %all-gather.4.cloned.1.call-done.top_ref.bottom_ref.w_ref, f32[1024,1024]{1,0:T(8,128)} %get-tuple-element.81.resid_in_ref.resid_ref, ...), custom_call_target="tpu_custom_call" | custom-call | flops 2147483648 | bytes 25202688 | tf_op jit(solution)/shard_map/pallas_call | solution.py:188
  323.1 66.5 %shard_map.182 = (bf16[1024,1024]{1,0:T(8,128)(2,1)}, f32[1024,1024]{1,0:T(8,128)}, bf16[2,4,128,4096]{3,2,1,0:T(8,128)(2,1)}, bf16[2,4,512,1024]{3,2,1,0:T(8,128)(2,1)}) custom-call(bf16[1024,1024]{1,0:T(8,128)(2,1)} %get-tuple-element.85.n_ref, bf16[1024,1024]{1,0:T(8,128)(2,1)} %pad_maximum_fusion.9.cot_ref, f32[1024,1024]{1,0:T(8,128)} %get-tuple-element.87.resid_ref, ...), custom_call_target="tpu_custom_call" | custom-call | flops 51539607552 | bytes 50331648 | tf_op jit(solution)/shard_map/pallas_call | solution.py:471
  398.6 10.7 %shard_map.183 = (f32[1024,1024]{1,0:T(8,128)}, bf16[1024,1024]{1,0:T(8,128)(2,1)}, bf16[1024,1024]{1,0:T(8,128)(2,1)}, f32[8,1024]{1,0:T(8,128)}, f32[8,1024]{1,0:T(8,128)}) custom-call(f32[1024,1024]{1,0:T(8,128)} %get-tuple-element.89.g_ref, f32[1024,1024]{1,0:T(8,128)} %get-tuple-element.87.resid_ref, bf16[1024,1024]{1,0:T(8,128)(2,1)} %pad_maximum_fusion.9.cot_ref, ...), custom_call_target="tpu_custom_call" | custom-call | flops 1 | bytes 1 | tf_op jit(solution)/shard_map/pallas_call | solution.py:188
  447.7 87.2 %shard_map.184 = bf16[2048,1536]{1,0:T(8,128)(2,1)} custom-call(s32[2,8]{1,0:T(2,128)} %pad_add_fusion.range_ref, bf16[2048,512]{1,0:T(8,128)(2,1)} %get-tuple-element.78.q_ref, bf16[2048,512]{1,0:T(8,128)(2,1)} %get-tuple-element.79.k_ref, bf16[2048,1536]{1,0:T(8,128)(2,1)} %shard_map.179.q_ref.k_ref.v_ref, bf16[2048,512]{1,0:T(8,128)(2,1)} %get-tuple-element.80.out_ref, ...), custom_call_target="tpu_custom_call" | custom-call | flops 42949672960 | bytes 16777216 | tf_op jit(solution)/shard_map/pallas_call | solution.py:380
  541.5 9.6 %reduce-scatter.2.cloned.1.call-done = bf16[32,4096]{1,0:T(8,128)(2,1)} async-done(((bf16[512,4096]{1,0:T(8,128)(2,1)}), bf16[32,4096]{1,0:T(8,128)(2,1)}) %reduce-scatter.2.cloned.1.call-update) | async-done | bytes 262160 | tf_op jit(solution)/shard_map/reduce_scatter | solution.py:713
  557.7 11.7 %all-to-all-start.2 = ((bf16[4,160,1024]{2,1,0:T(8,128)(2,1)}), bf16[4,160,1024]{2,1,0:T(8,128)(2,1)S(1)}, u32[]{:S(2)}, u32[]{:S(2)}) async-start(bf16[4,160,1024]{2,1,0:T(8,128)(2,1)} %bitcast.83), calls=%async_computation.3 | async-start | bytes 2621440 | tf_op jit(solution)/shard_map/all_to_all | solution.py:742
  569.5 8.2 %fusion.5.own_ref = f32[1024,1024]{1,0:T(8,128)} fusion(bf16[1024,1536]{1,0:T(8,128)(2,1)} %pad_maximum_fusion.3, bf16[2048,1536]{1,0:T(8,128)(2,1)} %shard_map.184, s32[]{:T(128)S(6)} %select_n.275), kind=kOutput, calls=%fused_computation.15 | convolution fusion | flops 3221225472 | bytes 10485764 | tf_op jit(solution)/shard_map/dot_general | solution.py:31
  577.7 9.8 %shard_map.185 = (bf16[1024,1024]{1,0:T(8,128)(2,1)}, f32[8,1024]{1,0:T(8,128)}, f32[8,1024]{1,0:T(8,128)}) custom-call(f32[1024,1024]{1,0:T(8,128)} %fusion.5.own_ref, bf16[1024,1024]{1,0:T(8,128)(2,1)} %collective-permute-done.24.other_ref, f32[1024,1024]{1,0:T(8,128)} %get-tuple-element.81.resid_in_ref.resid_ref, ...), custom_call_target="tpu_custom_call" | custom-call | bytes 16801792 | tf_op jit(solution)/shard_map/pallas_call | solution.py:188
  587.5 9.8 %convolution_convert_fusion = bf16[1024,1536]{1,0:T(8,128)(2,1)S(1)} fusion(bf16[2048,1536]{1,0:T(8,128)(2,1)} %shard_map.184, bf16[1024,1024]{1,0:T(8,128)(2,1)} %copy-done.8, bf16[1024,1024]{1,0:T(8,128)(2,1)S(1)} %copy-done.7), kind=kOutput, calls=%fused_computation.11 | convolution fusion | flops 6452412416 | bytes 13631488 | tf_op jit(solution)/shard_map/dot_general | solution.py:762
  612.8 19.1 %collective-permute-done.26 = bf16[512,1024]{1,0:T(8,128)(2,1)S(1)} collective-permute-done((bf16[512,1024]{1,0:T(8,128)(2,1)S(1)}, bf16[512,1024]{1,0:T(8,128)(2,1)S(1)}, u32[]{:S(2)}, u32[]{:S(2)}) %collective-permute-start.26) | collective-permute-done | bytes 1048608 | tf_op jit(solution)/shard_map/ppermute | solution.py:543
  641.7 26.1 %collective-permute-start.32 = (bf16[32,3072]{1,0:T(8,128)(2,1)}, bf16[32,3072]{1,0:T(8,128)(2,1)}, u32[]{:S(2)}, u32[]{:S(2)}) collective-permute-start(bf16[32,3072]{1,0:T(8,128)(2,1)} %get-tuple-element.246), channel_id=1, source_target_pairs={{0,2},{1,3},{2,0},{3,1},{4,6},{5,7},{6,4},{7,5},{8,10},{9,11},{10,... | collective-permute-start | bytes 589832 | tf_op jit(solution)/shard_map/ppermute | solution.py:702
  669.2 8.4 %shard_map.186 = (bf16[1024,1024]{1,0:T(8,128)(2,1)}, bf16[1024,1024]{1,0:T(8,128)(2,1)}) custom-call(bf16[1024,1024]{1,0:T(8,128)(2,1)} %bitcast.204, bf16[32,192,1024]{2,1,0:T(8,128)(2,1)} %all-gather.4.cloned.1.call-done.top_ref.bottom_ref.w_ref, bf16[32,192,1024]{2,1,0:T(8,128)(2,1)} %all-gather.4.cloned.1.call-done.top_ref.bottom_ref.w_ref), custom_call_target="tpu_custom_call" | custom-call | flops 4294967296 | bytes 31457280 | tf_op jit(solution)/shard_map/pallas_call | solution.py:188
  (274 shorter events, 213.2 us)
Async XLA Ops:
  7.2 201.2 %all-gather.4.cloned.1.call-start = ((), (), s32[]{:S(2)}) async-start(), calls=%async_computation.4 | async-start | bytes 14155776 | tf_op jit(solution)/shard_map/all_gather | solution.py:575
  14.6 29.8 %collective-permute-start.9 = (bf16[192,1024]{1,0:T(8,128)(2,1)S(1)}, bf16[192,1024]{1,0:T(8,128)(2,1)S(1)}, u32[]{:S(2)}, u32[]{:S(2)}) collective-permute-start(bf16[192,1024]{1,0:T(8,128)(2,1)S(1)} %constant_dynamic-update-slice_fusion.1), channel_id=1, source_target_pairs={{0,2},{1,3},{2,0},{3,1},{4,6},{5,7},{6,4},{7,5},{8,10},{9,11},{10,... | collective-permute-start | bytes 1179656 | tf_op jit(solution)/shard_map/ppermute | solution.py:570
  46.1 277.1 %all-gather.6.cloned.1.call-start = ((), (), s32[]{:S(2)}) async-start(), calls=%async_computation.5 | async-start | bytes 18874368 | tf_op jit(solution)/shard_map/all_gather | solution.py:575
  57.0 38.5 %collective-permute-start.1 = (bf16[256,1024]{1,0:T(8,128)(2,1)}, bf16[256,1024]{1,0:T(8,128)(2,1)}, u32[]{:S(2)}, u32[]{:S(2)}) collective-permute-start(bf16[256,1024]{1,0:T(8,128)(2,1)} %slice_dynamic-update-slice_fusion.9), channel_id=1, source_target_pairs={{0,2},{1,3},{2,0},{3,1},{4,6},{5,7},{6,4},{7,5},{8,10},{9,11},{10,... | collective-permute-start | bytes 1572872 | tf_op jit(solution)/shard_map/ppermute | solution.py:570
  58.0 37.5 %collective-permute-start.2 = (bf16[256,1024]{1,0:T(8,128)(2,1)}, bf16[256,1024]{1,0:T(8,128)(2,1)}, u32[]{:S(2)}, u32[]{:S(2)}) collective-permute-start(bf16[256,1024]{1,0:T(8,128)(2,1)} %slice_dynamic-update-slice_fusion.9), channel_id=1, source_target_pairs={{0,3},{1,2},{2,1},{3,0},{4,7},{5,6},{6,5},{7,4},{8,11},{9,10},{10,... | collective-permute-start | bytes 1572872 | tf_op jit(solution)/shard_map/ppermute | solution.py:570
  102.2 38.3 %collective-permute-start.6 = (bf16[512,1024]{1,0:T(8,128)(2,1)}, bf16[512,1024]{1,0:T(8,128)(2,1)}, u32[]{:S(2)}, u32[]{:S(2)}) collective-permute-start(bf16[512,1024]{1,0:T(8,128)(2,1)} %get-tuple-element.230), channel_id=1, source_target_pairs={{0,0},{1,1},{2,4},{3,5},{4,2},{5,3},{6,6},{7,7},{8,8},{9,9},{10,12... | collective-permute-start | bytes 3145736 | tf_op jit(solution)/shard_map/ppermute | solution.py:536
  111.6 44.6 %collective-permute-start.7 = (bf16[512,1024]{1,0:T(8,128)(2,1)}, bf16[512,1024]{1,0:T(8,128)(2,1)}, u32[]{:S(2)}, u32[]{:S(2)}) collective-permute-start(bf16[512,1024]{1,0:T(8,128)(2,1)} %get-tuple-element.231), channel_id=1, source_target_pairs={{0,1},{1,0},{2,5},{3,4},{4,3},{5,2},{6,7},{7,6},{8,9},{9,8},{10,13... | collective-permute-start | bytes 3145736 | tf_op jit(solution)/shard_map/ppermute | solution.py:537
  122.0 37.5 %collective-permute-start.4 = (bf16[512,1024]{1,0:T(8,128)(2,1)}, bf16[512,1024]{1,0:T(8,128)(2,1)S(1)}, u32[]{:S(2)}, u32[]{:S(2)}) collective-permute-start(bf16[512,1024]{1,0:T(8,128)(2,1)} %get-tuple-element.234), channel_id=1, source_target_pairs={{0,0},{1,1},{2,4},{3,5},{4,2},{5,3},{6,6},{7,7},{8,8},{9,9},{10,12... | collective-permute-start | bytes 3145736 | tf_op jit(solution)/shard_map/ppermute | solution.py:536
  124.1 43.6 %collective-permute-start.5 = (bf16[512,1024]{1,0:T(8,128)(2,1)S(1)}, bf16[512,1024]{1,0:T(8,128)(2,1)}, u32[]{:S(2)}, u32[]{:S(2)}) collective-permute-start(bf16[512,1024]{1,0:T(8,128)(2,1)S(1)} %get-tuple-element.235), channel_id=1, source_target_pairs={{0,1},{1,0},{2,5},{3,4},{4,3},{5,2},{6,7},{7,6},{8,9},{9,8},{10,13... | collective-permute-start | bytes 3145736 | tf_op jit(solution)/shard_map/ppermute | solution.py:537
  124.1 83.7 %all-to-all-start = ((f32[32,4,128]{2,1,0:T(4,128)}), f32[32,4,128]{2,1,0:T(4,128)S(1)}, u32[]{:S(2)}, u32[]{:S(2)}) async-start(f32[32,4,128]{2,1,0:T(4,128)} %bitcast.15), calls=%async_computation | async-start | bytes 131072 | tf_op jit(solution)/shard_map/all_to_all | solution.py:622
  128.2 422.9 %reduce-scatter.2.cloned.1.call-start = ((), (), s32[]{:S(2)}) async-start(), calls=%async_computation.6 | async-start | bytes 4456448 | tf_op jit(solution)/shard_map/reduce_scatter | solution.py:713
  223.6 80.0 %collective-permute-start.13 = (bf16[512,1024]{1,0:T(8,128)(2,1)}, bf16[512,1024]{1,0:T(8,128)(2,1)S(1)}, u32[]{:S(2)}, u32[]{:S(2)}) collective-permute-start(bf16[512,1024]{1,0:T(8,128)(2,1)} %get-tuple-element.226), channel_id=1, source_target_pairs={{0,0},{1,1},{2,4},{3,5},{4,2},{5,3},{6,6},{7,7},{8,8},{9,9},{10,12... | collective-permute-start | bytes 3145736 | tf_op jit(solution)/shard_map/ppermute | solution.py:536
  225.5 78.2 %collective-permute-start.14 = (bf16[512,1024]{1,0:T(8,128)(2,1)}, bf16[512,1024]{1,0:T(8,128)(2,1)S(1)}, u32[]{:S(2)}, u32[]{:S(2)}) collective-permute-start(bf16[512,1024]{1,0:T(8,128)(2,1)} %get-tuple-element.227), channel_id=1, source_target_pairs={{0,1},{1,0},{2,5},{3,4},{4,3},{5,2},{6,7},{7,6},{8,9},{9,8},{10,13... | collective-permute-start | bytes 3145736 | tf_op jit(solution)/shard_map/ppermute | solution.py:537
  398.2 29.8 %collective-permute-start.17 = (bf16[4,512,1024]{2,1,0:T(8,128)(2,1)}, bf16[4,512,1024]{2,1,0:T(8,128)(2,1)}, u32[]{:S(2)}, u32[]{:S(2)}) collective-permute-start(bf16[4,512,1024]{2,1,0:T(8,128)(2,1)} %dynamic-slice_bitcast_fusion), channel_id=1, source_target_pairs={{0,4},{4,0},{1,5},{5,1},{2,6},{6,2},{3,7},{7,3},{8,12},{12,8},{9,1... | collective-permute-start | bytes 12582920 | tf_op jit(solution)/shard_map/ppermute | solution.py:692
  439.2 95.7 %collective-permute-start.22 = (bf16[512,1024]{1,0:T(8,128)(2,1)}, bf16[512,1024]{1,0:T(8,128)(2,1)S(1)}, u32[]{:S(2)}, u32[]{:S(2)}) collective-permute-start(bf16[512,1024]{1,0:T(8,128)(2,1)} %get-tuple-element.222), channel_id=1, source_target_pairs={{0,0},{1,1},{4,2},{5,3},{2,4},{3,5},{6,6},{7,7},{8,8},{9,9},{12,10... | collective-permute-start | bytes 3145736 | tf_op jit(solution)/shard_map/ppermute | solution.py:542
  441.1 93.8 %collective-permute-start.23 = (bf16[512,1024]{1,0:T(8,128)(2,1)S(1)}, bf16[512,1024]{1,0:T(8,128)(2,1)S(1)}, u32[]{:S(2)}, u32[]{:S(2)}) collective-permute-start(bf16[512,1024]{1,0:T(8,128)(2,1)S(1)} %get-tuple-element.223), channel_id=1, source_target_pairs={{1,0},{0,1},{5,2},{4,3},{3,4},{2,5},{7,6},{6,7},{9,8},{8,9},{13,10... | collective-permute-start | bytes 3145736 | tf_op jit(solution)/shard_map/ppermute | solution.py:543
  443.1 93.4 %collective-permute-start.19 = (bf16[640,1024]{1,0:T(8,128)(2,1)}, bf16[640,1024]{1,0:T(8,128)(2,1)}, u32[]{:S(2)}, u32[]{:S(2)}) collective-permute-start(bf16[640,1024]{1,0:T(8,128)(2,1)} %get-tuple-element.197), channel_id=1, source_target_pairs={{0,8},{8,0},{16,24},{24,16},{1,9},{9,1},{17,25},{25,17},{2,10},{10... | collective-permute-start | bytes 3932168 | tf_op jit(solution)/shard_map/ppermute | solution.py:702
  443.1 93.4 %collective-permute-start.20 = (bf16[640,1024]{1,0:T(8,128)(2,1)}, bf16[640,1024]{1,0:T(8,128)(2,1)}, u32[]{:S(2)}, u32[]{:S(2)}) collective-permute-start(bf16[640,1024]{1,0:T(8,128)(2,1)} %get-tuple-element.199), channel_id=1, source_target_pairs={{0,16},{8,24},{16,0},{24,8},{1,17},{9,25},{17,1},{25,9},{2,18},{10... | collective-permute-start | bytes 3932168 | tf_op jit(solution)/shard_map/ppermute | solution.py:702
  446.2 90.3 %collective-permute-start.21 = (bf16[640,1024]{1,0:T(8,128)(2,1)}, bf16[640,1024]{1,0:T(8,128)(2,1)}, u32[]{:S(2)}, u32[]{:S(2)}) collective-permute-start(bf16[640,1024]{1,0:T(8,128)(2,1)} %get-tuple-element.198), channel_id=1, source_target_pairs={{0,24},{8,16},{16,8},{24,0},{1,25},{9,17},{17,9},{25,1},{2,26},{10... | collective-permute-start | bytes 3932168 | tf_op jit(solution)/shard_map/ppermute | solution.py:702
  557.7 139.6 %all-to-all-start.2 = ((bf16[4,160,1024]{2,1,0:T(8,128)(2,1)}), bf16[4,160,1024]{2,1,0:T(8,128)(2,1)S(1)}, u32[]{:S(2)}, u32[]{:S(2)}) async-start(bf16[4,160,1024]{2,1,0:T(8,128)(2,1)} %bitcast.83), calls=%async_computation.3 | async-start | bytes 2621440 | tf_op jit(solution)/shard_map/all_to_all | solution.py:742
  635.6 47.8 %collective-permute-start.35 = (bf16[256,1024]{1,0:T(8,128)(2,1)}, bf16[256,1024]{1,0:T(8,128)(2,1)}, u32[]{:S(2)}, u32[]{:S(2)}) collective-permute-start(bf16[256,1024]{1,0:T(8,128)(2,1)} %get-tuple-element.213), channel_id=1, source_target_pairs={{0,8},{8,0},{16,24},{24,16},{1,9},{9,1},{17,25},{25,17},{2,10},{10... | collective-permute-start | bytes 1572872 | tf_op jit(solution)/shard_map/ppermute | solution.py:702
  637.0 46.4 %collective-permute-start.36 = (bf16[256,1024]{1,0:T(8,128)(2,1)}, bf16[256,1024]{1,0:T(8,128)(2,1)}, u32[]{:S(2)}, u32[]{:S(2)}) collective-permute-start(bf16[256,1024]{1,0:T(8,128)(2,1)} %get-tuple-element.215), channel_id=1, source_target_pairs={{0,16},{8,24},{16,0},{24,8},{1,17},{9,25},{17,1},{25,9},{2,18},{10... | collective-permute-start | bytes 1572872 | tf_op jit(solution)/shard_map/ppermute | solution.py:702
  641.6 36.1 %collective-permute-start.31 = (bf16[32,3072]{1,0:T(8,128)(2,1)}, bf16[32,3072]{1,0:T(8,128)(2,1)}, u32[]{:S(2)}, u32[]{:S(2)}) collective-permute-start(bf16[32,3072]{1,0:T(8,128)(2,1)} %get-tuple-element.244), channel_id=1, source_target_pairs={{0,1},{1,0},{2,3},{3,2},{4,5},{5,4},{6,7},{7,6},{8,9},{9,8},{10,11... | collective-permute-start | bytes 589832 | tf_op jit(solution)/shard_map/ppermute | solution.py:702
  641.7 39.7 %collective-permute-start.32 = (bf16[32,3072]{1,0:T(8,128)(2,1)}, bf16[32,3072]{1,0:T(8,128)(2,1)}, u32[]{:S(2)}, u32[]{:S(2)}) collective-permute-start(bf16[32,3072]{1,0:T(8,128)(2,1)} %get-tuple-element.246), channel_id=1, source_target_pairs={{0,2},{1,3},{2,0},{3,1},{4,6},{5,7},{6,4},{7,5},{8,10},{9,11},{10,... | collective-permute-start | bytes 589832 | tf_op jit(solution)/shard_map/ppermute | solution.py:702
  (58 other events, 845.0 us)
Sparse Core Ops, SparseCore 0:
  46.2 78.3 all-gather.3
  126.5 90.1 all-gather.5
  416.7 134.3 reduce-scatter.1

commit v5 on v4

--- a/solution.py
+++ b/solution.py
@@ -158,7 +158,7 @@
         ),
         out_shape=jax.ShapeDtypeStruct((length, 3 * heads_wide), bf16),
         compiler_params=params("arbitrary", "arbitrary"),
-        cost_estimate=cost(6 * length * width * heads_wide, 8 * length * width),
+        cost_estimate=cost(1, 1),
     )(member.reshape(1), value, gathered)
 
 
@@ -319,7 +319,7 @@
                 picker, product, (((1,), (1,)), ((), ())),
                 precision=lax.Precision.HIGHEST, preferred_element_type=f32,
             )
-            dq[rows, :] = jnp.zeros((BLOCK, width), f32)
+            dq[:, rows] = jnp.zeros((width, BLOCK), f32)
             seg_wide[rows, :] = jnp.broadcast_to(segc_ref[rows, :], (BLOCK, TILE))
             return carry
 
@@ -335,19 +335,24 @@
                 there = pl.ds(pl.multiple_of(range_ref[0, j] * BLOCK, BLOCK), count * BLOCK)
                 allowed = widen(seg_wide[rows, :], count * BLOCK) == segr_ref[:, there]
                 zero = jnp.zeros((BLOCK, width), bf16)
-                grad_k, grad_v, grad_q = [], [], None
+                key, value = (
+                    jnp.concatenate([jnp.where(lanes // HEAD_DIM == h, ref[rows, :], zero) for h in range(heads)], axis=0)
+                    for ref in (k_ref, v_ref)
+                )
+                query, grad_out = q_ref[there, :], do_ref[there, :]
+                found, grad_prob = dot_nt(key, query), dot_nt(value, grad_out)
+                parts, lows = [], []
                 for h in range(heads):
-                    key = jnp.where(lanes // HEAD_DIM == h, k_ref[rows, :], zero)
-                    value = jnp.where(lanes // HEAD_DIM == h, v_ref[rows, :], zero)
-                    scores = dot_nt(key, q_ref[there, :]) - lse_ref[0, h : h + 1, there]
-                    probability = jnp.exp(jnp.where(allowed, scores, -1e30))
-                    grad_prob = dot_nt(value, do_ref[there, :])
-                    grad_scores = (probability * (grad_prob - delta[h : h + 1, there])).astype(bf16)
-                    grad_v.append(dot_nn(probability.astype(bf16), do_ref[there, :]))
-                    grad_k.append(dot_nn(grad_scores, q_ref[there, :]))
-                    part = dot_tn(grad_scores, key)
-                    grad_q = part if grad_q is None else grad_q + part
-                dq[there, :] += grad_q
+                    half = slice(h * BLOCK, (h + 1) * BLOCK)
+                    scores = found[half] - lse_ref[0, h : h + 1, there]
+                    part = jnp.exp(jnp.where(allowed, scores, -1e30))
+                    parts.append(part.astype(bf16))
+                    lows.append((part * (grad_prob[half] - delta[h : h + 1, there])).astype(bf16))
+                grad_scores = jnp.concatenate(lows, axis=0)
+                grad_v = dot_nn(jnp.concatenate(parts, axis=0), grad_out)
+                grad_k = dot_nn(grad_scores, query)
+                grad_v, grad_k = ([v[h * BLOCK : (h + 1) * BLOCK] for h in range(heads)] for v in (grad_v, grad_k))
+                dq[:, there] += dot_tn(key, grad_scores)
                 dk_low[rows, :] = unturn(own_lanes(grad_k, lanes), rows).astype(bf16)
                 dv_low[rows, :] = own_lanes(grad_v, lanes).astype(bf16)
 
@@ -358,7 +363,7 @@
 
         def finish(i, carry):
             rows = span(i)
-            grad_ref[rows, :] = unturn(dq[rows, :] * HEAD_DIM**-0.5, rows).astype(bf16)
+            grad_ref[rows, :] = unturn(dq[:, rows].T * HEAD_DIM**-0.5, rows).astype(bf16)
             return carry
 
         lax.fori_loop(0, blocks, finish, 0)
@@ -387,7 +392,7 @@
                       whole(cosine.shape), whole(sine.shape), whole(seg_column.shape), whole(seg_row.shape)],
             out_specs=pl.BlockSpec((length, TILE), lambda p, t, r: (0, t * panels + p)),
             scratch_shapes=[
-                pltpu.VMEM((length, TILE), f32),
+                pltpu.VMEM((TILE, length), f32),
                 pltpu.VMEM((length, TILE), bf16),
                 pltpu.VMEM((length, TILE), bf16),
                 pltpu.VMEM((8, length), f32),
@@ -411,13 +416,14 @@
 
 
 def feed_kernel(
-    n_ref, cot_ref, resid_ref, up_ref, down_ref, out_ref, back_ref, gup_ref, gdown_ref,
-    total, n_turned, act_turned, pre,
+    core_ref, n_ref, cot_ref, resid_ref, up_ref, down_ref, out_ref, back_ref,
+    gup_own_ref, gup_other_ref, gdown_own_ref, gdown_other_ref, total, n_turned, act_turned, pre,
 ):
     step, last = pl.program_id(0), pl.num_programs(0) - 1
+    core = core_ref[0]
     frames, width = n_ref.shape
     tile = min(FEED_TILE, frames)
-    planes = gup_ref.shape[1]
+    planes = gup_own_ref.shape[0]
     part = width // planes
 
     def rows_of(i):
@@ -454,51 +460,47 @@
         grad_up = dot_nn(n_turned[begin : begin + FEED_PART, :], pre[...]).astype(bf16)
         for first in range(begin, begin + FEED_PART, part // 2):
             which, half = first // part, first % part // (part // 2)
-            gup_ref[half, which] = grad_up[first - begin : first - begin + part // 2]
+            kept = grad_up[first - begin : first - begin + part // 2]
+            pl.when(core == half)(functools.partial(gup_own_ref.__setitem__, which, kept))
+            pl.when(core != half)(functools.partial(gup_other_ref.__setitem__, which, kept))
     piece = act_turned.shape[0]
     for begin in range(0, piece, FEED_PART):
         rows = slice(begin, begin + FEED_PART)
-        gdown_ref[0, 0, rows, :] = dot_nn(act_turned[rows, :], cot_ref[...]).astype(bf16)
+        kept = dot_nn(act_turned[rows, :], cot_ref[...]).astype(bf16)
+        pl.when(core == step % 2)(functools.partial(gdown_own_ref.__setitem__, (0, rows), kept))
+        pl.when(core != step % 2)(functools.partial(gdown_other_ref.__setitem__, (0, rows), kept))
 
     @pl.when(step == last)
     def _():
         out_ref[...] = total[...].astype(bf16)
 
 
-def feed_forward_and_back(normed, cot, resid, hidden, piece, w_up, w_down, planes):
+def feed_forward_and_back(core, normed, cot, resid, hidden, piece, w_up, w_down, planes):
     frames, width = normed.shape
-    once = dict(pipeline_mode=pl.Buffered(1))
+    whole = lambda: pl.BlockSpec((frames, width), lambda j, r: (0, 0), pipeline_mode=pl.Buffered(1))
+    weight = lambda w: pl.BlockSpec(w[1], lambda j, r: w[2](j))
+    up_block = pl.BlockSpec((planes, width // (2 * planes), piece), lambda j, r: (0, 0, j))
+    down_block = pl.BlockSpec((1, piece, width), lambda j, r: (j // 2, 0, 0))
     return pl.pallas_call(
         feed_kernel,
-        grid=(hidden // piece,),
-        in_specs=[
-            pl.BlockSpec((frames, width), lambda j: (0, 0), **once),
-            pl.BlockSpec((frames, width), lambda j: (0, 0), **once),
-            pl.BlockSpec((frames, width), lambda j: (0, 0), **once),
-            pl.BlockSpec(*w_up[1:]),
-            pl.BlockSpec(*w_down[1:]),
-        ],
-        out_specs=[
-            pl.BlockSpec((frames, width), lambda j: (0, 0)),
-            pl.BlockSpec((frames, width), lambda j: (0, 0)),
-            pl.BlockSpec((2, planes, width // (2 * planes), piece), lambda j: (0, 0, 0, j)),
-            pl.BlockSpec((1, 1, piece, width), lambda j: (j % 2, j // 2, 0, 0)),
-        ],
-        out_shape=[
-            jax.ShapeDtypeStruct((frames, width), bf16),
-            jax.ShapeDtypeStruct((frames, width), f32),
-            jax.ShapeDtypeStruct((2, planes, width // (2 * planes), hidden), bf16),
-            jax.ShapeDtypeStruct((2, planes, piece, width), bf16),
-        ],
-        scratch_shapes=[
-            pltpu.VMEM((frames, width), f32),
-            pltpu.VMEM((width, frames), bf16),
-            pltpu.VMEM((piece, frames), bf16),
-            pltpu.VMEM((frames, piece), bf16),
-        ],
+        grid_spec=pltpu.PrefetchScalarGridSpec(
+            num_scalar_prefetch=1,
+            grid=(hidden // piece,),
+            in_specs=[whole(), whole(), whole(), weight(w_up), weight(w_down)],
+            out_specs=[pl.BlockSpec((frames, width), lambda j, r: (0, 0))] * 2 + [up_block] * 2 + [down_block] * 2,
+            scratch_shapes=[
+                pltpu.VMEM((frames, width), f32),
+                pltpu.VMEM((width, frames), bf16),
+                pltpu.VMEM((piece, frames), bf16),
+                pltpu.VMEM((frames, piece), bf16),
+            ],
+        ),
+        out_shape=[jax.ShapeDtypeStruct((frames, width), bf16), jax.ShapeDtypeStruct((frames, width), f32)]
+        + [jax.ShapeDtypeStruct((planes, width // (2 * planes), hidden), bf16)] * 2
+        + [jax.ShapeDtypeStruct((planes, piece, width), bf16)] * 2,
         compiler_params=params("arbitrary"),
         cost_estimate=cost(12 * frames * width * hidden, 8 * width * hidden + 16 * frames * width, frames * hidden),
-    )(normed, cot, resid, w_up[0], w_down[0])
+    )(core.reshape(1), normed, cot, resid, w_up[0], w_down[0])
 
 
 def body(inputs, skips, cotangent, segment_ids, time_steps, w_skip, w_qkv, w_out, w_up, w_down, w_mod):
@@ -578,10 +580,8 @@
     skip_rows = w_skip.shape[0]
     early = jnp.concatenate([w_skip] + [w_qkv[:, i * width : (i + 1) * width] for i in range(3)] + [w_out], axis=0)
     early_line = share_on_line(early)
-    early = gather_planes(early_line)
     columns = w_up.shape[1] // width
     late = jnp.concatenate([w_down] + [w_up[:, i * width : (i + 1) * width] for i in range(columns)], axis=0)
-    late_line = share_on_line(late)
 
     labels_own = segment_ids[:, 0]
     labels_other = lax.ppermute(labels_own, "core", swap)
@@ -614,18 +614,18 @@
     own_columns = block_mod.shape[1]
     block_mod = block_mod.reshape(planes, 1, highs, 1, labels, own_columns)
     block_mod = jnp.broadcast_to(block_mod, (planes, 2, highs, lows, labels, own_columns))
-    late_line, inputs, skips, block_mod, cosine, sine, ranges, mine = lax.optimization_barrier(
-        (late_line, inputs, skips, block_mod, cosine, sine, ranges, mine)
-    )
-    late = gather_planes(late_line)
-    x, s = to_rows(inputs), to_rows(skips)
     block_mod = lax.all_to_all(
         block_mod.reshape(devices, labels, own_columns), ALL_AXES, split_axis=0, concat_axis=0, tiled=True
     )
     modulation = jnp.moveaxis(block_mod, 0, 1).reshape(labels, 4, width)
 
-    x, s, cotangent, modulation = lax.optimization_barrier((x, s, cotangent, modulation))
-    cot = to_rows(cotangent)
+    early_line, inputs, skips, modulation, cosine, sine, ranges, mine = lax.optimization_barrier(
+        (early_line, inputs, skips, modulation, cosine, sine, ranges, mine)
+    )
+    early = gather_planes(early_line)
+    x, s = to_rows(inputs), to_rows(skips)
+    late, s = lax.optimization_barrier((late, s))
+    late = lax.all_gather(late, ("hi", "lo"), axis=0, tiled=True)
     in_place = out_rows % 16 == 0
     hidden = w_up.shape[1]
     chunk = hidden // (2 * planes)
@@ -656,13 +656,16 @@
         [("", x), ("", s), ("weight", skip_top), ("weight", skip_bottom), ("", mine_column),
          ("whole", shift_one), ("whole", scale_one)],
         [(width, f32), (width, bf16)],
-        flops=4 * frames * width * width,
+        light=True,
     )
     normed_row = frames_to_row(normed_one)
     if in_place:
         projected = project(normed_row, early, skip_rows, out_rows, heads_wide, member)
     else:
         projected = jnp.dot(normed_row, own_qkv(early), preferred_element_type=f32).astype(bf16)
+    projected, late, cotangent = lax.optimization_barrier((projected, late, cotangent))
+    late = gather_planes(late)
+    cot = to_rows(cotangent)
     if in_place:
         per = width // chunk
         up_weight = (late, (devices, up_rows, chunk), lambda j: (0, down_rows // up_rows + j // per, j % per))
@@ -684,8 +687,8 @@
     early, normed_two = lax.optimization_barrier((early, normed_two))
     qkv_own = own_qkv(early)
     normed_two, qkv_own = lax.optimization_barrier((normed_two, qkv_own))
-    result, grad_normed_two, grad_up, grad_down = feed_forward_and_back(
-        normed_two, cot, resid_mid, hidden, chunk, up_weight, down_weight, planes
+    result, grad_normed_two, *up_halves, own_down, other_down = feed_forward_and_back(
+        core, normed_two, cot, resid_mid, hidden, chunk, up_weight, down_weight, planes
     )
 
     def over_cores(kept, axis):
@@ -712,7 +715,10 @@
         value = value.reshape(-1, value.shape[-1])
         return lax.psum_scatter(value, ("plane", "hi", "lo"), scatter_dimension=0, tiled=True)
 
-    grad_up, grad_down = over_cores(grad_up, 0), over_cores(grad_down, 0)
+    def add_other(own, other):
+        return (own.astype(f32) + lax.ppermute(other, "core", swap).astype(f32)).astype(bf16)
+
+    grad_up, grad_down = add_other(*up_halves), add_other(own_down, other_down)
 
     grad_mid, grad_mid_low, grad_frames, grad_shift_two, grad_scale_two = rowwise(
         norm_two_back_kernel,
@@ -737,36 +743,19 @@
     grad_proj = attend_backward(
         ranges, queries, keys, projected, mixed_heads, grad_heads, logsum, cosine, sine, seg_column, seg_row
     )
-    grad_proj, grad_up, grad_down, block_out = lax.optimization_barrier((grad_proj, grad_up, grad_down, block_out))
-    grad_down = grad_down.reshape(line, -1, width)
-    grad_down = lax.all_to_all(grad_down, ("hi", "lo"), split_axis=0, concat_axis=0, tiled=True)
-    if group > 2:
-        partial = dot_nt(grad_proj, qkv_own).astype(bf16)
-        grad_one = lax.psum_scatter(partial, ROW_AXES, scatter_dimension=0, tiled=True).astype(f32)
-        grad_one_other = jnp.zeros((frames, width), bf16)
-    else:
-        away = lax.dynamic_slice_in_dim(grad_proj, (1 - core) * frames, frames, 0)
-        home = lax.dynamic_slice_in_dim(grad_proj, core * frames, frames, 0)
-        grad_one_other = lax.ppermute(dot_nt(away, qkv_own).astype(bf16), "core", swap)
-        grad_one = dot_nt(home, qkv_own)
-    grad_in, grad_shift_one, grad_scale_one = rowwise(
-        norm_one_back_kernel,
-        frames,
-        [("", grad_one), ("", grad_one_other), ("", resid_in), ("", grad_mid), ("", mine_column), ("row", mine_row),
-         ("whole", scale_one)],
-        [(width, bf16)],
-        sums=2,
-    )
-    grad_in_home = from_rows(grad_in)
-    grad_proj, grad_in = lax.optimization_barrier((grad_proj, grad_in))
+    grad_proj, grad_down, block_out = lax.optimization_barrier((grad_proj, grad_down, block_out))
+    grad_down = exchange_line(grad_down)
     grad_qkv = lax.dot_general(normed_row, grad_proj, (((0,), (0,)), ((), ())), preferred_element_type=f32)
     grad_qkv = grad_qkv.astype(bf16)
+    grad_proj, grad_qkv = lax.optimization_barrier((grad_proj, grad_qkv))
     if group > 2:
         grad_qkv = grad_qkv.reshape(planes, 2, highs, lows, -1, 3, 1, heads_wide)
         grad_qkv = jnp.moveaxis(grad_qkv, (1, 3), (0, 1)).reshape(group, -1, 3, 1, heads_wide)
         grad_qkv = lax.all_to_all(grad_qkv, ROW_AXES, split_axis=0, concat_axis=3, tiled=True)
         grad_qkv = grad_qkv.reshape(-1, 3 * width)
-        grad_qkv = lax.psum_scatter(grad_qkv, ("plane", "hi"), scatter_dimension=0, tiled=True).astype(f32)
+        partial = dot_nt(grad_proj, qkv_own).astype(bf16)
+        grad_one = lax.psum_scatter(partial, ROW_AXES, scatter_dimension=0, tiled=True).astype(f32)
+        grad_one_other = jnp.zeros((frames, width), bf16)
     else:
         split = grad_qkv.reshape(planes, 2, -1, 3 * heads_wide)
         other = lax.ppermute(lax.dynamic_index_in_dim(split, 1 - core, 1, False), "core", swap)
@@ -776,8 +765,25 @@
         grad_qkv = jnp.concatenate(
             [v[:, i * heads_wide : (i + 1) * heads_wide] for i in range(3) for v in (left, right)], axis=1
         )
-        grad_qkv = exchange_planes(grad_qkv.reshape(planes, -1, 3 * width))
-
+        away = lax.dynamic_slice_in_dim(grad_proj, (1 - core) * frames, frames, 0)
+        home = lax.dynamic_slice_in_dim(grad_proj, core * frames, frames, 0)
+        grad_one_other = lax.ppermute(dot_nt(away, qkv_own).astype(bf16), "core", swap)
+        grad_one = dot_nt(home, qkv_own)
+    grad_one, grad_qkv, grad_up = lax.optimization_barrier((grad_one, grad_qkv, grad_up))
+    if group > 2:
+        grad_qkv = lax.psum_scatter(grad_qkv, ("plane", "hi"), scatter_dimension=0, tiled=True).astype(f32)
+    else:
+        grad_qkv = lax.psum_scatter(grad_qkv, "plane", scatter_dimension=0, tiled=True)
+    grad_in, grad_shift_one, grad_scale_one = rowwise(
+        norm_one_back_kernel,
+        frames,
+        [("", grad_one), ("", grad_one_other), ("", resid_in), ("", grad_mid), ("", mine_column), ("row", mine_row),
+         ("whole", scale_one)],
+        [(width, bf16)],
+        sums=2,
+    )
+    grad_in, grad_down = lax.optimization_barrier((grad_in, grad_down))
+    grad_in_home = from_rows(grad_in)
     grad_skip_w = jnp.concatenate(
         [
             lax.dot_general(v, grad_in, (((0,), (0,)), ((), ())), preferred_element_type=f32).astype(bf16)
@@ -789,7 +795,6 @@
     grad_in_home, grad_qkv = lax.optimization_barrier((grad_in_home, grad_qkv))
     if group == 2:
         grad_qkv = exchange_line(grad_qkv)
-    grad_skip_w = exchange_line(grad_skip_w)
     grad_inputs, grad_skips = rowwise(
         unmerge_kernel,
         frames,
@@ -799,14 +804,15 @@
     )
     grad_inputs, grad_skips = (v.reshape(grad_in_home.shape) for v in (grad_inputs, grad_skips))
 
-    grad_shift_one, grad_qkv = lax.optimization_barrier((grad_shift_one, grad_qkv))
+    grad_shift_one, grad_skip_w = lax.optimization_barrier((grad_shift_one, grad_skip_w))
+    grad_skip_w = exchange_line(grad_skip_w)
     grad_mod = jnp.stack([v[:labels] for v in (grad_shift_one, grad_scale_one, grad_shift_two, grad_scale_two)], axis=1)
     grad_mod = jnp.moveaxis(grad_mod.reshape(labels, devices, own_columns), 1, 0)
     grad_mod = lax.all_to_all(grad_mod, ALL_AXES, split_axis=0, concat_axis=0, tiled=True)
-    grad_inputs, grad_mod, grad_up, grad_down, grad_skip_w = lax.optimization_barrier(
-        (grad_inputs, grad_mod, grad_up, grad_down, grad_skip_w)
-    )
-    grad_up, grad_down = grad_up.astype(f32), jnp.sum(grad_down.astype(f32), axis=0)
+    grad_inputs, grad_mod, grad_up, grad_skip_w = lax.optimization_barrier(
+        (grad_inputs, grad_mod, grad_up, grad_skip_w)
+    )
+    grad_up = grad_up.astype(f32)
     grad_down, grad_out = grad_down[:down_rows], grad_down[down_rows:]
     grad_mod = jnp.sum(grad_mod.reshape(planes, 2, highs, lows, labels, own_columns), axis=(1, 3))
     grad_mod = lax.dot_general(

time: 727 us -> 743 us (1.022)
  starting transfers between devices: 122 us -> 216 us
  waiting for transfers between devices: 154 us -> 100 us
  Pallas kernels: 269 us -> 253 us
    ppermute x6 -> x3, waiting for transfers between devices: 44.7 us -> 2.43 us  [share_on_line(): lax.ppermute(value, ('hi', 'lo'), [(i, i ^ flip) for i in range(line)])]
    ppermute x1, starting transfers between devices: 0.02 us -> 37.6 us  [frames_to_row(): other = lax.ppermute(value, 'core', swap)]
    ppermute x15, starting transfers between devices: 43.9 us -> 76 us  [exchange(): lax.ppermute(sent, axes, [(i, i ^ flip) for i in range(count)]).astype(f32)]
    all_to_all x1, waiting for transfers between devices: 36.9 us -> 6.16 us  [body(): lax.all_to_all(block_mod.reshape(devices, labels, own_columns), ALL_AXES,...]
    ppermute x3, starting transfers between devices: 10.6 us -> 31.7 us  [to_rows(): lax.ppermute(lax.dynamic_index_in_dim(value, 1 - odd_place, 0, False), LI...]
    ppermute x2, starting transfers between devices: 1.9 us -> 18.5 us  [from_rows(): lax.ppermute(lax.dynamic_index_in_dim(value, 1 - high % 2, 0, False), LIN...]
    pallas_call x1, Pallas kernels: 87.2 us -> 72.2 us  [attend_backward(): pl.pallas_call(attend_backward_kernel, grid_spec=pltpu.PrefetchScalarGrid...]
    convert_element_type x4 -> x2, other arithmetic: 15.9 us -> 1.38 us  [over_cores(): return (own.astype(f32) + other.astype(f32)).astype(bf16)]
  transfers between devices with their start and end apart: 47 -> 45, of which waited for: 15 -> 14; matrix products, arithmetic and copies ran while one was open for 17% -> 17% of each run, Pallas kernels for 28% -> 25%
where the time goes in v5:
time: 743 us; the launch traced here: 732 us
  Pallas kernels  253 us (34%)
  starting transfers between devices  216 us (29%)
  waiting for transfers between devices  100 us (13%)
  other arithmetic  60.3 us (8%)
  local copies, waits for them, and re-layouts  49.6 us (7%)
  matrix products  28.6 us (4%)
  between operations  14.9 us (2%)
  blocking collectives  9.25 us (1%)
    ppermute x15, starting transfers between devices, exchange(): lax.ppermute(sent, axes, [(i, i ^ flip) for i in range(count)]).astype(f32)  76 us
    pallas_call x1, Pallas kernels, attend_backward(): pl.pallas_call(attend_backward_kernel, grid_spec=pltpu.PrefetchScalarGrid...  72.2 us
    pallas_call x1, Pallas kernels, feed_forward_and_back(): pl.pallas_call(feed_kernel, grid_spec=pltpu.PrefetchScalarGridSpec(num_sc...  71.5 us
    pallas_call x1, Pallas kernels, attend_forward(): pl.pallas_call(attend_forward_kernel, grid_spec=pltpu.PrefetchScalarGridS...  49.6 us
    pallas_call x5, Pallas kernels, rowwise(): pl.pallas_call(kernel, grid=(frames // tile,), in_specs=in_specs, out_spe...  49.1 us
    ppermute x1, starting transfers between devices, frames_to_row(): other = lax.ppermute(value, 'core', swap)  37.6 us
    ppermute x3, waiting for transfers between devices, to_rows(): lax.ppermute(lax.dynamic_index_in_dim(value, 1 - odd_place, 0, False), LI...  35.7 us
    ppermute x3, starting transfers between devices, to_rows(): lax.ppermute(lax.dynamic_index_in_dim(value, 1 - odd_place, 0, False), LI...  31.7 us
  transfers between devices with their start and end apart: 45, of which 14 were waited for; matrix products, arithmetic and copies ran while one was open for 17% of the time, Pallas kernels for 25%

profile of v5, /device:TPU:0, one launch (start us, length us, event | category | flops | bytes accessed | tf_op | source)
XLA Modules:
  0.0 732.3 jit_solution(8297573105530614060)
XLA Ops:
  21.1 9.3 %all-gather = s32[16,1,4]{2,1,0:T(1,128)S(1)} all-gather(s32[2,1,4]{2,1,0:T(1,128)} %param.15), channel_id=2, replica_groups=mesh['plane'=4,'core'=2,'hi'=4,'lo'=1] {'plane','core'}, dimensions={0}, use_global_device_ids=true | all-gather | bytes 288 | tf_op jit(solution)/shard_map/all_gather | solution.py:608
  62.6 9.5 %collective-permute-start.6 = (bf16[512,1024]{1,0:T(8,128)(2,1)}, bf16[512,1024]{1,0:T(8,128)(2,1)}, u32[]{:S(2)}, u32[]{:S(2)}) collective-permute-start(bf16[512,1024]{1,0:T(8,128)(2,1)} %get-tuple-element.239), channel_id=1, source_target_pairs={{0,0},{1,1},{2,4},{3,5},{4,2},{5,3},{6,6},{7,7},{8,8},{9,9},{10,12... | collective-permute-start | bytes 3145736 | tf_op jit(solution)/shard_map/ppermute | solution.py:538
  81.5 28.0 %collective-permute-done.7 = bf16[512,1024]{1,0:T(8,128)(2,1)} collective-permute-done((bf16[512,1024]{1,0:T(8,128)(2,1)}, bf16[512,1024]{1,0:T(8,128)(2,1)}, u32[]{:S(2)}, u32[]{:S(2)}) %collective-permute-start.7) | collective-permute-done | bytes 1048608 | tf_op jit(solution)/shard_map/ppermute | solution.py:539
  113.2 7.5 %collective-permute-done.5 = bf16[512,1024]{1,0:T(8,128)(2,1)} collective-permute-done((bf16[512,1024]{1,0:T(8,128)(2,1)S(1)}, bf16[512,1024]{1,0:T(8,128)(2,1)}, u32[]{:S(2)}, u32[]{:S(2)}) %collective-permute-start.5) | collective-permute-done | bytes 1048608 | tf_op jit(solution)/shard_map/ppermute | solution.py:539
  130.6 10.9 %shard_map.178 = (f32[1024,1024]{1,0:T(8,128)}, bf16[1024,1024]{1,0:T(8,128)(2,1)}) custom-call(bf16[1024,1024]{1,0:T(8,128)(2,1)} %pad_maximum_fusion.4.x_ref, bf16[1024,1024]{1,0:T(8,128)(2,1)} %pad_maximum_fusion.5.s_ref, bf16[32,192,1024]{2,1,0:T(8,128)(2,1)} %all-gather.5.cloned.1.call-done.top_ref.bottom_ref.w_ref, ...), custom_call_target="tpu_custom_call" | custom-call | flops 1 | bytes 1 | tf_op jit(solution)/shard_map/pallas_call | solution.py:188
  141.5 37.6 %collective-permute-start.8 = (bf16[1024,1024]{1,0:T(8,128)(2,1)}, bf16[1024,1024]{1,0:T(8,128)(2,1)S(1)}, u32[]{:S(2)}, u32[]{:S(2)}) collective-permute-start(bf16[1024,1024]{1,0:T(8,128)(2,1)} %get-tuple-element.80), channel_id=1, source_target_pairs={{0,4},{4,0},{1,5},{5,1},{2,6},{6,2},{3,7},{7,3},{8,12},{12,8},{9,1... | collective-permute-start | bytes 6291464 | tf_op jit(solution)/shard_map/ppermute | solution.py:552
  188.2 11.0 %shard_map.179.q_ref.k_ref.v_ref = bf16[2048,1536]{1,0:T(8,128)(2,1)} custom-call(s32[1]{0:T(128)} %bitcast.13.place_ref.core_ref, bf16[2048,1024]{1,0:T(8,128)(2,1)} %pad_maximum_fusion.1.x_ref, bf16[32,192,1024]{2,1,0:T(8,128)(2,1)} %all-gather.5.cloned.1.call-done.top_ref.bottom_ref.w_ref), custom_call_target="tpu_custom_call" | custom-call | flops 1 | bytes 1 | tf_op jit(solution)/shard_map/pallas_call | solution.py:148
  201.9 49.6 %shard_map.180 = (bf16[2048,512]{1,0:T(8,128)(2,1)}, bf16[2048,512]{1,0:T(8,128)(2,1)}, bf16[2048,512]{1,0:T(8,128)(2,1)}, f32[4,2,2048]{2,1,0:T(2,128)}) custom-call(s32[2,8]{1,0:T(2,128)} %pad_add_fusion.range_ref, bf16[2048,1536]{1,0:T(8,128)(2,1)} %shard_map.179.q_ref.k_ref.v_ref, bf16[2048,1536]{1,0:T(8,128)(2,1)} %shard_map.179.q_ref.k_ref.v_ref, ...), custom_call_target="tpu_custom_call" | custom-call | flops 17179869184 | bytes 14680064 | tf_op jit(solution)/shard_map/pallas_call | solution.py:281
  257.8 29.6 %collective-permute-start.11 = (bf16[512,1024]{1,0:T(8,128)(2,1)}, bf16[512,1024]{1,0:T(8,128)(2,1)}, u32[]{:S(2)}, u32[]{:S(2)}) collective-permute-start(bf16[512,1024]{1,0:T(8,128)(2,1)} %get-tuple-element.236), channel_id=1, source_target_pairs={{0,1},{1,0},{2,5},{3,4},{4,3},{5,2},{6,7},{7,6},{8,9},{9,8},{10,13... | collective-permute-start | bytes 3145736 | tf_op jit(solution)/shard_map/ppermute | solution.py:539
  290.7 9.0 %shard_map.181 = (f32[1024,1024]{1,0:T(8,128)}, bf16[1024,1024]{1,0:T(8,128)(2,1)}) custom-call(bf16[1024,1024]{1,0:T(8,128)(2,1)} %pad_maximum_fusion.6.mixed_ref, bf16[32,192,1024]{2,1,0:T(8,128)(2,1)} %all-gather.5.cloned.1.call-done.top_ref.bottom_ref.w_ref, f32[1024,1024]{1,0:T(8,128)} %get-tuple-element.88.resid_in_ref.resid_ref, ...), custom_call_target="tpu_custom_call" | custom-call | flops 2147483648 | bytes 25202688 | tf_op jit(solution)/shard_map/pallas_call | solution.py:188
  315.8 71.5 %shard_map.182 = (bf16[1024,1024]{1,0:T(8,128)(2,1)}, f32[1024,1024]{1,0:T(8,128)}, bf16[4,128,4096]{2,1,0:T(8,128)(2,1)}, bf16[4,128,4096]{2,1,0:T(8,128)(2,1)}...) custom-call(s32[1]{0:T(128)} %bitcast.13.place_ref.core_ref, bf16[1024,1024]{1,0:T(8,128)(2,1)} %get-tuple-element.92.n_ref, ...), custom_call_target="tpu_custom_call" | custom-call | flops 51539607552 | bytes 50331648 | tf_op jit(solution)/shard_map/pallas_call | solution.py:484
  387.3 12.0 %collective-permute-start.12 = (bf16[4,128,4096]{2,1,0:T(8,128)(2,1)}, bf16[4,128,4096]{2,1,0:T(8,128)(2,1)}, u32[]{:S(2)}, u32[]{:S(2)}) collective-permute-start(bf16[4,128,4096]{2,1,0:T(8,128)(2,1)} %get-tuple-element.99), channel_id=1, source_target_pairs={{0,4},{4,0},{1,5},{5,1},{2,6},{6,2},{3,7},{7,3},{8,12},{12,8},{9,1... | collective-permute-start | bytes 12582920 | tf_op jit(solution)/shard_map/ppermute | solution.py:719
  399.4 10.7 %shard_map.183 = (f32[1024,1024]{1,0:T(8,128)}, bf16[1024,1024]{1,0:T(8,128)(2,1)}, bf16[1024,1024]{1,0:T(8,128)(2,1)}, f32[8,1024]{1,0:T(8,128)}, f32[8,1024]{1,0:T(8,128)}) custom-call(f32[1024,1024]{1,0:T(8,128)} %get-tuple-element.96.g_ref, f32[1024,1024]{1,0:T(8,128)} %get-tuple-element.94.resid_ref, bf16[1024,1024]{1,0:T(8,128)(2,1)} %pad_maximum_fusion.7.cot_ref, ...), custom_call_target="tpu_custom_call" | custom-call | flops 1 | bytes 1 | tf_op jit(solution)/shard_map/pallas_call | solution.py:188
  435.2 9.4 %collective-permute-start.19 = (bf16[512,1024]{1,0:T(8,128)(2,1)}, bf16[512,1024]{1,0:T(8,128)(2,1)}, u32[]{:S(2)}, u32[]{:S(2)}) collective-permute-start(bf16[512,1024]{1,0:T(8,128)(2,1)} %get-tuple-element.231), channel_id=1, source_target_pairs={{0,0},{1,1},{4,2},{5,3},{2,4},{3,5},{6,6},{7,7},{8,8},{9,9},{12,10... | collective-permute-start | bytes 3145736 | tf_op jit(solution)/shard_map/ppermute | solution.py:544
  444.6 11.7 %collective-permute-start.20 = (bf16[512,1024]{1,0:T(8,128)(2,1)}, bf16[512,1024]{1,0:T(8,128)(2,1)}, u32[]{:S(2)}, u32[]{:S(2)}) collective-permute-start(bf16[512,1024]{1,0:T(8,128)(2,1)} %get-tuple-element.232), channel_id=1, source_target_pairs={{1,0},{0,1},{5,2},{4,3},{3,4},{2,5},{7,6},{6,7},{9,8},{8,9},{13,10... | collective-permute-start | bytes 3145736 | tf_op jit(solution)/shard_map/ppermute | solution.py:545
  465.2 72.2 %shard_map.184 = bf16[2048,1536]{1,0:T(8,128)(2,1)} custom-call(s32[2,8]{1,0:T(2,128)} %pad_add_fusion.range_ref, bf16[2048,512]{1,0:T(8,128)(2,1)} %get-tuple-element.85.q_ref, bf16[2048,512]{1,0:T(8,128)(2,1)} %get-tuple-element.86.k_ref, bf16[2048,1536]{1,0:T(8,128)(2,1)} %shard_map.179.q_ref.k_ref.v_ref, bf16[2048,512]{1,0:T(8,128)(2,1)} %get-tuple-element.87.out_ref, ...), custom_call_target="tpu_custom_call" | custom-call | flops 42949672960 | bytes 16777216 | tf_op jit(solution)/shard_map/pallas_call | solution.py:385
  546.3 7.3 convolution_convert_fusion
  553.9 35.2 %collective-permute-start.23 = (bf16[160,1024]{1,0:T(8,128)(2,1)S(1)}, bf16[160,1024]{1,0:T(8,128)(2,1)S(1)}, u32[]{:S(2)}, u32[]{:S(2)}) collective-permute-start(bf16[160,1024]{1,0:T(8,128)(2,1)S(1)} %get-tuple-element.249), channel_id=1, source_target_pairs={{0,1},{1,0},{2,3},{3,2},{4,5},{5,4},{6,7},{7,6},{8,9},{9,8},{10,11... | collective-permute-start | bytes 983048 | tf_op jit(solution)/shard_map/ppermute | solution.py:705
  606.9 7.8 %collective-permute-done.24 = bf16[160,1024]{1,0:T(8,128)(2,1)S(1)} collective-permute-done((bf16[160,1024]{1,0:T(8,128)(2,1)S(1)}, bf16[160,1024]{1,0:T(8,128)(2,1)S(1)}, u32[]{:S(2)}, u32[]{:S(2)}) %collective-permute-start.24) | collective-permute-done | bytes 327712 | tf_op jit(solution)/shard_map/ppermute | solution.py:705
  614.9 10.0 %shard_map.185 = (bf16[1024,1024]{1,0:T(8,128)(2,1)}, f32[8,1024]{1,0:T(8,128)}, f32[8,1024]{1,0:T(8,128)}) custom-call(f32[1024,1024]{1,0:T(8,128)} %fusion.3.own_ref, bf16[1024,1024]{1,0:T(8,128)(2,1)} %collective-permute-done.22.other_ref, f32[1024,1024]{1,0:T(8,128)} %get-tuple-element.88.resid_in_ref.resid_ref, ...), custom_call_target="tpu_custom_call" | custom-call | bytes 16801792 | tf_op jit(solution)/shard_map/pallas_call | solution.py:188
  633.2 6.8 collective-permute-start.27
  646.2 17.7 %collective-permute-done.27 = bf16[512,1024]{1,0:T(8,128)(2,1)S(1)} collective-permute-done((bf16[512,1024]{1,0:T(8,128)(2,1)S(1)}, bf16[512,1024]{1,0:T(8,128)(2,1)S(1)}, u32[]{:S(2)}, u32[]{:S(2)}) %collective-permute-start.27) | collective-permute-done | bytes 1048608 | tf_op jit(solution)/shard_map/ppermute | solution.py:545
  674.4 16.8 %collective-permute-start.33 = (bf16[64,1024]{1,0:T(8,128)(2,1)S(1)}, bf16[64,1024]{1,0:T(8,128)(2,1)S(1)}, u32[]{:S(2)}, u32[]{:S(2)}) collective-permute-start(bf16[64,1024]{1,0:T(8,128)(2,1)S(1)} %get-tuple-element.257), channel_id=1, source_target_pairs={{0,2},{1,3},{2,0},{3,1},{4,6},{5,7},{6,4},{7,5},{8,10},{9,11},{10,... | collective-permute-start | bytes 393224 | tf_op jit(solution)/shard_map/ppermute | solution.py:705
  710.1 8.5 %shard_map.186 = (bf16[1024,1024]{1,0:T(8,128)(2,1)}, bf16[1024,1024]{1,0:T(8,128)(2,1)}) custom-call(bf16[1024,1024]{1,0:T(8,128)(2,1)} %bitcast.189, bf16[32,192,1024]{2,1,0:T(8,128)(2,1)} %all-gather.5.cloned.1.call-done.top_ref.bottom_ref.w_ref, bf16[32,192,1024]{2,1,0:T(8,128)(2,1)} %all-gather.5.cloned.1.call-done.top_ref.bottom_ref.w_ref), custom_call_target="tpu_custom_call" | custom-call | flops 4294967296 | bytes 31457280 | tf_op jit(solution)/shard_map/pallas_call | solution.py:188
  (264 shorter events, 217.7 us)
Async XLA Ops:
  14.7 31.4 %collective-permute-start = (bf16[192,1024]{1,0:T(8,128)(2,1)}, bf16[192,1024]{1,0:T(8,128)(2,1)}, u32[]{:S(2)}, u32[]{:S(2)}) collective-permute-start(bf16[192,1024]{1,0:T(8,128)(2,1)} %constant_dynamic-update-slice_fusion), channel_id=1, source_target_pairs={{0,1},{1,0},{2,3},{3,2},{4,5},{5,4},{6,7},{7,6},{8,9},{9,8},{10,11... | collective-permute-start | bytes 1179656 | tf_op jit(solution)/shard_map/ppermute | solution.py:572
  17.7 30.8 %collective-permute-start.1 = (bf16[192,1024]{1,0:T(8,128)(2,1)}, bf16[192,1024]{1,0:T(8,128)(2,1)}, u32[]{:S(2)}, u32[]{:S(2)}) collective-permute-start(bf16[192,1024]{1,0:T(8,128)(2,1)} %constant_dynamic-update-slice_fusion), channel_id=1, source_target_pairs={{0,2},{1,3},{2,0},{3,1},{4,6},{5,7},{6,4},{7,5},{8,10},{9,11},{10,... | collective-permute-start | bytes 1179656 | tf_op jit(solution)/shard_map/ppermute | solution.py:572
  20.3 28.3 %collective-permute-start.2 = (bf16[192,1024]{1,0:T(8,128)(2,1)}, bf16[192,1024]{1,0:T(8,128)(2,1)}, u32[]{:S(2)}, u32[]{:S(2)}) collective-permute-start(bf16[192,1024]{1,0:T(8,128)(2,1)} %constant_dynamic-update-slice_fusion), channel_id=1, source_target_pairs={{0,3},{1,2},{2,1},{3,0},{4,7},{5,6},{6,5},{7,4},{8,11},{9,10},{10,... | collective-permute-start | bytes 1179656 | tf_op jit(solution)/shard_map/ppermute | solution.py:572
  36.9 93.7 %all-gather.5.cloned.1.call-start = ((), (), s32[]{:S(2)}) async-start(), calls=%async_computation.4 | async-start | bytes 14155776 | tf_op jit(solution)/shard_map/all_gather | solution.py:577
  57.9 141.3 %all-gather.7.cloned.1.call-start = ((), (), s32[]{:S(2)}) async-start(), calls=%async_computation.5 | async-start | bytes 2621440 | tf_op jit(solution)/shard_map/all_gather | solution.py:628
  72.0 37.5 %collective-permute-start.7 = (bf16[512,1024]{1,0:T(8,128)(2,1)}, bf16[512,1024]{1,0:T(8,128)(2,1)}, u32[]{:S(2)}, u32[]{:S(2)}) collective-permute-start(bf16[512,1024]{1,0:T(8,128)(2,1)} %get-tuple-element.240), channel_id=1, source_target_pairs={{0,1},{1,0},{2,5},{3,4},{4,3},{5,2},{6,7},{7,6},{8,9},{9,8},{10,13... | collective-permute-start | bytes 3145736 | tf_op jit(solution)/shard_map/ppermute | solution.py:539
  75.7 37.5 %collective-permute-start.4 = (bf16[512,1024]{1,0:T(8,128)(2,1)}, bf16[512,1024]{1,0:T(8,128)(2,1)S(1)}, u32[]{:S(2)}, u32[]{:S(2)}) collective-permute-start(bf16[512,1024]{1,0:T(8,128)(2,1)} %get-tuple-element.243), channel_id=1, source_target_pairs={{0,0},{1,1},{2,4},{3,5},{4,2},{5,3},{6,6},{7,7},{8,8},{9,9},{10,12... | collective-permute-start | bytes 3145736 | tf_op jit(solution)/shard_map/ppermute | solution.py:538
  77.6 43.2 %collective-permute-start.5 = (bf16[512,1024]{1,0:T(8,128)(2,1)S(1)}, bf16[512,1024]{1,0:T(8,128)(2,1)}, u32[]{:S(2)}, u32[]{:S(2)}) collective-permute-start(bf16[512,1024]{1,0:T(8,128)(2,1)S(1)} %get-tuple-element.244), channel_id=1, source_target_pairs={{0,1},{1,0},{2,5},{3,4},{4,3},{5,2},{6,7},{7,6},{8,9},{9,8},{10,13... | collective-permute-start | bytes 3145736 | tf_op jit(solution)/shard_map/ppermute | solution.py:539
  112.7 203.1 %all-gather.9.cloned.1.call-start = ((), (), s32[]{:S(2)}) async-start(), calls=%async_computation.6 | async-start | bytes 18874368 | tf_op jit(solution)/shard_map/all_gather | solution.py:577
  141.5 41.6 %collective-permute-start.8 = (bf16[1024,1024]{1,0:T(8,128)(2,1)}, bf16[1024,1024]{1,0:T(8,128)(2,1)S(1)}, u32[]{:S(2)}, u32[]{:S(2)}) collective-permute-start(bf16[1024,1024]{1,0:T(8,128)(2,1)} %get-tuple-element.80), channel_id=1, source_target_pairs={{0,4},{4,0},{1,5},{5,1},{2,6},{6,2},{3,7},{7,3},{8,12},{12,8},{9,1... | collective-permute-start | bytes 6291464 | tf_op jit(solution)/shard_map/ppermute | solution.py:552
  199.2 407.7 %reduce-scatter.3.cloned.1.call-start = ((), (), s32[]{:S(2)}) async-start(), calls=%async_computation.7 | async-start | bytes 4456448 | tf_op jit(solution)/shard_map/reduce_scatter | solution.py:716
  253.9 33.5 %collective-permute-start.9 = (bf16[1024,512]{1,0:T(8,128)(2,1)}, bf16[1024,512]{1,0:T(8,128)(2,1)}, u32[]{:S(2)}, u32[]{:S(2)}) collective-permute-start(bf16[1024,512]{1,0:T(8,128)(2,1)} %constant_dynamic-slice_fusion.5), channel_id=1, source_target_pairs={{0,4},{4,0},{1,5},{5,1},{2,6},{6,2},{3,7},{7,3},{8,12},{12,8},{9,1... | collective-permute-start | bytes 3145736 | tf_op jit(solution)/shard_map/ppermute | solution.py:558
  255.9 50.2 %collective-permute-start.10 = (bf16[512,1024]{1,0:T(8,128)(2,1)}, bf16[512,1024]{1,0:T(8,128)(2,1)S(1)}, u32[]{:S(2)}, u32[]{:S(2)}) collective-permute-start(bf16[512,1024]{1,0:T(8,128)(2,1)} %get-tuple-element.235), channel_id=1, source_target_pairs={{0,0},{1,1},{2,4},{3,5},{4,2},{5,3},{6,6},{7,7},{8,8},{9,9},{10,12... | collective-permute-start | bytes 3145736 | tf_op jit(solution)/shard_map/ppermute | solution.py:538
  257.8 48.4 %collective-permute-start.11 = (bf16[512,1024]{1,0:T(8,128)(2,1)}, bf16[512,1024]{1,0:T(8,128)(2,1)}, u32[]{:S(2)}, u32[]{:S(2)}) collective-permute-start(bf16[512,1024]{1,0:T(8,128)(2,1)} %get-tuple-element.236), channel_id=1, source_target_pairs={{0,1},{1,0},{2,5},{3,4},{4,3},{5,2},{6,7},{7,6},{8,9},{9,8},{10,13... | collective-permute-start | bytes 3145736 | tf_op jit(solution)/shard_map/ppermute | solution.py:539
  387.3 27.5 %collective-permute-start.12 = (bf16[4,128,4096]{2,1,0:T(8,128)(2,1)}, bf16[4,128,4096]{2,1,0:T(8,128)(2,1)}, u32[]{:S(2)}, u32[]{:S(2)}) collective-permute-start(bf16[4,128,4096]{2,1,0:T(8,128)(2,1)} %get-tuple-element.99), channel_id=1, source_target_pairs={{0,4},{4,0},{1,5},{5,1},{2,6},{6,2},{3,7},{7,3},{8,12},{12,8},{9,1... | collective-permute-start | bytes 12582920 | tf_op jit(solution)/shard_map/ppermute | solution.py:719
  422.3 279.4 %reduce-scatter.5.cloned.1.call-start = ((), (), s32[]{:S(2)}) async-start(), calls=%async_computation.8 | async-start | bytes 3932160 | tf_op jit(solution)/shard_map/reduce_scatter | solution.py:776
  435.2 102.2 %collective-permute-start.19 = (bf16[512,1024]{1,0:T(8,128)(2,1)}, bf16[512,1024]{1,0:T(8,128)(2,1)}, u32[]{:S(2)}, u32[]{:S(2)}) collective-permute-start(bf16[512,1024]{1,0:T(8,128)(2,1)} %get-tuple-element.231), channel_id=1, source_target_pairs={{0,0},{1,1},{4,2},{5,3},{2,4},{3,5},{6,6},{7,7},{8,8},{9,9},{12,10... | collective-permute-start | bytes 3145736 | tf_op jit(solution)/shard_map/ppermute | solution.py:544
  444.6 92.8 %collective-permute-start.20 = (bf16[512,1024]{1,0:T(8,128)(2,1)}, bf16[512,1024]{1,0:T(8,128)(2,1)}, u32[]{:S(2)}, u32[]{:S(2)}) collective-permute-start(bf16[512,1024]{1,0:T(8,128)(2,1)} %get-tuple-element.232), channel_id=1, source_target_pairs={{1,0},{0,1},{5,2},{4,3},{3,4},{2,5},{7,6},{6,7},{9,8},{8,9},{13,10... | collective-permute-start | bytes 3145736 | tf_op jit(solution)/shard_map/ppermute | solution.py:545
  458.3 82.4 %collective-permute-start.16 = (bf16[640,1024]{1,0:T(8,128)(2,1)}, bf16[640,1024]{1,0:T(8,128)(2,1)S(1)}, u32[]{:S(2)}, u32[]{:S(2)}) collective-permute-start(bf16[640,1024]{1,0:T(8,128)(2,1)} %get-tuple-element.209), channel_id=1, source_target_pairs={{0,8},{8,0},{16,24},{24,16},{1,9},{9,1},{17,25},{25,17},{2,10},{10... | collective-permute-start | bytes 3932168 | tf_op jit(solution)/shard_map/ppermute | solution.py:705
  463.7 78.7 %collective-permute-start.17 = (bf16[640,1024]{1,0:T(8,128)(2,1)}, bf16[640,1024]{1,0:T(8,128)(2,1)}, u32[]{:S(2)}, u32[]{:S(2)}) collective-permute-start(bf16[640,1024]{1,0:T(8,128)(2,1)} %get-tuple-element.211), channel_id=1, source_target_pairs={{0,16},{8,24},{16,0},{24,8},{1,17},{9,25},{17,1},{25,9},{2,18},{10... | collective-permute-start | bytes 3932168 | tf_op jit(solution)/shard_map/ppermute | solution.py:705
  463.7 78.7 %collective-permute-start.18 = (bf16[640,1024]{1,0:T(8,128)(2,1)S(1)}, bf16[640,1024]{1,0:T(8,128)(2,1)}, u32[]{:S(2)}, u32[]{:S(2)}) collective-permute-start(bf16[640,1024]{1,0:T(8,128)(2,1)S(1)} %get-tuple-element.210), channel_id=1, source_target_pairs={{0,24},{8,16},{16,8},{24,0},{1,25},{9,17},{17,9},{25,1},{2,26},{10... | collective-permute-start | bytes 3932168 | tf_op jit(solution)/shard_map/ppermute | solution.py:705
  553.7 47.5 %collective-permute-start.21 = (bf16[4,128,1536]{2,1,0:T(8,128)(2,1)S(1)}, bf16[4,128,1536]{2,1,0:T(8,128)(2,1)S(1)}, u32[]{:S(2)}, u32[]{:S(2)}) collective-permute-start(bf16[4,128,1536]{2,1,0:T(8,128)(2,1)S(1)} %get-tuple-element.217), channel_id=1, source_target_pairs={{0,4},{4,0},{1,5},{5,1},{2,6},{6,2},{3,7},{7,3},{8,12},{12,8},{9,1... | collective-permute-start | bytes 4718600 | tf_op jit(solution)/shard_map/ppermute | solution.py:761
  553.9 53.0 %collective-permute-start.23 = (bf16[160,1024]{1,0:T(8,128)(2,1)S(1)}, bf16[160,1024]{1,0:T(8,128)(2,1)S(1)}, u32[]{:S(2)}, u32[]{:S(2)}) collective-permute-start(bf16[160,1024]{1,0:T(8,128)(2,1)S(1)} %get-tuple-element.249), channel_id=1, source_target_pairs={{0,1},{1,0},{2,3},{3,2},{4,5},{5,4},{6,7},{7,6},{8,9},{9,8},{10,11... | collective-permute-start | bytes 983048 | tf_op jit(solution)/shard_map/ppermute | solution.py:705
  633.2 30.7 %collective-permute-start.27 = (bf16[512,1024]{1,0:T(8,128)(2,1)S(1)}, bf16[512,1024]{1,0:T(8,128)(2,1)S(1)}, u32[]{:S(2)}, u32[]{:S(2)}) collective-permute-start(bf16[512,1024]{1,0:T(8,128)(2,1)S(1)} %get-tuple-element.228), channel_id=1, source_target_pairs={{1,0},{0,1},{5,2},{4,3},{3,4},{2,5},{7,6},{6,7},{9,8},{8,9},{13,10... | collective-permute-start | bytes 3145736 | tf_op jit(solution)/shard_map/ppermute | solution.py:545
  (55 other events, 914.0 us)
Sparse Core Ops, SparseCore 0:
  58.0 72.5 all-gather.4
  132.7 54.3 all-gather.6
  199.3 116.4 all-gather.8
  422.4 149.9 reduce-scatter.2
  607.0 46.8 reduce-scatter.4

commit v6 on v5

--- a/solution.py
+++ b/solution.py
@@ -62,17 +62,20 @@
     return centred * inverse, inverse
 
 
-def skip_norm_kernel(x_ref, s_ref, top_ref, bottom_ref, seg_ref, shift_ref, scale_ref, resid_ref, normed_ref):
+def merge_kernel(x_ref, s_ref, top_ref, bottom_ref, resid_ref):
     resid = dot_nn(x_ref[...], flat(top_ref)) + dot_nn(s_ref[...], flat(bottom_ref))
-    resid_ref[...] = resid
-    unit, _ = normalise(resid)
+    resid_ref[...] = resid.astype(bf16)
+
+
+def norm_kernel(resid_ref, seg_ref, shift_ref, scale_ref, normed_ref):
+    unit, _ = normalise(resid_ref[...].astype(f32))
     label = seg_ref[...]
     normed = unit * (1.0 + choose(label, scale_ref)) + choose(label, shift_ref)
     normed_ref[...] = normed.astype(bf16)
 
 
 def out_norm_kernel(mixed_ref, w_ref, resid_in_ref, seg_ref, shift_ref, scale_ref, resid_ref, normed_ref):
-    resid = resid_in_ref[...] + dot_nn(mixed_ref[...], flat(w_ref))
+    resid = resid_in_ref[...].astype(f32) + dot_nn(mixed_ref[...], flat(w_ref))
     resid_ref[...] = resid
     unit, _ = normalise(resid)
     label = seg_ref[...]
@@ -127,7 +130,7 @@
         dscale_ref[...] = jnp.zeros_like(dscale_ref)
 
     grad = own_ref[...] + other_ref[...].astype(f32)
-    pulled, by_scale = norm_pull(grad, resid_ref[...], choose(seg_ref[...], scale_ref))
+    pulled, by_scale = norm_pull(grad, resid_ref[...].astype(f32), choose(seg_ref[...], scale_ref))
     grad_ref[...] = (mid_ref[...] + pulled).astype(bf16)
     segment_sums(segr_ref[...], grad, dshift_ref)
     segment_sums(segr_ref[...], by_scale, dscale_ref)
@@ -578,10 +581,16 @@
 
     up_rows, down_rows, out_rows = w_up.shape[0], w_down.shape[0], w_out.shape[0]
     skip_rows = w_skip.shape[0]
-    early = jnp.concatenate([w_skip] + [w_qkv[:, i * width : (i + 1) * width] for i in range(3)] + [w_out], axis=0)
-    early_line = share_on_line(early)
     columns = w_up.shape[1] // width
+    middle = jnp.concatenate([w_qkv[:, i * width : (i + 1) * width] for i in range(3)] + [w_out], axis=0)
     late = jnp.concatenate([w_down] + [w_up[:, i * width : (i + 1) * width] for i in range(columns)], axis=0)
+    early = share_on_line(w_skip)
+    early, middle = lax.optimization_barrier((early, middle))
+    early = gather_planes(early)
+    middle = share_on_line(middle)
+    middle, late, time_steps = lax.optimization_barrier((middle, late, time_steps))
+    middle = gather_planes(middle)
+    late = share_on_line(late)
 
     labels_own = segment_ids[:, 0]
     labels_other = lax.ppermute(labels_own, "core", swap)
@@ -619,13 +628,6 @@
     )
     modulation = jnp.moveaxis(block_mod, 0, 1).reshape(labels, 4, width)
 
-    early_line, inputs, skips, modulation, cosine, sine, ranges, mine = lax.optimization_barrier(
-        (early_line, inputs, skips, modulation, cosine, sine, ranges, mine)
-    )
-    early = gather_planes(early_line)
-    x, s = to_rows(inputs), to_rows(skips)
-    late, s = lax.optimization_barrier((late, s))
-    late = lax.all_gather(late, ("hi", "lo"), axis=0, tiled=True)
     in_place = out_rows % 16 == 0
     hidden = w_up.shape[1]
     chunk = hidden // (2 * planes)
@@ -638,32 +640,37 @@
         return taken.reshape(1, count, width), (1, count, width), (0, 0, 0)
 
     skip_top, skip_bottom = (weight(early, 0, skip_rows, i * width, width) for i in range(2))
-    out_weight = weight(early, skip_rows + 3 * out_rows, out_rows, 0, width)
+    out_weight = weight(middle, 3 * out_rows, out_rows, 0, width)
     def own_qkv(gathered):
         parts = []
         for i in range(3):
-            begin = skip_rows + i * out_rows
-            whole = gathered[:, begin : begin + out_rows].reshape(width, width)
+            whole = gathered[:, i * out_rows : (i + 1) * out_rows].reshape(width, width)
             parts.append(lax.dynamic_slice_in_dim(whole, member * heads_wide, heads_wide, 1))
         return jnp.concatenate(parts, axis=1)
 
     mine_column, mine_row = mine[:, None], mine[None, :]
     shift_one, scale_one, shift_two, scale_two = (modulation[:, i] for i in range(4))
 
-    resid_in, normed_one = rowwise(
-        skip_norm_kernel,
+    x, s = (v.reshape(frames, width) for v in (inputs, skips))
+    (resid_in,) = rowwise(
+        merge_kernel, frames, [("", x), ("", s), ("weight", skip_top), ("weight", skip_bottom)], [(width, bf16)], light=True
+    )
+    resid_in = to_rows(resid_in.reshape(inputs.shape))
+    resid_in, late, cotangent, modulation, cosine, sine, ranges = lax.optimization_barrier(
+        (resid_in, late, cotangent, modulation, cosine, sine, ranges)
+    )
+    (normed_one,) = rowwise(
+        norm_kernel,
         frames,
-        [("", x), ("", s), ("weight", skip_top), ("weight", skip_bottom), ("", mine_column),
-         ("whole", shift_one), ("whole", scale_one)],
-        [(width, f32), (width, bf16)],
+        [("", resid_in), ("", mine_column), ("whole", shift_one), ("whole", scale_one)],
+        [(width, bf16)],
         light=True,
     )
     normed_row = frames_to_row(normed_one)
     if in_place:
-        projected = project(normed_row, early, skip_rows, out_rows, heads_wide, member)
+        projected = project(normed_row, middle, 0, out_rows, heads_wide, member)
     else:
-        projected = jnp.dot(normed_row, own_qkv(early), preferred_element_type=f32).astype(bf16)
-    projected, late, cotangent = lax.optimization_barrier((projected, late, cotangent))
+        projected = jnp.dot(normed_row, own_qkv(middle), preferred_element_type=f32).astype(bf16)
     late = gather_planes(late)
     cot = to_rows(cotangent)
     if in_place:
@@ -684,8 +691,8 @@
         [(width, f32), (width, bf16)],
         flops=2 * frames * width * width,
     )
-    early, normed_two = lax.optimization_barrier((early, normed_two))
-    qkv_own = own_qkv(early)
+    middle, normed_two = lax.optimization_barrier((middle, normed_two))
+    qkv_own = own_qkv(middle)
     normed_two, qkv_own = lax.optimization_barrier((normed_two, qkv_own))
     result, grad_normed_two, *up_halves, own_down, other_down = feed_forward_and_back(
         core, normed_two, cot, resid_mid, hidden, chunk, up_weight, down_weight, planes
@@ -709,11 +716,11 @@
         return exchange(value, "plane", plane, planes).astype(bf16)
 
     def exchange_line(value):
-        return exchange(value.reshape(line, -1, value.shape[1]), ("hi", "lo"), place, line)
+        return exchange(value.reshape(line, -1, value.shape[-1]), ("hi", "lo"), place, line)
 
     def scatter(value):
         value = value.reshape(-1, value.shape[-1])
-        return lax.psum_scatter(value, ("plane", "hi", "lo"), scatter_dimension=0, tiled=True)
+        return lax.psum_scatter(value, "plane", scatter_dimension=0, tiled=True)
 
     def add_other(own, other):
         return (own.astype(f32) + lax.ppermute(other, "core", swap).astype(f32)).astype(bf16)
@@ -743,8 +750,13 @@
     grad_proj = attend_backward(
         ranges, queries, keys, projected, mixed_heads, grad_heads, logsum, cosine, sine, seg_column, seg_row
     )
-    grad_proj, grad_down, block_out = lax.optimization_barrier((grad_proj, grad_down, block_out))
-    grad_down = exchange_line(grad_down)
+    grad_proj, grad_up, grad_down, block_out = lax.optimization_barrier((grad_proj, grad_up, grad_down, block_out))
+    grad_down = jnp.concatenate(
+        [grad_up[:, i * width : (i + 1) * width].reshape(line, -1, width) for i in range(columns)]
+        + [grad_down.reshape(line, -1, width)],
+        axis=1,
+    )
+    grad_down = lax.psum_scatter(grad_down.reshape(-1, width), ("hi", "lo"), scatter_dimension=0, tiled=True)
     grad_qkv = lax.dot_general(normed_row, grad_proj, (((0,), (0,)), ((), ())), preferred_element_type=f32)
     grad_qkv = grad_qkv.astype(bf16)
     grad_proj, grad_qkv = lax.optimization_barrier((grad_proj, grad_qkv))
@@ -769,11 +781,11 @@
         home = lax.dynamic_slice_in_dim(grad_proj, core * frames, frames, 0)
         grad_one_other = lax.ppermute(dot_nt(away, qkv_own).astype(bf16), "core", swap)
         grad_one = dot_nt(home, qkv_own)
-    grad_one, grad_qkv, grad_up = lax.optimization_barrier((grad_one, grad_qkv, grad_up))
+    grad_one, grad_qkv = lax.optimization_barrier((grad_one, grad_qkv))
     if group > 2:
         grad_qkv = lax.psum_scatter(grad_qkv, ("plane", "hi"), scatter_dimension=0, tiled=True).astype(f32)
     else:
-        grad_qkv = lax.psum_scatter(grad_qkv, "plane", scatter_dimension=0, tiled=True)
+        grad_qkv = exchange_planes(grad_qkv.reshape(planes, -1, 3 * width))
     grad_in, grad_shift_one, grad_scale_one = rowwise(
         norm_one_back_kernel,
         frames,
@@ -782,23 +794,23 @@
         [(width, bf16)],
         sums=2,
     )
-    grad_in, grad_down = lax.optimization_barrier((grad_in, grad_down))
     grad_in_home = from_rows(grad_in)
+    grad_in_home, grad_qkv, grad_down = lax.optimization_barrier((grad_in_home, grad_qkv, grad_down))
+    if group == 2:
+        grad_qkv = exchange_line(grad_qkv)
+    home = grad_in_home.reshape(frames, width)
     grad_skip_w = jnp.concatenate(
         [
-            lax.dot_general(v, grad_in, (((0,), (0,)), ((), ())), preferred_element_type=f32).astype(bf16)
+            lax.dot_general(v, home, (((0,), (0,)), ((), ())), preferred_element_type=f32).astype(bf16)
             for v in (x, s)
         ],
         axis=0,
     )
     grad_skip_w = exchange_planes(over_cores(grad_skip_w.reshape(planes, 2, -1, width), 1))
-    grad_in_home, grad_qkv = lax.optimization_barrier((grad_in_home, grad_qkv))
-    if group == 2:
-        grad_qkv = exchange_line(grad_qkv)
     grad_inputs, grad_skips = rowwise(
         unmerge_kernel,
         frames,
-        [("", grad_in_home.reshape(frames, width)), ("weight", skip_top), ("weight", skip_bottom)],
+        [("", home), ("weight", skip_top), ("weight", skip_bottom)],
         [(width, bf16), (width, bf16)],
         flops=4 * frames * width * width,
     )
@@ -809,11 +821,11 @@
     grad_mod = jnp.stack([v[:labels] for v in (grad_shift_one, grad_scale_one, grad_shift_two, grad_scale_two)], axis=1)
     grad_mod = jnp.moveaxis(grad_mod.reshape(labels, devices, own_columns), 1, 0)
     grad_mod = lax.all_to_all(grad_mod, ALL_AXES, split_axis=0, concat_axis=0, tiled=True)
-    grad_inputs, grad_mod, grad_up, grad_skip_w = lax.optimization_barrier(
-        (grad_inputs, grad_mod, grad_up, grad_skip_w)
-    )
-    grad_up = grad_up.astype(f32)
-    grad_down, grad_out = grad_down[:down_rows], grad_down[down_rows:]
+    grad_inputs, grad_mod, grad_skip_w = lax.optimization_barrier((grad_inputs, grad_mod, grad_skip_w))
+    taken = columns * up_rows
+    grad_down = grad_down.astype(f32)
+    grad_up = jnp.concatenate([grad_down[i * up_rows : (i + 1) * up_rows] for i in range(columns)], axis=1)
+    grad_down, grad_out = grad_down[taken : taken + down_rows], grad_down[taken + down_rows :]
     grad_mod = jnp.sum(grad_mod.reshape(planes, 2, highs, lows, labels, own_columns), axis=(1, 3))
     grad_mod = lax.dot_general(
         embedded.astype(f32),

time: 743 us -> 681 us (0.917)
  starting transfers between devices: 216 us -> 101 us
  waiting for transfers between devices: 100 us -> 148 us
    ppermute x3 -> x9, waiting for transfers between devices: 2.43 us -> 48.4 us  [share_on_line(): lax.ppermute(value, ('hi', 'lo'), [(i, i ^ flip) for i in range(line)])]
    ppermute x1, starting transfers between devices: 37.6 us -> 0.12 us  [frames_to_row(): other = lax.ppermute(value, 'core', swap)]
    ppermute x3 -> x2, waiting for transfers between devices: 35.7 us -> 2.23 us  [to_rows(): lax.ppermute(lax.dynamic_index_in_dim(value, 1 - odd_place, 0, False), LI...]
    ppermute x15, starting transfers between devices: 76 us -> 45.6 us  [exchange(): lax.ppermute(sent, axes, [(i, i ^ flip) for i in range(count)]).astype(f32)]
    ppermute x3 -> x2, starting transfers between devices: 31.7 us -> 1.57 us  [to_rows(): lax.ppermute(lax.dynamic_index_in_dim(value, 1 - odd_place, 0, False), LI...]
    ppermute x15, waiting for transfers between devices: 21.9 us -> 49.9 us  [exchange(): lax.ppermute(sent, axes, [(i, i ^ flip) for i in range(count)]).astype(f32)]
    all_to_all x1, waiting for transfers between devices: 6.16 us -> 32.1 us  [body(): lax.all_to_all(block_mod.reshape(devices, labels, own_columns), ALL_AXES,...]
    ppermute x2, starting transfers between devices: 18.5 us -> 3.67 us  [from_rows(): lax.ppermute(lax.dynamic_index_in_dim(value, 1 - high % 2, 0, False), LIN...]
  transfers between devices with their start and end apart: 45 -> 49, of which waited for: 14 -> 20; matrix products, arithmetic and copies ran while one was open for 17% -> 16% of each run, Pallas kernels for 25% -> 27%
where the time goes in v6:
time: 681 us; the launch traced here: 669 us
  Pallas kernels  255 us (37%)
  waiting for transfers between devices  148 us (22%)
  starting transfers between devices  101 us (15%)
  other arithmetic  62 us (9%)
  local copies, waits for them, and re-layouts  43.9 us (6%)
  matrix products  34.6 us (5%)
  between operations  15.3 us (2%)
  blocking collectives  8.88 us (1%)
    pallas_call x1, Pallas kernels, attend_backward(): pl.pallas_call(attend_backward_kernel, grid_spec=pltpu.PrefetchScalarGrid...  72.1 us
    pallas_call x1, Pallas kernels, feed_forward_and_back(): pl.pallas_call(feed_kernel, grid_spec=pltpu.PrefetchScalarGridSpec(num_sc...  71.6 us
    pallas_call x6, Pallas kernels, rowwise(): pl.pallas_call(kernel, grid=(frames // tile,), in_specs=in_specs, out_spe...  51.1 us
    ppermute x15, waiting for transfers between devices, exchange(): lax.ppermute(sent, axes, [(i, i ^ flip) for i in range(count)]).astype(f32)  49.9 us
    pallas_call x1, Pallas kernels, attend_forward(): pl.pallas_call(attend_forward_kernel, grid_spec=pltpu.PrefetchScalarGridS...  49.7 us
    ppermute x9, waiting for transfers between devices, share_on_line(): lax.ppermute(value, ('hi', 'lo'), [(i, i ^ flip) for i in range(line)])  48.4 us
    ppermute x15, starting transfers between devices, exchange(): lax.ppermute(sent, axes, [(i, i ^ flip) for i in range(count)]).astype(f32)  45.6 us
    all_to_all x1, waiting for transfers between devices, body(): lax.all_to_all(block_mod.reshape(devices, labels, own_columns), ALL_AXES,...  32.1 us
  transfers between devices with their start and end apart: 49, of which 20 were waited for; matrix products, arithmetic and copies ran while one was open for 16% of the time, Pallas kernels for 27%

profile of v6, /device:TPU:0, one launch (start us, length us, event | category | flops | bytes accessed | tf_op | source)
XLA Modules:
  0.0 669.4 jit_solution(10871056651610858711)
XLA Ops:
  31.4 6.7 %collective-permute-done.7 = bf16[128,1024]{1,0:T(8,128)(2,1)S(1)} collective-permute-done((bf16[128,1024]{1,0:T(8,128)(2,1)S(1)}, bf16[128,1024]{1,0:T(8,128)(2,1)S(1)}, u32[]{:S(2)}, u32[]{:S(2)}) %collective-permute-start.7) | collective-permute-done | bytes 262176 | tf_op jit(solution)/shard_map/ppermute | solution.py:575
  38.1 12.2 %collective-permute-done.6 = bf16[128,1024]{1,0:T(8,128)(2,1)S(1)} collective-permute-done((bf16[128,1024]{1,0:T(8,128)(2,1)S(1)}, bf16[128,1024]{1,0:T(8,128)(2,1)S(1)}, u32[]{:S(2)}, u32[]{:S(2)}) %collective-permute-start.6) | collective-permute-done | bytes 262176 | tf_op jit(solution)/shard_map/ppermute | solution.py:575
  65.7 8.9 %all-gather = s32[16,1,4]{2,1,0:T(1,128)S(1)} all-gather(s32[2,1,4]{2,1,0:T(1,128)S(1)} %copy-done.37), channel_id=2, replica_groups=mesh['plane'=4,'core'=2,'hi'=4,'lo'=1] {'plane','core'}, dimensions={0}, use_global_device_ids=true | all-gather | bytes 288 | tf_op jit(solution)/shard_map/all_gather | solution.py:617
  74.6 8.9 %shard_map.178 = bf16[1024,1024]{1,0:T(8,128)(2,1)} custom-call(bf16[1024,1024]{1,0:T(8,128)(2,1)} %bitcast.242, bf16[1024,1024]{1,0:T(8,128)(2,1)} %bitcast.241, bf16[32,64,1024]{2,1,0:T(8,128)(2,1)} %all-gather.5.cloned.1.call-done.top_ref.bottom_ref, bf16[32,64,1024]{2,1,0:T(8,128)(2,1)} %all-gather.5.cloned.1.call-done.top_ref.bottom_ref), custom_call_target="tpu_custom_call" | custom-call | flops 1 | bytes 1 | tf_op jit(solution)/shard_map/pallas_call | solution.py:191
  95.1 19.4 %collective-permute-done.9 = bf16[256,1024]{1,0:T(8,128)(2,1)} collective-permute-done((bf16[256,1024]{1,0:T(8,128)(2,1)S(1)}, bf16[256,1024]{1,0:T(8,128)(2,1)}, u32[]{:S(2)}, u32[]{:S(2)}) %collective-permute-start.9) | collective-permute-done | bytes 524320 | tf_op jit(solution)/shard_map/ppermute | solution.py:575
  122.9 32.1 %all-to-all-done = f32[32,4,128]{2,1,0:T(4,128)S(1)} async-done(((f32[32,4,128]{2,1,0:T(4,128)}), f32[32,4,128]{2,1,0:T(4,128)S(1)}, u32[]{:S(2)}, u32[]{:S(2)}) %all-to-all-start) | async-done | bytes 65568 | tf_op jit(solution)/shard_map/all_to_all | solution.py:626
  177.0 11.0 %shard_map.180.q_ref.k_ref.v_ref = bf16[2048,1536]{1,0:T(8,128)(2,1)} custom-call(s32[1]{0:T(128)} %bitcast.25.place_ref.core_ref, bf16[2048,1024]{1,0:T(8,128)(2,1)} %pad_maximum_fusion.1.x_ref, bf16[32,128,1024]{2,1,0:T(8,128)(2,1)} %all-gather.7.cloned.1.call-done.w_ref), custom_call_target="tpu_custom_call" | custom-call | flops 1 | bytes 1 | tf_op jit(solution)/shard_map/pallas_call | solution.py:151
  188.0 49.7 %shard_map.181 = (bf16[2048,512]{1,0:T(8,128)(2,1)}, bf16[2048,512]{1,0:T(8,128)(2,1)}, bf16[2048,512]{1,0:T(8,128)(2,1)}, f32[4,2,2048]{2,1,0:T(2,128)}) custom-call(s32[2,8]{1,0:T(2,128)} %pad_add_fusion.range_ref, bf16[2048,1536]{1,0:T(8,128)(2,1)} %shard_map.180.q_ref.k_ref.v_ref, bf16[2048,1536]{1,0:T(8,128)(2,1)} %shard_map.180.q_ref.k_ref.v_ref, ...), custom_call_target="tpu_custom_call" | custom-call | flops 17179869184 | bytes 14680064 | tf_op jit(solution)/shard_map/pallas_call | solution.py:284
  246.8 8.2 %shard_map.182 = (f32[1024,1024]{1,0:T(8,128)}, bf16[1024,1024]{1,0:T(8,128)(2,1)}) custom-call(bf16[1024,1024]{1,0:T(8,128)(2,1)} %pad_maximum_fusion.7.mixed_ref, bf16[32,128,1024]{2,1,0:T(8,128)(2,1)} %all-gather.7.cloned.1.call-done.w_ref, bf16[1024,1024]{1,0:T(8,128)(2,1)} %pad_maximum_fusion.4.resid_ref.resid_in_ref, s32[1024,1]{1,0:T(8,128)} %copy.110.seg_ref, ...), custom_call_target="tpu_custom_call" | custom-call | flops 2147483648 | bytes 18911232 | tf_op jit(solution)/shard_map/pallas_call | solution.py:191
  261.3 71.6 %shard_map.183 = (bf16[1024,1024]{1,0:T(8,128)(2,1)}, f32[1024,1024]{1,0:T(8,128)}, bf16[4,128,4096]{2,1,0:T(8,128)(2,1)}, bf16[4,128,4096]{2,1,0:T(8,128)(2,1)}...) custom-call(s32[1]{0:T(128)} %bitcast.25.place_ref.core_ref, bf16[1024,1024]{1,0:T(8,128)(2,1)} %get-tuple-element.82.n_ref, ...), custom_call_target="tpu_custom_call" | custom-call | flops 51539607552 | bytes 50331648 | tf_op jit(solution)/shard_map/pallas_call | solution.py:487
  334.1 10.9 %shard_map.184 = (f32[1024,1024]{1,0:T(8,128)}, bf16[1024,1024]{1,0:T(8,128)(2,1)}, bf16[1024,1024]{1,0:T(8,128)(2,1)}, f32[8,1024]{1,0:T(8,128)}, f32[8,1024]{1,0:T(8,128)}) custom-call(f32[1024,1024]{1,0:T(8,128)} %get-tuple-element.86.g_ref, f32[1024,1024]{1,0:T(8,128)} %get-tuple-element.84.resid_ref, bf16[1024,1024]{1,0:T(8,128)(2,1)} %pad_maximum_fusion.8.cot_ref, ...), custom_call_target="tpu_custom_call" | custom-call | flops 1 | bytes 1 | tf_op jit(solution)/shard_map/pallas_call | solution.py:191
  345.0 7.2 %add_convert_fusion.1 = bf16[4,128,4096]{2,1,0:T(8,128)(2,1)} fusion(bf16[4,128,4096]{2,1,0:T(8,128)(2,1)} %collective-permute-done.16, bf16[4,128,4096]{2,1,0:T(8,128)(2,1)} %get-tuple-element.88), kind=kLoop, calls=%fused_computation.1 | loop fusion | flops 8388608 | bytes 12582912 | tf_op jit(solution)/shard_map/convert_element_type | solution.py:726
  388.0 72.1 %shard_map.185 = bf16[2048,1536]{1,0:T(8,128)(2,1)} custom-call(s32[2,8]{1,0:T(2,128)} %pad_add_fusion.range_ref, bf16[2048,512]{1,0:T(8,128)(2,1)} %get-tuple-element.76.q_ref, bf16[2048,512]{1,0:T(8,128)(2,1)} %get-tuple-element.77.k_ref, bf16[2048,1536]{1,0:T(8,128)(2,1)} %shard_map.180.q_ref.k_ref.v_ref, bf16[2048,512]{1,0:T(8,128)(2,1)} %get-tuple-element.78.out_ref, ...), custom_call_target="tpu_custom_call" | custom-call | flops 42949672960 | bytes 16777216 | tf_op jit(solution)/shard_map/pallas_call | solution.py:388
  467.8 9.6 %convolution_convert_fusion = bf16[1024,1536]{1,0:T(8,128)(2,1)S(1)} fusion(bf16[2048,1536]{1,0:T(8,128)(2,1)} %shard_map.185, bf16[1024,1024]{1,0:T(8,128)(2,1)} %copy-done.7, bf16[1024,1024]{1,0:T(8,128)(2,1)S(1)} %copy-done.6), kind=kOutput, calls=%fused_computation.9 | convolution fusion | flops 6452412416 | bytes 13631488 | tf_op jit(solution)/shard_map/dot_general | solution.py:760
  489.7 6.9 %fusion.3.own_ref = f32[1024,1024]{1,0:T(8,128)} fusion(bf16[1024,1536]{1,0:T(8,128)(2,1)S(1)} %copy-done.9, bf16[2048,1536]{1,0:T(8,128)(2,1)} %shard_map.185, s32[]{:T(128)S(6)} %select_n.268), kind=kOutput, calls=%fused_computation.13 | convolution fusion | flops 3221225472 | bytes 10485764 | tf_op jit(solution)/shard_map/dot_general | solution.py:31
  500.1 16.2 %collective-permute-start.29 = (bf16[128,3072]{1,0:T(8,128)(2,1)}, bf16[128,3072]{1,0:T(8,128)(2,1)S(1)}, u32[]{:S(2)}, u32[]{:S(2)}) collective-permute-start(bf16[128,3072]{1,0:T(8,128)(2,1)} %get-tuple-element.202), channel_id=1, source_target_pairs={{0,8},{8,0},{16,24},{24,16},{1,9},{9,1},{17,25},{25,17},{2,10},{10... | collective-permute-start | bytes 2359304 | tf_op jit(solution)/shard_map/ppermute | solution.py:712
  517.8 9.1 %shard_map.186 = (bf16[1024,1024]{1,0:T(8,128)(2,1)}, f32[8,1024]{1,0:T(8,128)}, f32[8,1024]{1,0:T(8,128)}) custom-call(f32[1024,1024]{1,0:T(8,128)} %fusion.3.own_ref, bf16[1024,1024]{1,0:T(8,128)(2,1)} %collective-permute-done.26.other_ref, bf16[1024,1024]{1,0:T(8,128)(2,1)} %pad_maximum_fusion.4.resid_ref.resid_in_ref, ...), custom_call_target="tpu_custom_call" | custom-call | bytes 14704640 | tf_op jit(solution)/shard_map/pallas_call | solution.py:191
  534.9 16.1 %collective-permute-done.31 = bf16[128,3072]{1,0:T(8,128)(2,1)} collective-permute-done((bf16[128,3072]{1,0:T(8,128)(2,1)}, bf16[128,3072]{1,0:T(8,128)(2,1)}, u32[]{:S(2)}, u32[]{:S(2)}) %collective-permute-start.31) | collective-permute-done | bytes 786464 | tf_op jit(solution)/shard_map/ppermute | solution.py:712
  555.3 9.7 %collective-permute-done.28 = bf16[512,1024]{1,0:T(8,128)(2,1)S(1)} collective-permute-done((bf16[512,1024]{1,0:T(8,128)(2,1)S(1)}, bf16[512,1024]{1,0:T(8,128)(2,1)S(1)}, u32[]{:S(2)}, u32[]{:S(2)}) %collective-permute-start.28) | collective-permute-done | bytes 1048608 | tf_op jit(solution)/shard_map/ppermute | solution.py:548
  577.2 13.3 %collective-permute-start.32 = (bf16[4,256,1024]{2,1,0:T(8,128)(2,1)}, bf16[4,256,1024]{2,1,0:T(8,128)(2,1)S(1)}, u32[]{:S(2)}, u32[]{:S(2)}) collective-permute-start(bf16[4,256,1024]{2,1,0:T(8,128)(2,1)} %dynamic-slice_bitcast_fusion), channel_id=1, source_target_pairs={{0,4},{4,0},{1,5},{5,1},{2,6},{6,2},{3,7},{7,3},{8,12},{12,8},{9,1... | collective-permute-start | bytes 6291464 | tf_op jit(solution)/shard_map/ppermute | solution.py:702
  592.2 10.4 %collective-permute-start.39 = (bf16[32,3072]{1,0:T(8,128)(2,1)}, bf16[32,3072]{1,0:T(8,128)(2,1)}, u32[]{:S(2)}, u32[]{:S(2)}) collective-permute-start(bf16[32,3072]{1,0:T(8,128)(2,1)} %get-tuple-element.244), channel_id=1, source_target_pairs={{0,1},{1,0},{2,3},{3,2},{4,5},{5,4},{6,7},{7,6},{8,9},{9,8},{10,11... | collective-permute-start | bytes 589832 | tf_op jit(solution)/shard_map/ppermute | solution.py:712
  605.0 8.4 %shard_map.187 = (bf16[1024,1024]{1,0:T(8,128)(2,1)}, bf16[1024,1024]{1,0:T(8,128)(2,1)}) custom-call(bf16[1024,1024]{1,0:T(8,128)(2,1)} %bitcast.248, bf16[32,64,1024]{2,1,0:T(8,128)(2,1)} %all-gather.5.cloned.1.call-done.top_ref.bottom_ref, bf16[32,64,1024]{2,1,0:T(8,128)(2,1)} %all-gather.5.cloned.1.call-done.top_ref.bottom_ref), custom_call_target="tpu_custom_call" | custom-call | flops 4294967296 | bytes 14680064 | tf_op jit(solution)/shard_map/pallas_call | solution.py:191
  623.6 8.2 %collective-permute-done.33 = bf16[256,1024]{1,0:T(8,128)(2,1)S(1)} collective-permute-done((bf16[256,1024]{1,0:T(8,128)(2,1)S(1)}, bf16[256,1024]{1,0:T(8,128)(2,1)S(1)}, u32[]{:S(2)}, u32[]{:S(2)}) %collective-permute-start.33) | collective-permute-done | bytes 524320 | tf_op jit(solution)/shard_map/ppermute | solution.py:712
  631.8 11.2 %collective-permute-done.35 = bf16[256,1024]{1,0:T(8,128)(2,1)S(1)} collective-permute-done((bf16[256,1024]{1,0:T(8,128)(2,1)S(1)}, bf16[256,1024]{1,0:T(8,128)(2,1)S(1)}, u32[]{:S(2)}, u32[]{:S(2)}) %collective-permute-start.35) | collective-permute-done | bytes 524320 | tf_op jit(solution)/shard_map/ppermute | solution.py:712
  (288 shorter events, 216.0 us)
Async XLA Ops:
  7.2 67.4 %all-gather.5.cloned.1.call-start = ((), (), s32[]{:S(2)}) async-start(), calls=%async_computation.4 | async-start | bytes 4718592 | tf_op jit(solution)/shard_map/all_gather | solution.py:580
  26.8 150.2 %all-gather.7.cloned.1.call-start = ((), (), s32[]{:S(2)}) async-start(), calls=%async_computation.5 | async-start | bytes 9437184 | tf_op jit(solution)/shard_map/all_gather | solution.py:580
  61.3 33.8 %collective-permute-start.10 = (bf16[256,1024]{1,0:T(8,128)(2,1)S(1)}, bf16[256,1024]{1,0:T(8,128)(2,1)S(1)}, u32[]{:S(2)}, u32[]{:S(2)}) collective-permute-start(bf16[256,1024]{1,0:T(8,128)(2,1)S(1)} %copy-done.22), channel_id=1, source_target_pairs={{0,3},{1,2},{2,1},{3,0},{4,7},{5,6},{6,5},{7,4},{8,11},{9,10},{10,... | collective-permute-start | bytes 1572872 | tf_op jit(solution)/shard_map/ppermute | solution.py:575
  62.7 51.8 %collective-permute-start.9 = (bf16[256,1024]{1,0:T(8,128)(2,1)S(1)}, bf16[256,1024]{1,0:T(8,128)(2,1)}, u32[]{:S(2)}, u32[]{:S(2)}) collective-permute-start(bf16[256,1024]{1,0:T(8,128)(2,1)S(1)} %copy-done.22), channel_id=1, source_target_pairs={{0,2},{1,3},{2,0},{3,1},{4,6},{5,7},{6,4},{7,5},{8,10},{9,11},{10,... | collective-permute-start | bytes 1572872 | tf_op jit(solution)/shard_map/ppermute | solution.py:575
  62.7 51.8 %collective-permute-start.8 = (bf16[256,1024]{1,0:T(8,128)(2,1)S(1)}, bf16[256,1024]{1,0:T(8,128)(2,1)}, u32[]{:S(2)}, u32[]{:S(2)}) collective-permute-start(bf16[256,1024]{1,0:T(8,128)(2,1)S(1)} %copy-done.22), channel_id=1, source_target_pairs={{0,1},{1,0},{2,3},{3,2},{4,5},{5,4},{6,7},{7,6},{8,9},{9,8},{10,11... | collective-permute-start | bytes 1572872 | tf_op jit(solution)/shard_map/ppermute | solution.py:575
  86.1 31.7 %collective-permute-start.3 = (bf16[512,1024]{1,0:T(8,128)(2,1)}, bf16[512,1024]{1,0:T(8,128)(2,1)S(1)}, u32[]{:S(2)}, u32[]{:S(2)}) collective-permute-start(bf16[512,1024]{1,0:T(8,128)(2,1)} %get-tuple-element.234), channel_id=1, source_target_pairs={{0,0},{1,1},{2,4},{3,5},{4,2},{5,3},{6,6},{7,7},{8,8},{9,9},{10,12... | collective-permute-start | bytes 3145736 | tf_op jit(solution)/shard_map/ppermute | solution.py:541
  88.0 32.0 %collective-permute-start.4 = (bf16[512,1024]{1,0:T(8,128)(2,1)S(1)}, bf16[512,1024]{1,0:T(8,128)(2,1)}, u32[]{:S(2)}, u32[]{:S(2)}) collective-permute-start(bf16[512,1024]{1,0:T(8,128)(2,1)S(1)} %get-tuple-element.235), channel_id=1, source_target_pairs={{0,1},{1,0},{2,5},{3,4},{4,3},{5,2},{6,7},{7,6},{8,9},{9,8},{10,13... | collective-permute-start | bytes 3145736 | tf_op jit(solution)/shard_map/ppermute | solution.py:542
  89.9 65.1 %all-to-all-start = ((f32[32,4,128]{2,1,0:T(4,128)}), f32[32,4,128]{2,1,0:T(4,128)S(1)}, u32[]{:S(2)}, u32[]{:S(2)}) async-start(f32[32,4,128]{2,1,0:T(4,128)} %bitcast.18), calls=%async_computation | async-start | bytes 131072 | tf_op jit(solution)/shard_map/all_to_all | solution.py:626
  95.1 166.2 %all-gather.9.cloned.1.call-start = ((), (), s32[]{:S(2)}) async-start(), calls=%async_computation.6 | async-start | bytes 18874368 | tf_op jit(solution)/shard_map/all_gather | solution.py:580
  155.1 312.6 %reduce-scatter.3.cloned.1.call-start = ((), (), s32[]{:S(2)}) async-start(), calls=%async_computation.7 | async-start | bytes 5242880 | tf_op jit(solution)/shard_map/reduce_scatter | solution.py:723
  166.9 75.2 %collective-permute-start.14 = (bf16[512,1024]{1,0:T(8,128)(2,1)}, bf16[512,1024]{1,0:T(8,128)(2,1)S(1)}, u32[]{:S(2)}, u32[]{:S(2)}) collective-permute-start(bf16[512,1024]{1,0:T(8,128)(2,1)} %get-tuple-element.226), channel_id=1, source_target_pairs={{0,0},{1,1},{2,4},{3,5},{4,2},{5,3},{6,6},{7,7},{8,8},{9,9},{10,12... | collective-permute-start | bytes 3145736 | tf_op jit(solution)/shard_map/ppermute | solution.py:541
  169.1 73.0 %collective-permute-start.15 = (bf16[512,1024]{1,0:T(8,128)(2,1)}, bf16[512,1024]{1,0:T(8,128)(2,1)S(1)}, u32[]{:S(2)}, u32[]{:S(2)}) collective-permute-start(bf16[512,1024]{1,0:T(8,128)(2,1)} %get-tuple-element.227), channel_id=1, source_target_pairs={{0,1},{1,0},{2,5},{3,4},{4,3},{5,2},{6,7},{7,6},{8,9},{9,8},{10,13... | collective-permute-start | bytes 3145736 | tf_op jit(solution)/shard_map/ppermute | solution.py:542
  333.1 29.3 %collective-permute-start.18 = (bf16[4,512,1024]{2,1,0:T(8,128)(2,1)}, bf16[4,512,1024]{2,1,0:T(8,128)(2,1)}, u32[]{:S(2)}, u32[]{:S(2)}) collective-permute-start(bf16[4,512,1024]{2,1,0:T(8,128)(2,1)} %get-tuple-element.92), channel_id=1, source_target_pairs={{0,4},{4,0},{1,5},{5,1},{2,6},{6,2},{3,7},{7,3},{8,12},{12,8},{9,1... | collective-permute-start | bytes 12582920 | tf_op jit(solution)/shard_map/ppermute | solution.py:726
  352.2 214.5 %reduce-scatter.5.cloned.1.call-start = ((), (), s32[]{:S(2)}) async-start(), calls=%async_computation.8 | async-start | bytes 2949120 | tf_op jit(solution)/shard_map/reduce_scatter | solution.py:759
  372.3 87.8 %collective-permute-start.23 = (bf16[512,1024]{1,0:T(8,128)(2,1)}, bf16[512,1024]{1,0:T(8,128)(2,1)S(1)}, u32[]{:S(2)}, u32[]{:S(2)}) collective-permute-start(bf16[512,1024]{1,0:T(8,128)(2,1)} %get-tuple-element.222), channel_id=1, source_target_pairs={{0,0},{1,1},{4,2},{5,3},{2,4},{3,5},{6,6},{7,7},{8,8},{9,9},{12,10... | collective-permute-start | bytes 3145736 | tf_op jit(solution)/shard_map/ppermute | solution.py:547
  374.2 85.9 %collective-permute-start.24 = (bf16[512,1024]{1,0:T(8,128)(2,1)S(1)}, bf16[512,1024]{1,0:T(8,128)(2,1)}, u32[]{:S(2)}, u32[]{:S(2)}) collective-permute-start(bf16[512,1024]{1,0:T(8,128)(2,1)S(1)} %get-tuple-element.223), channel_id=1, source_target_pairs={{1,0},{0,1},{5,2},{4,3},{3,4},{2,5},{7,6},{6,7},{9,8},{8,9},{13,10... | collective-permute-start | bytes 3145736 | tf_op jit(solution)/shard_map/ppermute | solution.py:548
  379.8 83.2 %collective-permute-start.20 = (bf16[640,1024]{1,0:T(8,128)(2,1)}, bf16[640,1024]{1,0:T(8,128)(2,1)S(1)}, u32[]{:S(2)}, u32[]{:S(2)}) collective-permute-start(bf16[640,1024]{1,0:T(8,128)(2,1)} %get-tuple-element.197), channel_id=1, source_target_pairs={{0,8},{8,0},{16,24},{24,16},{1,9},{9,1},{17,25},{25,17},{2,10},{10... | collective-permute-start | bytes 3932168 | tf_op jit(solution)/shard_map/ppermute | solution.py:712
  386.5 76.5 %collective-permute-start.22 = (bf16[640,1024]{1,0:T(8,128)(2,1)}, bf16[640,1024]{1,0:T(8,128)(2,1)}, u32[]{:S(2)}, u32[]{:S(2)}) collective-permute-start(bf16[640,1024]{1,0:T(8,128)(2,1)} %get-tuple-element.198), channel_id=1, source_target_pairs={{0,24},{8,16},{16,8},{24,0},{1,25},{9,17},{17,9},{25,1},{2,26},{10... | collective-permute-start | bytes 3932168 | tf_op jit(solution)/shard_map/ppermute | solution.py:712
  386.5 77.5 %collective-permute-start.21 = (bf16[640,1024]{1,0:T(8,128)(2,1)}, bf16[640,1024]{1,0:T(8,128)(2,1)}, u32[]{:S(2)}, u32[]{:S(2)}) collective-permute-start(bf16[640,1024]{1,0:T(8,128)(2,1)} %get-tuple-element.199), channel_id=1, source_target_pairs={{0,16},{8,24},{16,0},{24,8},{1,17},{9,25},{17,1},{25,9},{2,18},{10... | collective-permute-start | bytes 3932168 | tf_op jit(solution)/shard_map/ppermute | solution.py:712
  500.1 34.8 %collective-permute-start.29 = (bf16[128,3072]{1,0:T(8,128)(2,1)}, bf16[128,3072]{1,0:T(8,128)(2,1)S(1)}, u32[]{:S(2)}, u32[]{:S(2)}) collective-permute-start(bf16[128,3072]{1,0:T(8,128)(2,1)} %get-tuple-element.202), channel_id=1, source_target_pairs={{0,8},{8,0},{16,24},{24,16},{1,9},{9,1},{17,25},{25,17},{2,10},{10... | collective-permute-start | bytes 2359304 | tf_op jit(solution)/shard_map/ppermute | solution.py:712
  516.3 34.7 %collective-permute-start.31 = (bf16[128,3072]{1,0:T(8,128)(2,1)}, bf16[128,3072]{1,0:T(8,128)(2,1)}, u32[]{:S(2)}, u32[]{:S(2)}) collective-permute-start(bf16[128,3072]{1,0:T(8,128)(2,1)} %get-tuple-element.203), channel_id=1, source_target_pairs={{0,24},{8,16},{16,8},{24,0},{1,25},{9,17},{17,9},{25,1},{2,26},{10... | collective-permute-start | bytes 2359304 | tf_op jit(solution)/shard_map/ppermute | solution.py:712
  516.3 36.9 %collective-permute-start.30 = (bf16[128,3072]{1,0:T(8,128)(2,1)}, bf16[128,3072]{1,0:T(8,128)(2,1)}, u32[]{:S(2)}, u32[]{:S(2)}) collective-permute-start(bf16[128,3072]{1,0:T(8,128)(2,1)} %get-tuple-element.204), channel_id=1, source_target_pairs={{0,16},{8,24},{16,0},{24,8},{1,17},{9,25},{17,1},{25,9},{2,18},{10... | collective-permute-start | bytes 2359304 | tf_op jit(solution)/shard_map/ppermute | solution.py:712
  529.6 35.4 %collective-permute-start.28 = (bf16[512,1024]{1,0:T(8,128)(2,1)S(1)}, bf16[512,1024]{1,0:T(8,128)(2,1)S(1)}, u32[]{:S(2)}, u32[]{:S(2)}) collective-permute-start(bf16[512,1024]{1,0:T(8,128)(2,1)S(1)} %get-tuple-element.219), channel_id=1, source_target_pairs={{1,0},{0,1},{5,2},{4,3},{3,4},{2,5},{7,6},{6,7},{9,8},{8,9},{13,10... | collective-permute-start | bytes 3145736 | tf_op jit(solution)/shard_map/ppermute | solution.py:548
  577.2 37.0 %collective-permute-start.32 = (bf16[4,256,1024]{2,1,0:T(8,128)(2,1)}, bf16[4,256,1024]{2,1,0:T(8,128)(2,1)S(1)}, u32[]{:S(2)}, u32[]{:S(2)}) collective-permute-start(bf16[4,256,1024]{2,1,0:T(8,128)(2,1)} %dynamic-slice_bitcast_fusion), channel_id=1, source_target_pairs={{0,4},{4,0},{1,5},{5,1},{2,6},{6,2},{3,7},{7,3},{8,12},{12,8},{9,1... | collective-permute-start | bytes 6291464 | tf_op jit(solution)/shard_map/ppermute | solution.py:702
  (63 other events, 875.5 us)
Sparse Core Ops, SparseCore 0:
  26.9 36.9 all-gather.4
  66.4 54.8 all-gather.6
  155.3 90.4 all-gather.8
  352.3 76.0 reduce-scatter.2
  483.4 70.2 reduce-scatter.4

commit v7 on v6

--- a/solution.py
+++ b/solution.py
@@ -163,6 +163,38 @@
         compiler_params=params("arbitrary", "arbitrary"),
         cost_estimate=cost(1, 1),
     )(member.reshape(1), value, gathered)
+
+
+def pull_project_kernel(place_ref, dq_ref, dk_ref, dv_ref, q_ref, k_ref, v_ref, out_ref):
+    total = dot_nt(dq_ref[...], flat(q_ref))
+    total += dot_nt(dk_ref[...], flat(k_ref))
+    total += dot_nt(dv_ref[...], flat(v_ref))
+    out_ref[...] = total.astype(out_ref.dtype)
+
+
+def pull_project(grad_proj, gathered, rows, heads_wide, member, frames, half, kind):
+    width = gathered.shape[2]
+    tile = min(2 * ROW_TILE, frames)
+    steps = frames // tile
+    grads = [
+        pl.BlockSpec((tile, heads_wide), functools.partial(lambda t, i, r: (r[1] * steps + i, t), t)) for t in range(3)
+    ]
+    weights = [
+        pl.BlockSpec((width // rows, rows, heads_wide), functools.partial(lambda t, i, r: (0, t, r[0]), t))
+        for t in range(3)
+    ]
+    return pl.pallas_call(
+        pull_project_kernel,
+        grid_spec=pltpu.PrefetchScalarGridSpec(
+            num_scalar_prefetch=1,
+            grid=(steps,),
+            in_specs=grads + weights,
+            out_specs=pl.BlockSpec((tile, width), lambda i, r: (i, 0)),
+        ),
+        out_shape=jax.ShapeDtypeStruct((frames, width), kind),
+        compiler_params=params("arbitrary"),
+        cost_estimate=cost(6 * frames * width * heads_wide, 8 * frames * width),
+    )(jnp.stack([member, half]).astype(jnp.int32), *[grad_proj] * 3, *[gathered] * 3)
 
 
 def rowwise(kernel, frames, blocked, outs, sums=0, flops=0, light=False):
@@ -420,14 +452,12 @@
 
 def feed_kernel(
     core_ref, n_ref, cot_ref, resid_ref, up_ref, down_ref, out_ref, back_ref,
-    gup_own_ref, gup_other_ref, gdown_own_ref, gdown_other_ref, total, n_turned, act_turned, pre,
+    gup_ref, gdown_own_ref, gdown_other_ref, total, n_turned, act_turned, pre,
 ):
     step, last = pl.program_id(0), pl.num_programs(0) - 1
     core = core_ref[0]
     frames, width = n_ref.shape
     tile = min(FEED_TILE, frames)
-    planes = gup_own_ref.shape[0]
-    part = width // planes
 
     def rows_of(i):
         return pl.ds(pl.multiple_of(i * tile, tile), tile)
@@ -460,12 +490,8 @@
     lax.fori_loop(0, frames // tile, chunk, 0)
 
     for begin in range(0, width, FEED_PART):
-        grad_up = dot_nn(n_turned[begin : begin + FEED_PART, :], pre[...]).astype(bf16)
-        for first in range(begin, begin + FEED_PART, part // 2):
-            which, half = first // part, first % part // (part // 2)
-            kept = grad_up[first - begin : first - begin + part // 2]
-            pl.when(core == half)(functools.partial(gup_own_ref.__setitem__, which, kept))
-            pl.when(core != half)(functools.partial(gup_other_ref.__setitem__, which, kept))
+        rows = slice(begin, begin + FEED_PART)
+        gup_ref[rows, :] = dot_nn(n_turned[rows, :], pre[...]).astype(bf16)
     piece = act_turned.shape[0]
     for begin in range(0, piece, FEED_PART):
         rows = slice(begin, begin + FEED_PART)
@@ -482,7 +508,7 @@
     frames, width = normed.shape
     whole = lambda: pl.BlockSpec((frames, width), lambda j, r: (0, 0), pipeline_mode=pl.Buffered(1))
     weight = lambda w: pl.BlockSpec(w[1], lambda j, r: w[2](j))
-    up_block = pl.BlockSpec((planes, width // (2 * planes), piece), lambda j, r: (0, 0, j))
+    up_block = pl.BlockSpec((width, piece), lambda j, r: (0, j))
     down_block = pl.BlockSpec((1, piece, width), lambda j, r: (j // 2, 0, 0))
     return pl.pallas_call(
         feed_kernel,
@@ -490,7 +516,7 @@
             num_scalar_prefetch=1,
             grid=(hidden // piece,),
             in_specs=[whole(), whole(), whole(), weight(w_up), weight(w_down)],
-            out_specs=[pl.BlockSpec((frames, width), lambda j, r: (0, 0))] * 2 + [up_block] * 2 + [down_block] * 2,
+            out_specs=[pl.BlockSpec((frames, width), lambda j, r: (0, 0))] * 2 + [up_block] + [down_block] * 2,
             scratch_shapes=[
                 pltpu.VMEM((frames, width), f32),
                 pltpu.VMEM((width, frames), bf16),
@@ -499,7 +525,7 @@
             ],
         ),
         out_shape=[jax.ShapeDtypeStruct((frames, width), bf16), jax.ShapeDtypeStruct((frames, width), f32)]
-        + [jax.ShapeDtypeStruct((planes, width // (2 * planes), hidden), bf16)] * 2
+        + [jax.ShapeDtypeStruct((width, hidden), bf16)]
         + [jax.ShapeDtypeStruct((planes, piece, width), bf16)] * 2,
         compiler_params=params("arbitrary"),
         cost_estimate=cost(12 * frames * width * hidden, 8 * width * hidden + 16 * frames * width, frames * hidden),
@@ -585,12 +611,10 @@
     middle = jnp.concatenate([w_qkv[:, i * width : (i + 1) * width] for i in range(3)] + [w_out], axis=0)
     late = jnp.concatenate([w_down] + [w_up[:, i * width : (i + 1) * width] for i in range(columns)], axis=0)
     early = share_on_line(w_skip)
-    early, middle = lax.optimization_barrier((early, middle))
+    early, middle, late = lax.optimization_barrier((early, middle, late))
     early = gather_planes(early)
-    middle = share_on_line(middle)
-    middle, late, time_steps = lax.optimization_barrier((middle, late, time_steps))
+    middle, late = share_on_line(middle), share_on_line(late)
     middle = gather_planes(middle)
-    late = share_on_line(late)
 
     labels_own = segment_ids[:, 0]
     labels_other = lax.ppermute(labels_own, "core", swap)
@@ -691,10 +715,7 @@
         [(width, f32), (width, bf16)],
         flops=2 * frames * width * width,
     )
-    middle, normed_two = lax.optimization_barrier((middle, normed_two))
-    qkv_own = own_qkv(middle)
-    normed_two, qkv_own = lax.optimization_barrier((normed_two, qkv_own))
-    result, grad_normed_two, *up_halves, own_down, other_down = feed_forward_and_back(
+    result, grad_normed_two, grad_up, own_down, other_down = feed_forward_and_back(
         core, normed_two, cot, resid_mid, hidden, chunk, up_weight, down_weight, planes
     )
 
@@ -718,14 +739,11 @@
     def exchange_line(value):
         return exchange(value.reshape(line, -1, value.shape[-1]), ("hi", "lo"), place, line)
 
-    def scatter(value):
-        value = value.reshape(-1, value.shape[-1])
-        return lax.psum_scatter(value, "plane", scatter_dimension=0, tiled=True)
-
     def add_other(own, other):
         return (own.astype(f32) + lax.ppermute(other, "core", swap).astype(f32)).astype(bf16)
 
-    grad_up, grad_down = add_other(*up_halves), add_other(own_down, other_down)
+    grad_up = lax.psum_scatter(grad_up, ("plane", "core"), scatter_dimension=0, tiled=True)
+    grad_down = add_other(own_down, other_down)
 
     grad_mid, grad_mid_low, grad_frames, grad_shift_two, grad_scale_two = rowwise(
         norm_two_back_kernel,
@@ -736,8 +754,6 @@
         sums=2,
         light=True,
     )
-    grad_frames, grad_up = lax.optimization_barrier((grad_frames, grad_up))
-    grad_up = scatter(grad_up)
     grad_heads = frames_to_heads(grad_frames)
     grad_out = lax.dot_general(mixed, grad_mid_low, (((0,), (0,)), ((), ())), preferred_element_type=f32)
     grad_out = over_cores(grad_out.astype(bf16).reshape(planes, 2, -1, width), 1)
@@ -765,7 +781,7 @@
         grad_qkv = jnp.moveaxis(grad_qkv, (1, 3), (0, 1)).reshape(group, -1, 3, 1, heads_wide)
         grad_qkv = lax.all_to_all(grad_qkv, ROW_AXES, split_axis=0, concat_axis=3, tiled=True)
         grad_qkv = grad_qkv.reshape(-1, 3 * width)
-        partial = dot_nt(grad_proj, qkv_own).astype(bf16)
+        partial = dot_nt(grad_proj, own_qkv(middle)).astype(bf16)
         grad_one = lax.psum_scatter(partial, ROW_AXES, scatter_dimension=0, tiled=True).astype(f32)
         grad_one_other = jnp.zeros((frames, width), bf16)
     else:
@@ -777,15 +793,23 @@
         grad_qkv = jnp.concatenate(
             [v[:, i * heads_wide : (i + 1) * heads_wide] for i in range(3) for v in (left, right)], axis=1
         )
-        away = lax.dynamic_slice_in_dim(grad_proj, (1 - core) * frames, frames, 0)
-        home = lax.dynamic_slice_in_dim(grad_proj, core * frames, frames, 0)
-        grad_one_other = lax.ppermute(dot_nt(away, qkv_own).astype(bf16), "core", swap)
-        grad_one = dot_nt(home, qkv_own)
+        if in_place:
+            pull = functools.partial(pull_project, grad_proj, middle, out_rows, heads_wide, member, frames)
+            away, home = pull(1 - core, bf16), pull(core, f32)
+        else:
+            qkv_own = own_qkv(middle)
+            away = lax.dynamic_slice_in_dim(grad_proj, (1 - core) * frames, frames, 0)
+            home = lax.dynamic_slice_in_dim(grad_proj, core * frames, frames, 0)
+            away, home = dot_nt(away, qkv_own).astype(bf16), dot_nt(home, qkv_own)
+        grad_one_other = lax.ppermute(away, "core", swap)
+        grad_one = home
     grad_one, grad_qkv = lax.optimization_barrier((grad_one, grad_qkv))
     if group > 2:
         grad_qkv = lax.psum_scatter(grad_qkv, ("plane", "hi"), scatter_dimension=0, tiled=True).astype(f32)
     else:
-        grad_qkv = exchange_planes(grad_qkv.reshape(planes, -1, 3 * width))
+        grad_qkv = grad_qkv.reshape(planes, -1, 3 * width)
+        grad_qkv = lax.all_to_all(grad_qkv, "plane", split_axis=0, concat_axis=0, tiled=True)
+        grad_qkv = jnp.sum(grad_qkv.astype(f32), axis=0).astype(bf16)
     grad_in, grad_shift_one, grad_scale_one = rowwise(
         norm_one_back_kernel,
         frames,
@@ -797,7 +821,9 @@
     grad_in_home = from_rows(grad_in)
     grad_in_home, grad_qkv, grad_down = lax.optimization_barrier((grad_in_home, grad_qkv, grad_down))
     if group == 2:
-        grad_qkv = exchange_line(grad_qkv)
+        grad_qkv = grad_qkv.reshape(line, -1, 3 * width)
+        grad_qkv = lax.all_to_all(grad_qkv, ("hi", "lo"), split_axis=0, concat_axis=0, tiled=True)
+        grad_qkv = jnp.sum(grad_qkv.astype(f32), axis=0)
     home = grad_in_home.reshape(frames, width)
     grad_skip_w = jnp.concatenate(
         [

time: 681 us -> 679 us (level)
  Pallas kernels: 255 us -> 292 us
  waiting for transfers between devices: 148 us -> 122 us
  matrix products: 34.6 us -> 20.3 us
  other arithmetic: 62 us -> 54.3 us
  starting transfers between devices: 101 us -> 108 us
    ppermute x15 -> x9, starting transfers between devices: 45.6 us -> 11.1 us  [exchange(): lax.ppermute(sent, axes, [(i, i ^ flip) for i in range(count)]).astype(f32)]
    all_to_all x1, waiting for transfers between devices: 32.1 us -> 0.01 us  [body(): lax.all_to_all(block_mod.reshape(devices, labels, own_columns), ALL_AXES,...]
    ppermute x15 -> x9, waiting for transfers between devices: 49.9 us -> 18.7 us  [exchange(): lax.ppermute(sent, axes, [(i, i ^ flip) for i in range(count)]).astype(f32)]
    ppermute x2, waiting for transfers between devices: 9.71 us -> 40.4 us  [from_rows(): lax.ppermute(lax.dynamic_index_in_dim(value, 1 - high % 2, 0, False), LIN...]
    ppermute x1, starting transfers between devices: 0.12 us -> 20.1 us  [frames_to_row(): other = lax.ppermute(value, 'core', swap)]
    pallas_call x0 -> x2, Pallas kernels: none -> 15.9 us  [pull_project(): pl.pallas_call(pull_project_kernel, grid_spec=pltpu.PrefetchScalarGridSpe...]
    pallas_call x1, Pallas kernels: 72.1 us -> 88 us  [attend_backward(): pl.pallas_call(attend_backward_kernel, grid_spec=pltpu.PrefetchScalarGrid...]
    all_to_all x0 -> x2, starting transfers between devices: none -> 15.7 us  [the longest x1 12 us: body(): lax.all_to_all(grad_qkv, ('hi', 'lo'), split_axis=0, concat_axis=0, tiled...]
  transfers between devices with their start and end apart: 49 -> 44, of which waited for: 20 -> 14; matrix products, arithmetic and copies ran while one was open for 16% -> 13% of each run, Pallas kernels for 27% -> 33%
where the time goes in v7:
time: 679 us; the launch traced here: 670 us
  Pallas kernels  292 us (43%)
  waiting for transfers between devices  122 us (18%)
  starting transfers between devices  108 us (16%)
  other arithmetic  54.3 us (8%)
  local copies, waits for them, and re-layouts  50.1 us (7%)
  matrix products  20.3 us (3%)
  between operations  15.1 us (2%)
  blocking collectives  8.92 us (1%)
    pallas_call x1, Pallas kernels, attend_backward(): pl.pallas_call(attend_backward_kernel, grid_spec=pltpu.PrefetchScalarGrid...  88 us
    pallas_call x1, Pallas kernels, feed_forward_and_back(): pl.pallas_call(feed_kernel, grid_spec=pltpu.PrefetchScalarGridSpec(num_sc...  67.7 us
    ppermute x9, waiting for transfers between devices, share_on_line(): lax.ppermute(value, ('hi', 'lo'), [(i, i ^ flip) for i in range(line)])  58.9 us
    pallas_call x1, Pallas kernels, attend_forward(): pl.pallas_call(attend_forward_kernel, grid_spec=pltpu.PrefetchScalarGridS...  58 us
    pallas_call x6, Pallas kernels, rowwise(): pl.pallas_call(kernel, grid=(frames // tile,), in_specs=in_specs, out_spe...  51 us
    ppermute x2, waiting for transfers between devices, from_rows(): lax.ppermute(lax.dynamic_index_in_dim(value, 1 - high % 2, 0, False), LIN...  40.4 us
    ppermute x1, starting transfers between devices, frames_to_row(): other = lax.ppermute(value, 'core', swap)  20.1 us
    ppermute x9, waiting for transfers between devices, exchange(): lax.ppermute(sent, axes, [(i, i ^ flip) for i in range(count)]).astype(f32)  18.7 us
  transfers between devices with their start and end apart: 44, of which 14 were waited for; matrix products, arithmetic and copies ran while one was open for 13% of the time, Pallas kernels for 33%

profile of v7, /device:TPU:0, one launch (start us, length us, event | category | flops | bytes accessed | tf_op | source)
XLA Modules:
  0.0 670.3 jit_solution(2779339162814839989)
XLA Ops:
  30.3 6.8 %collective-permute-done.12 = bf16[128,1024]{1,0:T(8,128)(2,1)S(1)} collective-permute-done((bf16[128,1024]{1,0:T(8,128)(2,1)S(1)}, bf16[128,1024]{1,0:T(8,128)(2,1)S(1)}, u32[]{:S(2)}, u32[]{:S(2)}) %collective-permute-start.12) | collective-permute-done | bytes 262176 | tf_op jit(solution)/shard_map/ppermute | solution.py:601
  37.1 12.2 %collective-permute-done.11 = bf16[128,1024]{1,0:T(8,128)(2,1)S(1)} collective-permute-done((bf16[128,1024]{1,0:T(8,128)(2,1)S(1)}, bf16[128,1024]{1,0:T(8,128)(2,1)S(1)}, u32[]{:S(2)}, u32[]{:S(2)}) %collective-permute-start.11) | collective-permute-done | bytes 262176 | tf_op jit(solution)/shard_map/ppermute | solution.py:601
  50.8 8.9 %all-gather = s32[16,1,4]{2,1,0:T(1,128)S(1)} all-gather(s32[2,1,4]{2,1,0:T(1,128)S(1)} %copy-done.32), channel_id=2, replica_groups=mesh['plane'=4,'core'=2,'hi'=4,'lo'=1] {'plane','core'}, dimensions={0}, use_global_device_ids=true | all-gather | bytes 288 | tf_op jit(solution)/shard_map/all_gather | solution.py:641
  75.1 8.6 %shard_map.178 = bf16[1024,1024]{1,0:T(8,128)(2,1)} custom-call(bf16[1024,1024]{1,0:T(8,128)(2,1)} %bitcast.212, bf16[1024,1024]{1,0:T(8,128)(2,1)} %bitcast.211, bf16[32,64,1024]{2,1,0:T(8,128)(2,1)} %all-gather.5.cloned.1.call-done.top_ref.bottom_ref, bf16[32,64,1024]{2,1,0:T(8,128)(2,1)} %all-gather.5.cloned.1.call-done.top_ref.bottom_ref), custom_call_target="tpu_custom_call" | custom-call | flops 1 | bytes 1 | tf_op jit(solution)/shard_map/pallas_call | solution.py:223
  92.2 37.4 %collective-permute-done.6 = bf16[256,1024]{1,0:T(8,128)(2,1)} collective-permute-done((bf16[256,1024]{1,0:T(8,128)(2,1)}, bf16[256,1024]{1,0:T(8,128)(2,1)}, u32[]{:S(2)}, u32[]{:S(2)}) %collective-permute-start.6) | collective-permute-done | bytes 524320 | tf_op jit(solution)/shard_map/ppermute | solution.py:601
  138.0 5.6 shard_map.179
  143.6 20.1 %collective-permute-start.9 = (bf16[1024,1024]{1,0:T(8,128)(2,1)}, bf16[1024,1024]{1,0:T(8,128)(2,1)}, u32[]{:S(2)}, u32[]{:S(2)}) collective-permute-start(bf16[1024,1024]{1,0:T(8,128)(2,1)} %shard_map.179), channel_id=1, source_target_pairs={{0,4},{4,0},{1,5},{5,1},{2,6},{6,2},{3,7},{7,3},{8,12},{12,8},{9,1... | collective-permute-start | bytes 6291464 | tf_op jit(solution)/shard_map/ppermute | solution.py:581
  170.1 12.0 %collective-permute-start.15 = (bf16[512,1024]{1,0:T(8,128)(2,1)}, bf16[512,1024]{1,0:T(8,128)(2,1)S(1)}, u32[]{:S(2)}, u32[]{:S(2)}) collective-permute-start(bf16[512,1024]{1,0:T(8,128)(2,1)} %get-tuple-element.203), channel_id=1, source_target_pairs={{0,1},{1,0},{2,5},{3,4},{4,3},{5,2},{6,7},{7,6},{8,9},{9,8},{10,13... | collective-permute-start | bytes 3145736 | tf_op jit(solution)/shard_map/ppermute | solution.py:568
  188.8 11.0 %shard_map.180.q_ref.k_ref.v_ref = bf16[2048,1536]{1,0:T(8,128)(2,1)} custom-call(s32[1]{0:T(128)} %bitcast.21.place_ref.core_ref, bf16[2048,1024]{1,0:T(8,128)(2,1)} %pad_maximum_fusion.1.x_ref, bf16[32,128,1024]{2,1,0:T(8,128)(2,1)} %all-gather.7.cloned.1.call-done.w_ref.q_ref.k_ref.v_ref), custom_call_target="tpu_custom_call" | custom-call | flops 1 | bytes 1 | tf_op jit(solution)/shard_map/pallas_call | solution.py:151
  199.8 58.0 %shard_map.181 = (bf16[2048,512]{1,0:T(8,128)(2,1)}, bf16[2048,512]{1,0:T(8,128)(2,1)}, bf16[2048,512]{1,0:T(8,128)(2,1)}, f32[4,2,2048]{2,1,0:T(2,128)}) custom-call(s32[2,8]{1,0:T(2,128)} %pad_add_fusion.range_ref, bf16[2048,1536]{1,0:T(8,128)(2,1)} %shard_map.180.q_ref.k_ref.v_ref, bf16[2048,1536]{1,0:T(8,128)(2,1)} %shard_map.180.q_ref.k_ref.v_ref, ...), custom_call_target="tpu_custom_call" | custom-call | flops 17179869184 | bytes 14680064 | tf_op jit(solution)/shard_map/pallas_call | solution.py:316
  266.0 8.2 %shard_map.182 = (f32[1024,1024]{1,0:T(8,128)}, bf16[1024,1024]{1,0:T(8,128)(2,1)}) custom-call(bf16[1024,1024]{1,0:T(8,128)(2,1)} %pad_maximum_fusion.6.mixed_ref, bf16[32,128,1024]{2,1,0:T(8,128)(2,1)} %all-gather.7.cloned.1.call-done.w_ref.q_ref.k_ref.v_ref, bf16[1024,1024]{1,0:T(8,128)(2,1)} %pad_maximum_fusion.3.resid_ref.resid_in_ref, ...), custom_call_target="tpu_custom_call" | custom-call | flops 2147483648 | bytes 18911232 | tf_op jit(solution)/shard_map/pallas_call | solution.py:223
  274.2 67.7 %shard_map.183 = (bf16[1024,1024]{1,0:T(8,128)(2,1)}, f32[1024,1024]{1,0:T(8,128)}, bf16[1024,4096]{1,0:T(8,128)(2,1)}, bf16[4,512,1024]{2,1,0:T(8,128)(2,1)}, bf16[4,512,1024]{2,1,0:T(8,128)(2,1)}) custom-call(s32[1]{0:T(128)} %bitcast.21.place_ref.core_ref, bf16[1024,1024]{1,0:T(8,128)(2,1)} %get-tuple-element.68.n_ref, ...), custom_call_target="tpu_custom_call" | custom-call | flops 51539607552 | bytes 50331648 | tf_op jit(solution)/shard_map/pallas_call | solution.py:513
  342.8 11.2 %shard_map.184 = (f32[1024,1024]{1,0:T(8,128)}, bf16[1024,1024]{1,0:T(8,128)(2,1)}, bf16[1024,1024]{1,0:T(8,128)(2,1)}, f32[8,1024]{1,0:T(8,128)}, f32[8,1024]{1,0:T(8,128)}) custom-call(f32[1024,1024]{1,0:T(8,128)} %get-tuple-element.72.g_ref, f32[1024,1024]{1,0:T(8,128)} %get-tuple-element.70.resid_ref, bf16[1024,1024]{1,0:T(8,128)(2,1)} %pad_maximum_fusion.7.cot_ref, ...), custom_call_target="tpu_custom_call" | custom-call | flops 1 | bytes 1 | tf_op jit(solution)/shard_map/pallas_call | solution.py:223
  382.5 88.0 %shard_map.185.dq_ref.dk_ref.dv_ref = bf16[2048,1536]{1,0:T(8,128)(2,1)} custom-call(s32[2,8]{1,0:T(2,128)} %pad_add_fusion.range_ref, bf16[2048,512]{1,0:T(8,128)(2,1)} %get-tuple-element.65.q_ref, bf16[2048,512]{1,0:T(8,128)(2,1)} %get-tuple-element.66.k_ref, bf16[2048,1536]{1,0:T(8,128)(2,1)} %shard_map.180.q_ref.k_ref.v_ref, ...), custom_call_target="tpu_custom_call" | custom-call | flops 42949672960 | bytes 16777216 | tf_op jit(solution)/shard_map/pallas_call | solution.py:420
  478.2 9.6 %convolution_convert_fusion = bf16[1024,1536]{1,0:T(8,128)(2,1)S(1)} fusion(bf16[2048,1536]{1,0:T(8,128)(2,1)} %shard_map.185.dq_ref.dk_ref.dv_ref, bf16[1024,1024]{1,0:T(8,128)(2,1)} %copy-done.7, bf16[1024,1024]{1,0:T(8,128)(2,1)S(1)} %copy-done.6), kind=kOutput, calls=%fused_computation.8 | convolution fusion | flops 6452412416 | bytes 13631488 | tf_op jit(solution)/shard_map/dot_general | solution.py:776
  491.8 7.8 %shard_map.187 = bf16[1024,1024]{1,0:T(8,128)(2,1)} custom-call(s32[2]{0:T(128)} %pad_add_fusion.2.place_ref, bf16[2048,1536]{1,0:T(8,128)(2,1)} %shard_map.185.dq_ref.dk_ref.dv_ref, bf16[2048,1536]{1,0:T(8,128)(2,1)} %shard_map.185.dq_ref.dk_ref.dv_ref, bf16[2048,1536]{1,0:T(8,128)(2,1)} %shard_map.185.dq_ref.dk_ref.dv_ref, ...), custom_call_target="tpu_custom_call" | custom-call | flops 3221225472 | bytes 8388608 | tf_op jit(solution)/shard_map/pallas_call | solution.py:186
  502.6 8.1 %shard_map.186.own_ref = f32[1024,1024]{1,0:T(8,128)} custom-call(s32[2]{0:T(128)} %pad_add_fusion.1.place_ref, bf16[2048,1536]{1,0:T(8,128)(2,1)} %shard_map.185.dq_ref.dk_ref.dv_ref, bf16[2048,1536]{1,0:T(8,128)(2,1)} %shard_map.185.dq_ref.dk_ref.dv_ref, bf16[2048,1536]{1,0:T(8,128)(2,1)} %shard_map.185.dq_ref.dk_ref.dv_ref, ...), custom_call_target="tpu_custom_call" | custom-call | flops 3221225472 | bytes 8388608 | tf_op jit(solution)/shard_map/pallas_call | solution.py:186
  518.1 9.1 %shard_map.188 = (bf16[1024,1024]{1,0:T(8,128)(2,1)}, f32[8,1024]{1,0:T(8,128)}, f32[8,1024]{1,0:T(8,128)}) custom-call(f32[1024,1024]{1,0:T(8,128)} %shard_map.186.own_ref, bf16[1024,1024]{1,0:T(8,128)(2,1)} %collective-permute-done.25.other_ref, bf16[1024,1024]{1,0:T(8,128)(2,1)} %pad_maximum_fusion.3.resid_ref.resid_in_ref, ...), custom_call_target="tpu_custom_call" | custom-call | bytes 14704640 | tf_op jit(solution)/shard_map/pallas_call | solution.py:223
  530.0 40.4 %collective-permute-done.27 = bf16[512,1024]{1,0:T(8,128)(2,1)S(1)} collective-permute-done((bf16[512,1024]{1,0:T(8,128)(2,1)S(1)}, bf16[512,1024]{1,0:T(8,128)(2,1)S(1)}, u32[]{:S(2)}, u32[]{:S(2)}) %collective-permute-start.27) | collective-permute-done | bytes 1048608 | tf_op jit(solution)/shard_map/ppermute | solution.py:574
  584.1 13.3 %collective-permute-start.28 = (bf16[4,256,1024]{2,1,0:T(8,128)(2,1)}, bf16[4,256,1024]{2,1,0:T(8,128)(2,1)}, u32[]{:S(2)}, u32[]{:S(2)}) collective-permute-start(bf16[4,256,1024]{2,1,0:T(8,128)(2,1)} %dynamic-slice_bitcast_fusion), channel_id=1, source_target_pairs={{0,4},{4,0},{1,5},{5,1},{2,6},{6,2},{3,7},{7,3},{8,12},{12,8},{9,1... | collective-permute-start | bytes 6291464 | tf_op jit(solution)/shard_map/ppermute | solution.py:723
  597.4 12.0 %all-to-all-start.3 = ((bf16[4,32,3072]{2,1,0:T(8,128)(2,1)}), bf16[4,32,3072]{2,1,0:T(8,128)(2,1)S(1)}, u32[]{:S(2)}, u32[]{:S(2)}) async-start(bf16[4,32,3072]{2,1,0:T(8,128)(2,1)} %bitcast.99), calls=%async_computation.5 | async-start | bytes 1572864 | tf_op jit(solution)/shard_map/all_to_all | solution.py:825
  619.6 8.4 %shard_map.189 = (bf16[1024,1024]{1,0:T(8,128)(2,1)}, bf16[1024,1024]{1,0:T(8,128)(2,1)}) custom-call(bf16[1024,1024]{1,0:T(8,128)(2,1)} %bitcast.218, bf16[32,64,1024]{2,1,0:T(8,128)(2,1)} %all-gather.5.cloned.1.call-done.top_ref.bottom_ref, bf16[32,64,1024]{2,1,0:T(8,128)(2,1)} %all-gather.5.cloned.1.call-done.top_ref.bottom_ref), custom_call_target="tpu_custom_call" | custom-call | flops 4294967296 | bytes 14680064 | tf_op jit(solution)/shard_map/pallas_call | solution.py:223
  631.2 11.5 %collective-permute-done.31 = bf16[256,1024]{1,0:T(8,128)(2,1)} collective-permute-done((bf16[256,1024]{1,0:T(8,128)(2,1)}, bf16[256,1024]{1,0:T(8,128)(2,1)}, u32[]{:S(2)}, u32[]{:S(2)}) %collective-permute-start.31) | collective-permute-done | bytes 524320 | tf_op jit(solution)/shard_map/ppermute | solution.py:733
  655.3 5.3 collective-permute-done.33
  (264 shorter events, 173.9 us)
Async XLA Ops:
  7.2 67.9 %all-gather.5.cloned.1.call-start = ((), (), s32[]{:S(2)}) async-start(), calls=%async_computation.6 | async-start | bytes 4718592 | tf_op jit(solution)/shard_map/all_gather | solution.py:606
  25.8 163.0 %all-gather.7.cloned.1.call-start = ((), (), s32[]{:S(2)}) async-start(), calls=%async_computation.7 | async-start | bytes 9437184 | tf_op jit(solution)/shard_map/all_gather | solution.py:606
  61.5 74.6 %all-to-all-start = ((f32[32,4,128]{2,1,0:T(4,128)}), f32[32,4,128]{2,1,0:T(4,128)S(1)}, u32[]{:S(2)}, u32[]{:S(2)}) async-start(f32[32,4,128]{2,1,0:T(4,128)} %bitcast.14), calls=%async_computation | async-start | bytes 131072 | tf_op jit(solution)/shard_map/all_to_all | solution.py:650
  64.7 209.5 %all-gather.9.cloned.1.call-start = ((), (), s32[]{:S(2)}) async-start(), calls=%async_computation.8 | async-start | bytes 18874368 | tf_op jit(solution)/shard_map/all_gather | solution.py:606
  74.3 55.4 %collective-permute-start.6 = (bf16[256,1024]{1,0:T(8,128)(2,1)}, bf16[256,1024]{1,0:T(8,128)(2,1)}, u32[]{:S(2)}, u32[]{:S(2)}) collective-permute-start(bf16[256,1024]{1,0:T(8,128)(2,1)} %slice_dynamic-update-slice_fusion.6), channel_id=1, source_target_pairs={{0,2},{1,3},{2,0},{3,1},{4,6},{5,7},{6,4},{7,5},{8,10},{9,11},{10,... | collective-permute-start | bytes 1572872 | tf_op jit(solution)/shard_map/ppermute | solution.py:601
  74.3 55.4 %collective-permute-start.5 = (bf16[256,1024]{1,0:T(8,128)(2,1)}, bf16[256,1024]{1,0:T(8,128)(2,1)}, u32[]{:S(2)}, u32[]{:S(2)}) collective-permute-start(bf16[256,1024]{1,0:T(8,128)(2,1)} %slice_dynamic-update-slice_fusion.6), channel_id=1, source_target_pairs={{0,1},{1,0},{2,3},{3,2},{4,5},{5,4},{6,7},{7,6},{8,9},{9,8},{10,11... | collective-permute-start | bytes 1572872 | tf_op jit(solution)/shard_map/ppermute | solution.py:601
  86.7 46.6 %collective-permute-start.3 = (bf16[512,1024]{1,0:T(8,128)(2,1)}, bf16[512,1024]{1,0:T(8,128)(2,1)S(1)}, u32[]{:S(2)}, u32[]{:S(2)}) collective-permute-start(bf16[512,1024]{1,0:T(8,128)(2,1)} %get-tuple-element.210), channel_id=1, source_target_pairs={{0,0},{1,1},{2,4},{3,5},{4,2},{5,3},{6,6},{7,7},{8,8},{9,9},{10,12... | collective-permute-start | bytes 3145736 | tf_op jit(solution)/shard_map/ppermute | solution.py:567
  88.5 44.7 %collective-permute-start.4 = (bf16[512,1024]{1,0:T(8,128)(2,1)}, bf16[512,1024]{1,0:T(8,128)(2,1)}, u32[]{:S(2)}, u32[]{:S(2)}) collective-permute-start(bf16[512,1024]{1,0:T(8,128)(2,1)} %get-tuple-element.211), channel_id=1, source_target_pairs={{0,1},{1,0},{2,5},{3,4},{4,3},{5,2},{6,7},{7,6},{8,9},{9,8},{10,13... | collective-permute-start | bytes 3145736 | tf_op jit(solution)/shard_map/ppermute | solution.py:568
  136.2 342.0 %reduce-scatter.3.cloned.1.call-start = ((), (), s32[]{:S(2)}) async-start(), calls=%async_computation.9 | async-start | bytes 9437184 | tf_op jit(solution)/shard_map/reduce_scatter | solution.py:745
  143.6 38.5 %collective-permute-start.9 = (bf16[1024,1024]{1,0:T(8,128)(2,1)}, bf16[1024,1024]{1,0:T(8,128)(2,1)}, u32[]{:S(2)}, u32[]{:S(2)}) collective-permute-start(bf16[1024,1024]{1,0:T(8,128)(2,1)} %shard_map.179), channel_id=1, source_target_pairs={{0,4},{4,0},{1,5},{5,1},{2,6},{6,2},{3,7},{7,3},{8,12},{12,8},{9,1... | collective-permute-start | bytes 6291464 | tf_op jit(solution)/shard_map/ppermute | solution.py:581
  168.0 93.3 %collective-permute-start.14 = (bf16[512,1024]{1,0:T(8,128)(2,1)}, bf16[512,1024]{1,0:T(8,128)(2,1)S(1)}, u32[]{:S(2)}, u32[]{:S(2)}) collective-permute-start(bf16[512,1024]{1,0:T(8,128)(2,1)} %get-tuple-element.202), channel_id=1, source_target_pairs={{0,0},{1,1},{2,4},{3,5},{4,2},{5,3},{6,6},{7,7},{8,8},{9,9},{10,12... | collective-permute-start | bytes 3145736 | tf_op jit(solution)/shard_map/ppermute | solution.py:567
  170.1 91.3 %collective-permute-start.15 = (bf16[512,1024]{1,0:T(8,128)(2,1)}, bf16[512,1024]{1,0:T(8,128)(2,1)S(1)}, u32[]{:S(2)}, u32[]{:S(2)}) collective-permute-start(bf16[512,1024]{1,0:T(8,128)(2,1)} %get-tuple-element.203), channel_id=1, source_target_pairs={{0,1},{1,0},{2,5},{3,4},{4,3},{5,2},{6,7},{7,6},{8,9},{9,8},{10,13... | collective-permute-start | bytes 3145736 | tf_op jit(solution)/shard_map/ppermute | solution.py:568
  341.9 231.9 %reduce-scatter.5.cloned.1.call-start = ((), (), s32[]{:S(2)}) async-start(), calls=%async_computation.10 | async-start | bytes 2949120 | tf_op jit(solution)/shard_map/reduce_scatter | solution.py:775
  342.0 25.4 %collective-permute-start.17 = (bf16[4,512,1024]{2,1,0:T(8,128)(2,1)}, bf16[4,512,1024]{2,1,0:T(8,128)(2,1)}, u32[]{:S(2)}, u32[]{:S(2)}) collective-permute-start(bf16[4,512,1024]{2,1,0:T(8,128)(2,1)} %get-tuple-element.75), channel_id=1, source_target_pairs={{0,4},{4,0},{1,5},{5,1},{2,6},{6,2},{3,7},{7,3},{8,12},{12,8},{9,1... | collective-permute-start | bytes 12582920 | tf_op jit(solution)/shard_map/ppermute | solution.py:743
  375.0 95.5 %collective-permute-start.22 = (bf16[512,1024]{1,0:T(8,128)(2,1)}, bf16[512,1024]{1,0:T(8,128)(2,1)S(1)}, u32[]{:S(2)}, u32[]{:S(2)}) collective-permute-start(bf16[512,1024]{1,0:T(8,128)(2,1)} %get-tuple-element.198), channel_id=1, source_target_pairs={{0,0},{1,1},{4,2},{5,3},{2,4},{3,5},{6,6},{7,7},{8,8},{9,9},{12,10... | collective-permute-start | bytes 3145736 | tf_op jit(solution)/shard_map/ppermute | solution.py:573
  377.0 93.6 %collective-permute-start.23 = (bf16[512,1024]{1,0:T(8,128)(2,1)S(1)}, bf16[512,1024]{1,0:T(8,128)(2,1)}, u32[]{:S(2)}, u32[]{:S(2)}) collective-permute-start(bf16[512,1024]{1,0:T(8,128)(2,1)S(1)} %get-tuple-element.199), channel_id=1, source_target_pairs={{1,0},{0,1},{5,2},{4,3},{3,4},{2,5},{7,6},{6,7},{9,8},{8,9},{13,10... | collective-permute-start | bytes 3145736 | tf_op jit(solution)/shard_map/ppermute | solution.py:574
  379.0 94.4 %collective-permute-start.19 = (bf16[640,1024]{1,0:T(8,128)(2,1)}, bf16[640,1024]{1,0:T(8,128)(2,1)S(1)}, u32[]{:S(2)}, u32[]{:S(2)}) collective-permute-start(bf16[640,1024]{1,0:T(8,128)(2,1)} %get-tuple-element.176), channel_id=1, source_target_pairs={{0,8},{8,0},{16,24},{24,16},{1,9},{9,1},{17,25},{25,17},{2,10},{10... | collective-permute-start | bytes 3932168 | tf_op jit(solution)/shard_map/ppermute | solution.py:733
  379.9 93.5 %collective-permute-start.21 = (bf16[640,1024]{1,0:T(8,128)(2,1)}, bf16[640,1024]{1,0:T(8,128)(2,1)}, u32[]{:S(2)}, u32[]{:S(2)}) collective-permute-start(bf16[640,1024]{1,0:T(8,128)(2,1)} %get-tuple-element.177), channel_id=1, source_target_pairs={{0,24},{8,16},{16,8},{24,0},{1,25},{9,17},{17,9},{25,1},{2,26},{10... | collective-permute-start | bytes 3932168 | tf_op jit(solution)/shard_map/ppermute | solution.py:733
  382.1 92.4 %collective-permute-start.20 = (bf16[640,1024]{1,0:T(8,128)(2,1)}, bf16[640,1024]{1,0:T(8,128)(2,1)}, u32[]{:S(2)}, u32[]{:S(2)}) collective-permute-start(bf16[640,1024]{1,0:T(8,128)(2,1)} %get-tuple-element.178), channel_id=1, source_target_pairs={{0,16},{8,24},{16,0},{24,8},{1,17},{9,25},{17,1},{25,9},{2,18},{10... | collective-permute-start | bytes 3932168 | tf_op jit(solution)/shard_map/ppermute | solution.py:733
  514.3 57.8 %all-to-all-start.1 = ((bf16[4,128,3072]{2,1,0:T(8,128)(2,1)}), bf16[4,128,3072]{2,1,0:T(8,128)(2,1)S(1)}, u32[]{:S(2)}, u32[]{:S(2)}) async-start(bf16[4,128,3072]{2,1,0:T(8,128)(2,1)} %bitcast.206), calls=%async_computation.2 | async-start | bytes 6291456 | tf_op jit(solution)/shard_map/all_to_all | solution.py:811
  529.9 40.5 %collective-permute-start.27 = (bf16[512,1024]{1,0:T(8,128)(2,1)S(1)}, bf16[512,1024]{1,0:T(8,128)(2,1)S(1)}, u32[]{:S(2)}, u32[]{:S(2)}) collective-permute-start(bf16[512,1024]{1,0:T(8,128)(2,1)S(1)} %get-tuple-element.195), channel_id=1, source_target_pairs={{1,0},{0,1},{5,2},{4,3},{3,4},{2,5},{7,6},{6,7},{9,8},{8,9},{13,10... | collective-permute-start | bytes 3145736 | tf_op jit(solution)/shard_map/ppermute | solution.py:574
  584.1 27.7 %collective-permute-start.28 = (bf16[4,256,1024]{2,1,0:T(8,128)(2,1)}, bf16[4,256,1024]{2,1,0:T(8,128)(2,1)}, u32[]{:S(2)}, u32[]{:S(2)}) collective-permute-start(bf16[4,256,1024]{2,1,0:T(8,128)(2,1)} %dynamic-slice_bitcast_fusion), channel_id=1, source_target_pairs={{0,4},{4,0},{1,5},{5,1},{2,6},{6,2},{3,7},{7,3},{8,12},{12,8},{9,1... | collective-permute-start | bytes 6291464 | tf_op jit(solution)/shard_map/ppermute | solution.py:723
  597.4 32.7 %all-to-all-start.3 = ((bf16[4,32,3072]{2,1,0:T(8,128)(2,1)}), bf16[4,32,3072]{2,1,0:T(8,128)(2,1)S(1)}, u32[]{:S(2)}, u32[]{:S(2)}) async-start(bf16[4,32,3072]{2,1,0:T(8,128)(2,1)} %bitcast.99), calls=%async_computation.5 | async-start | bytes 1572864 | tf_op jit(solution)/shard_map/all_to_all | solution.py:825
  617.6 25.1 %collective-permute-start.31 = (bf16[256,1024]{1,0:T(8,128)(2,1)}, bf16[256,1024]{1,0:T(8,128)(2,1)}, u32[]{:S(2)}, u32[]{:S(2)}) collective-permute-start(bf16[256,1024]{1,0:T(8,128)(2,1)} %get-tuple-element.190), channel_id=1, source_target_pairs={{0,24},{8,16},{16,8},{24,0},{1,25},{9,17},{17,9},{25,1},{2,26},{10... | collective-permute-start | bytes 1572872 | tf_op jit(solution)/shard_map/ppermute | solution.py:733
  (54 other events, 712.8 us)
Sparse Core Ops, SparseCore 0:
  25.9 36.9 all-gather.4
  64.9 54.4 all-gather.6
  136.3 120.5 all-gather.8
  342.0 91.9 reduce-scatter.2
  502.7 62.2 reduce-scatter.4

commit v8 on v7

--- a/solution.py
+++ b/solution.py
@@ -451,11 +451,10 @@
 
 
 def feed_kernel(
-    core_ref, n_ref, cot_ref, resid_ref, up_ref, down_ref, out_ref, back_ref,
-    gup_ref, gdown_own_ref, gdown_other_ref, total, n_turned, act_turned, pre,
+    n_ref, cot_ref, resid_ref, up_ref, down_ref, out_ref, back_ref, gup_ref, gdown_ref,
+    total, n_turned, act_turned, pre,
 ):
     step, last = pl.program_id(0), pl.num_programs(0) - 1
-    core = core_ref[0]
     frames, width = n_ref.shape
     tile = min(FEED_TILE, frames)
 
@@ -495,41 +494,37 @@
     piece = act_turned.shape[0]
     for begin in range(0, piece, FEED_PART):
         rows = slice(begin, begin + FEED_PART)
-        kept = dot_nn(act_turned[rows, :], cot_ref[...]).astype(bf16)
-        pl.when(core == step % 2)(functools.partial(gdown_own_ref.__setitem__, (0, rows), kept))
-        pl.when(core != step % 2)(functools.partial(gdown_other_ref.__setitem__, (0, rows), kept))
+        gdown_ref[rows, :] = dot_nn(act_turned[rows, :], cot_ref[...]).astype(bf16)
 
     @pl.when(step == last)
     def _():
         out_ref[...] = total[...].astype(bf16)
 
 
-def feed_forward_and_back(core, normed, cot, resid, hidden, piece, w_up, w_down, planes):
+def feed_forward_and_back(normed, cot, resid, hidden, piece, w_up, w_down):
     frames, width = normed.shape
-    whole = lambda: pl.BlockSpec((frames, width), lambda j, r: (0, 0), pipeline_mode=pl.Buffered(1))
-    weight = lambda w: pl.BlockSpec(w[1], lambda j, r: w[2](j))
-    up_block = pl.BlockSpec((width, piece), lambda j, r: (0, j))
-    down_block = pl.BlockSpec((1, piece, width), lambda j, r: (j // 2, 0, 0))
+    whole = lambda: pl.BlockSpec((frames, width), lambda j: (0, 0), pipeline_mode=pl.Buffered(1))
     return pl.pallas_call(
         feed_kernel,
-        grid_spec=pltpu.PrefetchScalarGridSpec(
-            num_scalar_prefetch=1,
-            grid=(hidden // piece,),
-            in_specs=[whole(), whole(), whole(), weight(w_up), weight(w_down)],
-            out_specs=[pl.BlockSpec((frames, width), lambda j, r: (0, 0))] * 2 + [up_block] + [down_block] * 2,
-            scratch_shapes=[
-                pltpu.VMEM((frames, width), f32),
-                pltpu.VMEM((width, frames), bf16),
-                pltpu.VMEM((piece, frames), bf16),
-                pltpu.VMEM((frames, piece), bf16),
-            ],
-        ),
-        out_shape=[jax.ShapeDtypeStruct((frames, width), bf16), jax.ShapeDtypeStruct((frames, width), f32)]
-        + [jax.ShapeDtypeStruct((width, hidden), bf16)]
-        + [jax.ShapeDtypeStruct((planes, piece, width), bf16)] * 2,
+        grid=(hidden // piece,),
+        in_specs=[whole(), whole(), whole(), pl.BlockSpec(*w_up[1:]), pl.BlockSpec(*w_down[1:])],
+        out_specs=[pl.BlockSpec((frames, width), lambda j: (0, 0))] * 2
+        + [pl.BlockSpec((width, piece), lambda j: (0, j)), pl.BlockSpec((piece, width), lambda j: (j, 0))],
+        out_shape=[
+            jax.ShapeDtypeStruct((frames, width), bf16),
+            jax.ShapeDtypeStruct((frames, width), f32),
+            jax.ShapeDtypeStruct((width, hidden), bf16),
+            jax.ShapeDtypeStruct((hidden, width), bf16),
+        ],
+        scratch_shapes=[
+            pltpu.VMEM((frames, width), f32),
+            pltpu.VMEM((width, frames), bf16),
+            pltpu.VMEM((piece, frames), bf16),
+            pltpu.VMEM((frames, piece), bf16),
+        ],
         compiler_params=params("arbitrary"),
         cost_estimate=cost(12 * frames * width * hidden, 8 * width * hidden + 16 * frames * width, frames * hidden),
-    )(core.reshape(1), normed, cot, resid, w_up[0], w_down[0])
+    )(normed, cot, resid, w_up[0], w_down[0])
 
 
 def body(inputs, skips, cotangent, segment_ids, time_steps, w_skip, w_qkv, w_out, w_up, w_down, w_mod):
@@ -715,8 +710,8 @@
         [(width, f32), (width, bf16)],
         flops=2 * frames * width * width,
     )
-    result, grad_normed_two, grad_up, own_down, other_down = feed_forward_and_back(
-        core, normed_two, cot, resid_mid, hidden, chunk, up_weight, down_weight, planes
+    result, grad_normed_two, grad_up, grad_down = feed_forward_and_back(
+        normed_two, cot, resid_mid, hidden, chunk, up_weight, down_weight
     )
 
     def over_cores(kept, axis):
@@ -739,11 +734,9 @@
     def exchange_line(value):
         return exchange(value.reshape(line, -1, value.shape[-1]), ("hi", "lo"), place, line)
 
-    def add_other(own, other):
-        return (own.astype(f32) + lax.ppermute(other, "core", swap).astype(f32)).astype(bf16)
-
-    grad_up = lax.psum_scatter(grad_up, ("plane", "core"), scatter_dimension=0, tiled=True)
-    grad_down = add_other(own_down, other_down)
+    grad_up, grad_down = (
+        lax.psum_scatter(v, ("plane", "core"), scatter_dimension=0, tiled=True) for v in (grad_up, grad_down)
+    )
 
     grad_mid, grad_mid_low, grad_frames, grad_shift_two, grad_scale_two = rowwise(
         norm_two_back_kernel,
@@ -757,22 +750,12 @@
     grad_heads = frames_to_heads(grad_frames)
     grad_out = lax.dot_general(mixed, grad_mid_low, (((0,), (0,)), ((), ())), preferred_element_type=f32)
     grad_out = over_cores(grad_out.astype(bf16).reshape(planes, 2, -1, width), 1)
-    grad_down = jnp.concatenate(
-        [v.reshape(planes, line, -1, width) for v in (grad_down, grad_out)], axis=2
-    )
-    grad_heads, grad_down, result = lax.optimization_barrier((grad_heads, grad_down, result))
+    grad_heads, grad_out, result = lax.optimization_barrier((grad_heads, grad_out, result))
     block_out = from_rows(result)
-    grad_down = exchange_planes(grad_down.reshape(planes, -1, width))
     grad_proj = attend_backward(
         ranges, queries, keys, projected, mixed_heads, grad_heads, logsum, cosine, sine, seg_column, seg_row
     )
-    grad_proj, grad_up, grad_down, block_out = lax.optimization_barrier((grad_proj, grad_up, grad_down, block_out))
-    grad_down = jnp.concatenate(
-        [grad_up[:, i * width : (i + 1) * width].reshape(line, -1, width) for i in range(columns)]
-        + [grad_down.reshape(line, -1, width)],
-        axis=1,
-    )
-    grad_down = lax.psum_scatter(grad_down.reshape(-1, width), ("hi", "lo"), scatter_dimension=0, tiled=True)
+    grad_proj, block_out = lax.optimization_barrier((grad_proj, block_out))
     grad_qkv = lax.dot_general(normed_row, grad_proj, (((0,), (0,)), ((), ())), preferred_element_type=f32)
     grad_qkv = grad_qkv.astype(bf16)
     grad_proj, grad_qkv = lax.optimization_barrier((grad_proj, grad_qkv))
@@ -807,9 +790,8 @@
     if group > 2:
         grad_qkv = lax.psum_scatter(grad_qkv, ("plane", "hi"), scatter_dimension=0, tiled=True).astype(f32)
     else:
-        grad_qkv = grad_qkv.reshape(planes, -1, 3 * width)
-        grad_qkv = lax.all_to_all(grad_qkv, "plane", split_axis=0, concat_axis=0, tiled=True)
-        grad_qkv = jnp.sum(grad_qkv.astype(f32), axis=0).astype(bf16)
+        grad_qkv = jnp.concatenate([grad_qkv.reshape(planes, -1, 3 * width), grad_out], axis=2)
+        grad_qkv = exchange_planes(grad_qkv)
     grad_in, grad_shift_one, grad_scale_one = rowwise(
         norm_one_back_kernel,
         frames,
@@ -819,11 +801,28 @@
         sums=2,
     )
     grad_in_home = from_rows(grad_in)
-    grad_in_home, grad_qkv, grad_down = lax.optimization_barrier((grad_in_home, grad_qkv, grad_down))
+    grad_mod = jnp.stack([v[:labels] for v in (grad_shift_one, grad_scale_one, grad_shift_two, grad_scale_two)], axis=1)
+    grad_mod = jnp.moveaxis(grad_mod.reshape(labels, devices, own_columns), 1, 0)
+    grad_mod = lax.all_to_all(grad_mod, ALL_AXES, split_axis=0, concat_axis=0, tiled=True)
+    grad_in_home, grad_qkv, grad_up, grad_down, grad_mod = lax.optimization_barrier(
+        (grad_in_home, grad_qkv, grad_up, grad_down, grad_mod)
+    )
+    both = jnp.concatenate(
+        [grad_up[:, i * width : (i + 1) * width].reshape(line, -1, width) for i in range(columns)]
+        + [grad_down.reshape(line, -1, width)],
+        axis=1,
+    )
+    both = lax.psum_scatter(both.reshape(-1, width), ("hi", "lo"), scatter_dimension=0, tiled=True).astype(f32)
+    taken = columns * up_rows
+    grad_up = jnp.concatenate([both[i * up_rows : (i + 1) * up_rows] for i in range(columns)], axis=1)
+    grad_down = both[taken:]
     if group == 2:
-        grad_qkv = grad_qkv.reshape(line, -1, 3 * width)
+        grad_qkv = grad_qkv.reshape(line, -1, 4 * width)
         grad_qkv = lax.all_to_all(grad_qkv, ("hi", "lo"), split_axis=0, concat_axis=0, tiled=True)
         grad_qkv = jnp.sum(grad_qkv.astype(f32), axis=0)
+        grad_qkv, grad_out = grad_qkv[:, : 3 * width], grad_qkv[:, 3 * width :]
+    else:
+        grad_out = exchange_line(exchange_planes(grad_out))
     home = grad_in_home.reshape(frames, width)
     grad_skip_w = jnp.concatenate(
         [
@@ -842,16 +841,7 @@
     )
     grad_inputs, grad_skips = (v.reshape(grad_in_home.shape) for v in (grad_inputs, grad_skips))
 
-    grad_shift_one, grad_skip_w = lax.optimization_barrier((grad_shift_one, grad_skip_w))
     grad_skip_w = exchange_line(grad_skip_w)
-    grad_mod = jnp.stack([v[:labels] for v in (grad_shift_one, grad_scale_one, grad_shift_two, grad_scale_two)], axis=1)
-    grad_mod = jnp.moveaxis(grad_mod.reshape(labels, devices, own_columns), 1, 0)
-    grad_mod = lax.all_to_all(grad_mod, ALL_AXES, split_axis=0, concat_axis=0, tiled=True)
-    grad_inputs, grad_mod, grad_skip_w = lax.optimization_barrier((grad_inputs, grad_mod, grad_skip_w))
-    taken = columns * up_rows
-    grad_down = grad_down.astype(f32)
-    grad_up = jnp.concatenate([grad_down[i * up_rows : (i + 1) * up_rows] for i in range(columns)], axis=1)
-    grad_down, grad_out = grad_down[taken : taken + down_rows], grad_down[taken + down_rows :]
     grad_mod = jnp.sum(grad_mod.reshape(planes, 2, highs, lows, labels, own_columns), axis=(1, 3))
     grad_mod = lax.dot_general(
         embedded.astype(f32),

time: 679 us -> 678 us (level)
  Pallas kernels: 292 us -> 276 us
  waiting for transfers between devices: 122 us -> 131 us
  starting transfers between devices: 108 us -> 116 us
    ppermute x2, waiting for transfers between devices: 40.4 us -> 6.7 us  [from_rows(): lax.ppermute(lax.dynamic_index_in_dim(value, 1 - high % 2, 0, False), LIN...]
    ppermute x9, waiting for transfers between devices: 18.7 us -> 42.7 us  [exchange(): lax.ppermute(sent, axes, [(i, i ^ flip) for i in range(count)]).astype(f32)]
    ppermute x9, starting transfers between devices: 11.1 us -> 31.4 us  [exchange(): lax.ppermute(sent, axes, [(i, i ^ flip) for i in range(count)]).astype(f32)]
    all_to_all x1, waiting for transfers between devices: 2.09 us -> 19.6 us  [body(): lax.all_to_all(grad_qkv, ('hi', 'lo'), split_axis=0, concat_axis=0, tiled...]
    pallas_call x1, Pallas kernels: 88 us -> 72.5 us  [attend_backward(): pl.pallas_call(attend_backward_kernel, grid_spec=pltpu.PrefetchScalarGrid...]
    ppermute x2, starting transfers between devices: 13.3 us -> 0.48 us  [over_cores(): lax.ppermute(lax.dynamic_index_in_dim(kept, 1 - core, axis, False), 'core...]
    ppermute x2, starting transfers between devices: 2.91 us -> 11.4 us  [from_rows(): lax.ppermute(lax.dynamic_index_in_dim(value, high % 2, 0, False), LINE_AX...]
    all_to_all x1, starting transfers between devices: 12 us -> 4.53 us  [body(): lax.all_to_all(grad_qkv, ('hi', 'lo'), split_axis=0, concat_axis=0, tiled...]
  transfers between devices with their start and end apart: 44 -> 43, of which waited for: 14 -> 13; matrix products, arithmetic and copies ran while one was open for 13% -> 14% of each run, Pallas kernels for 33% -> 31%
where the time goes in v8:
time: 678 us; the launch traced here: 671 us
  Pallas kernels  276 us (41%)
  waiting for transfers between devices  131 us (19%)
  starting transfers between devices  116 us (17%)
  other arithmetic  52.6 us (8%)
  local copies, waits for them, and re-layouts  52.1 us (8%)
  matrix products  19.7 us (3%)
  between operations  15.2 us (2%)
  blocking collectives  8.92 us (1%)
    pallas_call x1, Pallas kernels, attend_backward(): pl.pallas_call(attend_backward_kernel, grid_spec=pltpu.PrefetchScalarGrid...  72.5 us
    pallas_call x1, Pallas kernels, feed_forward_and_back(): pl.pallas_call(feed_kernel, grid=(hidden // piece,), in_specs=[whole(), w...  66.4 us
    pallas_call x1, Pallas kernels, attend_forward(): pl.pallas_call(attend_forward_kernel, grid_spec=pltpu.PrefetchScalarGridS...  59.9 us
    ppermute x9, waiting for transfers between devices, share_on_line(): lax.ppermute(value, ('hi', 'lo'), [(i, i ^ flip) for i in range(line)])  58.9 us
    pallas_call x6, Pallas kernels, rowwise(): pl.pallas_call(kernel, grid=(frames // tile,), in_specs=in_specs, out_spe...  50.3 us
    ppermute x9, waiting for transfers between devices, exchange(): lax.ppermute(sent, axes, [(i, i ^ flip) for i in range(count)]).astype(f32)  42.7 us
    ppermute x9, starting transfers between devices, exchange(): lax.ppermute(sent, axes, [(i, i ^ flip) for i in range(count)]).astype(f32)  31.4 us
    unnamed x88, local copies, waits for them, and re-layouts  20.7 us
  transfers between devices with their start and end apart: 43, of which 13 were waited for; matrix products, arithmetic and copies ran while one was open for 14% of the time, Pallas kernels for 31%

profile of v8, /device:TPU:0, one launch (start us, length us, event | category | flops | bytes accessed | tf_op | source)
XLA Modules:
  0.0 671.4 jit_solution(9556677577833366735)
XLA Ops:
  30.3 6.8 %collective-permute-done.12 = bf16[128,1024]{1,0:T(8,128)(2,1)S(1)} collective-permute-done((bf16[128,1024]{1,0:T(8,128)(2,1)S(1)}, bf16[128,1024]{1,0:T(8,128)(2,1)S(1)}, u32[]{:S(2)}, u32[]{:S(2)}) %collective-permute-start.12) | collective-permute-done | bytes 262176 | tf_op jit(solution)/shard_map/ppermute | solution.py:596
  37.1 12.2 %collective-permute-done.11 = bf16[128,1024]{1,0:T(8,128)(2,1)S(1)} collective-permute-done((bf16[128,1024]{1,0:T(8,128)(2,1)S(1)}, bf16[128,1024]{1,0:T(8,128)(2,1)S(1)}, u32[]{:S(2)}, u32[]{:S(2)}) %collective-permute-start.11) | collective-permute-done | bytes 262176 | tf_op jit(solution)/shard_map/ppermute | solution.py:596
  50.8 8.9 %all-gather = s32[16,1,4]{2,1,0:T(1,128)S(1)} all-gather(s32[2,1,4]{2,1,0:T(1,128)S(1)} %copy-done.35), channel_id=2, replica_groups=mesh['plane'=4,'core'=2,'hi'=4,'lo'=1] {'plane','core'}, dimensions={0}, use_global_device_ids=true | all-gather | bytes 288 | tf_op jit(solution)/shard_map/all_gather | solution.py:636
  75.0 8.6 %shard_map.178 = bf16[1024,1024]{1,0:T(8,128)(2,1)} custom-call(bf16[1024,1024]{1,0:T(8,128)(2,1)} %bitcast.208, bf16[1024,1024]{1,0:T(8,128)(2,1)} %bitcast.207, bf16[32,64,1024]{2,1,0:T(8,128)(2,1)} %all-gather.5.cloned.1.call-done.top_ref.bottom_ref, bf16[32,64,1024]{2,1,0:T(8,128)(2,1)} %all-gather.5.cloned.1.call-done.top_ref.bottom_ref), custom_call_target="tpu_custom_call" | custom-call | flops 1 | bytes 1 | tf_op jit(solution)/shard_map/pallas_call | solution.py:223
  92.2 37.4 %collective-permute-done.6 = bf16[256,1024]{1,0:T(8,128)(2,1)} collective-permute-done((bf16[256,1024]{1,0:T(8,128)(2,1)}, bf16[256,1024]{1,0:T(8,128)(2,1)}, u32[]{:S(2)}, u32[]{:S(2)}) %collective-permute-start.6) | collective-permute-done | bytes 524320 | tf_op jit(solution)/shard_map/ppermute | solution.py:596
  143.6 20.1 %collective-permute-start.9 = (bf16[1024,1024]{1,0:T(8,128)(2,1)}, bf16[1024,1024]{1,0:T(8,128)(2,1)}, u32[]{:S(2)}, u32[]{:S(2)}) collective-permute-start(bf16[1024,1024]{1,0:T(8,128)(2,1)} %shard_map.179), channel_id=1, source_target_pairs={{0,4},{4,0},{1,5},{5,1},{2,6},{6,2},{3,7},{7,3},{8,12},{12,8},{9,1... | collective-permute-start | bytes 6291464 | tf_op jit(solution)/shard_map/ppermute | solution.py:576
  170.1 12.0 %collective-permute-start.15 = (bf16[512,1024]{1,0:T(8,128)(2,1)}, bf16[512,1024]{1,0:T(8,128)(2,1)S(1)}, u32[]{:S(2)}, u32[]{:S(2)}) collective-permute-start(bf16[512,1024]{1,0:T(8,128)(2,1)} %get-tuple-element.191), channel_id=1, source_target_pairs={{0,1},{1,0},{2,5},{3,4},{4,3},{5,2},{6,7},{7,6},{8,9},{9,8},{10,13... | collective-permute-start | bytes 3145736 | tf_op jit(solution)/shard_map/ppermute | solution.py:563
  188.8 11.0 %shard_map.180.q_ref.k_ref.v_ref = bf16[2048,1536]{1,0:T(8,128)(2,1)} custom-call(s32[1]{0:T(128)} %bitcast.21.place_ref, bf16[2048,1024]{1,0:T(8,128)(2,1)} %pad_maximum_fusion.x_ref, bf16[32,128,1024]{2,1,0:T(8,128)(2,1)} %all-gather.7.cloned.1.call-done.w_ref.q_ref.k_ref.v_ref), custom_call_target="tpu_custom_call" | custom-call | flops 1 | bytes 1 | tf_op jit(solution)/shard_map/pallas_call | solution.py:151
  199.8 59.9 %shard_map.181 = (bf16[2048,512]{1,0:T(8,128)(2,1)}, bf16[2048,512]{1,0:T(8,128)(2,1)}, bf16[2048,512]{1,0:T(8,128)(2,1)}, f32[4,2,2048]{2,1,0:T(2,128)}) custom-call(s32[2,8]{1,0:T(2,128)} %pad_add_fusion.range_ref, bf16[2048,1536]{1,0:T(8,128)(2,1)} %shard_map.180.q_ref.k_ref.v_ref, bf16[2048,1536]{1,0:T(8,128)(2,1)} %shard_map.180.q_ref.k_ref.v_ref, ...), custom_call_target="tpu_custom_call" | custom-call | flops 17179869184 | bytes 14680064 | tf_op jit(solution)/shard_map/pallas_call | solution.py:316
  267.9 8.2 %shard_map.182 = (f32[1024,1024]{1,0:T(8,128)}, bf16[1024,1024]{1,0:T(8,128)(2,1)}) custom-call(bf16[1024,1024]{1,0:T(8,128)(2,1)} %pad_maximum_fusion.5.mixed_ref, bf16[32,128,1024]{2,1,0:T(8,128)(2,1)} %all-gather.7.cloned.1.call-done.w_ref.q_ref.k_ref.v_ref, bf16[1024,1024]{1,0:T(8,128)(2,1)} %pad_maximum_fusion.2.resid_ref.resid_in_ref, ...), custom_call_target="tpu_custom_call" | custom-call | flops 2147483648 | bytes 18911232 | tf_op jit(solution)/shard_map/pallas_call | solution.py:223
  276.0 66.4 %shard_map.183 = (bf16[1024,1024]{1,0:T(8,128)(2,1)}, f32[1024,1024]{1,0:T(8,128)}, bf16[1024,4096]{1,0:T(8,128)(2,1)}, bf16[4096,1024]{1,0:T(8,128)(2,1)}) custom-call(bf16[1024,1024]{1,0:T(8,128)(2,1)} %get-tuple-element.62.n_ref, bf16[1024,1024]{1,0:T(8,128)(2,1)} %pad_maximum_fusion.6.cot_ref, f32[1024,1024]{1,0:T(8,128)} %get-tuple-element.64.resid_ref, ...), custom_call_target="tpu_custom_call" | custom-call | flops 51539607552 | bytes 50331648 | tf_op jit(solution)/shard_map/pallas_call | solution.py:507
  343.2 10.5 %shard_map.184 = (f32[1024,1024]{1,0:T(8,128)}, bf16[1024,1024]{1,0:T(8,128)(2,1)}, bf16[1024,1024]{1,0:T(8,128)(2,1)}, f32[8,1024]{1,0:T(8,128)}, f32[8,1024]{1,0:T(8,128)}) custom-call(f32[1024,1024]{1,0:T(8,128)} %get-tuple-element.66.g_ref, f32[1024,1024]{1,0:T(8,128)} %get-tuple-element.64.resid_ref, bf16[1024,1024]{1,0:T(8,128)(2,1)} %pad_maximum_fusion.6.cot_ref, ...), custom_call_target="tpu_custom_call" | custom-call | flops 1 | bytes 1 | tf_op jit(solution)/shard_map/pallas_call | solution.py:223
  376.1 72.5 %shard_map.185.dq_ref.dk_ref.dv_ref = bf16[2048,1536]{1,0:T(8,128)(2,1)} custom-call(s32[2,8]{1,0:T(2,128)} %pad_add_fusion.range_ref, bf16[2048,512]{1,0:T(8,128)(2,1)} %get-tuple-element.59.q_ref, bf16[2048,512]{1,0:T(8,128)(2,1)} %get-tuple-element.60.k_ref, bf16[2048,1536]{1,0:T(8,128)(2,1)} %shard_map.180.q_ref.k_ref.v_ref, ...), custom_call_target="tpu_custom_call" | custom-call | flops 42949672960 | bytes 16777216 | tf_op jit(solution)/shard_map/pallas_call | solution.py:420
  453.8 7.0 %convolution_convert_fusion = bf16[1024,1536]{1,0:T(8,128)(2,1)S(1)} fusion(bf16[2048,1536]{1,0:T(8,128)(2,1)S(1)} %copy-done.2, bf16[1024,1024]{1,0:T(8,128)(2,1)S(1)} %copy-done.9, bf16[1024,1024]{1,0:T(8,128)(2,1)S(1)} %copy-done.7), kind=kOutput, calls=%fused_computation.14 | convolution fusion | flops 6452412416 | bytes 13631488 | tf_op jit(solution)/shard_map/dot_general | solution.py:759
  465.9 7.9 %shard_map.187 = bf16[1024,1024]{1,0:T(8,128)(2,1)} custom-call(s32[2]{0:T(128)} %pad_add_fusion.2.place_ref, bf16[2048,1536]{1,0:T(8,128)(2,1)} %shard_map.185.dq_ref.dk_ref.dv_ref, bf16[2048,1536]{1,0:T(8,128)(2,1)} %shard_map.185.dq_ref.dk_ref.dv_ref, bf16[2048,1536]{1,0:T(8,128)(2,1)} %shard_map.185.dq_ref.dk_ref.dv_ref, ...), custom_call_target="tpu_custom_call" | custom-call | flops 3221225472 | bytes 8388608 | tf_op jit(solution)/shard_map/pallas_call | solution.py:186
  473.8 8.2 %shard_map.186.own_ref = f32[1024,1024]{1,0:T(8,128)} custom-call(s32[2]{0:T(128)} %pad_add_fusion.1.place_ref, bf16[2048,1536]{1,0:T(8,128)(2,1)} %shard_map.185.dq_ref.dk_ref.dv_ref, bf16[2048,1536]{1,0:T(8,128)(2,1)} %shard_map.185.dq_ref.dk_ref.dv_ref, bf16[2048,1536]{1,0:T(8,128)(2,1)} %shard_map.185.dq_ref.dk_ref.dv_ref, ...), custom_call_target="tpu_custom_call" | custom-call | flops 3221225472 | bytes 8388608 | tf_op jit(solution)/shard_map/pallas_call | solution.py:186
  485.6 22.4 %collective-permute-start.24 = (bf16[128,4096]{1,0:T(8,128)(2,1)}, bf16[128,4096]{1,0:T(8,128)(2,1)}, u32[]{:S(2)}, u32[]{:S(2)}) collective-permute-start(bf16[128,4096]{1,0:T(8,128)(2,1)} %get-tuple-element.164), channel_id=1, source_target_pairs={{0,8},{8,0},{16,24},{24,16},{1,9},{9,1},{17,25},{25,17},{2,10},{10... | collective-permute-start | bytes 3145736 | tf_op jit(solution)/shard_map/ppermute | solution.py:728
  509.5 9.1 %shard_map.188 = (bf16[1024,1024]{1,0:T(8,128)(2,1)}, f32[8,1024]{1,0:T(8,128)}, f32[8,1024]{1,0:T(8,128)}) custom-call(f32[1024,1024]{1,0:T(8,128)} %shard_map.186.own_ref, bf16[1024,1024]{1,0:T(8,128)(2,1)} %collective-permute-done.21.other_ref, bf16[1024,1024]{1,0:T(8,128)(2,1)} %pad_maximum_fusion.2.resid_ref.resid_in_ref, ...), custom_call_target="tpu_custom_call" | custom-call | bytes 14704640 | tf_op jit(solution)/shard_map/pallas_call | solution.py:223
  521.7 9.5 %collective-permute-start.22 = (bf16[512,1024]{1,0:T(8,128)(2,1)}, bf16[512,1024]{1,0:T(8,128)(2,1)}, u32[]{:S(2)}, u32[]{:S(2)}) collective-permute-start(bf16[512,1024]{1,0:T(8,128)(2,1)} %get-tuple-element.182), channel_id=1, source_target_pairs={{0,0},{1,1},{4,2},{5,3},{2,4},{3,5},{6,6},{7,7},{8,8},{9,9},{12,10... | collective-permute-start | bytes 3145736 | tf_op jit(solution)/shard_map/ppermute | solution.py:568
  536.1 19.9 %collective-permute-done.25 = bf16[128,4096]{1,0:T(8,128)(2,1)} collective-permute-done((bf16[128,4096]{1,0:T(8,128)(2,1)}, bf16[128,4096]{1,0:T(8,128)(2,1)}, u32[]{:S(2)}, u32[]{:S(2)}) %collective-permute-start.25) | collective-permute-done | bytes 1048608 | tf_op jit(solution)/shard_map/ppermute | solution.py:728
  601.7 8.4 %shard_map.189 = (bf16[1024,1024]{1,0:T(8,128)(2,1)}, bf16[1024,1024]{1,0:T(8,128)(2,1)}) custom-call(bf16[1024,1024]{1,0:T(8,128)(2,1)} %bitcast.214, bf16[32,64,1024]{2,1,0:T(8,128)(2,1)} %all-gather.5.cloned.1.call-done.top_ref.bottom_ref, bf16[32,64,1024]{2,1,0:T(8,128)(2,1)} %all-gather.5.cloned.1.call-done.top_ref.bottom_ref), custom_call_target="tpu_custom_call" | custom-call | flops 4294967296 | bytes 14680064 | tf_op jit(solution)/shard_map/pallas_call | solution.py:223
  612.4 10.9 %collective-permute-done.30 = bf16[256,1024]{1,0:T(8,128)(2,1)} collective-permute-done((bf16[256,1024]{1,0:T(8,128)(2,1)}, bf16[256,1024]{1,0:T(8,128)(2,1)}, u32[]{:S(2)}, u32[]{:S(2)}) %collective-permute-start.30) | collective-permute-done | bytes 524320 | tf_op jit(solution)/shard_map/ppermute | solution.py:728
  630.3 19.6 %all-to-all-done.2 = bf16[4,32,4096]{2,1,0:T(8,128)(2,1)S(1)} async-done(((bf16[4,32,4096]{2,1,0:T(8,128)(2,1)}), bf16[4,32,4096]{2,1,0:T(8,128)(2,1)S(1)}, u32[]{:S(2)}, u32[]{:S(2)}) %all-to-all-start.2) | async-done | bytes 1048608 | tf_op jit(solution)/shard_map/all_to_all | solution.py:821
  651.5 8.4 %collective-permute-done.32 = bf16[64,1024]{1,0:T(8,128)(2,1)S(1)} collective-permute-done((bf16[64,1024]{1,0:T(8,128)(2,1)S(1)}, bf16[64,1024]{1,0:T(8,128)(2,1)S(1)}, u32[]{:S(2)}, u32[]{:S(2)}) %collective-permute-start.32) | collective-permute-done | bytes 131104 | tf_op jit(solution)/shard_map/ppermute | solution.py:728
  (268 shorter events, 190.5 us)
Async XLA Ops:
  7.2 67.8 %all-gather.5.cloned.1.call-start = ((), (), s32[]{:S(2)}) async-start(), calls=%async_computation.6 | async-start | bytes 4718592 | tf_op jit(solution)/shard_map/all_gather | solution.py:601
  25.8 163.0 %all-gather.7.cloned.1.call-start = ((), (), s32[]{:S(2)}) async-start(), calls=%async_computation.7 | async-start | bytes 9437184 | tf_op jit(solution)/shard_map/all_gather | solution.py:601
  61.4 74.6 %all-to-all-start = ((f32[32,4,128]{2,1,0:T(4,128)}), f32[32,4,128]{2,1,0:T(4,128)S(1)}, u32[]{:S(2)}, u32[]{:S(2)}) async-start(f32[32,4,128]{2,1,0:T(4,128)} %bitcast.14), calls=%async_computation | async-start | bytes 131072 | tf_op jit(solution)/shard_map/all_to_all | solution.py:645
  64.6 211.4 %all-gather.9.cloned.1.call-start = ((), (), s32[]{:S(2)}) async-start(), calls=%async_computation.8 | async-start | bytes 18874368 | tf_op jit(solution)/shard_map/all_gather | solution.py:601
  74.3 55.4 %collective-permute-start.6 = (bf16[256,1024]{1,0:T(8,128)(2,1)}, bf16[256,1024]{1,0:T(8,128)(2,1)}, u32[]{:S(2)}, u32[]{:S(2)}) collective-permute-start(bf16[256,1024]{1,0:T(8,128)(2,1)} %slice_dynamic-update-slice_fusion.6), channel_id=1, source_target_pairs={{0,2},{1,3},{2,0},{3,1},{4,6},{5,7},{6,4},{7,5},{8,10},{9,11},{10,... | collective-permute-start | bytes 1572872 | tf_op jit(solution)/shard_map/ppermute | solution.py:596
  74.3 55.4 %collective-permute-start.5 = (bf16[256,1024]{1,0:T(8,128)(2,1)}, bf16[256,1024]{1,0:T(8,128)(2,1)}, u32[]{:S(2)}, u32[]{:S(2)}) collective-permute-start(bf16[256,1024]{1,0:T(8,128)(2,1)} %slice_dynamic-update-slice_fusion.6), channel_id=1, source_target_pairs={{0,1},{1,0},{2,3},{3,2},{4,5},{5,4},{6,7},{7,6},{8,9},{9,8},{10,11... | collective-permute-start | bytes 1572872 | tf_op jit(solution)/shard_map/ppermute | solution.py:596
  86.6 46.6 %collective-permute-start.3 = (bf16[512,1024]{1,0:T(8,128)(2,1)}, bf16[512,1024]{1,0:T(8,128)(2,1)S(1)}, u32[]{:S(2)}, u32[]{:S(2)}) collective-permute-start(bf16[512,1024]{1,0:T(8,128)(2,1)} %get-tuple-element.198), channel_id=1, source_target_pairs={{0,0},{1,1},{2,4},{3,5},{4,2},{5,3},{6,6},{7,7},{8,8},{9,9},{10,12... | collective-permute-start | bytes 3145736 | tf_op jit(solution)/shard_map/ppermute | solution.py:562
  88.5 44.7 %collective-permute-start.4 = (bf16[512,1024]{1,0:T(8,128)(2,1)}, bf16[512,1024]{1,0:T(8,128)(2,1)}, u32[]{:S(2)}, u32[]{:S(2)}) collective-permute-start(bf16[512,1024]{1,0:T(8,128)(2,1)} %get-tuple-element.199), channel_id=1, source_target_pairs={{0,1},{1,0},{2,5},{3,4},{4,3},{5,2},{6,7},{7,6},{8,9},{9,8},{10,13... | collective-permute-start | bytes 3145736 | tf_op jit(solution)/shard_map/ppermute | solution.py:563
  136.2 435.4 %reduce-scatter.4.cloned.1.call-start = ((), (), s32[]{:S(2)}) async-start(), calls=%async_computation.9 | async-start | bytes 9437184 | tf_op jit(solution)/shard_map/reduce_scatter | solution.py:738
  143.6 38.5 %collective-permute-start.9 = (bf16[1024,1024]{1,0:T(8,128)(2,1)}, bf16[1024,1024]{1,0:T(8,128)(2,1)}, u32[]{:S(2)}, u32[]{:S(2)}) collective-permute-start(bf16[1024,1024]{1,0:T(8,128)(2,1)} %shard_map.179), channel_id=1, source_target_pairs={{0,4},{4,0},{1,5},{5,1},{2,6},{6,2},{3,7},{7,3},{8,12},{12,8},{9,1... | collective-permute-start | bytes 6291464 | tf_op jit(solution)/shard_map/ppermute | solution.py:576
  168.0 95.3 %collective-permute-start.14 = (bf16[512,1024]{1,0:T(8,128)(2,1)}, bf16[512,1024]{1,0:T(8,128)(2,1)S(1)}, u32[]{:S(2)}, u32[]{:S(2)}) collective-permute-start(bf16[512,1024]{1,0:T(8,128)(2,1)} %get-tuple-element.190), channel_id=1, source_target_pairs={{0,0},{1,1},{2,4},{3,5},{4,2},{5,3},{6,6},{7,7},{8,8},{9,9},{10,12... | collective-permute-start | bytes 3145736 | tf_op jit(solution)/shard_map/ppermute | solution.py:562
  170.1 93.1 %collective-permute-start.15 = (bf16[512,1024]{1,0:T(8,128)(2,1)}, bf16[512,1024]{1,0:T(8,128)(2,1)S(1)}, u32[]{:S(2)}, u32[]{:S(2)}) collective-permute-start(bf16[512,1024]{1,0:T(8,128)(2,1)} %get-tuple-element.191), channel_id=1, source_target_pairs={{0,1},{1,0},{2,5},{3,4},{4,3},{5,2},{6,7},{7,6},{8,9},{9,8},{10,13... | collective-permute-start | bytes 3145736 | tf_op jit(solution)/shard_map/ppermute | solution.py:563
  342.4 229.1 %reduce-scatter.6.cloned.1.call-start = ((), (), s32[]{:S(2)}) async-start(), calls=%async_computation.10 | async-start | bytes 9437184 | tf_op jit(solution)/shard_map/reduce_scatter | solution.py:738
  370.5 78.2 %collective-permute-start.18 = (bf16[512,1024]{1,0:T(8,128)(2,1)}, bf16[512,1024]{1,0:T(8,128)(2,1)S(1)}, u32[]{:S(2)}, u32[]{:S(2)}) collective-permute-start(bf16[512,1024]{1,0:T(8,128)(2,1)} %get-tuple-element.186), channel_id=1, source_target_pairs={{0,0},{1,1},{4,2},{5,3},{2,4},{3,5},{6,6},{7,7},{8,8},{9,9},{12,10... | collective-permute-start | bytes 3145736 | tf_op jit(solution)/shard_map/ppermute | solution.py:568
  372.4 76.3 %collective-permute-start.19 = (bf16[512,1024]{1,0:T(8,128)(2,1)}, bf16[512,1024]{1,0:T(8,128)(2,1)}, u32[]{:S(2)}, u32[]{:S(2)}) collective-permute-start(bf16[512,1024]{1,0:T(8,128)(2,1)} %get-tuple-element.187), channel_id=1, source_target_pairs={{1,0},{0,1},{5,2},{4,3},{3,4},{2,5},{7,6},{6,7},{9,8},{8,9},{13,10... | collective-permute-start | bytes 3145736 | tf_op jit(solution)/shard_map/ppermute | solution.py:569
  473.8 35.7 %collective-permute-start.21 = (bf16[1024,1024]{1,0:T(8,128)(2,1)}, bf16[1024,1024]{1,0:T(8,128)(2,1)}, u32[]{:S(2)}, u32[]{:S(2)}) collective-permute-start(bf16[1024,1024]{1,0:T(8,128)(2,1)} %shard_map.187), channel_id=1, source_target_pairs={{0,4},{4,0},{1,5},{5,1},{2,6},{6,2},{3,7},{7,3},{8,12},{12,8},{9,1... | collective-permute-start | bytes 6291464 | tf_op jit(solution)/shard_map/ppermute | solution.py:787
  485.6 50.5 %collective-permute-start.24 = (bf16[128,4096]{1,0:T(8,128)(2,1)}, bf16[128,4096]{1,0:T(8,128)(2,1)}, u32[]{:S(2)}, u32[]{:S(2)}) collective-permute-start(bf16[128,4096]{1,0:T(8,128)(2,1)} %get-tuple-element.164), channel_id=1, source_target_pairs={{0,8},{8,0},{16,24},{24,16},{1,9},{9,1},{17,25},{25,17},{2,10},{10... | collective-permute-start | bytes 3145736 | tf_op jit(solution)/shard_map/ppermute | solution.py:728
  508.0 48.0 %collective-permute-start.25 = (bf16[128,4096]{1,0:T(8,128)(2,1)}, bf16[128,4096]{1,0:T(8,128)(2,1)}, u32[]{:S(2)}, u32[]{:S(2)}) collective-permute-start(bf16[128,4096]{1,0:T(8,128)(2,1)} %get-tuple-element.165), channel_id=1, source_target_pairs={{0,16},{8,24},{16,0},{24,8},{1,17},{9,25},{17,1},{25,9},{2,18},{10... | collective-permute-start | bytes 3145736 | tf_op jit(solution)/shard_map/ppermute | solution.py:728
  508.0 48.0 %collective-permute-start.26 = (bf16[128,4096]{1,0:T(8,128)(2,1)}, bf16[128,4096]{1,0:T(8,128)(2,1)}, u32[]{:S(2)}, u32[]{:S(2)}) collective-permute-start(bf16[128,4096]{1,0:T(8,128)(2,1)} %get-tuple-element.166), channel_id=1, source_target_pairs={{0,24},{8,16},{16,8},{24,0},{1,25},{9,17},{17,9},{25,1},{2,26},{10... | collective-permute-start | bytes 3145736 | tf_op jit(solution)/shard_map/ppermute | solution.py:728
  521.7 37.9 %collective-permute-start.22 = (bf16[512,1024]{1,0:T(8,128)(2,1)}, bf16[512,1024]{1,0:T(8,128)(2,1)}, u32[]{:S(2)}, u32[]{:S(2)}) collective-permute-start(bf16[512,1024]{1,0:T(8,128)(2,1)} %get-tuple-element.182), channel_id=1, source_target_pairs={{0,0},{1,1},{4,2},{5,3},{2,4},{3,5},{6,6},{7,7},{8,8},{9,9},{12,10... | collective-permute-start | bytes 3145736 | tf_op jit(solution)/shard_map/ppermute | solution.py:568
  531.2 35.1 %collective-permute-start.23 = (bf16[512,1024]{1,0:T(8,128)(2,1)}, bf16[512,1024]{1,0:T(8,128)(2,1)}, u32[]{:S(2)}, u32[]{:S(2)}) collective-permute-start(bf16[512,1024]{1,0:T(8,128)(2,1)} %get-tuple-element.183), channel_id=1, source_target_pairs={{1,0},{0,1},{5,2},{4,3},{3,4},{2,5},{7,6},{6,7},{9,8},{8,9},{13,10... | collective-permute-start | bytes 3145736 | tf_op jit(solution)/shard_map/ppermute | solution.py:569
  532.0 39.6 %all-to-all-start.1 = ((f32[32,4,128]{2,1,0:T(4,128)}), f32[32,4,128]{2,1,0:T(4,128)S(1)}, u32[]{:S(2)}, u32[]{:S(2)}) async-start(f32[32,4,128]{2,1,0:T(4,128)} %copy.119), calls=%async_computation.3 | async-start | bytes 131072 | tf_op jit(solution)/shard_map/all_to_all | solution.py:806
  535.8 125.8 %reduce-scatter.8.cloned.1.call-start = ((), (), s32[]{:S(2)}) async-start(), calls=%async_computation.11 | async-start | bytes 2621440 | tf_op jit(solution)/shard_map/reduce_scatter | solution.py:815
  588.4 61.6 %all-to-all-start.2 = ((bf16[4,32,4096]{2,1,0:T(8,128)(2,1)}), bf16[4,32,4096]{2,1,0:T(8,128)(2,1)S(1)}, u32[]{:S(2)}, u32[]{:S(2)}) async-start(bf16[4,32,4096]{2,1,0:T(8,128)(2,1)} %bitcast.90), calls=%async_computation.4 | async-start | bytes 2097152 | tf_op jit(solution)/shard_map/all_to_all | solution.py:821
  (56 other events, 749.5 us)
Sparse Core Ops, SparseCore 0:
  25.9 36.9 all-gather.4
  64.9 54.4 all-gather.6
  136.3 120.5 all-gather.8
  342.6 78.9 reduce-scatter.3
  425.3 71.2 reduce-scatter.5
  583.7 68.7 reduce-scatter.7

commit v9 on v8

--- a/solution.py
+++ b/solution.py
@@ -611,6 +611,26 @@
     middle, late = share_on_line(middle), share_on_line(late)
     middle = gather_planes(middle)
 
+    in_place = out_rows % 16 == 0
+    hidden = w_up.shape[1]
+    chunk = hidden // (2 * planes)
+
+    def weight(gathered, begin, rows, first, count):
+        block = (count // rows, rows, width)
+        if in_place:
+            return gathered, block, (first // count, begin // rows, 0)
+        taken = gathered[first // rows : (first + count) // rows, begin : begin + rows]
+        return taken.reshape(1, count, width), (1, count, width), (0, 0, 0)
+
+    skip_top, skip_bottom = (weight(early, 0, skip_rows, i * width, width) for i in range(2))
+    out_weight = weight(middle, 3 * out_rows, out_rows, 0, width)
+    x, s = (v.reshape(frames, width) for v in (inputs, skips))
+    (resid_in,) = rowwise(
+        merge_kernel, frames, [("", x), ("", s), ("weight", skip_top), ("weight", skip_bottom)], [(width, bf16)], light=True
+    )
+    stacked = jnp.concatenate([x, s], axis=1)
+    resid_in, segment_ids, time_steps = lax.optimization_barrier((resid_in, segment_ids, time_steps))
+
     labels_own = segment_ids[:, 0]
     labels_other = lax.ppermute(labels_own, "core", swap)
     labels_pick = jnp.where(core == high // micro, labels_own, labels_other)
@@ -647,19 +667,6 @@
     )
     modulation = jnp.moveaxis(block_mod, 0, 1).reshape(labels, 4, width)
 
-    in_place = out_rows % 16 == 0
-    hidden = w_up.shape[1]
-    chunk = hidden // (2 * planes)
-
-    def weight(gathered, begin, rows, first, count):
-        block = (count // rows, rows, width)
-        if in_place:
-            return gathered, block, (first // count, begin // rows, 0)
-        taken = gathered[first // rows : (first + count) // rows, begin : begin + rows]
-        return taken.reshape(1, count, width), (1, count, width), (0, 0, 0)
-
-    skip_top, skip_bottom = (weight(early, 0, skip_rows, i * width, width) for i in range(2))
-    out_weight = weight(middle, 3 * out_rows, out_rows, 0, width)
     def own_qkv(gathered):
         parts = []
         for i in range(3):
@@ -670,13 +677,9 @@
     mine_column, mine_row = mine[:, None], mine[None, :]
     shift_one, scale_one, shift_two, scale_two = (modulation[:, i] for i in range(4))
 
-    x, s = (v.reshape(frames, width) for v in (inputs, skips))
-    (resid_in,) = rowwise(
-        merge_kernel, frames, [("", x), ("", s), ("weight", skip_top), ("weight", skip_bottom)], [(width, bf16)], light=True
-    )
     resid_in = to_rows(resid_in.reshape(inputs.shape))
-    resid_in, late, cotangent, modulation, cosine, sine, ranges = lax.optimization_barrier(
-        (resid_in, late, cotangent, modulation, cosine, sine, ranges)
+    resid_in, late, cotangent, stacked, modulation, cosine, sine, ranges = lax.optimization_barrier(
+        (resid_in, late, cotangent, stacked, modulation, cosine, sine, ranges)
     )
     (normed_one,) = rowwise(
         norm_kernel,
@@ -755,7 +758,8 @@
     grad_proj = attend_backward(
         ranges, queries, keys, projected, mixed_heads, grad_heads, logsum, cosine, sine, seg_column, seg_row
     )
-    grad_proj, block_out = lax.optimization_barrier((grad_proj, block_out))
+    grad_proj, block_out, grad_up = lax.optimization_barrier((grad_proj, block_out, grad_up))
+    grad_up = lax.psum_scatter(grad_up, ("hi", "lo"), scatter_dimension=0, tiled=True)
     grad_qkv = lax.dot_general(normed_row, grad_proj, (((0,), (0,)), ((), ())), preferred_element_type=f32)
     grad_qkv = grad_qkv.astype(bf16)
     grad_proj, grad_qkv = lax.optimization_barrier((grad_proj, grad_qkv))
@@ -804,18 +808,9 @@
     grad_mod = jnp.stack([v[:labels] for v in (grad_shift_one, grad_scale_one, grad_shift_two, grad_scale_two)], axis=1)
     grad_mod = jnp.moveaxis(grad_mod.reshape(labels, devices, own_columns), 1, 0)
     grad_mod = lax.all_to_all(grad_mod, ALL_AXES, split_axis=0, concat_axis=0, tiled=True)
-    grad_in_home, grad_qkv, grad_up, grad_down, grad_mod = lax.optimization_barrier(
-        (grad_in_home, grad_qkv, grad_up, grad_down, grad_mod)
-    )
-    both = jnp.concatenate(
-        [grad_up[:, i * width : (i + 1) * width].reshape(line, -1, width) for i in range(columns)]
-        + [grad_down.reshape(line, -1, width)],
-        axis=1,
-    )
-    both = lax.psum_scatter(both.reshape(-1, width), ("hi", "lo"), scatter_dimension=0, tiled=True).astype(f32)
-    taken = columns * up_rows
-    grad_up = jnp.concatenate([both[i * up_rows : (i + 1) * up_rows] for i in range(columns)], axis=1)
-    grad_down = both[taken:]
+    grad_in_home, grad_qkv, grad_down, grad_mod = lax.optimization_barrier((grad_in_home, grad_qkv, grad_down, grad_mod))
+    grad_down = lax.psum_scatter(grad_down, ("hi", "lo"), scatter_dimension=0, tiled=True)
+    grad_up, grad_down = grad_up.astype(f32), grad_down.astype(f32)
     if group == 2:
         grad_qkv = grad_qkv.reshape(line, -1, 4 * width)
         grad_qkv = lax.all_to_all(grad_qkv, ("hi", "lo"), split_axis=0, concat_axis=0, tiled=True)
@@ -824,13 +819,7 @@
     else:
         grad_out = exchange_line(exchange_planes(grad_out))
     home = grad_in_home.reshape(frames, width)
-    grad_skip_w = jnp.concatenate(
-        [
-            lax.dot_general(v, home, (((0,), (0,)), ((), ())), preferred_element_type=f32).astype(bf16)
-            for v in (x, s)
-        ],
-        axis=0,
-    )
+    grad_skip_w = lax.dot_general(stacked, home, (((0,), (0,)), ((), ())), preferred_element_type=f32).astype(bf16)
     grad_skip_w = exchange_planes(over_cores(grad_skip_w.reshape(planes, 2, -1, width), 1))
     grad_inputs, grad_skips = rowwise(
         unmerge_kernel,

time: 678 us -> 671 us (0.990)
  starting transfers between devices: 116 us -> 85.9 us
  waiting for transfers between devices: 131 us -> 154 us
  local copies, waits for them, and re-layouts: 52.1 us -> 43.5 us
  Pallas kernels: 276 us -> 284 us
    ppermute x2, waiting for transfers between devices: 0.01 us -> 26.3 us  [to_rows(): lax.ppermute(lax.dynamic_index_in_dim(value, 1 - odd_place, 0, False), LI...]
    ppermute x1, starting transfers between devices: 20.1 us -> 0.01 us  [frames_to_row(): other = lax.ppermute(value, 'core', swap)]
    all_to_all x1, waiting for transfers between devices: 2.1 us -> 19.9 us  [body(): lax.all_to_all(grad_mod, ALL_AXES, split_axis=0, concat_axis=0, tiled=True)]
    ppermute x9, starting transfers between devices: 31.4 us -> 14.8 us  [exchange(): lax.ppermute(sent, axes, [(i, i ^ flip) for i in range(count)]).astype(f32)]
    ppermute x9, waiting for transfers between devices: 42.7 us -> 32.9 us  [exchange(): lax.ppermute(sent, axes, [(i, i ^ flip) for i in range(count)]).astype(f32)]
    all_to_all x1, waiting for transfers between devices: 19.6 us -> 9.99 us  [body(): lax.all_to_all(grad_qkv, ('hi', 'lo'), split_axis=0, concat_axis=0, tiled...]
    ppermute x2, starting transfers between devices: 4 us -> 11.5 us  [to_rows(): lax.ppermute(lax.dynamic_index_in_dim(value, odd_place, 0, False), LINE_A...]
    unnamed x88 -> x68, local copies, waits for them, and re-layouts: 20.7 us -> 13.6 us
  transfers between devices with their start and end apart: 43 -> 44, of which waited for: 13 -> 16; matrix products, arithmetic and copies ran while one was open for 14% -> 16% of each run, Pallas kernels for 31% -> 33%
where the time goes in v9:
time: 671 us; the launch traced here: 664 us
  Pallas kernels  284 us (42%)
  waiting for transfers between devices  154 us (23%)
  starting transfers between devices  85.9 us (13%)
  other arithmetic  52.1 us (8%)
  local copies, waits for them, and re-layouts  43.5 us (6%)
  matrix products  20.4 us (3%)
  between operations  15.1 us (2%)
  blocking collectives  8.86 us (1%)
    pallas_call x1, Pallas kernels, attend_backward(): pl.pallas_call(attend_backward_kernel, grid_spec=pltpu.PrefetchScalarGrid...  78 us
    pallas_call x1, Pallas kernels, feed_forward_and_back(): pl.pallas_call(feed_kernel, grid=(hidden // piece,), in_specs=[whole(), w...  66.3 us
    pallas_call x1, Pallas kernels, attend_forward(): pl.pallas_call(attend_forward_kernel, grid_spec=pltpu.PrefetchScalarGridS...  62.2 us
    ppermute x9, waiting for transfers between devices, share_on_line(): lax.ppermute(value, ('hi', 'lo'), [(i, i ^ flip) for i in range(line)])  60.1 us
    pallas_call x6, Pallas kernels, rowwise(): pl.pallas_call(kernel, grid=(frames // tile,), in_specs=in_specs, out_spe...  50.4 us
    ppermute x9, waiting for transfers between devices, exchange(): lax.ppermute(sent, axes, [(i, i ^ flip) for i in range(count)]).astype(f32)  32.9 us
    ppermute x2, waiting for transfers between devices, to_rows(): lax.ppermute(lax.dynamic_index_in_dim(value, 1 - odd_place, 0, False), LI...  26.3 us
    all_to_all x1, waiting for transfers between devices, body(): lax.all_to_all(grad_mod, ALL_AXES, split_axis=0, concat_axis=0, tiled=True)  19.9 us
  transfers between devices with their start and end apart: 44, of which 16 were waited for; matrix products, arithmetic and copies ran while one was open for 16% of the time, Pallas kernels for 33%

profile of v9, /device:TPU:0, one launch (start us, length us, event | category | flops | bytes accessed | tf_op | source)
XLA Modules:
  0.0 664.2 jit_solution(12534653822029261885)
XLA Ops:
  37.1 12.2 %collective-permute-done.11 = bf16[128,1024]{1,0:T(8,128)(2,1)S(1)} collective-permute-done((bf16[128,1024]{1,0:T(8,128)(2,1)S(1)}, bf16[128,1024]{1,0:T(8,128)(2,1)S(1)}, u32[]{:S(2)}, u32[]{:S(2)}) %collective-permute-start.11) | collective-permute-done | bytes 262176 | tf_op jit(solution)/shard_map/ppermute | solution.py:596
  59.3 8.2 %collective-permute-done.7 = bf16[256,1024]{1,0:T(8,128)(2,1)S(1)} collective-permute-done((bf16[256,1024]{1,0:T(8,128)(2,1)S(1)}, bf16[256,1024]{1,0:T(8,128)(2,1)S(1)}, u32[]{:S(2)}, u32[]{:S(2)}) %collective-permute-start.7) | collective-permute-done | bytes 524320 | tf_op jit(solution)/shard_map/ppermute | solution.py:596
  67.6 27.2 %collective-permute-done.6 = bf16[256,1024]{1,0:T(8,128)(2,1)S(1)} collective-permute-done((bf16[256,1024]{1,0:T(8,128)(2,1)S(1)}, bf16[256,1024]{1,0:T(8,128)(2,1)S(1)}, u32[]{:S(2)}, u32[]{:S(2)}) %collective-permute-start.6) | collective-permute-done | bytes 524320 | tf_op jit(solution)/shard_map/ppermute | solution.py:596
  96.9 8.7 %shard_map.178 = bf16[1024,1024]{1,0:T(8,128)(2,1)} custom-call(bf16[1024,1024]{1,0:T(8,128)(2,1)} %bitcast.167, bf16[1024,1024]{1,0:T(8,128)(2,1)} %bitcast.170, bf16[32,64,1024]{2,1,0:T(8,128)(2,1)} %all-gather.5.cloned.1.call-done.top_ref.bottom_ref, bf16[32,64,1024]{2,1,0:T(8,128)(2,1)} %all-gather.5.cloned.1.call-done.top_ref.bottom_ref), custom_call_target="tpu_custom_call" | custom-call | flops 1 | bytes 1 | tf_op jit(solution)/shard_map/pallas_call | solution.py:223
  105.6 8.9 %all-gather = s32[16,1,4]{2,1,0:T(1,128)S(1)} all-gather(s32[2,1,4]{2,1,0:T(1,128)S(1)} %copy-done.27), channel_id=2, replica_groups=mesh['plane'=4,'core'=2,'hi'=4,'lo'=1] {'plane','core'}, dimensions={0}, use_global_device_ids=true | all-gather | bytes 288 | tf_op jit(solution)/shard_map/all_gather | solution.py:656
  123.0 9.5 %collective-permute-start.3 = (bf16[512,1024]{1,0:T(8,128)(2,1)}, bf16[512,1024]{1,0:T(8,128)(2,1)}, u32[]{:S(2)}, u32[]{:S(2)}) collective-permute-start(bf16[512,1024]{1,0:T(8,128)(2,1)} %get-tuple-element.206), channel_id=1, source_target_pairs={{0,0},{1,1},{2,4},{3,5},{4,2},{5,3},{6,6},{7,7},{8,8},{9,9},{10,12... | collective-permute-start | bytes 3145736 | tf_op jit(solution)/shard_map/ppermute | solution.py:562
  142.6 26.2 %collective-permute-done.4 = bf16[512,1024]{1,0:T(8,128)(2,1)} collective-permute-done((bf16[512,1024]{1,0:T(8,128)(2,1)}, bf16[512,1024]{1,0:T(8,128)(2,1)}, u32[]{:S(2)}, u32[]{:S(2)}) %collective-permute-start.4) | collective-permute-done | bytes 1048608 | tf_op jit(solution)/shard_map/ppermute | solution.py:563
  199.0 11.0 %shard_map.180.q_ref.k_ref.v_ref = bf16[2048,1536]{1,0:T(8,128)(2,1)} custom-call(s32[1]{0:T(128)} %bitcast.21.place_ref, bf16[2048,1024]{1,0:T(8,128)(2,1)} %pad_maximum_fusion.1.x_ref, bf16[32,128,1024]{2,1,0:T(8,128)(2,1)} %all-gather.7.cloned.1.call-done.w_ref.q_ref.k_ref.v_ref), custom_call_target="tpu_custom_call" | custom-call | flops 1 | bytes 1 | tf_op jit(solution)/shard_map/pallas_call | solution.py:151
  210.0 62.2 %shard_map.181 = (bf16[2048,512]{1,0:T(8,128)(2,1)}, bf16[2048,512]{1,0:T(8,128)(2,1)}, bf16[2048,512]{1,0:T(8,128)(2,1)}, f32[4,2,2048]{2,1,0:T(2,128)}) custom-call(s32[2,8]{1,0:T(2,128)} %pad_add_fusion.range_ref, bf16[2048,1536]{1,0:T(8,128)(2,1)} %shard_map.180.q_ref.k_ref.v_ref, bf16[2048,1536]{1,0:T(8,128)(2,1)} %shard_map.180.q_ref.k_ref.v_ref, ...), custom_call_target="tpu_custom_call" | custom-call | flops 17179869184 | bytes 14680064 | tf_op jit(solution)/shard_map/pallas_call | solution.py:316
  280.3 8.2 %shard_map.182 = (f32[1024,1024]{1,0:T(8,128)}, bf16[1024,1024]{1,0:T(8,128)(2,1)}) custom-call(bf16[1024,1024]{1,0:T(8,128)(2,1)} %pad_maximum_fusion.5.mixed_ref, bf16[32,128,1024]{2,1,0:T(8,128)(2,1)} %all-gather.7.cloned.1.call-done.w_ref.q_ref.k_ref.v_ref, bf16[1024,1024]{1,0:T(8,128)(2,1)} %pad_maximum_fusion.2.resid_ref.resid_in_ref, ...), custom_call_target="tpu_custom_call" | custom-call | flops 2147483648 | bytes 18911232 | tf_op jit(solution)/shard_map/pallas_call | solution.py:223
  288.5 66.3 %shard_map.183 = (bf16[1024,1024]{1,0:T(8,128)(2,1)}, f32[1024,1024]{1,0:T(8,128)}, bf16[1024,4096]{1,0:T(8,128)(2,1)}, bf16[4096,1024]{1,0:T(8,128)(2,1)}) custom-call(bf16[1024,1024]{1,0:T(8,128)(2,1)} %get-tuple-element.69.n_ref, bf16[1024,1024]{1,0:T(8,128)(2,1)} %pad_maximum_fusion.6.cot_ref, f32[1024,1024]{1,0:T(8,128)} %get-tuple-element.71.resid_ref, ...), custom_call_target="tpu_custom_call" | custom-call | flops 51539607552 | bytes 50331648 | tf_op jit(solution)/shard_map/pallas_call | solution.py:507
  355.5 10.5 %shard_map.184 = (f32[1024,1024]{1,0:T(8,128)}, bf16[1024,1024]{1,0:T(8,128)(2,1)}, bf16[1024,1024]{1,0:T(8,128)(2,1)}, f32[8,1024]{1,0:T(8,128)}, f32[8,1024]{1,0:T(8,128)}) custom-call(f32[1024,1024]{1,0:T(8,128)} %get-tuple-element.73.g_ref, f32[1024,1024]{1,0:T(8,128)} %get-tuple-element.71.resid_ref, bf16[1024,1024]{1,0:T(8,128)(2,1)} %pad_maximum_fusion.6.cot_ref, ...), custom_call_target="tpu_custom_call" | custom-call | flops 1 | bytes 1 | tf_op jit(solution)/shard_map/pallas_call | solution.py:223
  389.4 78.0 %shard_map.185.dq_ref.dk_ref.dv_ref = bf16[2048,1536]{1,0:T(8,128)(2,1)} custom-call(s32[2,8]{1,0:T(2,128)} %pad_add_fusion.range_ref, bf16[2048,512]{1,0:T(8,128)(2,1)} %get-tuple-element.66.q_ref, bf16[2048,512]{1,0:T(8,128)(2,1)} %get-tuple-element.67.k_ref, bf16[2048,1536]{1,0:T(8,128)(2,1)} %shard_map.180.q_ref.k_ref.v_ref, ...), custom_call_target="tpu_custom_call" | custom-call | flops 42949672960 | bytes 16777216 | tf_op jit(solution)/shard_map/pallas_call | solution.py:420
  469.9 9.7 %convolution_convert_fusion = bf16[1024,1536]{1,0:T(8,128)(2,1)S(1)} fusion(bf16[2048,1536]{1,0:T(8,128)(2,1)} %shard_map.185.dq_ref.dk_ref.dv_ref, bf16[1024,1024]{1,0:T(8,128)(2,1)} %copy-done.7, bf16[1024,1024]{1,0:T(8,128)(2,1)S(1)} %copy-done.6), kind=kOutput, calls=%fused_computation.12 | convolution fusion | flops 6452412416 | bytes 13631488 | tf_op jit(solution)/shard_map/dot_general | solution.py:763
  484.7 7.9 %shard_map.187 = bf16[1024,1024]{1,0:T(8,128)(2,1)} custom-call(s32[2]{0:T(128)} %pad_add_fusion.2.place_ref, bf16[2048,1536]{1,0:T(8,128)(2,1)} %shard_map.185.dq_ref.dk_ref.dv_ref, bf16[2048,1536]{1,0:T(8,128)(2,1)} %shard_map.185.dq_ref.dk_ref.dv_ref, bf16[2048,1536]{1,0:T(8,128)(2,1)} %shard_map.185.dq_ref.dk_ref.dv_ref, ...), custom_call_target="tpu_custom_call" | custom-call | flops 3221225472 | bytes 8388608 | tf_op jit(solution)/shard_map/pallas_call | solution.py:186
  492.6 8.1 %shard_map.186.own_ref = f32[1024,1024]{1,0:T(8,128)} custom-call(s32[2]{0:T(128)} %pad_add_fusion.1.place_ref, bf16[2048,1536]{1,0:T(8,128)(2,1)} %shard_map.185.dq_ref.dk_ref.dv_ref, bf16[2048,1536]{1,0:T(8,128)(2,1)} %shard_map.185.dq_ref.dk_ref.dv_ref, bf16[2048,1536]{1,0:T(8,128)(2,1)} %shard_map.185.dq_ref.dk_ref.dv_ref, ...), custom_call_target="tpu_custom_call" | custom-call | flops 3221225472 | bytes 8388608 | tf_op jit(solution)/shard_map/pallas_call | solution.py:186
  511.5 9.0 %shard_map.188 = (bf16[1024,1024]{1,0:T(8,128)(2,1)}, f32[8,1024]{1,0:T(8,128)}, f32[8,1024]{1,0:T(8,128)}) custom-call(f32[1024,1024]{1,0:T(8,128)} %shard_map.186.own_ref, bf16[1024,1024]{1,0:T(8,128)(2,1)} %collective-permute-done.21.other_ref, bf16[1024,1024]{1,0:T(8,128)(2,1)} %pad_maximum_fusion.2.resid_ref.resid_in_ref, ...), custom_call_target="tpu_custom_call" | custom-call | bytes 14704640 | tf_op jit(solution)/shard_map/pallas_call | solution.py:223
  523.6 9.5 %collective-permute-start.22 = (bf16[512,1024]{1,0:T(8,128)(2,1)}, bf16[512,1024]{1,0:T(8,128)(2,1)}, u32[]{:S(2)}, u32[]{:S(2)}) collective-permute-start(bf16[512,1024]{1,0:T(8,128)(2,1)} %get-tuple-element.190), channel_id=1, source_target_pairs={{0,0},{1,1},{4,2},{5,3},{2,4},{3,5},{6,6},{7,7},{8,8},{9,9},{12,10... | collective-permute-start | bytes 3145736 | tf_op jit(solution)/shard_map/ppermute | solution.py:568
  541.7 16.6 %collective-permute-done.25 = bf16[128,4096]{1,0:T(8,128)(2,1)} collective-permute-done((bf16[128,4096]{1,0:T(8,128)(2,1)}, bf16[128,4096]{1,0:T(8,128)(2,1)}, u32[]{:S(2)}, u32[]{:S(2)}) %collective-permute-start.25) | collective-permute-done | bytes 1048608 | tf_op jit(solution)/shard_map/ppermute | solution.py:731
  568.2 19.9 %all-to-all-done.1 = f32[32,4,128]{2,1,0:T(4,128)S(1)} async-done(((f32[32,4,128]{2,1,0:T(4,128)}), f32[32,4,128]{2,1,0:T(4,128)S(1)}, u32[]{:S(2)}, u32[]{:S(2)}) %all-to-all-start.1) | async-done | bytes 65568 | tf_op jit(solution)/shard_map/all_to_all | solution.py:810
  588.2 7.2 %convolution_convert_fusion.1 = bf16[2048,1024]{1,0:T(8,128)(2,1)S(1)} fusion(bf16[1024,2048]{1,0:T(8,128)(2,1)} %pad_maximum_fusion, bf16[1024,1024]{1,0:T(8,128)(2,1)S(1)} %bitcast.180), kind=kOutput, calls=%fused_computation.13 | convolution fusion | flops 4297064448 | bytes 10485760 | tf_op jit(solution)/shard_map/dot_general | solution.py:822
  612.4 8.4 %shard_map.189 = (bf16[1024,1024]{1,0:T(8,128)(2,1)}, bf16[1024,1024]{1,0:T(8,128)(2,1)}) custom-call(bf16[1024,1024]{1,0:T(8,128)(2,1)} %bitcast.181, bf16[32,64,1024]{2,1,0:T(8,128)(2,1)} %all-gather.5.cloned.1.call-done.top_ref.bottom_ref, bf16[32,64,1024]{2,1,0:T(8,128)(2,1)} %all-gather.5.cloned.1.call-done.top_ref.bottom_ref), custom_call_target="tpu_custom_call" | custom-call | flops 4294967296 | bytes 14680064 | tf_op jit(solution)/shard_map/pallas_call | solution.py:223
  623.1 11.0 %collective-permute-done.30 = bf16[256,1024]{1,0:T(8,128)(2,1)} collective-permute-done((bf16[256,1024]{1,0:T(8,128)(2,1)}, bf16[256,1024]{1,0:T(8,128)(2,1)}, u32[]{:S(2)}, u32[]{:S(2)}) %collective-permute-start.30) | collective-permute-done | bytes 524320 | tf_op jit(solution)/shard_map/ppermute | solution.py:731
  641.1 10.0 %all-to-all-done.2 = bf16[4,32,4096]{2,1,0:T(8,128)(2,1)S(1)} async-done(((bf16[4,32,4096]{2,1,0:T(8,128)(2,1)}), bf16[4,32,4096]{2,1,0:T(8,128)(2,1)S(1)}, u32[]{:S(2)}, u32[]{:S(2)}) %all-to-all-start.2) | async-done | bytes 1048608 | tf_op jit(solution)/shard_map/all_to_all | solution.py:816
  (247 shorter events, 194.6 us)
Async XLA Ops:
  7.2 89.7 %all-gather.5.cloned.1.call-start = ((), (), s32[]{:S(2)}) async-start(), calls=%async_computation.7 | async-start | bytes 4718592 | tf_op jit(solution)/shard_map/all_gather | solution.py:601
  25.8 173.1 %all-gather.7.cloned.1.call-start = ((), (), s32[]{:S(2)}) async-start(), calls=%async_computation.8 | async-start | bytes 9437184 | tf_op jit(solution)/shard_map/all_gather | solution.py:601
  52.3 42.5 %collective-permute-start.6 = (bf16[256,1024]{1,0:T(8,128)(2,1)S(1)}, bf16[256,1024]{1,0:T(8,128)(2,1)S(1)}, u32[]{:S(2)}, u32[]{:S(2)}) collective-permute-start(bf16[256,1024]{1,0:T(8,128)(2,1)S(1)} %slice_dynamic-update-slice_fusion.6), channel_id=1, source_target_pairs={{0,2},{1,3},{2,0},{3,1},{4,6},{5,7},{6,4},{7,5},{8,10},{9,11},{10,... | collective-permute-start | bytes 1572872 | tf_op jit(solution)/shard_map/ppermute | solution.py:596
  52.3 42.5 %collective-permute-start.5 = (bf16[256,1024]{1,0:T(8,128)(2,1)S(1)}, bf16[256,1024]{1,0:T(8,128)(2,1)S(1)}, u32[]{:S(2)}, u32[]{:S(2)}) collective-permute-start(bf16[256,1024]{1,0:T(8,128)(2,1)S(1)} %slice_dynamic-update-slice_fusion.6), channel_id=1, source_target_pairs={{0,1},{1,0},{2,3},{3,2},{4,5},{5,4},{6,7},{7,6},{8,9},{9,8},{10,11... | collective-permute-start | bytes 1572872 | tf_op jit(solution)/shard_map/ppermute | solution.py:596
  116.6 55.5 %all-to-all-start = ((f32[32,4,128]{2,1,0:T(4,128)}), f32[32,4,128]{2,1,0:T(4,128)S(1)}, u32[]{:S(2)}, u32[]{:S(2)}) async-start(f32[32,4,128]{2,1,0:T(4,128)} %bitcast.14), calls=%async_computation | async-start | bytes 131072 | tf_op jit(solution)/shard_map/all_to_all | solution.py:665
  119.9 168.5 %all-gather.9.cloned.1.call-start = ((), (), s32[]{:S(2)}) async-start(), calls=%async_computation.9 | async-start | bytes 18874368 | tf_op jit(solution)/shard_map/all_gather | solution.py:601
  132.5 36.4 %collective-permute-start.4 = (bf16[512,1024]{1,0:T(8,128)(2,1)}, bf16[512,1024]{1,0:T(8,128)(2,1)}, u32[]{:S(2)}, u32[]{:S(2)}) collective-permute-start(bf16[512,1024]{1,0:T(8,128)(2,1)} %get-tuple-element.207), channel_id=1, source_target_pairs={{0,1},{1,0},{2,5},{3,4},{4,3},{5,2},{6,7},{7,6},{8,9},{9,8},{10,13... | collective-permute-start | bytes 3145736 | tf_op jit(solution)/shard_map/ppermute | solution.py:563
  172.2 296.9 %reduce-scatter.5.cloned.1.call-start = ((), (), s32[]{:S(2)}) async-start(), calls=%async_computation.10 | async-start | bytes 9437184 | tf_op jit(solution)/shard_map/reduce_scatter | solution.py:741
  184.2 91.5 %collective-permute-start.14 = (bf16[512,1024]{1,0:T(8,128)(2,1)}, bf16[512,1024]{1,0:T(8,128)(2,1)S(1)}, u32[]{:S(2)}, u32[]{:S(2)}) collective-permute-start(bf16[512,1024]{1,0:T(8,128)(2,1)} %get-tuple-element.198), channel_id=1, source_target_pairs={{0,0},{1,1},{2,4},{3,5},{4,2},{5,3},{6,6},{7,7},{8,8},{9,9},{10,12... | collective-permute-start | bytes 3145736 | tf_op jit(solution)/shard_map/ppermute | solution.py:562
  186.2 89.4 %collective-permute-start.15 = (bf16[512,1024]{1,0:T(8,128)(2,1)}, bf16[512,1024]{1,0:T(8,128)(2,1)S(1)}, u32[]{:S(2)}, u32[]{:S(2)}) collective-permute-start(bf16[512,1024]{1,0:T(8,128)(2,1)} %get-tuple-element.199), channel_id=1, source_target_pairs={{0,1},{1,0},{2,5},{3,4},{4,3},{5,2},{6,7},{7,6},{8,9},{9,8},{10,13... | collective-permute-start | bytes 3145736 | tf_op jit(solution)/shard_map/ppermute | solution.py:563
  354.8 213.4 %reduce-scatter.7.cloned.1.call-start = ((), (), s32[]{:S(2)}) async-start(), calls=%async_computation.11 | async-start | bytes 9437184 | tf_op jit(solution)/shard_map/reduce_scatter | solution.py:741
  373.9 227.8 %reduce-scatter.9.cloned.1.call-start = ((), (), s32[]{:S(2)}) async-start(), calls=%async_computation.12 | async-start | bytes 1310720 | tf_op jit(solution)/shard_map/reduce_scatter | solution.py:762
  382.5 84.9 %collective-permute-start.18 = (bf16[512,1024]{1,0:T(8,128)(2,1)}, bf16[512,1024]{1,0:T(8,128)(2,1)S(1)}, u32[]{:S(2)}, u32[]{:S(2)}) collective-permute-start(bf16[512,1024]{1,0:T(8,128)(2,1)} %get-tuple-element.194), channel_id=1, source_target_pairs={{0,0},{1,1},{4,2},{5,3},{2,4},{3,5},{6,6},{7,7},{8,8},{9,9},{12,10... | collective-permute-start | bytes 3145736 | tf_op jit(solution)/shard_map/ppermute | solution.py:568
  384.4 83.0 %collective-permute-start.19 = (bf16[512,1024]{1,0:T(8,128)(2,1)S(1)}, bf16[512,1024]{1,0:T(8,128)(2,1)S(1)}, u32[]{:S(2)}, u32[]{:S(2)}) collective-permute-start(bf16[512,1024]{1,0:T(8,128)(2,1)S(1)} %get-tuple-element.195), channel_id=1, source_target_pairs={{1,0},{0,1},{5,2},{4,3},{3,4},{2,5},{7,6},{6,7},{9,8},{8,9},{13,10... | collective-permute-start | bytes 3145736 | tf_op jit(solution)/shard_map/ppermute | solution.py:569
  504.2 37.5 %collective-permute-start.24 = (bf16[128,4096]{1,0:T(8,128)(2,1)}, bf16[128,4096]{1,0:T(8,128)(2,1)}, u32[]{:S(2)}, u32[]{:S(2)}) collective-permute-start(bf16[128,4096]{1,0:T(8,128)(2,1)} %get-tuple-element.172), channel_id=1, source_target_pairs={{0,8},{8,0},{16,24},{24,16},{1,9},{9,1},{17,25},{25,17},{2,10},{10... | collective-permute-start | bytes 3145736 | tf_op jit(solution)/shard_map/ppermute | solution.py:731
  510.0 48.3 %collective-permute-start.25 = (bf16[128,4096]{1,0:T(8,128)(2,1)}, bf16[128,4096]{1,0:T(8,128)(2,1)}, u32[]{:S(2)}, u32[]{:S(2)}) collective-permute-start(bf16[128,4096]{1,0:T(8,128)(2,1)} %get-tuple-element.173), channel_id=1, source_target_pairs={{0,16},{8,24},{16,0},{24,8},{1,17},{9,25},{17,1},{25,9},{2,18},{10... | collective-permute-start | bytes 3145736 | tf_op jit(solution)/shard_map/ppermute | solution.py:731
  510.0 48.3 %collective-permute-start.26 = (bf16[128,4096]{1,0:T(8,128)(2,1)}, bf16[128,4096]{1,0:T(8,128)(2,1)}, u32[]{:S(2)}, u32[]{:S(2)}) collective-permute-start(bf16[128,4096]{1,0:T(8,128)(2,1)} %get-tuple-element.174), channel_id=1, source_target_pairs={{0,24},{8,16},{16,8},{24,0},{1,25},{9,17},{17,9},{25,1},{2,26},{10... | collective-permute-start | bytes 3145736 | tf_op jit(solution)/shard_map/ppermute | solution.py:731
  523.6 38.2 %collective-permute-start.22 = (bf16[512,1024]{1,0:T(8,128)(2,1)}, bf16[512,1024]{1,0:T(8,128)(2,1)}, u32[]{:S(2)}, u32[]{:S(2)}) collective-permute-start(bf16[512,1024]{1,0:T(8,128)(2,1)} %get-tuple-element.190), channel_id=1, source_target_pairs={{0,0},{1,1},{4,2},{5,3},{2,4},{3,5},{6,6},{7,7},{8,8},{9,9},{12,10... | collective-permute-start | bytes 3145736 | tf_op jit(solution)/shard_map/ppermute | solution.py:568
  533.1 33.2 %collective-permute-start.23 = (bf16[512,1024]{1,0:T(8,128)(2,1)}, bf16[512,1024]{1,0:T(8,128)(2,1)}, u32[]{:S(2)}, u32[]{:S(2)}) collective-permute-start(bf16[512,1024]{1,0:T(8,128)(2,1)} %get-tuple-element.191), channel_id=1, source_target_pairs={{1,0},{0,1},{5,2},{4,3},{3,4},{2,5},{7,6},{6,7},{9,8},{8,9},{13,10... | collective-permute-start | bytes 3145736 | tf_op jit(solution)/shard_map/ppermute | solution.py:569
  535.6 52.5 %all-to-all-start.1 = ((f32[32,4,128]{2,1,0:T(4,128)}), f32[32,4,128]{2,1,0:T(4,128)S(1)}, u32[]{:S(2)}, u32[]{:S(2)}) async-start(f32[32,4,128]{2,1,0:T(4,128)} %copy.107), calls=%async_computation.3 | async-start | bytes 131072 | tf_op jit(solution)/shard_map/all_to_all | solution.py:810
  541.6 111.0 %reduce-scatter.11.cloned.1.call-start = ((), (), s32[]{:S(2)}) async-start(), calls=%async_computation.13 | async-start | bytes 1310720 | tf_op jit(solution)/shard_map/reduce_scatter | solution.py:812
  598.2 52.8 %all-to-all-start.2 = ((bf16[4,32,4096]{2,1,0:T(8,128)(2,1)}), bf16[4,32,4096]{2,1,0:T(8,128)(2,1)S(1)}, u32[]{:S(2)}, u32[]{:S(2)}) async-start(bf16[4,32,4096]{2,1,0:T(8,128)(2,1)} %bitcast.83), calls=%async_computation.4 | async-start | bytes 2097152 | tf_op jit(solution)/shard_map/all_to_all | solution.py:816
  608.8 25.2 %collective-permute-start.30 = (bf16[256,1024]{1,0:T(8,128)(2,1)}, bf16[256,1024]{1,0:T(8,128)(2,1)}, u32[]{:S(2)}, u32[]{:S(2)}) collective-permute-start(bf16[256,1024]{1,0:T(8,128)(2,1)} %get-tuple-element.186), channel_id=1, source_target_pairs={{0,24},{8,16},{16,8},{24,0},{1,25},{9,17},{17,9},{25,1},{2,26},{10... | collective-permute-start | bytes 1572872 | tf_op jit(solution)/shard_map/ppermute | solution.py:731
  610.2 24.9 %collective-permute-start.29 = (bf16[256,1024]{1,0:T(8,128)(2,1)S(1)}, bf16[256,1024]{1,0:T(8,128)(2,1)}, u32[]{:S(2)}, u32[]{:S(2)}) collective-permute-start(bf16[256,1024]{1,0:T(8,128)(2,1)S(1)} %get-tuple-element.187), channel_id=1, source_target_pairs={{0,16},{8,24},{16,0},{24,8},{1,17},{9,25},{17,1},{25,9},{2,18},{10... | collective-permute-start | bytes 1572872 | tf_op jit(solution)/shard_map/ppermute | solution.py:731
  (49 other events, 616.5 us)
Sparse Core Ops, SparseCore 0:
  25.9 36.9 all-gather.4
  64.8 54.3 all-gather.6
  172.3 95.3 all-gather.8
  354.9 77.1 reduce-scatter.4
  435.9 71.2 reduce-scatter.6
  511.6 36.5 reduce-scatter.8
  598.3 41.9 reduce-scatter.10

commit v10 on v9

--- a/solution.py
+++ b/solution.py
@@ -629,7 +629,6 @@
         merge_kernel, frames, [("", x), ("", s), ("weight", skip_top), ("weight", skip_bottom)], [(width, bf16)], light=True
     )
     stacked = jnp.concatenate([x, s], axis=1)
-    resid_in, segment_ids, time_steps = lax.optimization_barrier((resid_in, segment_ids, time_steps))
 
     labels_own = segment_ids[:, 0]
     labels_other = lax.ppermute(labels_own, "core", swap)

time: 671 us -> 666 us (level)
  waiting for transfers between devices: 154 us -> 126 us
  starting transfers between devices: 85.9 us -> 107 us
    ppermute x2, waiting for transfers between devices: 26.3 us -> 0.01 us  [to_rows(): lax.ppermute(lax.dynamic_index_in_dim(value, 1 - odd_place, 0, False), LI...]
    ppermute x1, starting transfers between devices: 0.01 us -> 20 us  [frames_to_row(): other = lax.ppermute(value, 'core', swap)]
    ppermute x9, starting transfers between devices: 14.8 us -> 26.5 us  [exchange(): lax.ppermute(sent, axes, [(i, i ^ flip) for i in range(count)]).astype(f32)]
    all_to_all x1, waiting for transfers between devices: 19.9 us -> 9.83 us  [body(): lax.all_to_all(grad_mod, ALL_AXES, split_axis=0, concat_axis=0, tiled=True)]
    ppermute x2, starting transfers between devices: 11.5 us -> 3.74 us  [to_rows(): lax.ppermute(lax.dynamic_index_in_dim(value, odd_place, 0, False), LINE_A...]
  transfers between devices with their start and end apart: 44 -> 44, of which waited for: 16 -> 13; matrix products, arithmetic and copies ran while one was open for 16% -> 17% of each run, Pallas kernels for 33% -> 33%
where the time goes in v10:
time: 666 us; the launch traced here: 661 us
  Pallas kernels  284 us (43%)
  waiting for transfers between devices  126 us (19%)
  starting transfers between devices  107 us (16%)
  other arithmetic  53.3 us (8%)
  local copies, waits for them, and re-layouts  46.8 us (7%)
  matrix products  20.5 us (3%)
  between operations  15.1 us (2%)
  blocking collectives  8.92 us (1%)
    pallas_call x1, Pallas kernels, attend_backward(): pl.pallas_call(attend_backward_kernel, grid_spec=pltpu.PrefetchScalarGrid...  78 us
    pallas_call x1, Pallas kernels, feed_forward_and_back(): pl.pallas_call(feed_kernel, grid=(hidden // piece,), in_specs=[whole(), w...  66.3 us
    pallas_call x1, Pallas kernels, attend_forward(): pl.pallas_call(attend_forward_kernel, grid_spec=pltpu.PrefetchScalarGridS...  62.2 us
    ppermute x9, waiting for transfers between devices, share_on_line(): lax.ppermute(value, ('hi', 'lo'), [(i, i ^ flip) for i in range(line)])  58.9 us
    pallas_call x6, Pallas kernels, rowwise(): pl.pallas_call(kernel, grid=(frames // tile,), in_specs=in_specs, out_spe...  50.5 us
    ppermute x9, waiting for transfers between devices, exchange(): lax.ppermute(sent, axes, [(i, i ^ flip) for i in range(count)]).astype(f32)  35.1 us
    ppermute x9, starting transfers between devices, exchange(): lax.ppermute(sent, axes, [(i, i ^ flip) for i in range(count)]).astype(f32)  26.5 us
    ppermute x1, starting transfers between devices, frames_to_row(): other = lax.ppermute(value, 'core', swap)  20 us
  transfers between devices with their start and end apart: 44, of which 13 were waited for; matrix products, arithmetic and copies ran while one was open for 17% of the time, Pallas kernels for 33%

profile of v10, /device:TPU:0, one launch (start us, length us, event | category | flops | bytes accessed | tf_op | source)
XLA Modules:
  0.0 661.1 jit_solution(6005521706914128828)
XLA Ops:
  37.1 12.2 %collective-permute-done.11 = bf16[128,1024]{1,0:T(8,128)(2,1)S(1)} collective-permute-done((bf16[128,1024]{1,0:T(8,128)(2,1)S(1)}, bf16[128,1024]{1,0:T(8,128)(2,1)S(1)}, u32[]{:S(2)}, u32[]{:S(2)}) %collective-permute-start.11) | collective-permute-done | bytes 262176 | tf_op jit(solution)/shard_map/ppermute | solution.py:596
  50.9 8.9 %all-gather = s32[16,1,4]{2,1,0:T(1,128)S(1)} all-gather(s32[2,1,4]{2,1,0:T(1,128)S(1)} %copy-done.27), channel_id=2, replica_groups=mesh['plane'=4,'core'=2,'hi'=4,'lo'=1] {'plane','core'}, dimensions={0}, use_global_device_ids=true | all-gather | bytes 288 | tf_op jit(solution)/shard_map/all_gather | solution.py:655
  79.2 8.6 %shard_map.178 = bf16[1024,1024]{1,0:T(8,128)(2,1)} custom-call(bf16[1024,1024]{1,0:T(8,128)(2,1)} %bitcast.167, bf16[1024,1024]{1,0:T(8,128)(2,1)} %bitcast.170, bf16[32,64,1024]{2,1,0:T(8,128)(2,1)} %all-gather.5.cloned.1.call-done.top_ref.bottom_ref, bf16[32,64,1024]{2,1,0:T(8,128)(2,1)} %all-gather.5.cloned.1.call-done.top_ref.bottom_ref), custom_call_target="tpu_custom_call" | custom-call | flops 1 | bytes 1 | tf_op jit(solution)/shard_map/pallas_call | solution.py:223
  96.4 37.4 %collective-permute-done.6 = bf16[256,1024]{1,0:T(8,128)(2,1)} collective-permute-done((bf16[256,1024]{1,0:T(8,128)(2,1)}, bf16[256,1024]{1,0:T(8,128)(2,1)}, u32[]{:S(2)}, u32[]{:S(2)}) %collective-permute-start.6) | collective-permute-done | bytes 524320 | tf_op jit(solution)/shard_map/ppermute | solution.py:596
  148.1 20.0 %collective-permute-start.9 = (bf16[1024,1024]{1,0:T(8,128)(2,1)}, bf16[1024,1024]{1,0:T(8,128)(2,1)}, u32[]{:S(2)}, u32[]{:S(2)}) collective-permute-start(bf16[1024,1024]{1,0:T(8,128)(2,1)} %shard_map.179), channel_id=1, source_target_pairs={{0,4},{4,0},{1,5},{5,1},{2,6},{6,2},{3,7},{7,3},{8,12},{12,8},{9,1... | collective-permute-start | bytes 6291464 | tf_op jit(solution)/shard_map/ppermute | solution.py:576
  174.2 12.0 %collective-permute-start.15 = (bf16[512,1024]{1,0:T(8,128)(2,1)}, bf16[512,1024]{1,0:T(8,128)(2,1)S(1)}, u32[]{:S(2)}, u32[]{:S(2)}) collective-permute-start(bf16[512,1024]{1,0:T(8,128)(2,1)} %get-tuple-element.193), channel_id=1, source_target_pairs={{0,1},{1,0},{2,5},{3,4},{4,3},{5,2},{6,7},{7,6},{8,9},{9,8},{10,13... | collective-permute-start | bytes 3145736 | tf_op jit(solution)/shard_map/ppermute | solution.py:563
  192.9 11.0 %shard_map.180.q_ref.k_ref.v_ref = bf16[2048,1536]{1,0:T(8,128)(2,1)} custom-call(s32[1]{0:T(128)} %bitcast.21.place_ref, bf16[2048,1024]{1,0:T(8,128)(2,1)} %pad_maximum_fusion.1.x_ref, bf16[32,128,1024]{2,1,0:T(8,128)(2,1)} %all-gather.7.cloned.1.call-done.w_ref.q_ref.k_ref.v_ref), custom_call_target="tpu_custom_call" | custom-call | flops 1 | bytes 1 | tf_op jit(solution)/shard_map/pallas_call | solution.py:151
  203.9 62.2 %shard_map.181 = (bf16[2048,512]{1,0:T(8,128)(2,1)}, bf16[2048,512]{1,0:T(8,128)(2,1)}, bf16[2048,512]{1,0:T(8,128)(2,1)}, f32[4,2,2048]{2,1,0:T(2,128)}) custom-call(s32[2,8]{1,0:T(2,128)} %pad_add_fusion.range_ref, bf16[2048,1536]{1,0:T(8,128)(2,1)} %shard_map.180.q_ref.k_ref.v_ref, bf16[2048,1536]{1,0:T(8,128)(2,1)} %shard_map.180.q_ref.k_ref.v_ref, ...), custom_call_target="tpu_custom_call" | custom-call | flops 17179869184 | bytes 14680064 | tf_op jit(solution)/shard_map/pallas_call | solution.py:316
  274.3 8.2 %shard_map.182 = (f32[1024,1024]{1,0:T(8,128)}, bf16[1024,1024]{1,0:T(8,128)(2,1)}) custom-call(bf16[1024,1024]{1,0:T(8,128)(2,1)} %pad_maximum_fusion.5.mixed_ref, bf16[32,128,1024]{2,1,0:T(8,128)(2,1)} %all-gather.7.cloned.1.call-done.w_ref.q_ref.k_ref.v_ref, bf16[1024,1024]{1,0:T(8,128)(2,1)} %pad_maximum_fusion.2.resid_ref.resid_in_ref, ...), custom_call_target="tpu_custom_call" | custom-call | flops 2147483648 | bytes 18911232 | tf_op jit(solution)/shard_map/pallas_call | solution.py:223
  282.5 66.3 %shard_map.183 = (bf16[1024,1024]{1,0:T(8,128)(2,1)}, f32[1024,1024]{1,0:T(8,128)}, bf16[1024,4096]{1,0:T(8,128)(2,1)}, bf16[4096,1024]{1,0:T(8,128)(2,1)}) custom-call(bf16[1024,1024]{1,0:T(8,128)(2,1)} %get-tuple-element.63.n_ref, bf16[1024,1024]{1,0:T(8,128)(2,1)} %pad_maximum_fusion.6.cot_ref, f32[1024,1024]{1,0:T(8,128)} %get-tuple-element.65.resid_ref, ...), custom_call_target="tpu_custom_call" | custom-call | flops 51539607552 | bytes 50331648 | tf_op jit(solution)/shard_map/pallas_call | solution.py:507
  349.6 10.5 %shard_map.184 = (f32[1024,1024]{1,0:T(8,128)}, bf16[1024,1024]{1,0:T(8,128)(2,1)}, bf16[1024,1024]{1,0:T(8,128)(2,1)}, f32[8,1024]{1,0:T(8,128)}, f32[8,1024]{1,0:T(8,128)}) custom-call(f32[1024,1024]{1,0:T(8,128)} %get-tuple-element.67.g_ref, f32[1024,1024]{1,0:T(8,128)} %get-tuple-element.65.resid_ref, bf16[1024,1024]{1,0:T(8,128)(2,1)} %pad_maximum_fusion.6.cot_ref, ...), custom_call_target="tpu_custom_call" | custom-call | flops 1 | bytes 1 | tf_op jit(solution)/shard_map/pallas_call | solution.py:223
  378.6 78.0 %shard_map.185.dq_ref.dk_ref.dv_ref = bf16[2048,1536]{1,0:T(8,128)(2,1)} custom-call(s32[2,8]{1,0:T(2,128)} %pad_add_fusion.range_ref, bf16[2048,512]{1,0:T(8,128)(2,1)} %get-tuple-element.60.q_ref, bf16[2048,512]{1,0:T(8,128)(2,1)} %get-tuple-element.61.k_ref, bf16[2048,1536]{1,0:T(8,128)(2,1)} %shard_map.180.q_ref.k_ref.v_ref, ...), custom_call_target="tpu_custom_call" | custom-call | flops 42949672960 | bytes 16777216 | tf_op jit(solution)/shard_map/pallas_call | solution.py:420
  459.1 9.8 %convolution_convert_fusion = bf16[1024,1536]{1,0:T(8,128)(2,1)S(1)} fusion(bf16[2048,1536]{1,0:T(8,128)(2,1)} %shard_map.185.dq_ref.dk_ref.dv_ref, bf16[1024,1024]{1,0:T(8,128)(2,1)} %copy-done.7, bf16[1024,1024]{1,0:T(8,128)(2,1)S(1)} %copy-done.6), kind=kOutput, calls=%fused_computation.12 | convolution fusion | flops 6452412416 | bytes 13631488 | tf_op jit(solution)/shard_map/dot_general | solution.py:762
  474.2 7.8 %shard_map.187 = bf16[1024,1024]{1,0:T(8,128)(2,1)} custom-call(s32[2]{0:T(128)} %pad_add_fusion.2.place_ref, bf16[2048,1536]{1,0:T(8,128)(2,1)} %shard_map.185.dq_ref.dk_ref.dv_ref, bf16[2048,1536]{1,0:T(8,128)(2,1)} %shard_map.185.dq_ref.dk_ref.dv_ref, bf16[2048,1536]{1,0:T(8,128)(2,1)} %shard_map.185.dq_ref.dk_ref.dv_ref, ...), custom_call_target="tpu_custom_call" | custom-call | flops 3221225472 | bytes 8388608 | tf_op jit(solution)/shard_map/pallas_call | solution.py:186
  482.0 8.1 %shard_map.186.own_ref = f32[1024,1024]{1,0:T(8,128)} custom-call(s32[2]{0:T(128)} %pad_add_fusion.1.place_ref, bf16[2048,1536]{1,0:T(8,128)(2,1)} %shard_map.185.dq_ref.dk_ref.dv_ref, bf16[2048,1536]{1,0:T(8,128)(2,1)} %shard_map.185.dq_ref.dk_ref.dv_ref, bf16[2048,1536]{1,0:T(8,128)(2,1)} %shard_map.185.dq_ref.dk_ref.dv_ref, ...), custom_call_target="tpu_custom_call" | custom-call | flops 3221225472 | bytes 8388608 | tf_op jit(solution)/shard_map/pallas_call | solution.py:186
  496.3 16.2 %collective-permute-start.25 = (bf16[128,4096]{1,0:T(8,128)(2,1)}, bf16[128,4096]{1,0:T(8,128)(2,1)}, u32[]{:S(2)}, u32[]{:S(2)}) collective-permute-start(bf16[128,4096]{1,0:T(8,128)(2,1)} %get-tuple-element.167), channel_id=1, source_target_pairs={{0,16},{8,24},{16,0},{24,8},{1,17},{9,25},{17,1},{25,9},{2,18},{10... | collective-permute-start | bytes 3145736 | tf_op jit(solution)/shard_map/ppermute | solution.py:730
  512.6 9.2 %shard_map.188 = (bf16[1024,1024]{1,0:T(8,128)(2,1)}, f32[8,1024]{1,0:T(8,128)}, f32[8,1024]{1,0:T(8,128)}) custom-call(f32[1024,1024]{1,0:T(8,128)} %shard_map.186.own_ref, bf16[1024,1024]{1,0:T(8,128)(2,1)} %collective-permute-done.21.other_ref, bf16[1024,1024]{1,0:T(8,128)(2,1)} %pad_maximum_fusion.2.resid_ref.resid_in_ref, ...), custom_call_target="tpu_custom_call" | custom-call | bytes 14704640 | tf_op jit(solution)/shard_map/pallas_call | solution.py:223
  524.8 9.5 %collective-permute-start.22 = (bf16[512,1024]{1,0:T(8,128)(2,1)}, bf16[512,1024]{1,0:T(8,128)(2,1)}, u32[]{:S(2)}, u32[]{:S(2)}) collective-permute-start(bf16[512,1024]{1,0:T(8,128)(2,1)} %get-tuple-element.184), channel_id=1, source_target_pairs={{0,0},{1,1},{4,2},{5,3},{2,4},{3,5},{6,6},{7,7},{8,8},{9,9},{12,10... | collective-permute-start | bytes 3145736 | tf_op jit(solution)/shard_map/ppermute | solution.py:568
  540.0 18.8 %collective-permute-done.25 = bf16[128,4096]{1,0:T(8,128)(2,1)} collective-permute-done((bf16[128,4096]{1,0:T(8,128)(2,1)}, bf16[128,4096]{1,0:T(8,128)(2,1)}, u32[]{:S(2)}, u32[]{:S(2)}) %collective-permute-start.25) | collective-permute-done | bytes 1048608 | tf_op jit(solution)/shard_map/ppermute | solution.py:730
  562.2 11.0 %collective-permute-done.23 = bf16[512,1024]{1,0:T(8,128)(2,1)} collective-permute-done((bf16[512,1024]{1,0:T(8,128)(2,1)}, bf16[512,1024]{1,0:T(8,128)(2,1)}, u32[]{:S(2)}, u32[]{:S(2)}) %collective-permute-start.23) | collective-permute-done | bytes 1048608 | tf_op jit(solution)/shard_map/ppermute | solution.py:569
  575.2 9.8 %all-to-all-done.1 = f32[32,4,128]{2,1,0:T(4,128)S(1)} async-done(((f32[32,4,128]{2,1,0:T(4,128)}), f32[32,4,128]{2,1,0:T(4,128)S(1)}, u32[]{:S(2)}, u32[]{:S(2)}) %all-to-all-start.1) | async-done | bytes 65568 | tf_op jit(solution)/shard_map/all_to_all | solution.py:809
  609.2 8.4 %shard_map.189 = (bf16[1024,1024]{1,0:T(8,128)(2,1)}, bf16[1024,1024]{1,0:T(8,128)(2,1)}) custom-call(bf16[1024,1024]{1,0:T(8,128)(2,1)} %bitcast.181, bf16[32,64,1024]{2,1,0:T(8,128)(2,1)} %all-gather.5.cloned.1.call-done.top_ref.bottom_ref, bf16[32,64,1024]{2,1,0:T(8,128)(2,1)} %all-gather.5.cloned.1.call-done.top_ref.bottom_ref), custom_call_target="tpu_custom_call" | custom-call | flops 4294967296 | bytes 14680064 | tf_op jit(solution)/shard_map/pallas_call | solution.py:223
  619.9 11.0 %collective-permute-done.30 = bf16[256,1024]{1,0:T(8,128)(2,1)} collective-permute-done((bf16[256,1024]{1,0:T(8,128)(2,1)}, bf16[256,1024]{1,0:T(8,128)(2,1)}, u32[]{:S(2)}, u32[]{:S(2)}) %collective-permute-start.30) | collective-permute-done | bytes 524320 | tf_op jit(solution)/shard_map/ppermute | solution.py:730
  637.9 10.0 %all-to-all-done.2 = bf16[4,32,4096]{2,1,0:T(8,128)(2,1)S(1)} async-done(((bf16[4,32,4096]{2,1,0:T(8,128)(2,1)}), bf16[4,32,4096]{2,1,0:T(8,128)(2,1)S(1)}, u32[]{:S(2)}, u32[]{:S(2)}) %all-to-all-start.2) | async-done | bytes 1048608 | tf_op jit(solution)/shard_map/all_to_all | solution.py:815
  (247 shorter events, 181.1 us)
Async XLA Ops:
  7.2 72.0 %all-gather.5.cloned.1.call-start = ((), (), s32[]{:S(2)}) async-start(), calls=%async_computation.7 | async-start | bytes 4718592 | tf_op jit(solution)/shard_map/all_gather | solution.py:601
  25.8 167.1 %all-gather.7.cloned.1.call-start = ((), (), s32[]{:S(2)}) async-start(), calls=%async_computation.8 | async-start | bytes 9437184 | tf_op jit(solution)/shard_map/all_gather | solution.py:601
  61.5 78.7 %all-to-all-start = ((f32[32,4,128]{2,1,0:T(4,128)}), f32[32,4,128]{2,1,0:T(4,128)S(1)}, u32[]{:S(2)}, u32[]{:S(2)}) async-start(f32[32,4,128]{2,1,0:T(4,128)} %bitcast.14), calls=%async_computation | async-start | bytes 131072 | tf_op jit(solution)/shard_map/all_to_all | solution.py:664
  64.7 217.7 %all-gather.9.cloned.1.call-start = ((), (), s32[]{:S(2)}) async-start(), calls=%async_computation.9 | async-start | bytes 18874368 | tf_op jit(solution)/shard_map/all_gather | solution.py:601
  78.4 55.4 %collective-permute-start.6 = (bf16[256,1024]{1,0:T(8,128)(2,1)}, bf16[256,1024]{1,0:T(8,128)(2,1)}, u32[]{:S(2)}, u32[]{:S(2)}) collective-permute-start(bf16[256,1024]{1,0:T(8,128)(2,1)} %slice_dynamic-update-slice_fusion.6), channel_id=1, source_target_pairs={{0,2},{1,3},{2,0},{3,1},{4,6},{5,7},{6,4},{7,5},{8,10},{9,11},{10,... | collective-permute-start | bytes 1572872 | tf_op jit(solution)/shard_map/ppermute | solution.py:596
  78.4 55.4 %collective-permute-start.5 = (bf16[256,1024]{1,0:T(8,128)(2,1)}, bf16[256,1024]{1,0:T(8,128)(2,1)}, u32[]{:S(2)}, u32[]{:S(2)}) collective-permute-start(bf16[256,1024]{1,0:T(8,128)(2,1)} %slice_dynamic-update-slice_fusion.6), channel_id=1, source_target_pairs={{0,1},{1,0},{2,3},{3,2},{4,5},{5,4},{6,7},{7,6},{8,9},{9,8},{10,11... | collective-permute-start | bytes 1572872 | tf_op jit(solution)/shard_map/ppermute | solution.py:596
  90.8 46.6 %collective-permute-start.3 = (bf16[512,1024]{1,0:T(8,128)(2,1)}, bf16[512,1024]{1,0:T(8,128)(2,1)S(1)}, u32[]{:S(2)}, u32[]{:S(2)}) collective-permute-start(bf16[512,1024]{1,0:T(8,128)(2,1)} %get-tuple-element.200), channel_id=1, source_target_pairs={{0,0},{1,1},{2,4},{3,5},{4,2},{5,3},{6,6},{7,7},{8,8},{9,9},{10,12... | collective-permute-start | bytes 3145736 | tf_op jit(solution)/shard_map/ppermute | solution.py:562
  92.6 44.8 %collective-permute-start.4 = (bf16[512,1024]{1,0:T(8,128)(2,1)}, bf16[512,1024]{1,0:T(8,128)(2,1)}, u32[]{:S(2)}, u32[]{:S(2)}) collective-permute-start(bf16[512,1024]{1,0:T(8,128)(2,1)} %get-tuple-element.201), channel_id=1, source_target_pairs={{0,1},{1,0},{2,5},{3,4},{4,3},{5,2},{6,7},{7,6},{8,9},{9,8},{10,13... | collective-permute-start | bytes 3145736 | tf_op jit(solution)/shard_map/ppermute | solution.py:563
  140.4 317.8 %reduce-scatter.5.cloned.1.call-start = ((), (), s32[]{:S(2)}) async-start(), calls=%async_computation.10 | async-start | bytes 9437184 | tf_op jit(solution)/shard_map/reduce_scatter | solution.py:740
  148.1 38.2 %collective-permute-start.9 = (bf16[1024,1024]{1,0:T(8,128)(2,1)}, bf16[1024,1024]{1,0:T(8,128)(2,1)}, u32[]{:S(2)}, u32[]{:S(2)}) collective-permute-start(bf16[1024,1024]{1,0:T(8,128)(2,1)} %shard_map.179), channel_id=1, source_target_pairs={{0,4},{4,0},{1,5},{5,1},{2,6},{6,2},{3,7},{7,3},{8,12},{12,8},{9,1... | collective-permute-start | bytes 6291464 | tf_op jit(solution)/shard_map/ppermute | solution.py:576
  172.4 97.3 %collective-permute-start.14 = (bf16[512,1024]{1,0:T(8,128)(2,1)}, bf16[512,1024]{1,0:T(8,128)(2,1)S(1)}, u32[]{:S(2)}, u32[]{:S(2)}) collective-permute-start(bf16[512,1024]{1,0:T(8,128)(2,1)} %get-tuple-element.192), channel_id=1, source_target_pairs={{0,0},{1,1},{2,4},{3,5},{4,2},{5,3},{6,6},{7,7},{8,8},{9,9},{10,12... | collective-permute-start | bytes 3145736 | tf_op jit(solution)/shard_map/ppermute | solution.py:562
  174.2 95.4 %collective-permute-start.15 = (bf16[512,1024]{1,0:T(8,128)(2,1)}, bf16[512,1024]{1,0:T(8,128)(2,1)S(1)}, u32[]{:S(2)}, u32[]{:S(2)}) collective-permute-start(bf16[512,1024]{1,0:T(8,128)(2,1)} %get-tuple-element.193), channel_id=1, source_target_pairs={{0,1},{1,0},{2,5},{3,4},{4,3},{5,2},{6,7},{7,6},{8,9},{9,8},{10,13... | collective-permute-start | bytes 3145736 | tf_op jit(solution)/shard_map/ppermute | solution.py:563
  348.8 226.3 %reduce-scatter.7.cloned.1.call-start = ((), (), s32[]{:S(2)}) async-start(), calls=%async_computation.11 | async-start | bytes 9437184 | tf_op jit(solution)/shard_map/reduce_scatter | solution.py:740
  368.2 230.4 %reduce-scatter.9.cloned.1.call-start = ((), (), s32[]{:S(2)}) async-start(), calls=%async_computation.12 | async-start | bytes 1310720 | tf_op jit(solution)/shard_map/reduce_scatter | solution.py:761
  376.7 79.8 %collective-permute-start.18 = (bf16[512,1024]{1,0:T(8,128)(2,1)}, bf16[512,1024]{1,0:T(8,128)(2,1)S(1)}, u32[]{:S(2)}, u32[]{:S(2)}) collective-permute-start(bf16[512,1024]{1,0:T(8,128)(2,1)} %get-tuple-element.188), channel_id=1, source_target_pairs={{0,0},{1,1},{4,2},{5,3},{2,4},{3,5},{6,6},{7,7},{8,8},{9,9},{12,10... | collective-permute-start | bytes 3145736 | tf_op jit(solution)/shard_map/ppermute | solution.py:568
  378.6 78.0 %collective-permute-start.19 = (bf16[512,1024]{1,0:T(8,128)(2,1)S(1)}, bf16[512,1024]{1,0:T(8,128)(2,1)S(1)}, u32[]{:S(2)}, u32[]{:S(2)}) collective-permute-start(bf16[512,1024]{1,0:T(8,128)(2,1)S(1)} %get-tuple-element.189), channel_id=1, source_target_pairs={{1,0},{0,1},{5,2},{4,3},{3,4},{2,5},{7,6},{6,7},{9,8},{8,9},{13,10... | collective-permute-start | bytes 3145736 | tf_op jit(solution)/shard_map/ppermute | solution.py:569
  493.7 46.3 %collective-permute-start.24 = (bf16[128,4096]{1,0:T(8,128)(2,1)}, bf16[128,4096]{1,0:T(8,128)(2,1)}, u32[]{:S(2)}, u32[]{:S(2)}) collective-permute-start(bf16[128,4096]{1,0:T(8,128)(2,1)} %get-tuple-element.166), channel_id=1, source_target_pairs={{0,8},{8,0},{16,24},{24,16},{1,9},{9,1},{17,25},{25,17},{2,10},{10... | collective-permute-start | bytes 3145736 | tf_op jit(solution)/shard_map/ppermute | solution.py:730
  496.3 62.4 %collective-permute-start.25 = (bf16[128,4096]{1,0:T(8,128)(2,1)}, bf16[128,4096]{1,0:T(8,128)(2,1)}, u32[]{:S(2)}, u32[]{:S(2)}) collective-permute-start(bf16[128,4096]{1,0:T(8,128)(2,1)} %get-tuple-element.167), channel_id=1, source_target_pairs={{0,16},{8,24},{16,0},{24,8},{1,17},{9,25},{17,1},{25,9},{2,18},{10... | collective-permute-start | bytes 3145736 | tf_op jit(solution)/shard_map/ppermute | solution.py:730
  512.5 46.2 %collective-permute-start.26 = (bf16[128,4096]{1,0:T(8,128)(2,1)}, bf16[128,4096]{1,0:T(8,128)(2,1)}, u32[]{:S(2)}, u32[]{:S(2)}) collective-permute-start(bf16[128,4096]{1,0:T(8,128)(2,1)} %get-tuple-element.168), channel_id=1, source_target_pairs={{0,24},{8,16},{16,8},{24,0},{1,25},{9,17},{17,9},{25,1},{2,26},{10... | collective-permute-start | bytes 3145736 | tf_op jit(solution)/shard_map/ppermute | solution.py:730
  524.8 37.4 %collective-permute-start.22 = (bf16[512,1024]{1,0:T(8,128)(2,1)}, bf16[512,1024]{1,0:T(8,128)(2,1)}, u32[]{:S(2)}, u32[]{:S(2)}) collective-permute-start(bf16[512,1024]{1,0:T(8,128)(2,1)} %get-tuple-element.184), channel_id=1, source_target_pairs={{0,0},{1,1},{4,2},{5,3},{2,4},{3,5},{6,6},{7,7},{8,8},{9,9},{12,10... | collective-permute-start | bytes 3145736 | tf_op jit(solution)/shard_map/ppermute | solution.py:568
  534.3 38.9 %collective-permute-start.23 = (bf16[512,1024]{1,0:T(8,128)(2,1)}, bf16[512,1024]{1,0:T(8,128)(2,1)}, u32[]{:S(2)}, u32[]{:S(2)}) collective-permute-start(bf16[512,1024]{1,0:T(8,128)(2,1)} %get-tuple-element.185), channel_id=1, source_target_pairs={{1,0},{0,1},{5,2},{4,3},{3,4},{2,5},{7,6},{6,7},{9,8},{8,9},{13,10... | collective-permute-start | bytes 3145736 | tf_op jit(solution)/shard_map/ppermute | solution.py:569
  535.2 49.8 %all-to-all-start.1 = ((f32[32,4,128]{2,1,0:T(4,128)}), f32[32,4,128]{2,1,0:T(4,128)S(1)}, u32[]{:S(2)}, u32[]{:S(2)}) async-start(f32[32,4,128]{2,1,0:T(4,128)} %copy.107), calls=%async_computation.3 | async-start | bytes 131072 | tf_op jit(solution)/shard_map/all_to_all | solution.py:809
  539.9 109.6 %reduce-scatter.11.cloned.1.call-start = ((), (), s32[]{:S(2)}) async-start(), calls=%async_computation.13 | async-start | bytes 1310720 | tf_op jit(solution)/shard_map/reduce_scatter | solution.py:811
  595.1 52.8 %all-to-all-start.2 = ((bf16[4,32,4096]{2,1,0:T(8,128)(2,1)}), bf16[4,32,4096]{2,1,0:T(8,128)(2,1)S(1)}, u32[]{:S(2)}, u32[]{:S(2)}) async-start(bf16[4,32,4096]{2,1,0:T(8,128)(2,1)} %bitcast.83), calls=%async_computation.4 | async-start | bytes 2097152 | tf_op jit(solution)/shard_map/all_to_all | solution.py:815
  (49 other events, 674.8 us)
Sparse Core Ops, SparseCore 0:
  25.9 36.9 all-gather.4
  64.9 54.5 all-gather.6
  140.5 120.4 all-gather.8
  349.0 76.6 reduce-scatter.4
  429.3 72.4 reduce-scatter.6
  512.7 32.6 reduce-scatter.8
  595.2 41.9 reduce-scatter.10

commit v11 on v10

--- a/solution.py
+++ b/solution.py
@@ -759,26 +759,11 @@
     )
     grad_proj, block_out, grad_up = lax.optimization_barrier((grad_proj, block_out, grad_up))
     grad_up = lax.psum_scatter(grad_up, ("hi", "lo"), scatter_dimension=0, tiled=True)
-    grad_qkv = lax.dot_general(normed_row, grad_proj, (((0,), (0,)), ((), ())), preferred_element_type=f32)
-    grad_qkv = grad_qkv.astype(bf16)
-    grad_proj, grad_qkv = lax.optimization_barrier((grad_proj, grad_qkv))
     if group > 2:
-        grad_qkv = grad_qkv.reshape(planes, 2, highs, lows, -1, 3, 1, heads_wide)
-        grad_qkv = jnp.moveaxis(grad_qkv, (1, 3), (0, 1)).reshape(group, -1, 3, 1, heads_wide)
-        grad_qkv = lax.all_to_all(grad_qkv, ROW_AXES, split_axis=0, concat_axis=3, tiled=True)
-        grad_qkv = grad_qkv.reshape(-1, 3 * width)
         partial = dot_nt(grad_proj, own_qkv(middle)).astype(bf16)
         grad_one = lax.psum_scatter(partial, ROW_AXES, scatter_dimension=0, tiled=True).astype(f32)
         grad_one_other = jnp.zeros((frames, width), bf16)
     else:
-        split = grad_qkv.reshape(planes, 2, -1, 3 * heads_wide)
-        other = lax.ppermute(lax.dynamic_index_in_dim(split, 1 - core, 1, False), "core", swap)
-        own = lax.dynamic_index_in_dim(split, core, 1, False)
-        own, other = (v.reshape(-1, 3 * heads_wide) for v in (own, other))
-        left, right = jnp.where(first_core, own, other), jnp.where(first_core, other, own)
-        grad_qkv = jnp.concatenate(
-            [v[:, i * heads_wide : (i + 1) * heads_wide] for i in range(3) for v in (left, right)], axis=1
-        )
         if in_place:
             pull = functools.partial(pull_project, grad_proj, middle, out_rows, heads_wide, member, frames)
             away, home = pull(1 - core, bf16), pull(core, f32)
@@ -789,12 +774,6 @@
             away, home = dot_nt(away, qkv_own).astype(bf16), dot_nt(home, qkv_own)
         grad_one_other = lax.ppermute(away, "core", swap)
         grad_one = home
-    grad_one, grad_qkv = lax.optimization_barrier((grad_one, grad_qkv))
-    if group > 2:
-        grad_qkv = lax.psum_scatter(grad_qkv, ("plane", "hi"), scatter_dimension=0, tiled=True).astype(f32)
-    else:
-        grad_qkv = jnp.concatenate([grad_qkv.reshape(planes, -1, 3 * width), grad_out], axis=2)
-        grad_qkv = exchange_planes(grad_qkv)
     grad_in, grad_shift_one, grad_scale_one = rowwise(
         norm_one_back_kernel,
         frames,
@@ -804,6 +783,26 @@
         sums=2,
     )
     grad_in_home = from_rows(grad_in)
+    grad_proj, grad_in = lax.optimization_barrier((grad_proj, grad_in))
+    grad_qkv = lax.dot_general(normed_row, grad_proj, (((0,), (0,)), ((), ())), preferred_element_type=f32)
+    grad_qkv = grad_qkv.astype(bf16)
+    if group > 2:
+        grad_qkv = grad_qkv.reshape(planes, 2, highs, lows, -1, 3, 1, heads_wide)
+        grad_qkv = jnp.moveaxis(grad_qkv, (1, 3), (0, 1)).reshape(group, -1, 3, 1, heads_wide)
+        grad_qkv = lax.all_to_all(grad_qkv, ROW_AXES, split_axis=0, concat_axis=3, tiled=True)
+        grad_qkv = grad_qkv.reshape(-1, 3 * width)
+        grad_qkv = lax.psum_scatter(grad_qkv, ("plane", "hi"), scatter_dimension=0, tiled=True).astype(f32)
+    else:
+        split = grad_qkv.reshape(planes, 2, -1, 3 * heads_wide)
+        other = lax.ppermute(lax.dynamic_index_in_dim(split, 1 - core, 1, False), "core", swap)
+        own = lax.dynamic_index_in_dim(split, core, 1, False)
+        own, other = (v.reshape(-1, 3 * heads_wide) for v in (own, other))
+        left, right = jnp.where(first_core, own, other), jnp.where(first_core, other, own)
+        grad_qkv = jnp.concatenate(
+            [v[:, i * heads_wide : (i + 1) * heads_wide] for i in range(3) for v in (left, right)], axis=1
+        )
+        grad_qkv = jnp.concatenate([grad_qkv.reshape(planes, -1, 3 * width), grad_out], axis=2)
+        grad_qkv = exchange_planes(grad_qkv)
     grad_mod = jnp.stack([v[:labels] for v in (grad_shift_one, grad_scale_one, grad_shift_two, grad_scale_two)], axis=1)
     grad_mod = jnp.moveaxis(grad_mod.reshape(labels, devices, own_columns), 1, 0)
     grad_mod = lax.all_to_all(grad_mod, ALL_AXES, split_axis=0, concat_axis=0, tiled=True)

time: 666 us -> 670 us (level)
    ppermute x2, waiting for transfers between devices: 11 us -> 32.6 us  [from_rows(): lax.ppermute(lax.dynamic_index_in_dim(value, 1 - high % 2, 0, False), LIN...]
    ppermute x9, waiting for transfers between devices: 35.1 us -> 22.6 us  [exchange(): lax.ppermute(sent, axes, [(i, i ^ flip) for i in range(count)]).astype(f32)]
    all_to_all x1, waiting for transfers between devices: 9.99 us -> 2.63 us  [body(): lax.all_to_all(grad_qkv, ('hi', 'lo'), split_axis=0, concat_axis=0, tiled...]
    unnamed x68 -> x70, local copies, waits for them, and re-layouts: 16.1 us -> 14.6 us
  transfers between devices with their start and end apart: 44 -> 44, of which waited for: 13 -> 15; matrix products, arithmetic and copies ran while one was open for 17% -> 17% of each run, Pallas kernels for 33% -> 34%
where the time goes in v11:
time: 670 us; the launch traced here: 664 us
  Pallas kernels  290 us (43%)
  waiting for transfers between devices  123 us (18%)
  starting transfers between devices  107 us (16%)
  other arithmetic  54.7 us (8%)
  local copies, waits for them, and re-layouts  45.2 us (7%)
  matrix products  20.5 us (3%)
  between operations  15.1 us (2%)
  blocking collectives  8.92 us (1%)
    pallas_call x1, Pallas kernels, attend_backward(): pl.pallas_call(attend_backward_kernel, grid_spec=pltpu.PrefetchScalarGrid...  81 us
    pallas_call x1, Pallas kernels, feed_forward_and_back(): pl.pallas_call(feed_kernel, grid=(hidden // piece,), in_specs=[whole(), w...  66.3 us
    pallas_call x1, Pallas kernels, attend_forward(): pl.pallas_call(attend_forward_kernel, grid_spec=pltpu.PrefetchScalarGridS...  64 us
    ppermute x9, waiting for transfers between devices, share_on_line(): lax.ppermute(value, ('hi', 'lo'), [(i, i ^ flip) for i in range(line)])  58.9 us
    pallas_call x6, Pallas kernels, rowwise(): pl.pallas_call(kernel, grid=(frames // tile,), in_specs=in_specs, out_spe...  51.3 us
    ppermute x2, waiting for transfers between devices, from_rows(): lax.ppermute(lax.dynamic_index_in_dim(value, 1 - high % 2, 0, False), LIN...  32.6 us
    ppermute x9, starting transfers between devices, exchange(): lax.ppermute(sent, axes, [(i, i ^ flip) for i in range(count)]).astype(f32)  23 us
    ppermute x9, waiting for transfers between devices, exchange(): lax.ppermute(sent, axes, [(i, i ^ flip) for i in range(count)]).astype(f32)  22.6 us
  transfers between devices with their start and end apart: 44, of which 15 were waited for; matrix products, arithmetic and copies ran while one was open for 17% of the time, Pallas kernels for 34%

profile of v11, /device:TPU:0, one launch (start us, length us, event | category | flops | bytes accessed | tf_op | source)
XLA Modules:
  0.0 664.3 jit_solution(8616830052392103625)
XLA Ops:
  30.3 6.8 %collective-permute-done.12 = bf16[128,1024]{1,0:T(8,128)(2,1)S(1)} collective-permute-done((bf16[128,1024]{1,0:T(8,128)(2,1)S(1)}, bf16[128,1024]{1,0:T(8,128)(2,1)S(1)}, u32[]{:S(2)}, u32[]{:S(2)}) %collective-permute-start.12) | collective-permute-done | bytes 262176 | tf_op jit(solution)/shard_map/ppermute | solution.py:596
  37.1 12.2 %collective-permute-done.11 = bf16[128,1024]{1,0:T(8,128)(2,1)S(1)} collective-permute-done((bf16[128,1024]{1,0:T(8,128)(2,1)S(1)}, bf16[128,1024]{1,0:T(8,128)(2,1)S(1)}, u32[]{:S(2)}, u32[]{:S(2)}) %collective-permute-start.11) | collective-permute-done | bytes 262176 | tf_op jit(solution)/shard_map/ppermute | solution.py:596
  50.9 8.9 %all-gather = s32[16,1,4]{2,1,0:T(1,128)S(1)} all-gather(s32[2,1,4]{2,1,0:T(1,128)S(1)} %copy-done.28), channel_id=2, replica_groups=mesh['plane'=4,'core'=2,'hi'=4,'lo'=1] {'plane','core'}, dimensions={0}, use_global_device_ids=true | all-gather | bytes 288 | tf_op jit(solution)/shard_map/all_gather | solution.py:655
  79.2 8.6 %shard_map.178 = bf16[1024,1024]{1,0:T(8,128)(2,1)} custom-call(bf16[1024,1024]{1,0:T(8,128)(2,1)} %bitcast.167, bf16[1024,1024]{1,0:T(8,128)(2,1)} %bitcast.170, bf16[32,64,1024]{2,1,0:T(8,128)(2,1)} %all-gather.5.cloned.1.call-done.top_ref.bottom_ref, bf16[32,64,1024]{2,1,0:T(8,128)(2,1)} %all-gather.5.cloned.1.call-done.top_ref.bottom_ref), custom_call_target="tpu_custom_call" | custom-call | flops 1 | bytes 1 | tf_op jit(solution)/shard_map/pallas_call | solution.py:223
  96.4 37.4 %collective-permute-done.6 = bf16[256,1024]{1,0:T(8,128)(2,1)} collective-permute-done((bf16[256,1024]{1,0:T(8,128)(2,1)}, bf16[256,1024]{1,0:T(8,128)(2,1)}, u32[]{:S(2)}, u32[]{:S(2)}) %collective-permute-start.6) | collective-permute-done | bytes 524320 | tf_op jit(solution)/shard_map/ppermute | solution.py:596
  142.4 5.6 shard_map.179
  148.1 20.0 %collective-permute-start.9 = (bf16[1024,1024]{1,0:T(8,128)(2,1)}, bf16[1024,1024]{1,0:T(8,128)(2,1)}, u32[]{:S(2)}, u32[]{:S(2)}) collective-permute-start(bf16[1024,1024]{1,0:T(8,128)(2,1)} %shard_map.179), channel_id=1, source_target_pairs={{0,4},{4,0},{1,5},{5,1},{2,6},{6,2},{3,7},{7,3},{8,12},{12,8},{9,1... | collective-permute-start | bytes 6291464 | tf_op jit(solution)/shard_map/ppermute | solution.py:576
  174.2 12.0 %collective-permute-start.15 = (bf16[512,1024]{1,0:T(8,128)(2,1)}, bf16[512,1024]{1,0:T(8,128)(2,1)S(1)}, u32[]{:S(2)}, u32[]{:S(2)}) collective-permute-start(bf16[512,1024]{1,0:T(8,128)(2,1)} %get-tuple-element.187), channel_id=1, source_target_pairs={{0,1},{1,0},{2,5},{3,4},{4,3},{5,2},{6,7},{7,6},{8,9},{9,8},{10,13... | collective-permute-start | bytes 3145736 | tf_op jit(solution)/shard_map/ppermute | solution.py:563
  192.9 11.0 %shard_map.180.q_ref.k_ref.v_ref = bf16[2048,1536]{1,0:T(8,128)(2,1)} custom-call(s32[1]{0:T(128)} %bitcast.21.place_ref, bf16[2048,1024]{1,0:T(8,128)(2,1)} %pad_maximum_fusion.1.x_ref, bf16[32,128,1024]{2,1,0:T(8,128)(2,1)} %all-gather.7.cloned.1.call-done.w_ref.q_ref.k_ref.v_ref), custom_call_target="tpu_custom_call" | custom-call | flops 1 | bytes 1 | tf_op jit(solution)/shard_map/pallas_call | solution.py:151
  203.9 64.0 %shard_map.181 = (bf16[2048,512]{1,0:T(8,128)(2,1)}, bf16[2048,512]{1,0:T(8,128)(2,1)}, bf16[2048,512]{1,0:T(8,128)(2,1)}, f32[4,2,2048]{2,1,0:T(2,128)}) custom-call(s32[2,8]{1,0:T(2,128)} %pad_add_fusion.range_ref, bf16[2048,1536]{1,0:T(8,128)(2,1)} %shard_map.180.q_ref.k_ref.v_ref, bf16[2048,1536]{1,0:T(8,128)(2,1)} %shard_map.180.q_ref.k_ref.v_ref, ...), custom_call_target="tpu_custom_call" | custom-call | flops 17179869184 | bytes 14680064 | tf_op jit(solution)/shard_map/pallas_call | solution.py:316
  276.1 8.2 %shard_map.182 = (f32[1024,1024]{1,0:T(8,128)}, bf16[1024,1024]{1,0:T(8,128)(2,1)}) custom-call(bf16[1024,1024]{1,0:T(8,128)(2,1)} %pad_maximum_fusion.5.mixed_ref, bf16[32,128,1024]{2,1,0:T(8,128)(2,1)} %all-gather.7.cloned.1.call-done.w_ref.q_ref.k_ref.v_ref, bf16[1024,1024]{1,0:T(8,128)(2,1)} %pad_maximum_fusion.2.resid_ref.resid_in_ref, ...), custom_call_target="tpu_custom_call" | custom-call | flops 2147483648 | bytes 18911232 | tf_op jit(solution)/shard_map/pallas_call | solution.py:223
  284.3 66.3 %shard_map.183 = (bf16[1024,1024]{1,0:T(8,128)(2,1)}, f32[1024,1024]{1,0:T(8,128)}, bf16[1024,4096]{1,0:T(8,128)(2,1)}, bf16[4096,1024]{1,0:T(8,128)(2,1)}) custom-call(bf16[1024,1024]{1,0:T(8,128)(2,1)} %get-tuple-element.60.n_ref, bf16[1024,1024]{1,0:T(8,128)(2,1)} %pad_maximum_fusion.6.cot_ref, f32[1024,1024]{1,0:T(8,128)} %get-tuple-element.62.resid_ref, ...), custom_call_target="tpu_custom_call" | custom-call | flops 51539607552 | bytes 50331648 | tf_op jit(solution)/shard_map/pallas_call | solution.py:507
  352.0 11.2 %shard_map.184 = (f32[1024,1024]{1,0:T(8,128)}, bf16[1024,1024]{1,0:T(8,128)(2,1)}, bf16[1024,1024]{1,0:T(8,128)(2,1)}, f32[8,1024]{1,0:T(8,128)}, f32[8,1024]{1,0:T(8,128)}) custom-call(f32[1024,1024]{1,0:T(8,128)} %get-tuple-element.64.g_ref, f32[1024,1024]{1,0:T(8,128)} %get-tuple-element.62.resid_ref, bf16[1024,1024]{1,0:T(8,128)(2,1)} %pad_maximum_fusion.6.cot_ref, ...), custom_call_target="tpu_custom_call" | custom-call | flops 1 | bytes 1 | tf_op jit(solution)/shard_map/pallas_call | solution.py:223
  382.5 81.0 %shard_map.185.dq_ref.dk_ref.dv_ref = bf16[2048,1536]{1,0:T(8,128)(2,1)} custom-call(s32[2,8]{1,0:T(2,128)} %pad_add_fusion.range_ref, bf16[2048,512]{1,0:T(8,128)(2,1)} %get-tuple-element.57.q_ref, bf16[2048,512]{1,0:T(8,128)(2,1)} %get-tuple-element.58.k_ref, bf16[2048,1536]{1,0:T(8,128)(2,1)} %shard_map.180.q_ref.k_ref.v_ref, ...), custom_call_target="tpu_custom_call" | custom-call | flops 42949672960 | bytes 16777216 | tf_op jit(solution)/shard_map/pallas_call | solution.py:420
  465.2 8.1 %shard_map.187 = bf16[1024,1024]{1,0:T(8,128)(2,1)} custom-call(s32[2]{0:T(128)} %pad_add_fusion.2.place_ref, bf16[2048,1536]{1,0:T(8,128)(2,1)} %shard_map.185.dq_ref.dk_ref.dv_ref, bf16[2048,1536]{1,0:T(8,128)(2,1)} %shard_map.185.dq_ref.dk_ref.dv_ref, bf16[2048,1536]{1,0:T(8,128)(2,1)} %shard_map.185.dq_ref.dk_ref.dv_ref, ...), custom_call_target="tpu_custom_call" | custom-call | flops 3221225472 | bytes 8388608 | tf_op jit(solution)/shard_map/pallas_call | solution.py:186
  476.3 8.2 %shard_map.186.own_ref = f32[1024,1024]{1,0:T(8,128)} custom-call(s32[2]{0:T(128)} %pad_add_fusion.1.place_ref, bf16[2048,1536]{1,0:T(8,128)(2,1)} %shard_map.185.dq_ref.dk_ref.dv_ref, bf16[2048,1536]{1,0:T(8,128)(2,1)} %shard_map.185.dq_ref.dk_ref.dv_ref, bf16[2048,1536]{1,0:T(8,128)(2,1)} %shard_map.185.dq_ref.dk_ref.dv_ref, ...), custom_call_target="tpu_custom_call" | custom-call | flops 3221225472 | bytes 8388608 | tf_op jit(solution)/shard_map/pallas_call | solution.py:186
  485.8 9.3 %shard_map.188 = (bf16[1024,1024]{1,0:T(8,128)(2,1)}, f32[8,1024]{1,0:T(8,128)}, f32[8,1024]{1,0:T(8,128)}) custom-call(f32[1024,1024]{1,0:T(8,128)} %shard_map.186.own_ref, bf16[1024,1024]{1,0:T(8,128)(2,1)} %copy-done.16, bf16[1024,1024]{1,0:T(8,128)(2,1)} %pad_maximum_fusion.2.resid_ref.resid_in_ref, f32[1024,1024]{1,0:T(8,128)} %get-tuple-element.74.mid_ref, ...), custom_call_target="tpu_custom_call" | custom-call | bytes 14704640 | tf_op jit(solution)/shard_map/pallas_call | solution.py:223
  495.1 9.6 %convolution_convert_fusion = bf16[1024,1536]{1,0:T(8,128)(2,1)S(1)} fusion(bf16[2048,1536]{1,0:T(8,128)(2,1)} %shard_map.185.dq_ref.dk_ref.dv_ref, bf16[1024,1024]{1,0:T(8,128)(2,1)} %copy-done.8, bf16[1024,1024]{1,0:T(8,128)(2,1)S(1)} %copy-done.7), kind=kOutput, calls=%fused_computation.12 | convolution fusion | flops 6452412416 | bytes 13631488 | tf_op jit(solution)/shard_map/dot_general | solution.py:787
  509.6 9.4 %collective-permute-start.21 = (bf16[512,1024]{1,0:T(8,128)(2,1)}, bf16[512,1024]{1,0:T(8,128)(2,1)}, u32[]{:S(2)}, u32[]{:S(2)}) collective-permute-start(bf16[512,1024]{1,0:T(8,128)(2,1)} %get-tuple-element.178), channel_id=1, source_target_pairs={{0,0},{1,1},{4,2},{5,3},{2,4},{3,5},{6,6},{7,7},{8,8},{9,9},{12,10... | collective-permute-start | bytes 3145736 | tf_op jit(solution)/shard_map/ppermute | solution.py:568
  525.3 10.5 %collective-permute-start.24 = (bf16[128,4096]{1,0:T(8,128)(2,1)}, bf16[128,4096]{1,0:T(8,128)(2,1)}, u32[]{:S(2)}, u32[]{:S(2)}) collective-permute-start(bf16[128,4096]{1,0:T(8,128)(2,1)} %get-tuple-element.160), channel_id=1, source_target_pairs={{0,8},{8,0},{16,24},{24,16},{1,9},{9,1},{17,25},{25,17},{2,10},{10... | collective-permute-start | bytes 3145736 | tf_op jit(solution)/shard_map/ppermute | solution.py:730
  540.9 32.6 %collective-permute-done.22 = bf16[512,1024]{1,0:T(8,128)(2,1)} collective-permute-done((bf16[512,1024]{1,0:T(8,128)(2,1)}, bf16[512,1024]{1,0:T(8,128)(2,1)}, u32[]{:S(2)}, u32[]{:S(2)}) %collective-permute-start.22) | collective-permute-done | bytes 1048608 | tf_op jit(solution)/shard_map/ppermute | solution.py:569
  588.0 7.4 %convolution_convert_fusion.1 = bf16[2048,1024]{1,0:T(8,128)(2,1)S(1)} fusion(bf16[1024,2048]{1,0:T(8,128)(2,1)} %pad_maximum_fusion, bf16[1024,1024]{1,0:T(8,128)(2,1)} %bitcast.180), kind=kOutput, calls=%fused_computation.13 | convolution fusion | flops 4297064448 | bytes 10485760 | tf_op jit(solution)/shard_map/dot_general | solution.py:820
  615.9 8.4 %shard_map.189 = (bf16[1024,1024]{1,0:T(8,128)(2,1)}, bf16[1024,1024]{1,0:T(8,128)(2,1)}) custom-call(bf16[1024,1024]{1,0:T(8,128)(2,1)} %bitcast.181, bf16[32,64,1024]{2,1,0:T(8,128)(2,1)} %all-gather.5.cloned.1.call-done.top_ref.bottom_ref, bf16[32,64,1024]{2,1,0:T(8,128)(2,1)} %all-gather.5.cloned.1.call-done.top_ref.bottom_ref), custom_call_target="tpu_custom_call" | custom-call | flops 4294967296 | bytes 14680064 | tf_op jit(solution)/shard_map/pallas_call | solution.py:223
  626.5 10.2 %collective-permute-done.30 = bf16[256,1024]{1,0:T(8,128)(2,1)} collective-permute-done((bf16[256,1024]{1,0:T(8,128)(2,1)}, bf16[256,1024]{1,0:T(8,128)(2,1)}, u32[]{:S(2)}, u32[]{:S(2)}) %collective-permute-start.30) | collective-permute-done | bytes 524320 | tf_op jit(solution)/shard_map/ppermute | solution.py:730
  (249 shorter events, 182.3 us)
Async XLA Ops:
  7.2 72.0 %all-gather.5.cloned.1.call-start = ((), (), s32[]{:S(2)}) async-start(), calls=%async_computation.7 | async-start | bytes 4718592 | tf_op jit(solution)/shard_map/all_gather | solution.py:601
  25.8 167.1 %all-gather.7.cloned.1.call-start = ((), (), s32[]{:S(2)}) async-start(), calls=%async_computation.8 | async-start | bytes 9437184 | tf_op jit(solution)/shard_map/all_gather | solution.py:601
  61.5 78.7 %all-to-all-start = ((f32[32,4,128]{2,1,0:T(4,128)}), f32[32,4,128]{2,1,0:T(4,128)S(1)}, u32[]{:S(2)}, u32[]{:S(2)}) async-start(f32[32,4,128]{2,1,0:T(4,128)} %bitcast.14), calls=%async_computation | async-start | bytes 131072 | tf_op jit(solution)/shard_map/all_to_all | solution.py:664
  64.7 219.6 %all-gather.9.cloned.1.call-start = ((), (), s32[]{:S(2)}) async-start(), calls=%async_computation.9 | async-start | bytes 18874368 | tf_op jit(solution)/shard_map/all_gather | solution.py:601
  78.4 55.4 %collective-permute-start.6 = (bf16[256,1024]{1,0:T(8,128)(2,1)}, bf16[256,1024]{1,0:T(8,128)(2,1)}, u32[]{:S(2)}, u32[]{:S(2)}) collective-permute-start(bf16[256,1024]{1,0:T(8,128)(2,1)} %slice_dynamic-update-slice_fusion.6), channel_id=1, source_target_pairs={{0,2},{1,3},{2,0},{3,1},{4,6},{5,7},{6,4},{7,5},{8,10},{9,11},{10,... | collective-permute-start | bytes 1572872 | tf_op jit(solution)/shard_map/ppermute | solution.py:596
  78.4 55.4 %collective-permute-start.5 = (bf16[256,1024]{1,0:T(8,128)(2,1)}, bf16[256,1024]{1,0:T(8,128)(2,1)}, u32[]{:S(2)}, u32[]{:S(2)}) collective-permute-start(bf16[256,1024]{1,0:T(8,128)(2,1)} %slice_dynamic-update-slice_fusion.6), channel_id=1, source_target_pairs={{0,1},{1,0},{2,3},{3,2},{4,5},{5,4},{6,7},{7,6},{8,9},{9,8},{10,11... | collective-permute-start | bytes 1572872 | tf_op jit(solution)/shard_map/ppermute | solution.py:596
  90.8 46.6 %collective-permute-start.3 = (bf16[512,1024]{1,0:T(8,128)(2,1)}, bf16[512,1024]{1,0:T(8,128)(2,1)S(1)}, u32[]{:S(2)}, u32[]{:S(2)}) collective-permute-start(bf16[512,1024]{1,0:T(8,128)(2,1)} %get-tuple-element.194), channel_id=1, source_target_pairs={{0,0},{1,1},{2,4},{3,5},{4,2},{5,3},{6,6},{7,7},{8,8},{9,9},{10,12... | collective-permute-start | bytes 3145736 | tf_op jit(solution)/shard_map/ppermute | solution.py:562
  92.6 44.8 %collective-permute-start.4 = (bf16[512,1024]{1,0:T(8,128)(2,1)}, bf16[512,1024]{1,0:T(8,128)(2,1)}, u32[]{:S(2)}, u32[]{:S(2)}) collective-permute-start(bf16[512,1024]{1,0:T(8,128)(2,1)} %get-tuple-element.195), channel_id=1, source_target_pairs={{0,1},{1,0},{2,5},{3,4},{4,3},{5,2},{6,7},{7,6},{8,9},{9,8},{10,13... | collective-permute-start | bytes 3145736 | tf_op jit(solution)/shard_map/ppermute | solution.py:563
  140.4 324.8 %reduce-scatter.5.cloned.1.call-start = ((), (), s32[]{:S(2)}) async-start(), calls=%async_computation.10 | async-start | bytes 9437184 | tf_op jit(solution)/shard_map/reduce_scatter | solution.py:740
  148.1 38.2 %collective-permute-start.9 = (bf16[1024,1024]{1,0:T(8,128)(2,1)}, bf16[1024,1024]{1,0:T(8,128)(2,1)}, u32[]{:S(2)}, u32[]{:S(2)}) collective-permute-start(bf16[1024,1024]{1,0:T(8,128)(2,1)} %shard_map.179), channel_id=1, source_target_pairs={{0,4},{4,0},{1,5},{5,1},{2,6},{6,2},{3,7},{7,3},{8,12},{12,8},{9,1... | collective-permute-start | bytes 6291464 | tf_op jit(solution)/shard_map/ppermute | solution.py:576
  172.3 99.1 %collective-permute-start.14 = (bf16[512,1024]{1,0:T(8,128)(2,1)}, bf16[512,1024]{1,0:T(8,128)(2,1)S(1)}, u32[]{:S(2)}, u32[]{:S(2)}) collective-permute-start(bf16[512,1024]{1,0:T(8,128)(2,1)} %get-tuple-element.186), channel_id=1, source_target_pairs={{0,0},{1,1},{2,4},{3,5},{4,2},{5,3},{6,6},{7,7},{8,8},{9,9},{10,12... | collective-permute-start | bytes 3145736 | tf_op jit(solution)/shard_map/ppermute | solution.py:562
  174.2 97.3 %collective-permute-start.15 = (bf16[512,1024]{1,0:T(8,128)(2,1)}, bf16[512,1024]{1,0:T(8,128)(2,1)S(1)}, u32[]{:S(2)}, u32[]{:S(2)}) collective-permute-start(bf16[512,1024]{1,0:T(8,128)(2,1)} %get-tuple-element.187), channel_id=1, source_target_pairs={{0,1},{1,0},{2,5},{3,4},{4,3},{5,2},{6,7},{7,6},{8,9},{9,8},{10,13... | collective-permute-start | bytes 3145736 | tf_op jit(solution)/shard_map/ppermute | solution.py:563
  350.7 231.9 %reduce-scatter.7.cloned.1.call-start = ((), (), s32[]{:S(2)}) async-start(), calls=%async_computation.11 | async-start | bytes 9437184 | tf_op jit(solution)/shard_map/reduce_scatter | solution.py:740
  351.3 250.6 %reduce-scatter.9.cloned.1.call-start = ((), (), s32[]{:S(2)}) async-start(), calls=%async_computation.12 | async-start | bytes 1310720 | tf_op jit(solution)/shard_map/reduce_scatter | solution.py:761
  378.4 85.0 %collective-permute-start.18 = (bf16[512,1024]{1,0:T(8,128)(2,1)}, bf16[512,1024]{1,0:T(8,128)(2,1)S(1)}, u32[]{:S(2)}, u32[]{:S(2)}) collective-permute-start(bf16[512,1024]{1,0:T(8,128)(2,1)} %get-tuple-element.182), channel_id=1, source_target_pairs={{0,0},{1,1},{4,2},{5,3},{2,4},{3,5},{6,6},{7,7},{8,8},{9,9},{12,10... | collective-permute-start | bytes 3145736 | tf_op jit(solution)/shard_map/ppermute | solution.py:568
  380.6 82.9 %collective-permute-start.19 = (bf16[512,1024]{1,0:T(8,128)(2,1)S(1)}, bf16[512,1024]{1,0:T(8,128)(2,1)S(1)}, u32[]{:S(2)}, u32[]{:S(2)}) collective-permute-start(bf16[512,1024]{1,0:T(8,128)(2,1)S(1)} %get-tuple-element.183), channel_id=1, source_target_pairs={{1,0},{0,1},{5,2},{4,3},{3,4},{2,5},{7,6},{6,7},{9,8},{8,9},{13,10... | collective-permute-start | bytes 3145736 | tf_op jit(solution)/shard_map/ppermute | solution.py:569
  509.6 31.4 %collective-permute-start.21 = (bf16[512,1024]{1,0:T(8,128)(2,1)}, bf16[512,1024]{1,0:T(8,128)(2,1)}, u32[]{:S(2)}, u32[]{:S(2)}) collective-permute-start(bf16[512,1024]{1,0:T(8,128)(2,1)} %get-tuple-element.178), channel_id=1, source_target_pairs={{0,0},{1,1},{4,2},{5,3},{2,4},{3,5},{6,6},{7,7},{8,8},{9,9},{12,10... | collective-permute-start | bytes 3145736 | tf_op jit(solution)/shard_map/ppermute | solution.py:568
  519.0 54.5 %collective-permute-start.22 = (bf16[512,1024]{1,0:T(8,128)(2,1)}, bf16[512,1024]{1,0:T(8,128)(2,1)}, u32[]{:S(2)}, u32[]{:S(2)}) collective-permute-start(bf16[512,1024]{1,0:T(8,128)(2,1)} %get-tuple-element.179), channel_id=1, source_target_pairs={{1,0},{0,1},{5,2},{4,3},{3,4},{2,5},{7,6},{6,7},{9,8},{8,9},{13,10... | collective-permute-start | bytes 3145736 | tf_op jit(solution)/shard_map/ppermute | solution.py:569
  525.3 51.4 %collective-permute-start.24 = (bf16[128,4096]{1,0:T(8,128)(2,1)}, bf16[128,4096]{1,0:T(8,128)(2,1)}, u32[]{:S(2)}, u32[]{:S(2)}) collective-permute-start(bf16[128,4096]{1,0:T(8,128)(2,1)} %get-tuple-element.160), channel_id=1, source_target_pairs={{0,8},{8,0},{16,24},{24,16},{1,9},{9,1},{17,25},{25,17},{2,10},{10... | collective-permute-start | bytes 3145736 | tf_op jit(solution)/shard_map/ppermute | solution.py:730
  535.8 43.3 %collective-permute-start.25 = (bf16[128,4096]{1,0:T(8,128)(2,1)}, bf16[128,4096]{1,0:T(8,128)(2,1)}, u32[]{:S(2)}, u32[]{:S(2)}) collective-permute-start(bf16[128,4096]{1,0:T(8,128)(2,1)} %get-tuple-element.161), channel_id=1, source_target_pairs={{0,16},{8,24},{16,0},{24,8},{1,17},{9,25},{17,1},{25,9},{2,18},{10... | collective-permute-start | bytes 3145736 | tf_op jit(solution)/shard_map/ppermute | solution.py:730
  535.8 43.3 %collective-permute-start.26 = (bf16[128,4096]{1,0:T(8,128)(2,1)}, bf16[128,4096]{1,0:T(8,128)(2,1)}, u32[]{:S(2)}, u32[]{:S(2)}) collective-permute-start(bf16[128,4096]{1,0:T(8,128)(2,1)} %get-tuple-element.162), channel_id=1, source_target_pairs={{0,24},{8,16},{16,8},{24,0},{1,25},{9,17},{17,9},{25,1},{2,26},{10... | collective-permute-start | bytes 3145736 | tf_op jit(solution)/shard_map/ppermute | solution.py:730
  538.1 49.9 %all-to-all-start.1 = ((f32[32,4,128]{2,1,0:T(4,128)}), f32[32,4,128]{2,1,0:T(4,128)S(1)}, u32[]{:S(2)}, u32[]{:S(2)}) async-start(f32[32,4,128]{2,1,0:T(4,128)} %copy.107), calls=%async_computation.3 | async-start | bytes 131072 | tf_op jit(solution)/shard_map/all_to_all | solution.py:808
  540.7 108.1 %reduce-scatter.11.cloned.1.call-start = ((), (), s32[]{:S(2)}) async-start(), calls=%async_computation.13 | async-start | bytes 1310720 | tf_op jit(solution)/shard_map/reduce_scatter | solution.py:810
  598.3 48.8 %all-to-all-start.2 = ((bf16[4,32,4096]{2,1,0:T(8,128)(2,1)}), bf16[4,32,4096]{2,1,0:T(8,128)(2,1)S(1)}, u32[]{:S(2)}, u32[]{:S(2)}) async-start(bf16[4,32,4096]{2,1,0:T(8,128)(2,1)} %bitcast.83), calls=%async_computation.4 | async-start | bytes 2097152 | tf_op jit(solution)/shard_map/all_to_all | solution.py:814
  (50 other events, 598.3 us)
Sparse Core Ops, SparseCore 0:
  25.9 36.9 all-gather.4
  64.9 54.5 all-gather.6
  140.5 120.4 all-gather.8
  350.8 74.8 reduce-scatter.4
  429.4 71.2 reduce-scatter.6
  506.6 51.7 reduce-scatter.8
  598.5 46.6 reduce-scatter.10

commit v12 on v11

--- a/solution.py
+++ b/solution.py
@@ -628,7 +628,6 @@
     (resid_in,) = rowwise(
         merge_kernel, frames, [("", x), ("", s), ("weight", skip_top), ("weight", skip_bottom)], [(width, bf16)], light=True
     )
-    stacked = jnp.concatenate([x, s], axis=1)
 
     labels_own = segment_ids[:, 0]
     labels_other = lax.ppermute(labels_own, "core", swap)
@@ -677,8 +676,8 @@
     shift_one, scale_one, shift_two, scale_two = (modulation[:, i] for i in range(4))
 
     resid_in = to_rows(resid_in.reshape(inputs.shape))
-    resid_in, late, cotangent, stacked, modulation, cosine, sine, ranges = lax.optimization_barrier(
-        (resid_in, late, cotangent, stacked, modulation, cosine, sine, ranges)
+    resid_in, late, cotangent, modulation, cosine, sine, ranges = lax.optimization_barrier(
+        (resid_in, late, cotangent, modulation, cosine, sine, ranges)
     )
     (normed_one,) = rowwise(
         norm_kernel,
@@ -688,6 +687,8 @@
         light=True,
     )
     normed_row = frames_to_row(normed_one)
+    normed_row, x, s = lax.optimization_barrier((normed_row, x, s))
+    stacked = jnp.concatenate([x, s], axis=1)
     if in_place:
         projected = project(normed_row, middle, 0, out_rows, heads_wide, member)
     else:
@@ -712,6 +713,7 @@
         [(width, f32), (width, bf16)],
         flops=2 * frames * width * width,
     )
+    normed_two, stacked = lax.optimization_barrier((normed_two, stacked))
     result, grad_normed_two, grad_up, grad_down = feed_forward_and_back(
         normed_two, cot, resid_mid, hidden, chunk, up_weight, down_weight
     )

time: 670 us -> 671 us (level)
  Pallas kernels: 290 us -> 277 us
  starting transfers between devices: 107 us -> 118 us
    ppermute x2, waiting for transfers between devices: 32.6 us -> 0.74 us  [from_rows(): lax.ppermute(lax.dynamic_index_in_dim(value, 1 - high % 2, 0, False), LIN...]
    ppermute x9, waiting for transfers between devices: 22.6 us -> 53.6 us  [exchange(): lax.ppermute(sent, axes, [(i, i ^ flip) for i in range(count)]).astype(f32)]
    ppermute x9, starting transfers between devices: 23 us -> 31.8 us  [exchange(): lax.ppermute(sent, axes, [(i, i ^ flip) for i in range(count)]).astype(f32)]
    pallas_call x1, Pallas kernels: 81 us -> 72.7 us  [attend_backward(): pl.pallas_call(attend_backward_kernel, grid_spec=pltpu.PrefetchScalarGrid...]
    unnamed x70 -> x64, local copies, waits for them, and re-layouts: 14.6 us -> 13.6 us
  transfers between devices with their start and end apart: 44 -> 44, of which waited for: 15 -> 12; matrix products, arithmetic and copies ran while one was open for 17% -> 17% of each run, Pallas kernels for 34% -> 32%
where the time goes in v12:
time: 671 us; the launch traced here: 664 us
  Pallas kernels  277 us (41%)
  waiting for transfers between devices  124 us (18%)
  starting transfers between devices  118 us (18%)
  other arithmetic  52.7 us (8%)
  local copies, waits for them, and re-layouts  44.2 us (7%)
  matrix products  23.1 us (3%)
  between operations  15.1 us (2%)
  blocking collectives  8.92 us (1%)
    pallas_call x1, Pallas kernels, attend_backward(): pl.pallas_call(attend_backward_kernel, grid_spec=pltpu.PrefetchScalarGrid...  72.7 us
    pallas_call x1, Pallas kernels, feed_forward_and_back(): pl.pallas_call(feed_kernel, grid=(hidden // piece,), in_specs=[whole(), w...  66.3 us
    pallas_call x1, Pallas kernels, attend_forward(): pl.pallas_call(attend_forward_kernel, grid_spec=pltpu.PrefetchScalarGridS...  60.1 us
    ppermute x9, waiting for transfers between devices, share_on_line(): lax.ppermute(value, ('hi', 'lo'), [(i, i ^ flip) for i in range(line)])  58.9 us
    ppermute x9, waiting for transfers between devices, exchange(): lax.ppermute(sent, axes, [(i, i ^ flip) for i in range(count)]).astype(f32)  53.6 us
    pallas_call x6, Pallas kernels, rowwise(): pl.pallas_call(kernel, grid=(frames // tile,), in_specs=in_specs, out_spe...  50.7 us
    ppermute x9, starting transfers between devices, exchange(): lax.ppermute(sent, axes, [(i, i ^ flip) for i in range(count)]).astype(f32)  31.8 us
    ppermute x1, starting transfers between devices, frames_to_row(): other = lax.ppermute(value, 'core', swap)  20.1 us
  transfers between devices with their start and end apart: 44, of which 12 were waited for; matrix products, arithmetic and copies ran while one was open for 17% of the time, Pallas kernels for 32%

profile of v12, /device:TPU:0, one launch (start us, length us, event | category | flops | bytes accessed | tf_op | source)
XLA Modules:
  0.0 663.7 jit_solution(1125784959605140164)
XLA Ops:
  37.1 12.2 %collective-permute-done.11 = bf16[128,1024]{1,0:T(8,128)(2,1)S(1)} collective-permute-done((bf16[128,1024]{1,0:T(8,128)(2,1)S(1)}, bf16[128,1024]{1,0:T(8,128)(2,1)S(1)}, u32[]{:S(2)}, u32[]{:S(2)}) %collective-permute-start.11) | collective-permute-done | bytes 262176 | tf_op jit(solution)/shard_map/ppermute | solution.py:596
  50.8 8.9 %all-gather = s32[16,1,4]{2,1,0:T(1,128)S(1)} all-gather(s32[2,1,4]{2,1,0:T(1,128)S(1)} %copy-done.26), channel_id=2, replica_groups=mesh['plane'=4,'core'=2,'hi'=4,'lo'=1] {'plane','core'}, dimensions={0}, use_global_device_ids=true | all-gather | bytes 288 | tf_op jit(solution)/shard_map/all_gather | solution.py:654
  75.0 8.6 %shard_map.178 = bf16[1024,1024]{1,0:T(8,128)(2,1)} custom-call(bf16[1024,1024]{1,0:T(8,128)(2,1)} %bitcast.168, bf16[1024,1024]{1,0:T(8,128)(2,1)} %bitcast.170, bf16[32,64,1024]{2,1,0:T(8,128)(2,1)} %all-gather.5.cloned.1.call-done.top_ref.bottom_ref, bf16[32,64,1024]{2,1,0:T(8,128)(2,1)} %all-gather.5.cloned.1.call-done.top_ref.bottom_ref), custom_call_target="tpu_custom_call" | custom-call | flops 1 | bytes 1 | tf_op jit(solution)/shard_map/pallas_call | solution.py:223
  92.2 37.4 %collective-permute-done.6 = bf16[256,1024]{1,0:T(8,128)(2,1)} collective-permute-done((bf16[256,1024]{1,0:T(8,128)(2,1)}, bf16[256,1024]{1,0:T(8,128)(2,1)}, u32[]{:S(2)}, u32[]{:S(2)}) %collective-permute-start.6) | collective-permute-done | bytes 524320 | tf_op jit(solution)/shard_map/ppermute | solution.py:596
  143.6 20.1 %collective-permute-start.9 = (bf16[1024,1024]{1,0:T(8,128)(2,1)}, bf16[1024,1024]{1,0:T(8,128)(2,1)}, u32[]{:S(2)}, u32[]{:S(2)}) collective-permute-start(bf16[1024,1024]{1,0:T(8,128)(2,1)} %shard_map.179), channel_id=1, source_target_pairs={{0,4},{4,0},{1,5},{5,1},{2,6},{6,2},{3,7},{7,3},{8,12},{12,8},{9,1... | collective-permute-start | bytes 6291464 | tf_op jit(solution)/shard_map/ppermute | solution.py:576
  170.1 12.0 %collective-permute-start.15 = (bf16[512,1024]{1,0:T(8,128)(2,1)}, bf16[512,1024]{1,0:T(8,128)(2,1)S(1)}, u32[]{:S(2)}, u32[]{:S(2)}) collective-permute-start(bf16[512,1024]{1,0:T(8,128)(2,1)} %get-tuple-element.195), channel_id=1, source_target_pairs={{0,1},{1,0},{2,5},{3,4},{4,3},{5,2},{6,7},{7,6},{8,9},{9,8},{10,13... | collective-permute-start | bytes 3145736 | tf_op jit(solution)/shard_map/ppermute | solution.py:563
  186.7 11.0 %shard_map.180.q_ref.k_ref.v_ref = bf16[2048,1536]{1,0:T(8,128)(2,1)} custom-call(s32[1]{0:T(128)} %bitcast.21.place_ref, bf16[2048,1024]{1,0:T(8,128)(2,1)} %pad_maximum_fusion.x_ref, bf16[32,128,1024]{2,1,0:T(8,128)(2,1)} %all-gather.7.cloned.1.call-done.w_ref.q_ref.k_ref.v_ref), custom_call_target="tpu_custom_call" | custom-call | flops 1 | bytes 1 | tf_op jit(solution)/shard_map/pallas_call | solution.py:151
  197.7 60.1 %shard_map.181 = (bf16[2048,512]{1,0:T(8,128)(2,1)}, bf16[2048,512]{1,0:T(8,128)(2,1)}, bf16[2048,512]{1,0:T(8,128)(2,1)}, f32[4,2,2048]{2,1,0:T(2,128)}) custom-call(s32[2,8]{1,0:T(2,128)} %pad_add_fusion.range_ref, bf16[2048,1536]{1,0:T(8,128)(2,1)} %shard_map.180.q_ref.k_ref.v_ref, bf16[2048,1536]{1,0:T(8,128)(2,1)} %shard_map.180.q_ref.k_ref.v_ref, ...), custom_call_target="tpu_custom_call" | custom-call | flops 17179869184 | bytes 14680064 | tf_op jit(solution)/shard_map/pallas_call | solution.py:316
  269.1 8.2 %shard_map.182 = (f32[1024,1024]{1,0:T(8,128)}, bf16[1024,1024]{1,0:T(8,128)(2,1)}) custom-call(bf16[1024,1024]{1,0:T(8,128)(2,1)} %pad_maximum_fusion.5.mixed_ref, bf16[32,128,1024]{2,1,0:T(8,128)(2,1)} %all-gather.7.cloned.1.call-done.w_ref.q_ref.k_ref.v_ref, bf16[1024,1024]{1,0:T(8,128)(2,1)} %pad_maximum_fusion.2.resid_ref.resid_in_ref, ...), custom_call_target="tpu_custom_call" | custom-call | flops 2147483648 | bytes 18911232 | tf_op jit(solution)/shard_map/pallas_call | solution.py:223
  277.2 66.3 %shard_map.183 = (bf16[1024,1024]{1,0:T(8,128)(2,1)}, f32[1024,1024]{1,0:T(8,128)}, bf16[1024,4096]{1,0:T(8,128)(2,1)}, bf16[4096,1024]{1,0:T(8,128)(2,1)}) custom-call(bf16[1024,1024]{1,0:T(8,128)(2,1)} %get-tuple-element.68.n_ref, bf16[1024,1024]{1,0:T(8,128)(2,1)} %pad_maximum_fusion.6.cot_ref, f32[1024,1024]{1,0:T(8,128)} %get-tuple-element.70.resid_ref, ...), custom_call_target="tpu_custom_call" | custom-call | flops 51539607552 | bytes 50331648 | tf_op jit(solution)/shard_map/pallas_call | solution.py:507
  344.3 10.5 %shard_map.184 = (f32[1024,1024]{1,0:T(8,128)}, bf16[1024,1024]{1,0:T(8,128)(2,1)}, bf16[1024,1024]{1,0:T(8,128)(2,1)}, f32[8,1024]{1,0:T(8,128)}, f32[8,1024]{1,0:T(8,128)}) custom-call(f32[1024,1024]{1,0:T(8,128)} %get-tuple-element.72.g_ref, f32[1024,1024]{1,0:T(8,128)} %get-tuple-element.70.resid_ref, bf16[1024,1024]{1,0:T(8,128)(2,1)} %pad_maximum_fusion.6.cot_ref, ...), custom_call_target="tpu_custom_call" | custom-call | flops 1 | bytes 1 | tf_op jit(solution)/shard_map/pallas_call | solution.py:223
  374.1 72.7 %shard_map.185.dq_ref.dk_ref.dv_ref = bf16[2048,1536]{1,0:T(8,128)(2,1)} custom-call(s32[2,8]{1,0:T(2,128)} %pad_add_fusion.range_ref, bf16[2048,512]{1,0:T(8,128)(2,1)} %get-tuple-element.62.q_ref, bf16[2048,512]{1,0:T(8,128)(2,1)} %get-tuple-element.63.k_ref, bf16[2048,1536]{1,0:T(8,128)(2,1)} %shard_map.180.q_ref.k_ref.v_ref, ...), custom_call_target="tpu_custom_call" | custom-call | flops 42949672960 | bytes 16777216 | tf_op jit(solution)/shard_map/pallas_call | solution.py:420
  448.5 8.2 %shard_map.187 = bf16[1024,1024]{1,0:T(8,128)(2,1)} custom-call(s32[2]{0:T(128)} %pad_add_fusion.2.place_ref, bf16[2048,1536]{1,0:T(8,128)(2,1)} %shard_map.185.dq_ref.dk_ref.dv_ref, bf16[2048,1536]{1,0:T(8,128)(2,1)} %shard_map.185.dq_ref.dk_ref.dv_ref, bf16[2048,1536]{1,0:T(8,128)(2,1)} %shard_map.185.dq_ref.dk_ref.dv_ref, ...), custom_call_target="tpu_custom_call" | custom-call | flops 3221225472 | bytes 8388608 | tf_op jit(solution)/shard_map/pallas_call | solution.py:186
  456.7 9.2 %collective-permute-start.20 = (bf16[1024,1024]{1,0:T(8,128)(2,1)}, bf16[1024,1024]{1,0:T(8,128)(2,1)S(1)}, u32[]{:S(2)}, u32[]{:S(2)}) collective-permute-start(bf16[1024,1024]{1,0:T(8,128)(2,1)} %shard_map.187), channel_id=1, source_target_pairs={{0,4},{4,0},{1,5},{5,1},{2,6},{6,2},{3,7},{7,3},{8,12},{12,8},{9,1... | collective-permute-start | bytes 6291464 | tf_op jit(solution)/shard_map/ppermute | solution.py:777
  466.4 8.2 %shard_map.186.own_ref = f32[1024,1024]{1,0:T(8,128)} custom-call(s32[2]{0:T(128)} %pad_add_fusion.1.place_ref, bf16[2048,1536]{1,0:T(8,128)(2,1)} %shard_map.185.dq_ref.dk_ref.dv_ref, bf16[2048,1536]{1,0:T(8,128)(2,1)} %shard_map.185.dq_ref.dk_ref.dv_ref, bf16[2048,1536]{1,0:T(8,128)(2,1)} %shard_map.185.dq_ref.dk_ref.dv_ref, ...), custom_call_target="tpu_custom_call" | custom-call | flops 3221225472 | bytes 8388608 | tf_op jit(solution)/shard_map/pallas_call | solution.py:186
  475.9 9.5 %shard_map.188 = (bf16[1024,1024]{1,0:T(8,128)(2,1)}, f32[8,1024]{1,0:T(8,128)}, f32[8,1024]{1,0:T(8,128)}) custom-call(f32[1024,1024]{1,0:T(8,128)} %shard_map.186.own_ref, bf16[1024,1024]{1,0:T(8,128)(2,1)} %copy-done.14, bf16[1024,1024]{1,0:T(8,128)(2,1)} %pad_maximum_fusion.2.resid_ref.resid_in_ref, f32[1024,1024]{1,0:T(8,128)} %get-tuple-element.82.mid_ref, ...), custom_call_target="tpu_custom_call" | custom-call | bytes 14704640 | tf_op jit(solution)/shard_map/pallas_call | solution.py:223
  485.4 10.3 %convolution_convert_fusion = bf16[1024,1536]{1,0:T(8,128)(2,1)S(1)} fusion(bf16[2048,1024]{1,0:T(8,128)(2,1)} %pad_maximum_fusion.x_ref, bf16[2048,1536]{1,0:T(8,128)(2,1)} %shard_map.185.dq_ref.dk_ref.dv_ref), kind=kOutput, calls=%fused_computation.12 | convolution fusion | flops 6444023808 | bytes 13631488 | tf_op jit(solution)/shard_map/dot_general | solution.py:789
  500.3 9.5 %collective-permute-start.21 = (bf16[512,1024]{1,0:T(8,128)(2,1)}, bf16[512,1024]{1,0:T(8,128)(2,1)}, u32[]{:S(2)}, u32[]{:S(2)}) collective-permute-start(bf16[512,1024]{1,0:T(8,128)(2,1)} %get-tuple-element.186), channel_id=1, source_target_pairs={{0,0},{1,1},{4,2},{5,3},{2,4},{3,5},{6,6},{7,7},{8,8},{9,9},{12,10... | collective-permute-start | bytes 3145736 | tf_op jit(solution)/shard_map/ppermute | solution.py:568
  518.3 16.4 %collective-permute-start.25 = (bf16[128,4096]{1,0:T(8,128)(2,1)}, bf16[128,4096]{1,0:T(8,128)(2,1)}, u32[]{:S(2)}, u32[]{:S(2)}) collective-permute-start(bf16[128,4096]{1,0:T(8,128)(2,1)} %get-tuple-element.169), channel_id=1, source_target_pairs={{0,16},{8,24},{16,0},{24,8},{1,17},{9,25},{17,1},{25,9},{2,18},{10... | collective-permute-start | bytes 3145736 | tf_op jit(solution)/shard_map/ppermute | solution.py:732
  543.1 33.0 %collective-permute-done.25 = bf16[128,4096]{1,0:T(8,128)(2,1)} collective-permute-done((bf16[128,4096]{1,0:T(8,128)(2,1)}, bf16[128,4096]{1,0:T(8,128)(2,1)}, u32[]{:S(2)}, u32[]{:S(2)}) %collective-permute-start.25) | collective-permute-done | bytes 1048608 | tf_op jit(solution)/shard_map/ppermute | solution.py:732
  579.7 7.7 %all-to-all-done.1 = f32[32,4,128]{2,1,0:T(4,128)S(1)} async-done(((f32[32,4,128]{2,1,0:T(4,128)}), f32[32,4,128]{2,1,0:T(4,128)S(1)}, u32[]{:S(2)}, u32[]{:S(2)}) %all-to-all-start.1) | async-done | bytes 65568 | tf_op jit(solution)/shard_map/all_to_all | solution.py:810
  587.4 7.4 %convolution_convert_fusion.1 = bf16[2048,1024]{1,0:T(8,128)(2,1)S(1)} fusion(bf16[1024,2048]{1,0:T(8,128)(2,1)} %pad_maximum_fusion.1, bf16[1024,1024]{1,0:T(8,128)(2,1)} %bitcast.181), kind=kOutput, calls=%fused_computation.13 | convolution fusion | flops 4297064448 | bytes 10485760 | tf_op jit(solution)/shard_map/dot_general | solution.py:822
  614.6 8.4 %shard_map.189 = (bf16[1024,1024]{1,0:T(8,128)(2,1)}, bf16[1024,1024]{1,0:T(8,128)(2,1)}) custom-call(bf16[1024,1024]{1,0:T(8,128)(2,1)} %bitcast.182, bf16[32,64,1024]{2,1,0:T(8,128)(2,1)} %all-gather.5.cloned.1.call-done.top_ref.bottom_ref, bf16[32,64,1024]{2,1,0:T(8,128)(2,1)} %all-gather.5.cloned.1.call-done.top_ref.bottom_ref), custom_call_target="tpu_custom_call" | custom-call | flops 4294967296 | bytes 14680064 | tf_op jit(solution)/shard_map/pallas_call | solution.py:223
  623.1 14.0 %collective-permute-done.30 = bf16[256,1024]{1,0:T(8,128)(2,1)} collective-permute-done((bf16[256,1024]{1,0:T(8,128)(2,1)}, bf16[256,1024]{1,0:T(8,128)(2,1)}, u32[]{:S(2)}, u32[]{:S(2)}) %collective-permute-start.30) | collective-permute-done | bytes 524320 | tf_op jit(solution)/shard_map/ppermute | solution.py:732
  (243 shorter events, 178.7 us)
Async XLA Ops:
  7.2 67.8 %all-gather.5.cloned.1.call-start = ((), (), s32[]{:S(2)}) async-start(), calls=%async_computation.7 | async-start | bytes 4718592 | tf_op jit(solution)/shard_map/all_gather | solution.py:601
  25.8 160.9 %all-gather.7.cloned.1.call-start = ((), (), s32[]{:S(2)}) async-start(), calls=%async_computation.8 | async-start | bytes 9437184 | tf_op jit(solution)/shard_map/all_gather | solution.py:601
  61.4 74.6 %all-to-all-start = ((f32[32,4,128]{2,1,0:T(4,128)}), f32[32,4,128]{2,1,0:T(4,128)S(1)}, u32[]{:S(2)}, u32[]{:S(2)}) async-start(f32[32,4,128]{2,1,0:T(4,128)} %bitcast.14), calls=%async_computation | async-start | bytes 131072 | tf_op jit(solution)/shard_map/all_to_all | solution.py:663
  64.6 212.6 %all-gather.9.cloned.1.call-start = ((), (), s32[]{:S(2)}) async-start(), calls=%async_computation.9 | async-start | bytes 18874368 | tf_op jit(solution)/shard_map/all_gather | solution.py:601
  74.3 55.4 %collective-permute-start.6 = (bf16[256,1024]{1,0:T(8,128)(2,1)}, bf16[256,1024]{1,0:T(8,128)(2,1)}, u32[]{:S(2)}, u32[]{:S(2)}) collective-permute-start(bf16[256,1024]{1,0:T(8,128)(2,1)} %slice_dynamic-update-slice_fusion.6), channel_id=1, source_target_pairs={{0,2},{1,3},{2,0},{3,1},{4,6},{5,7},{6,4},{7,5},{8,10},{9,11},{10,... | collective-permute-start | bytes 1572872 | tf_op jit(solution)/shard_map/ppermute | solution.py:596
  74.3 55.4 %collective-permute-start.5 = (bf16[256,1024]{1,0:T(8,128)(2,1)}, bf16[256,1024]{1,0:T(8,128)(2,1)}, u32[]{:S(2)}, u32[]{:S(2)}) collective-permute-start(bf16[256,1024]{1,0:T(8,128)(2,1)} %slice_dynamic-update-slice_fusion.6), channel_id=1, source_target_pairs={{0,1},{1,0},{2,3},{3,2},{4,5},{5,4},{6,7},{7,6},{8,9},{9,8},{10,11... | collective-permute-start | bytes 1572872 | tf_op jit(solution)/shard_map/ppermute | solution.py:596
  86.6 46.5 %collective-permute-start.3 = (bf16[512,1024]{1,0:T(8,128)(2,1)}, bf16[512,1024]{1,0:T(8,128)(2,1)S(1)}, u32[]{:S(2)}, u32[]{:S(2)}) collective-permute-start(bf16[512,1024]{1,0:T(8,128)(2,1)} %get-tuple-element.202), channel_id=1, source_target_pairs={{0,0},{1,1},{2,4},{3,5},{4,2},{5,3},{6,6},{7,7},{8,8},{9,9},{10,12... | collective-permute-start | bytes 3145736 | tf_op jit(solution)/shard_map/ppermute | solution.py:562
  88.5 44.7 %collective-permute-start.4 = (bf16[512,1024]{1,0:T(8,128)(2,1)}, bf16[512,1024]{1,0:T(8,128)(2,1)}, u32[]{:S(2)}, u32[]{:S(2)}) collective-permute-start(bf16[512,1024]{1,0:T(8,128)(2,1)} %get-tuple-element.203), channel_id=1, source_target_pairs={{0,1},{1,0},{2,5},{3,4},{4,3},{5,2},{6,7},{7,6},{8,9},{9,8},{10,13... | collective-permute-start | bytes 3145736 | tf_op jit(solution)/shard_map/ppermute | solution.py:563
  136.2 312.3 %reduce-scatter.5.cloned.1.call-start = ((), (), s32[]{:S(2)}) async-start(), calls=%async_computation.10 | async-start | bytes 9437184 | tf_op jit(solution)/shard_map/reduce_scatter | solution.py:742
  143.6 38.6 %collective-permute-start.9 = (bf16[1024,1024]{1,0:T(8,128)(2,1)}, bf16[1024,1024]{1,0:T(8,128)(2,1)}, u32[]{:S(2)}, u32[]{:S(2)}) collective-permute-start(bf16[1024,1024]{1,0:T(8,128)(2,1)} %shard_map.179), channel_id=1, source_target_pairs={{0,4},{4,0},{1,5},{5,1},{2,6},{6,2},{3,7},{7,3},{8,12},{12,8},{9,1... | collective-permute-start | bytes 6291464 | tf_op jit(solution)/shard_map/ppermute | solution.py:576
  168.0 93.4 %collective-permute-start.14 = (bf16[512,1024]{1,0:T(8,128)(2,1)}, bf16[512,1024]{1,0:T(8,128)(2,1)S(1)}, u32[]{:S(2)}, u32[]{:S(2)}) collective-permute-start(bf16[512,1024]{1,0:T(8,128)(2,1)} %get-tuple-element.194), channel_id=1, source_target_pairs={{0,0},{1,1},{2,4},{3,5},{4,2},{5,3},{6,6},{7,7},{8,8},{9,9},{10,12... | collective-permute-start | bytes 3145736 | tf_op jit(solution)/shard_map/ppermute | solution.py:562
  170.1 91.3 %collective-permute-start.15 = (bf16[512,1024]{1,0:T(8,128)(2,1)}, bf16[512,1024]{1,0:T(8,128)(2,1)S(1)}, u32[]{:S(2)}, u32[]{:S(2)}) collective-permute-start(bf16[512,1024]{1,0:T(8,128)(2,1)} %get-tuple-element.195), channel_id=1, source_target_pairs={{0,1},{1,0},{2,5},{3,4},{4,3},{5,2},{6,7},{7,6},{8,9},{9,8},{10,13... | collective-permute-start | bytes 3145736 | tf_op jit(solution)/shard_map/ppermute | solution.py:563
  343.6 236.1 %reduce-scatter.7.cloned.1.call-start = ((), (), s32[]{:S(2)}) async-start(), calls=%async_computation.11 | async-start | bytes 9437184 | tf_op jit(solution)/shard_map/reduce_scatter | solution.py:742
  357.4 243.8 %reduce-scatter.9.cloned.1.call-start = ((), (), s32[]{:S(2)}) async-start(), calls=%async_computation.12 | async-start | bytes 1310720 | tf_op jit(solution)/shard_map/reduce_scatter | solution.py:763
  372.2 74.6 %collective-permute-start.18 = (bf16[512,1024]{1,0:T(8,128)(2,1)}, bf16[512,1024]{1,0:T(8,128)(2,1)S(1)}, u32[]{:S(2)}, u32[]{:S(2)}) collective-permute-start(bf16[512,1024]{1,0:T(8,128)(2,1)} %get-tuple-element.190), channel_id=1, source_target_pairs={{0,0},{1,1},{4,2},{5,3},{2,4},{3,5},{6,6},{7,7},{8,8},{9,9},{12,10... | collective-permute-start | bytes 3145736 | tf_op jit(solution)/shard_map/ppermute | solution.py:568
  374.1 72.7 %collective-permute-start.19 = (bf16[512,1024]{1,0:T(8,128)(2,1)S(1)}, bf16[512,1024]{1,0:T(8,128)(2,1)S(1)}, u32[]{:S(2)}, u32[]{:S(2)}) collective-permute-start(bf16[512,1024]{1,0:T(8,128)(2,1)S(1)} %get-tuple-element.191), channel_id=1, source_target_pairs={{1,0},{0,1},{5,2},{4,3},{3,4},{2,5},{7,6},{6,7},{9,8},{8,9},{13,10... | collective-permute-start | bytes 3145736 | tf_op jit(solution)/shard_map/ppermute | solution.py:569
  500.3 38.8 %collective-permute-start.21 = (bf16[512,1024]{1,0:T(8,128)(2,1)}, bf16[512,1024]{1,0:T(8,128)(2,1)}, u32[]{:S(2)}, u32[]{:S(2)}) collective-permute-start(bf16[512,1024]{1,0:T(8,128)(2,1)} %get-tuple-element.186), channel_id=1, source_target_pairs={{0,0},{1,1},{4,2},{5,3},{2,4},{3,5},{6,6},{7,7},{8,8},{9,9},{12,10... | collective-permute-start | bytes 3145736 | tf_op jit(solution)/shard_map/ppermute | solution.py:568
  509.8 30.1 %collective-permute-start.22 = (bf16[512,1024]{1,0:T(8,128)(2,1)}, bf16[512,1024]{1,0:T(8,128)(2,1)}, u32[]{:S(2)}, u32[]{:S(2)}) collective-permute-start(bf16[512,1024]{1,0:T(8,128)(2,1)} %get-tuple-element.187), channel_id=1, source_target_pairs={{1,0},{0,1},{5,2},{4,3},{3,4},{2,5},{7,6},{6,7},{9,8},{8,9},{13,10... | collective-permute-start | bytes 3145736 | tf_op jit(solution)/shard_map/ppermute | solution.py:569
  513.3 29.8 %collective-permute-start.24 = (bf16[128,4096]{1,0:T(8,128)(2,1)}, bf16[128,4096]{1,0:T(8,128)(2,1)}, u32[]{:S(2)}, u32[]{:S(2)}) collective-permute-start(bf16[128,4096]{1,0:T(8,128)(2,1)} %get-tuple-element.168), channel_id=1, source_target_pairs={{0,8},{8,0},{16,24},{24,16},{1,9},{9,1},{17,25},{25,17},{2,10},{10... | collective-permute-start | bytes 3145736 | tf_op jit(solution)/shard_map/ppermute | solution.py:732
  518.3 57.9 %collective-permute-start.25 = (bf16[128,4096]{1,0:T(8,128)(2,1)}, bf16[128,4096]{1,0:T(8,128)(2,1)}, u32[]{:S(2)}, u32[]{:S(2)}) collective-permute-start(bf16[128,4096]{1,0:T(8,128)(2,1)} %get-tuple-element.169), channel_id=1, source_target_pairs={{0,16},{8,24},{16,0},{24,8},{1,17},{9,25},{17,1},{25,9},{2,18},{10... | collective-permute-start | bytes 3145736 | tf_op jit(solution)/shard_map/ppermute | solution.py:732
  534.7 41.4 %collective-permute-start.26 = (bf16[128,4096]{1,0:T(8,128)(2,1)}, bf16[128,4096]{1,0:T(8,128)(2,1)}, u32[]{:S(2)}, u32[]{:S(2)}) collective-permute-start(bf16[128,4096]{1,0:T(8,128)(2,1)} %get-tuple-element.170), channel_id=1, source_target_pairs={{0,24},{8,16},{16,8},{24,0},{1,25},{9,17},{17,9},{25,1},{2,26},{10... | collective-permute-start | bytes 3145736 | tf_op jit(solution)/shard_map/ppermute | solution.py:732
  535.5 51.9 %all-to-all-start.1 = ((f32[32,4,128]{2,1,0:T(4,128)}), f32[32,4,128]{2,1,0:T(4,128)S(1)}, u32[]{:S(2)}, u32[]{:S(2)}) async-start(f32[32,4,128]{2,1,0:T(4,128)} %copy.107), calls=%async_computation.3 | async-start | bytes 131072 | tf_op jit(solution)/shard_map/all_to_all | solution.py:810
  538.8 109.9 %reduce-scatter.11.cloned.1.call-start = ((), (), s32[]{:S(2)}) async-start(), calls=%async_computation.13 | async-start | bytes 1310720 | tf_op jit(solution)/shard_map/reduce_scatter | solution.py:812
  597.7 49.4 %all-to-all-start.2 = ((bf16[4,32,4096]{2,1,0:T(8,128)(2,1)}), bf16[4,32,4096]{2,1,0:T(8,128)(2,1)S(1)}, u32[]{:S(2)}, u32[]{:S(2)}) async-start(bf16[4,32,4096]{2,1,0:T(8,128)(2,1)} %bitcast.83), calls=%async_computation.4 | async-start | bytes 2097152 | tf_op jit(solution)/shard_map/all_to_all | solution.py:816
  (47 other events, 629.7 us)
Sparse Core Ops, SparseCore 0:
  25.9 36.9 all-gather.4
  64.9 54.4 all-gather.6
  136.3 120.5 all-gather.8
  343.7 78.6 reduce-scatter.4
  426.1 71.2 reduce-scatter.6
  499.5 57.3 reduce-scatter.8
  597.8 46.4 reduce-scatter.10
